TPU v7x, 256 devices: a whole 4x4x8 slice. The times are simulated.
256 devices in a mesh: prow: 32 (over y, z), pcol: 8 (over x, core).
Axes of the slice: x: 4, y: 4, z: 8, core: 2. Of those that a mesh axis runs over, the one named last changes fastest.
Arguments:
- panel_rows: float32 [2, 1024, 98304], P(None, None, ('prow', 'pcol')), may hold values from -0.078125 to 0.078125
- solved: float32 [98304, 1024], P(('prow', 'pcol')), may hold values from -6 to 6
- right_side: float32 [2, 1024, 1024], P(None, 'prow', 'pcol'), may hold values from -6 to 6
- coupling: float32 [1024, 1024], P(None, 'prow'), may hold values from -0.1875 to 0.1875
- inverses: float32 [2, 1024, 1024], P(None, 'prow'), may hold values from -2 to 2, as said below
Outputs:
- panels: float32 [2, 1024, 1024], P(None, 'prow', 'pcol')
Inputs may be any that keep to these rules, and one draw needn't show every extreme that they name: `inverses`: each tile is zero above its diagonal, and its diagonal entries are positive.
All inputs are finite; a program needn't handle non-finite values.
Results may differ from a plain program's by a relative error of at most 0.000088.
Values sent between devices are 32-bit elements; how exact they have to be, the bound alone decides.
No kernel may reach another device: no remote copies, remote signals or barrier semaphores. Data moves between devices by JAX's collectives and lax.ppermute only.
A program may use at most 64 MiB of HBM per device.

v0:
```python
import jax
import jax.numpy as jnp
from jax import lax
from jax.experimental import pallas as pl
from jax.experimental.pallas import tpu as pltpu
from jax.sharding import Mesh
from jax.sharding import PartitionSpec as P


AXES = ("y", "z", "x", "core")
F32 = jnp.float32
BF16 = jnp.bfloat16
EXACT = lax.Precision.HIGHEST
SMEM = pl.BlockSpec(memory_space=pltpu.SMEM)
ORDER = pl.BlockSpec(memory_space=pl.ANY)
SMALL = pltpu.CompilerParams(vmem_limit_bytes=4 << 20)


def shift(value, axis, step, size):
    return lax.ppermute(value, axis, [(i, (i + step) % size) for i in range(size)])


def halves(value):
    high = value.astype(BF16)
    return high, (value - high.astype(F32)).astype(BF16)


def product_kernel(by_column, has_received, nx, ny):
    def kernel(place, rows, cols, *refs):
        received = refs[0] if has_received else None
        outs = refs[1:-2] if has_received else refs[:-2]
        left, right = refs[-2:]
        depth = rows.shape[1]
        high_rows = rows.shape[0] // ny
        for jx in range(nx):
            at = lax.rem(place[0] + jx, nx) * 256 + place[2] * 128
            high, low = halves(cols[:, pl.ds(pl.multiple_of(at, 128), 128)])
            span = slice(jx * 128, (jx + 1) * 128)
            right[0:depth, span] = high
            right[depth : 2 * depth, span] = low
            right[2 * depth : 3 * depth, span] = high
        for jy in range(ny):
            at = lax.rem(place[1] + jy, ny) * high_rows
            high, low = halves(rows[pl.ds(pl.multiple_of(at, high_rows), high_rows), :])
            left[:, 0:depth] = high
            left[:, depth : 2 * depth] = high
            left[:, 2 * depth : 3 * depth] = low
            value = jnp.dot(left[...], right[...], preferred_element_type=F32)
            for jx in range(nx):
                block = value[:, jx * 128 : (jx + 1) * 128]
                first, second = (jx, jy) if by_column else (jy, jx)
                span = slice(second * high_rows, (second + 1) * high_rows)
                if has_received:
                    outs[first][span, :] = block + received[first, span, :]
                else:
                    outs[0][first, span, :] = block

    return kernel


def products(place, panel, rows, cols, received, by_column, nx, ny):
    kernel = product_kernel(by_column, received is not None, nx, ny)
    _, size, depth = rows.shape
    first = nx if by_column else ny
    if received is None:
        shapes = jax.ShapeDtypeStruct((first, size, 128), F32)
        args = (place, rows, cols)
    else:
        shapes = [jax.ShapeDtypeStruct((size, 128), F32)] * first
        args = (place, rows, cols, received)
    return pl.pallas_call(
        kernel,
        out_shape=shapes,
        grid=(1,),
        in_specs=[
            SMEM,
            pl.BlockSpec((pl.Squeezed(), size, depth), lambda i: (panel, 0, 0)),
        ]
        + [pl.BlockSpec()] * (len(args) - 2),
        scratch_shapes=[
            pltpu.VMEM((size // ny, 3 * depth), BF16),
            pltpu.VMEM((3 * depth, nx * 128), BF16),
        ],
        compiler_params=pltpu.CompilerParams(vmem_limit_bytes=16 << 20),
        cost_estimate=pl.CostEstimate(
            flops=6 * size * depth * nx * 128, transcendentals=0, bytes_accessed=6 << 20
        ),
    )(*args)


def pack_kernel(place, inverses, across, out):
    at = pl.multiple_of(place[0] * 256 + place[2] * 128, 128)
    strip_of_coupling = across[:, pl.ds(at, 128)]
    strip_of_second = inverses[1, :, pl.ds(at, 128)]
    nz = out.shape[0]
    for z in range(nz):
        out[z, :, 0:128] = strip_of_coupling
        out[z, :, 128:256] = strip_of_second
        for panel in range(2):
            pieces = [inverses[panel, :, y * 256 + z * 32 : y * 256 + z * 32 + 32] for y in range(4)]
            out[z, :, 256 + panel * 128 : 384 + panel * 128] = jnp.concatenate(pieces, axis=1)


def couple_kernel(tiles, out):
    out[...] = lax.dot_general(
        tiles[:, 0:128],
        tiles[:, 256:384],
        (((0,), (0,)), ((), ())),
        precision=EXACT,
        preferred_element_type=F32,
    )


def chain_kernel(tiles, part0, part1, part2, part3, out):
    total = (part0[...] + part1[...]) + (part2[...] + part3[...])
    out[...] = jnp.dot(tiles[:, 128:256], total, precision=EXACT, preferred_element_type=F32)


def apply_kernel(place, tiles, mix0, mix1, mix2, mix3, rest0, rest1, rest2, rest3, out, first, second):
    ny = 4
    for step, rest in enumerate((rest0, rest1, rest2, rest3)):
        at = pl.multiple_of(lax.rem(place[1] + ny - step, ny) * 32, 32)
        first[pl.ds(at, 32), :] = rest[0:32, :]
        second[pl.ds(at, 32), :] = rest[32:64, :]
    mix = (mix0[...] + mix1[...]) + (mix2[...] + mix3[...])
    low = jnp.dot(tiles[:, 256:384], first[...], precision=EXACT, preferred_element_type=F32)
    high = jnp.dot(tiles[:, 384:512], second[...], precision=EXACT, preferred_element_type=F32)
    high = high - jnp.dot(mix, first[...], precision=EXACT, preferred_element_type=F32)
    for z in range(out.shape[0]):
        out[z, 0:32, :] = low[z * 32 : (z + 1) * 32, :]
        out[z, 32:64, :] = high[z * 32 : (z + 1) * 32, :]


def interleave_kernel(a0, a1, a2, a3, b0, b1, b2, b3, after, out):
    low = (a0[...] + a1[...]) + (a2[...] + a3[...])
    high = (b0[...] + b1[...]) + (b2[...] + b3[...])
    for z in range(out.shape[0]):
        out[z, 0:32, :] = low[z * 32 : (z + 1) * 32, :]
        out[z, 32:64, :] = high[z * 32 : (z + 1) * 32, :]


def summed_blocks(parts, count):
    rows = parts[0].shape[0] // count
    out = []
    for j in range(count):
        a, b, c, d = [part[j * rows : (j + 1) * rows] for part in parts]
        out.append((a + b) + (c + d))
    return out


def steps(panel_rows, solved, right_side, coupling, inverses):
    nx, ny, nz, nc = (lax.axis_size(a) for a in ("x", "y", "z", "core"))
    x, y, core = lax.axis_index("x"), lax.axis_index("y"), lax.axis_index("core")
    own = jnp.stack([x, y, core]).astype(jnp.int32)
    other = jnp.stack([x, y, 1 - core]).astype(jnp.int32)

    to_partner0 = products(other, 0, panel_rows, solved, None, True, nx, ny)
    from_partner0 = shift(to_partner0, "core", 1, nc)
    to_partner1 = products(other, 1, panel_rows, solved, None, False, nx, ny)
    from_partner1 = shift(to_partner1, "core", 1, nc)
    blocks0 = products(own, 0, panel_rows, solved, from_partner0, True, nx, ny)
    got0 = [blocks0[0]] + [shift(blocks0[j], "x", j, nx) for j in range(1, nx)]
    blocks1 = products(own, 1, panel_rows, solved, from_partner1, False, nx, ny)
    got1 = [blocks1[0]] + [shift(blocks1[j], "y", j, ny) for j in range(1, ny)]

    packed = pl.pallas_call(
        pack_kernel,
        out_shape=jax.ShapeDtypeStruct((nz, 32, 512), F32),
        in_specs=[SMEM, pl.BlockSpec(), pl.BlockSpec()],
        compiler_params=SMALL,
    )(own, inverses, coupling.T)
    tiles = lax.all_to_all(packed, "z", 0, 0, tiled=True).reshape(nz * 32, 512)
    coupled = pl.pallas_call(
        couple_kernel, out_shape=jax.ShapeDtypeStruct((128, 128), F32), compiler_params=SMALL
    )(tiles)
    coupled_all = [coupled] + [shift(coupled, "y", j, ny) for j in range(1, ny)]
    chained = pl.pallas_call(
        chain_kernel, out_shape=jax.ShapeDtypeStruct((256, 128), F32), compiler_params=SMALL
    )(
        tiles, *coupled_all
    )
    both = chained + shift(chained, "core", 1, nc)
    mixes = [both] + [shift(both, "x", j, nx) for j in range(1, nx)]

    sums0 = summed_blocks(got0, ny)
    again0 = [sums0[0]] + [shift(sums0[j], "y", j, ny) for j in range(1, ny)]
    sums1 = summed_blocks(got1, nx)
    again1 = [sums1[0]] + [shift(sums1[j], "x", j, nx) for j in range(1, nx)]
    by_z = pl.pallas_call(
        interleave_kernel,
        out_shape=jax.ShapeDtypeStruct((nz, 64, 128), F32),
        in_specs=[pl.BlockSpec()] * 8 + [ORDER],
        compiler_params=SMALL,
    )(*again0, *again1, chained)
    old = lax.all_to_all(by_z, "z", 0, 0, tiled=True).sum(axis=0)
    rest = right_side.reshape(64, 128) - old

    rests = [rest] + [shift(rest, "y", j, ny) for j in range(1, ny)]
    solved_part = pl.pallas_call(
        apply_kernel,
        out_shape=jax.ShapeDtypeStruct((nz, 64, 128), F32),
        in_specs=[SMEM] + [pl.BlockSpec()] * 9,
        scratch_shapes=[pltpu.VMEM((128, 128), F32), pltpu.VMEM((128, 128), F32)],
        compiler_params=SMALL,
    )(own, tiles, *mixes, *rests)
    panels = lax.all_to_all(solved_part, "z", 0, 0, tiled=True).sum(axis=0)
    return panels.reshape(right_side.shape)


def solution(mesh):
    finer = Mesh(mesh.devices.reshape(4, 8, 4, 2), AXES)
    prow, pcol = ("y", "z"), ("x", "core")
    return jax.shard_map(
        steps,
        mesh=finer,
        in_specs=(
            P(None, None, AXES),
            P(AXES, None),
            P(None, prow, pcol),
            P(None, prow),
            P(None, prow, None),
        ),
        out_specs=P(None, prow, pcol),
        check_vma=False,
    )
```

profile of v0, /device:TPU:2, one launch (start us, length us, event | category | flops | bytes accessed | tf_op | source)
XLA Modules:
  0.0 122.6 jit_solution(17380398363519545260)
XLA Ops:
  0.0 0.1 pad_add_fusion.2.place
  0.1 1.9 %copy-done = f32[2,1024,384]{2,1,0:T(8,128)S(1)} copy-done((f32[2,1024,384]{2,1,0:T(8,128)S(1)}, f32[2,1024,384]{2,1,0:T(8,128)}, u32[]{:S(2)}) %copy-start) | copy-done | bytes 3145752
  2.0 1.4 %copy-done.2 = f32[384,1024]{1,0:T(8,128)S(1)} copy-done((f32[384,1024]{1,0:T(8,128)S(1)}, f32[384,1024]{1,0:T(8,128)}, u32[]{:S(2)}) %copy-start.2) | copy-done | bytes 1572888
  3.4 3.7 %shard_map.60 = f32[4,1024,128]{2,1,0:T(8,128)} custom-call(s32[3]{0:T(128)S(1)} %pad_add_fusion.2.place, f32[2,1024,384]{2,1,0:T(8,128)S(1)} %copy-done, f32[384,1024]{1,0:T(8,128)S(1)} %copy-done.2), custom_call_target="tpu_custom_call" | custom-call | flops 1207959552 | bytes 6291456 | tf_op jit(solution)/shard_map/pallas_call | solution.py:71
  7.1 0.0 collective-permute-start.14
  7.1 3.7 %shard_map.58 = f32[4,1024,128]{2,1,0:T(8,128)} custom-call(s32[3]{0:T(128)S(1)} %pad_add_fusion.2.place, f32[2,1024,384]{2,1,0:T(8,128)S(1)} %copy-done, f32[384,1024]{1,0:T(8,128)S(1)} %copy-done.2), custom_call_target="tpu_custom_call" | custom-call | flops 1207959552 | bytes 6291456 | tf_op jit(solution)/shard_map/pallas_call | solution.py:71
  10.8 0.5 collective-permute-start.7
  11.3 0.1 pad_add_fusion.place
  11.4 0.8 shard_map.55
  12.2 0.8 copy-done.4
  13.0 8.5 %all-to-all-start = ((f32[8,32,512]{2,1,0:T(8,128)}), f32[8,32,512]{2,1,0:T(8,128)}, u32[]{:S(2)}, u32[]{:S(2)}) async-start(f32[8,32,512]{2,1,0:T(8,128)} %copy-done.4), calls=%async_computation | async-start | bytes 1048576 | tf_op jit(solution)/shard_map/all_to_all | solution.py:172
  21.5 0.0 collective-permute-done.14.refs_0_
  21.5 0.0 copy-start.3
  21.5 1.4 %copy-done.3 = f32[384,1024]{1,0:T(8,128)S(1)} copy-done((f32[384,1024]{1,0:T(8,128)S(1)}, f32[384,1024]{1,0:T(8,128)}, u32[]{:S(2)}) %copy-start.3) | copy-done | bytes 1572888
  22.9 4.2 %shard_map.61 = (f32[1024,128]{1,0:T(8,128)S(1)}, f32[1024,128]{1,0:T(8,128)S(1)}, f32[1024,128]{1,0:T(8,128)}, f32[1024,128]{1,0:T(8,128)}) custom-call(s32[3]{0:T(128)S(1)} %pad_add_fusion.place, f32[2,1024,384]{2,1,0:T(8,128)S(1)} %copy-done.1, f32[384,1024]{1,0:T(8,128)S(1)} %copy-done.3, f32[4,1024,128]{2,1,0:T(8,128)} %collective-permute-done.14.refs_0_), custom_call_target="tpu_custom_call" | custom-call | flops 1207959552 | bytes 6291456 | tf_op jit(solution)/shard_map/pallas_call | solution.py:71
  27.1 0.8 copy-done.7
  27.9 1.6 %collective-permute-start.15 = (f32[1024,128]{1,0:T(8,128)S(1)}, f32[1024,128]{1,0:T(8,128)S(1)}, u32[]{:S(2)}, u32[]{:S(2)}) collective-permute-start(f32[1024,128]{1,0:T(8,128)S(1)} %get-tuple-element.18), channel_id=1, source_target_pairs={{0,64},{64,128},{128,192},{192,0},{1,65},{65,129},{129,193},{193,1... | collective-permute-start | bytes 1572872 | tf_op jit(solution)/shard_map/ppermute | solution.py:20
  29.5 2.9 %collective-permute-start.16 = (f32[1024,128]{1,0:T(8,128)}, f32[1024,128]{1,0:T(8,128)}, u32[]{:S(2)}, u32[]{:S(2)}) collective-permute-start(f32[1024,128]{1,0:T(8,128)} %get-tuple-element.19), channel_id=1, source_target_pairs={{0,128},{64,192},{128,0},{192,64},{1,129},{65,193},{129,1},{193,65... | collective-permute-start | bytes 1572872 | tf_op jit(solution)/shard_map/ppermute | solution.py:20
  32.4 1.3 %collective-permute-start.17 = (f32[1024,128]{1,0:T(8,128)}, f32[1024,128]{1,0:T(8,128)}, u32[]{:S(2)}, u32[]{:S(2)}) collective-permute-start(f32[1024,128]{1,0:T(8,128)} %get-tuple-element.20), channel_id=1, source_target_pairs={{0,192},{64,0},{128,64},{192,128},{1,193},{65,1},{129,65},{193,129... | collective-permute-start | bytes 1572872 | tf_op jit(solution)/shard_map/ppermute | solution.py:20
  33.7 0.0 collective-permute-done.7.refs_0_
  33.7 4.7 %shard_map.59 = (f32[1024,128]{1,0:T(8,128)S(1)}, f32[1024,128]{1,0:T(8,128)}, f32[1024,128]{1,0:T(8,128)}, f32[1024,128]{1,0:T(8,128)}) custom-call(s32[3]{0:T(128)S(1)} %pad_add_fusion.place, f32[2,1024,384]{2,1,0:T(8,128)S(1)} %copy-done.1, f32[384,1024]{1,0:T(8,128)S(1)} %copy-done.3, f32[4,1024,128]{2,1,0:T(8,128)} %collective-permute-done.7.refs_0_), custom_call_target="tpu_custom_call" | custom-call | flops 1207959552 | bytes 6291456 | tf_op jit(solution)/shard_map/pallas_call | solution.py:71
  38.4 0.8 copy-done.5
  39.2 0.5 collective-permute-start.10
  39.8 1.5 %collective-permute-start.8 = (f32[1024,128]{1,0:T(8,128)}, f32[1024,128]{1,0:T(8,128)S(1)}, u32[]{:S(2)}, u32[]{:S(2)}) collective-permute-start(f32[1024,128]{1,0:T(8,128)} %get-tuple-element.14), channel_id=1, source_target_pairs={{0,2},{2,4},{4,6},{6,0},{1,3},{3,5},{5,7},{7,1},{8,10},{10,12},{12... | collective-permute-start | bytes 1572872 | tf_op jit(solution)/shard_map/ppermute | solution.py:20
  41.3 1.5 %collective-permute-done.15 = f32[1024,128]{1,0:T(8,128)S(1)} collective-permute-done((f32[1024,128]{1,0:T(8,128)S(1)}, f32[1024,128]{1,0:T(8,128)S(1)}, u32[]{:S(2)}, u32[]{:S(2)}) %collective-permute-start.15) | collective-permute-done | bytes 524320 | tf_op jit(solution)/shard_map/ppermute | solution.py:20
  42.8 0.8 copy-done.10
  43.6 2.1 %collective-permute-start.9 = (f32[1024,128]{1,0:T(8,128)}, f32[1024,128]{1,0:T(8,128)S(1)}, u32[]{:S(2)}, u32[]{:S(2)}) collective-permute-start(f32[1024,128]{1,0:T(8,128)} %get-tuple-element.15), channel_id=1, source_target_pairs={{0,4},{2,6},{4,0},{6,2},{1,5},{3,7},{5,1},{7,3},{8,12},{10,14},{12... | collective-permute-start | bytes 1572872 | tf_op jit(solution)/shard_map/ppermute | solution.py:20
  45.7 0.0 all-to-all-done
  45.7 1.3 %shard_map.56.part0 = f32[128,128]{1,0:T(8,128)S(1)} custom-call(f32[256,512]{1,0:T(8,128)} %bitcast.4.tiles), custom_call_target="tpu_custom_call" | custom-call | tf_op jit(solution)/shard_map/pallas_call | solution.py:173
  47.1 8.2 %collective-permute-done.16 = f32[1024,128]{1,0:T(8,128)} collective-permute-done((f32[1024,128]{1,0:T(8,128)}, f32[1024,128]{1,0:T(8,128)}, u32[]{:S(2)}, u32[]{:S(2)}) %collective-permute-start.16) | collective-permute-done | bytes 524320 | tf_op jit(solution)/shard_map/ppermute | solution.py:20
  55.2 0.0 collective-permute-start
  55.2 5.3 %collective-permute-start.1 = (f32[128,128]{1,0:T(8,128)S(1)}, f32[128,128]{1,0:T(8,128)S(1)}, u32[]{:S(2)}, u32[]{:S(2)}) collective-permute-start(f32[128,128]{1,0:T(8,128)S(1)} %shard_map.56.part0), channel_id=1, source_target_pairs={{0,128},{64,192},{128,0},{192,64},{1,129},{65,193},{129,1},{193,65... | collective-permute-start | bytes 196616 | tf_op jit(solution)/shard_map/ppermute | solution.py:20
  60.5 1.7 %fusion = (f32[256,128]{1,0:T(8,128)S(1)}, f32[256,128]{1,0:T(8,128)S(1)}, f32[256,128]{1,0:T(8,128)S(1)}, f32[256,128]{1,0:T(8,128)S(1)}) fusion(f32[1024,128]{1,0:T(8,128)} %collective-permute-done.17, f32[1024,128]{1,0:T(8,128)} %collective-permute-done.16, f32[1024,128]{1,0:T(8,128)} %copy-done.10, f32[1024,128]{1,0:T(8,128)} %copy-done.7), kind=kLoop, calls=%fused_computation.1 | loop fusion | flops 393216 | bytes 2621440 | tf_op jit(solution)/shard_map/add | solution.py:147
  62.2 0.0 collective-permute-done.10
  62.2 2.6 %collective-permute-start.2 = (f32[128,128]{1,0:T(8,128)S(1)}, f32[128,128]{1,0:T(8,128)S(1)}, u32[]{:S(2)}, u32[]{:S(2)}) collective-permute-start(f32[128,128]{1,0:T(8,128)S(1)} %shard_map.56.part0), channel_id=1, source_target_pairs={{0,192},{64,0},{128,64},{192,128},{1,193},{65,1},{129,65},{193,129... | collective-permute-start | bytes 196616 | tf_op jit(solution)/shard_map/ppermute | solution.py:20
  64.8 5.7 %collective-permute-start.19 = (f32[256,128]{1,0:T(8,128)S(1)}, f32[256,128]{1,0:T(8,128)S(1)}, u32[]{:S(2)}, u32[]{:S(2)}) collective-permute-start(f32[256,128]{1,0:T(8,128)S(1)} %get-tuple-element.22), channel_id=1, source_target_pairs={{0,4},{2,6},{4,0},{6,2},{1,5},{3,7},{5,1},{7,3},{8,12},{10,14},{12... | collective-permute-start | bytes 393224 | tf_op jit(solution)/shard_map/ppermute | solution.py:20
  70.5 0.1 fusion.4
  70.6 0.0 copy-start.11
  70.6 0.0 collective-permute-done.part1
  70.6 0.1 collective-permute-start.20
  70.7 0.0 collective-permute-done.1.part2
  70.7 0.8 collective-permute-start.11
  71.5 2.8 %collective-permute-start.12 = (f32[256,128]{1,0:T(8,128)S(1)}, f32[256,128]{1,0:T(8,128)S(1)}, u32[]{:S(2)}, u32[]{:S(2)}) collective-permute-start(f32[256,128]{1,0:T(8,128)S(1)} %get-tuple-element.26), channel_id=1, source_target_pairs={{0,128},{64,192},{128,0},{192,64},{1,129},{65,193},{129,1},{193,65... | collective-permute-start | bytes 393224 | tf_op jit(solution)/shard_map/ppermute | solution.py:20
  74.3 0.0 collective-permute-done.18.b1
  74.3 2.5 %collective-permute-start.13 = (f32[256,128]{1,0:T(8,128)S(1)}, f32[256,128]{1,0:T(8,128)S(1)}, u32[]{:S(2)}, u32[]{:S(2)}) collective-permute-start(f32[256,128]{1,0:T(8,128)S(1)} %get-tuple-element.25), channel_id=1, source_target_pairs={{0,192},{64,0},{128,64},{192,128},{1,193},{65,1},{129,65},{193,129... | collective-permute-start | bytes 393224 | tf_op jit(solution)/shard_map/ppermute | solution.py:20
  76.8 1.3 %shard_map.57.after = f32[256,128]{1,0:T(8,128)S(1)} custom-call(f32[256,512]{1,0:T(8,128)} %bitcast.4.tiles, f32[128,128]{1,0:T(8,128)S(1)} %shard_map.56.part0, f32[128,128]{1,0:T(8,128)S(1)} %collective-permute-done.part1, f32[128,128]{1,0:T(8,128)S(1)} %collective-permute-done.1.part2, f32[128,128]{1,0:T(8,128)S(1)} %collective-permute-done.2.part3), custom_call_target="tpu_custom_call" | custom-call | tf_op jit(solution)/shard_map/pallas_call | solution.py:177
  78.2 0.4 collective-permute-done.12.a2
  78.5 0.8 collective-permute-done.13.a3
  79.4 0.8 shard_map.62
  80.1 8.2 %all-to-all-start.1 = ((f32[8,64,128]{2,1,0:T(8,128)}), f32[8,64,128]{2,1,0:T(8,128)S(1)}, u32[]{:S(2)}, u32[]{:S(2)}) async-start(f32[8,64,128]{2,1,0:T(8,128)} %shard_map.62), calls=%async_computation.1 | async-start | bytes 524288 | tf_op jit(solution)/shard_map/all_to_all | solution.py:195
  88.3 1.3 %collective-permute-done.3 = f32[256,128]{1,0:T(8,128)S(1)} collective-permute-done((f32[256,128]{1,0:T(8,128)S(1)}, f32[256,128]{1,0:T(8,128)S(1)}, u32[]{:S(2)}, u32[]{:S(2)}) %collective-permute-start.3) | collective-permute-done | bytes 131104 | tf_op jit(solution)/shard_map/ppermute | solution.py:20
  89.7 2.1 %collective-permute-start.4 = (f32[256,128]{1,0:T(8,128)S(1)}, f32[256,128]{1,0:T(8,128)S(1)}, u32[]{:S(2)}, u32[]{:S(2)}) collective-permute-start(f32[256,128]{1,0:T(8,128)S(1)} %add.75.mix0), channel_id=1, source_target_pairs={{0,2},{2,4},{4,6},{6,0},{1,3},{3,5},{5,7},{7,1},{8,10},{10,12},{12... | collective-permute-start | bytes 393224 | tf_op jit(solution)/shard_map/ppermute | solution.py:20
  91.7 1.8 %collective-permute-start.5 = (f32[256,128]{1,0:T(8,128)S(1)}, f32[256,128]{1,0:T(8,128)S(1)}, u32[]{:S(2)}, u32[]{:S(2)}) collective-permute-start(f32[256,128]{1,0:T(8,128)S(1)} %add.75.mix0), channel_id=1, source_target_pairs={{0,4},{2,6},{4,0},{6,2},{1,5},{3,7},{5,1},{7,3},{8,12},{10,14},{12... | collective-permute-start | bytes 393224 | tf_op jit(solution)/shard_map/ppermute | solution.py:20
  93.6 0.3 collective-permute-start.6
  93.9 4.9 %all-to-all-done.1 = f32[8,64,128]{2,1,0:T(8,128)S(1)} async-done(((f32[8,64,128]{2,1,0:T(8,128)}), f32[8,64,128]{2,1,0:T(8,128)S(1)}, u32[]{:S(2)}, u32[]{:S(2)}) %all-to-all-start.1) | async-done | bytes 262176 | tf_op jit(solution)/shard_map/all_to_all | solution.py:195
  98.8 1.5 %collective-permute-start.21 = (f32[64,128]{1,0:T(8,128)S(1)}, f32[64,128]{1,0:T(8,128)S(1)}, u32[]{:S(2)}, u32[]{:S(2)}) collective-permute-start(f32[64,128]{1,0:T(8,128)S(1)} %bitcast_subtract_fusion.rest0), channel_id=1, source_target_pairs={{0,64},{64,128},{128,192},{192,0},{1,65},{65,129},{129,193},{193,1... | collective-permute-start | bytes 98312 | tf_op jit(solution)/shard_map/ppermute | solution.py:20
  100.3 2.7 %collective-permute-start.22 = (f32[64,128]{1,0:T(8,128)S(1)}, f32[64,128]{1,0:T(8,128)S(1)}, u32[]{:S(2)}, u32[]{:S(2)}) collective-permute-start(f32[64,128]{1,0:T(8,128)S(1)} %bitcast_subtract_fusion.rest0), channel_id=1, source_target_pairs={{0,128},{64,192},{128,0},{192,64},{1,129},{65,193},{129,1},{193,65... | collective-permute-start | bytes 98312 | tf_op jit(solution)/shard_map/ppermute | solution.py:20
  103.1 0.5 collective-permute-start.23
  103.6 0.5 collective-permute-done.21.rest1
  104.0 1.7 %collective-permute-done.22.rest2 = f32[64,128]{1,0:T(8,128)S(1)} collective-permute-done((f32[64,128]{1,0:T(8,128)S(1)}, f32[64,128]{1,0:T(8,128)S(1)}, u32[]{:S(2)}, u32[]{:S(2)}) %collective-permute-start.22) | collective-permute-done | bytes 32800 | tf_op jit(solution)/shard_map/ppermute | solution.py:20
  105.7 1.2 %collective-permute-done.23.rest3 = f32[64,128]{1,0:T(8,128)S(1)} collective-permute-done((f32[64,128]{1,0:T(8,128)S(1)}, f32[64,128]{1,0:T(8,128)S(1)}, u32[]{:S(2)}, u32[]{:S(2)}) %collective-permute-start.23) | collective-permute-done | bytes 32800 | tf_op jit(solution)/shard_map/ppermute | solution.py:20
  107.0 1.5 %shard_map.63 = f32[8,64,128]{2,1,0:T(8,128)S(1)} custom-call(s32[3]{0:T(128)S(1)} %pad_add_fusion.place, f32[256,512]{1,0:T(8,128)} %bitcast.4.tiles, f32[256,128]{1,0:T(8,128)S(1)} %add.75.mix0, f32[256,128]{1,0:T(8,128)S(1)} %collective-permute-done.4.mix1, f32[256,128]{1,0:T(8,128)S(1)} %collective-permute-done.5.mix2, ...), custom_call_target="tpu_custom_call" | custom-call | tf_op jit(solution)/shard_map/pallas_call | solution.py:199
  108.5 13.4 %all_to_all.15 = f32[8,64,128]{2,1,0:T(8,128)S(1)} all-to-all(f32[8,64,128]{2,1,0:T(8,128)S(1)} %shard_map.63), channel_id=1, replica_groups=mesh['y'=4,'z'=8,'x'=4,'core'=2] {'z'}, dimensions={0} | all-to-all | bytes 524288 | tf_op jit(solution)/shard_map/all_to_all | solution.py:206
  121.9 0.6 reduce_sum.19
  (30 shorter events, 0.1 us)
Async XLA Ops:
  0.1 1.9 %copy-start = (f32[2,1024,384]{2,1,0:T(8,128)S(1)}, f32[2,1024,384]{2,1,0:T(8,128)}, u32[]{:S(2)}) copy-start(f32[2,1024,384]{2,1,0:T(8,128)} %rows.7) | copy-start | bytes 9437188
  2.0 1.4 %copy-start.2 = (f32[384,1024]{1,0:T(8,128)S(1)}, f32[384,1024]{1,0:T(8,128)}, u32[]{:S(2)}) copy-start(f32[384,1024]{1,0:T(8,128)} %cols.7) | copy-start | bytes 4718596
  7.1 4.3 %copy-start.8 = (f32[2,32,1024]{2,1,0:T(8,128)S(1)}, f32[2,32,1024]{2,1,0:T(8,128)}, u32[]{:S(2)}) copy-start(f32[2,32,1024]{2,1,0:T(8,128)} %inverses.1) | copy-start | bytes 786436
  7.1 4.3 %copy-start.9 = (f32[1024,32]{0,1:T(8,128)S(1)}, f32[1024,32]{0,1:T(8,128)}, u32[]{:S(2)}) copy-start(f32[1024,32]{0,1:T(8,128)} %param.8) | copy-start | bytes 393220
  7.1 14.4 %collective-permute-start.14 = (f32[4,1024,128]{2,1,0:T(8,128)}, f32[4,1024,128]{2,1,0:T(8,128)}, u32[]{:S(2)}, u32[]{:S(2)}) collective-permute-start(f32[4,1024,128]{2,1,0:T(8,128)} %shard_map.60), channel_id=1, source_target_pairs={{0,1},{1,0},{2,3},{3,2},{4,5},{5,4},{6,7},{7,6},{8,9},{9,8},{10,11... | collective-permute-start | bytes 6291464 | tf_op jit(solution)/shard_map/ppermute | solution.py:20
  7.1 14.4 %copy-start.1 = (f32[2,1024,384]{2,1,0:T(8,128)S(1)}, f32[2,1024,384]{2,1,0:T(8,128)}, u32[]{:S(2)}) copy-start(f32[2,1024,384]{2,1,0:T(8,128)} %rows.7) | copy-start | bytes 9437188
  10.8 22.9 %collective-permute-start.7 = (f32[4,1024,128]{2,1,0:T(8,128)}, f32[4,1024,128]{2,1,0:T(8,128)}, u32[]{:S(2)}, u32[]{:S(2)}) collective-permute-start(f32[4,1024,128]{2,1,0:T(8,128)} %shard_map.58), channel_id=1, source_target_pairs={{0,1},{1,0},{2,3},{3,2},{4,5},{5,4},{6,7},{7,6},{8,9},{9,8},{10,11... | collective-permute-start | bytes 6291464 | tf_op jit(solution)/shard_map/ppermute | solution.py:20
  12.2 0.8 copy-start.4
  13.0 32.7 %all-to-all-start = ((f32[8,32,512]{2,1,0:T(8,128)}), f32[8,32,512]{2,1,0:T(8,128)}, u32[]{:S(2)}, u32[]{:S(2)}) async-start(f32[8,32,512]{2,1,0:T(8,128)} %copy-done.4), calls=%async_computation | async-start | bytes 1048576 | tf_op jit(solution)/shard_map/all_to_all | solution.py:172
  21.5 1.4 %copy-start.3 = (f32[384,1024]{1,0:T(8,128)S(1)}, f32[384,1024]{1,0:T(8,128)}, u32[]{:S(2)}) copy-start(f32[384,1024]{1,0:T(8,128)} %cols.7) | copy-start | bytes 4718596
  27.1 0.8 copy-start.7
  27.9 14.9 %collective-permute-start.15 = (f32[1024,128]{1,0:T(8,128)S(1)}, f32[1024,128]{1,0:T(8,128)S(1)}, u32[]{:S(2)}, u32[]{:S(2)}) collective-permute-start(f32[1024,128]{1,0:T(8,128)S(1)} %get-tuple-element.18), channel_id=1, source_target_pairs={{0,64},{64,128},{128,192},{192,0},{1,65},{65,129},{129,193},{193,1... | collective-permute-start | bytes 1572872 | tf_op jit(solution)/shard_map/ppermute | solution.py:20
  29.5 25.7 %collective-permute-start.16 = (f32[1024,128]{1,0:T(8,128)}, f32[1024,128]{1,0:T(8,128)}, u32[]{:S(2)}, u32[]{:S(2)}) collective-permute-start(f32[1024,128]{1,0:T(8,128)} %get-tuple-element.19), channel_id=1, source_target_pairs={{0,128},{64,192},{128,0},{192,64},{1,129},{65,193},{129,1},{193,65... | collective-permute-start | bytes 1572872 | tf_op jit(solution)/shard_map/ppermute | solution.py:20
  32.4 22.8 %collective-permute-start.17 = (f32[1024,128]{1,0:T(8,128)}, f32[1024,128]{1,0:T(8,128)}, u32[]{:S(2)}, u32[]{:S(2)}) collective-permute-start(f32[1024,128]{1,0:T(8,128)} %get-tuple-element.20), channel_id=1, source_target_pairs={{0,192},{64,0},{128,64},{192,128},{1,193},{65,1},{129,65},{193,129... | collective-permute-start | bytes 1572872 | tf_op jit(solution)/shard_map/ppermute | solution.py:20
  38.4 0.8 copy-start.5
  39.2 31.2 %copy-start.6 = (f32[1024,128]{1,0:T(8,128)S(1)}, f32[1024,128]{1,0:T(8,128)}, u32[]{:S(2)}) copy-start(f32[1024,128]{1,0:T(8,128)} %copy-done.5) | copy-start | bytes 1572868
  39.2 23.0 %collective-permute-start.10 = (f32[1024,128]{1,0:T(8,128)}, f32[1024,128]{1,0:T(8,128)S(1)}, u32[]{:S(2)}, u32[]{:S(2)}) collective-permute-start(f32[1024,128]{1,0:T(8,128)} %get-tuple-element.16), channel_id=1, source_target_pairs={{0,6},{2,0},{4,2},{6,4},{1,7},{3,1},{5,3},{7,5},{8,14},{10,8},{12,... | collective-permute-start | bytes 1572872 | tf_op jit(solution)/shard_map/ppermute | solution.py:20
  39.8 25.1 %collective-permute-start.8 = (f32[1024,128]{1,0:T(8,128)}, f32[1024,128]{1,0:T(8,128)S(1)}, u32[]{:S(2)}, u32[]{:S(2)}) collective-permute-start(f32[1024,128]{1,0:T(8,128)} %get-tuple-element.14), channel_id=1, source_target_pairs={{0,2},{2,4},{4,6},{6,0},{1,3},{3,5},{5,7},{7,1},{8,10},{10,12},{12... | collective-permute-start | bytes 1572872 | tf_op jit(solution)/shard_map/ppermute | solution.py:20
  42.8 0.8 copy-start.10
  43.6 21.2 %collective-permute-start.9 = (f32[1024,128]{1,0:T(8,128)}, f32[1024,128]{1,0:T(8,128)S(1)}, u32[]{:S(2)}, u32[]{:S(2)}) collective-permute-start(f32[1024,128]{1,0:T(8,128)} %get-tuple-element.15), channel_id=1, source_target_pairs={{0,4},{2,6},{4,0},{6,2},{1,5},{3,7},{5,1},{7,3},{8,12},{10,14},{12... | collective-permute-start | bytes 1572872 | tf_op jit(solution)/shard_map/ppermute | solution.py:20
  55.2 15.4 %collective-permute-start = (f32[128,128]{1,0:T(8,128)S(1)}, f32[128,128]{1,0:T(8,128)S(1)}, u32[]{:S(2)}, u32[]{:S(2)}) collective-permute-start(f32[128,128]{1,0:T(8,128)S(1)} %shard_map.56.part0), channel_id=1, source_target_pairs={{0,64},{64,128},{128,192},{192,0},{1,65},{65,129},{129,193},{193,1... | collective-permute-start | bytes 196616 | tf_op jit(solution)/shard_map/ppermute | solution.py:20
  55.2 15.5 %collective-permute-start.1 = (f32[128,128]{1,0:T(8,128)S(1)}, f32[128,128]{1,0:T(8,128)S(1)}, u32[]{:S(2)}, u32[]{:S(2)}) collective-permute-start(f32[128,128]{1,0:T(8,128)S(1)} %shard_map.56.part0), channel_id=1, source_target_pairs={{0,128},{64,192},{128,0},{192,64},{1,129},{65,193},{129,1},{193,65... | collective-permute-start | bytes 196616 | tf_op jit(solution)/shard_map/ppermute | solution.py:20
  62.2 9.3 %collective-permute-start.2 = (f32[128,128]{1,0:T(8,128)S(1)}, f32[128,128]{1,0:T(8,128)S(1)}, u32[]{:S(2)}, u32[]{:S(2)}) collective-permute-start(f32[128,128]{1,0:T(8,128)S(1)} %shard_map.56.part0), channel_id=1, source_target_pairs={{0,192},{64,0},{128,64},{192,128},{1,193},{65,1},{129,65},{193,129... | collective-permute-start | bytes 196616 | tf_op jit(solution)/shard_map/ppermute | solution.py:20
  64.8 9.5 %collective-permute-start.18 = (f32[256,128]{1,0:T(8,128)S(1)}, f32[256,128]{1,0:T(8,128)S(1)}, u32[]{:S(2)}, u32[]{:S(2)}) collective-permute-start(f32[256,128]{1,0:T(8,128)S(1)} %get-tuple-element.23), channel_id=1, source_target_pairs={{0,2},{2,4},{4,6},{6,0},{1,3},{3,5},{5,7},{7,1},{8,10},{10,12},{12... | collective-permute-start | bytes 393224 | tf_op jit(solution)/shard_map/ppermute | solution.py:20
  64.8 13.3 %collective-permute-start.19 = (f32[256,128]{1,0:T(8,128)S(1)}, f32[256,128]{1,0:T(8,128)S(1)}, u32[]{:S(2)}, u32[]{:S(2)}) collective-permute-start(f32[256,128]{1,0:T(8,128)S(1)} %get-tuple-element.22), channel_id=1, source_target_pairs={{0,4},{2,6},{4,0},{6,2},{1,5},{3,7},{5,1},{7,3},{8,12},{10,14},{12... | collective-permute-start | bytes 393224 | tf_op jit(solution)/shard_map/ppermute | solution.py:20
  70.6 28.2 %copy-start.11 = (f32[2,32,128]{2,1,0:T(8,128)S(1)}, f32[2,32,128]{2,1,0:T(8,128)}, u32[]{:S(2)}) copy-start(f32[2,32,128]{2,1,0:T(8,128)} %param.7) | copy-start | bytes 98308
  70.6 7.6 %collective-permute-start.20 = (f32[256,128]{1,0:T(8,128)S(1)}, f32[256,128]{1,0:T(8,128)S(1)}, u32[]{:S(2)}, u32[]{:S(2)}) collective-permute-start(f32[256,128]{1,0:T(8,128)S(1)} %get-tuple-element.21), channel_id=1, source_target_pairs={{0,6},{2,0},{4,2},{6,4},{1,7},{3,1},{5,3},{7,5},{8,14},{10,8},{12,... | collective-permute-start | bytes 393224 | tf_op jit(solution)/shard_map/ppermute | solution.py:20
  70.7 7.5 %collective-permute-start.11 = (f32[256,128]{1,0:T(8,128)S(1)}, f32[256,128]{1,0:T(8,128)S(1)}, u32[]{:S(2)}, u32[]{:S(2)}) collective-permute-start(f32[256,128]{1,0:T(8,128)S(1)} %get-tuple-element.27), channel_id=1, source_target_pairs={{0,64},{64,128},{128,192},{192,0},{1,65},{65,129},{129,193},{193,1... | collective-permute-start | bytes 393224 | tf_op jit(solution)/shard_map/ppermute | solution.py:20
  71.5 7.0 %collective-permute-start.12 = (f32[256,128]{1,0:T(8,128)S(1)}, f32[256,128]{1,0:T(8,128)S(1)}, u32[]{:S(2)}, u32[]{:S(2)}) collective-permute-start(f32[256,128]{1,0:T(8,128)S(1)} %get-tuple-element.26), channel_id=1, source_target_pairs={{0,128},{64,192},{128,0},{192,64},{1,129},{65,193},{129,1},{193,65... | collective-permute-start | bytes 393224 | tf_op jit(solution)/shard_map/ppermute | solution.py:20
  74.3 5.1 %collective-permute-start.13 = (f32[256,128]{1,0:T(8,128)S(1)}, f32[256,128]{1,0:T(8,128)S(1)}, u32[]{:S(2)}, u32[]{:S(2)}) collective-permute-start(f32[256,128]{1,0:T(8,128)S(1)} %get-tuple-element.25), channel_id=1, source_target_pairs={{0,192},{64,0},{128,64},{192,128},{1,193},{65,1},{129,65},{193,129... | collective-permute-start | bytes 393224 | tf_op jit(solution)/shard_map/ppermute | solution.py:20
  80.1 18.7 %all-to-all-start.1 = ((f32[8,64,128]{2,1,0:T(8,128)}), f32[8,64,128]{2,1,0:T(8,128)S(1)}, u32[]{:S(2)}, u32[]{:S(2)}) async-start(f32[8,64,128]{2,1,0:T(8,128)} %shard_map.62), calls=%async_computation.1 | async-start | bytes 524288 | tf_op jit(solution)/shard_map/all_to_all | solution.py:195
  88.3 1.3 %collective-permute-start.3 = (f32[256,128]{1,0:T(8,128)S(1)}, f32[256,128]{1,0:T(8,128)S(1)}, u32[]{:S(2)}, u32[]{:S(2)}) collective-permute-start(f32[256,128]{1,0:T(8,128)S(1)} %shard_map.57.after), channel_id=1, source_target_pairs={{0,1},{1,0},{2,3},{3,2},{4,5},{5,4},{6,7},{7,6},{8,9},{9,8},{10,11... | collective-permute-start | bytes 393224 | tf_op jit(solution)/shard_map/ppermute | solution.py:20
  89.7 13.4 %collective-permute-start.4 = (f32[256,128]{1,0:T(8,128)S(1)}, f32[256,128]{1,0:T(8,128)S(1)}, u32[]{:S(2)}, u32[]{:S(2)}) collective-permute-start(f32[256,128]{1,0:T(8,128)S(1)} %add.75.mix0), channel_id=1, source_target_pairs={{0,2},{2,4},{4,6},{6,0},{1,3},{3,5},{5,7},{7,1},{8,10},{10,12},{12... | collective-permute-start | bytes 393224 | tf_op jit(solution)/shard_map/ppermute | solution.py:20
  91.7 11.8 %collective-permute-start.5 = (f32[256,128]{1,0:T(8,128)S(1)}, f32[256,128]{1,0:T(8,128)S(1)}, u32[]{:S(2)}, u32[]{:S(2)}) collective-permute-start(f32[256,128]{1,0:T(8,128)S(1)} %add.75.mix0), channel_id=1, source_target_pairs={{0,4},{2,6},{4,0},{6,2},{1,5},{3,7},{5,1},{7,3},{8,12},{10,14},{12... | collective-permute-start | bytes 393224 | tf_op jit(solution)/shard_map/ppermute | solution.py:20
  93.6 10.0 %collective-permute-start.6 = (f32[256,128]{1,0:T(8,128)S(1)}, f32[256,128]{1,0:T(8,128)S(1)}, u32[]{:S(2)}, u32[]{:S(2)}) collective-permute-start(f32[256,128]{1,0:T(8,128)S(1)} %add.75.mix0), channel_id=1, source_target_pairs={{0,6},{2,0},{4,2},{6,4},{1,7},{3,1},{5,3},{7,5},{8,14},{10,8},{12,... | collective-permute-start | bytes 393224 | tf_op jit(solution)/shard_map/ppermute | solution.py:20
  98.8 5.2 %collective-permute-start.21 = (f32[64,128]{1,0:T(8,128)S(1)}, f32[64,128]{1,0:T(8,128)S(1)}, u32[]{:S(2)}, u32[]{:S(2)}) collective-permute-start(f32[64,128]{1,0:T(8,128)S(1)} %bitcast_subtract_fusion.rest0), channel_id=1, source_target_pairs={{0,64},{64,128},{128,192},{192,0},{1,65},{65,129},{129,193},{193,1... | collective-permute-start | bytes 98312 | tf_op jit(solution)/shard_map/ppermute | solution.py:20
  100.3 5.4 %collective-permute-start.22 = (f32[64,128]{1,0:T(8,128)S(1)}, f32[64,128]{1,0:T(8,128)S(1)}, u32[]{:S(2)}, u32[]{:S(2)}) collective-permute-start(f32[64,128]{1,0:T(8,128)S(1)} %bitcast_subtract_fusion.rest0), channel_id=1, source_target_pairs={{0,128},{64,192},{128,0},{192,64},{1,129},{65,193},{129,1},{193,65... | collective-permute-start | bytes 98312 | tf_op jit(solution)/shard_map/ppermute | solution.py:20
  103.1 3.9 %collective-permute-start.23 = (f32[64,128]{1,0:T(8,128)S(1)}, f32[64,128]{1,0:T(8,128)S(1)}, u32[]{:S(2)}, u32[]{:S(2)}) collective-permute-start(f32[64,128]{1,0:T(8,128)S(1)} %bitcast_subtract_fusion.rest0), channel_id=1, source_target_pairs={{0,192},{64,0},{128,64},{192,128},{1,193},{65,1},{129,65},{193,129... | collective-permute-start | bytes 98312 | tf_op jit(solution)/shard_map/ppermute | solution.py:20
where the time goes:
time: 125 us; the launch traced here: 123 us
  starting transfers between devices  55.9 us (45%)
  Pallas kernels  22 us (18%)
  waiting for transfers between devices  20.5 us (16%)
  blocking collectives  13.4 us (11%)
  local copies, waits for them, and re-layouts  7.91 us (6%)
  other arithmetic  2.62 us (2%)
    ppermute x24, starting transfers between devices, shift(): lax.ppermute(value, axis, [(i, (i + step) % size) for i in range(size)])  39.2 us
    pallas_call x4, Pallas kernels, products(): pl.pallas_call(kernel, out_shape=shapes, grid=(1,), in_specs=[SMEM, pl.Bl...  16.3 us
    ppermute x24, waiting for transfers between devices, shift(): lax.ppermute(value, axis, [(i, (i + step) % size) for i in range(size)])  15.6 us
    all_to_all x1, blocking collectives, steps(): panels = lax.all_to_all(solved_part, 'z', 0, 0, tiled=True).sum(axis=0)  13.4 us
    all_to_all x1, starting transfers between devices, steps(): tiles = lax.all_to_all(packed, 'z', 0, 0, tiled=True).reshape(nz * 32, 512)  8.46 us
    all_to_all x1, starting transfers between devices, steps(): old = lax.all_to_all(by_z, 'z', 0, 0, tiled=True).sum(axis=0)  8.2 us
    unnamed x24, local copies, waits for them, and re-layouts  7.91 us
    all_to_all x1, waiting for transfers between devices, steps(): old = lax.all_to_all(by_z, 'z', 0, 0, tiled=True).sum(axis=0)  4.89 us
  transfers between devices with their start and end apart: 26, of which 9 were waited for; matrix products, arithmetic and copies ran while one was open for 2% of the time, Pallas kernels for 13%

commit v1 on v0

--- a/solution.py
+++ b/solution.py
@@ -12,8 +12,8 @@
 BF16 = jnp.bfloat16
 EXACT = lax.Precision.HIGHEST
 SMEM = pl.BlockSpec(memory_space=pltpu.SMEM)
-ORDER = pl.BlockSpec(memory_space=pl.ANY)
-SMALL = pltpu.CompilerParams(vmem_limit_bytes=4 << 20)
+FAR = pl.BlockSpec(memory_space=pltpu.HBM)
+SMALL = pltpu.CompilerParams(vmem_limit_bytes=6 << 20)
 
 
 def shift(value, axis, step, size):
@@ -25,23 +25,38 @@
     return high, (value - high.astype(F32)).astype(BF16)
 
 
-def product_kernel(by_column, has_received, nx, ny):
+def product_kernel(panel, by_column, has_received, nx, ny):
     def kernel(place, rows, cols, *refs):
         received = refs[0] if has_received else None
-        outs = refs[1:-2] if has_received else refs[:-2]
-        left, right = refs[-2:]
-        depth = rows.shape[1]
-        high_rows = rows.shape[0] // ny
+        outs = refs[1:-5] if has_received else refs[:-5]
+        left, right, strips, blocks, sems = refs[-5:]
+        depth = cols.shape[0]
+        size = blocks.shape[1]
+        copies = []
         for jx in range(nx):
-            at = lax.rem(place[0] + jx, nx) * 256 + place[2] * 128
-            high, low = halves(cols[:, pl.ds(pl.multiple_of(at, 128), 128)])
+            at = pl.multiple_of(lax.rem(place[0] + jx, nx) * 256 + place[2] * 128, 128)
+            copies.append(
+                pltpu.make_async_copy(cols.at[:, pl.ds(at, 128)], strips.at[jx], sems.at[jx])
+            )
+        for jy in range(ny):
+            at = pl.multiple_of(lax.rem(place[1] + jy, ny) * size, size)
+            copies.append(
+                pltpu.make_async_copy(
+                    rows.at[panel, pl.ds(at, size), :], blocks.at[jy], sems.at[nx + jy]
+                )
+            )
+        for copy in copies:
+            copy.start()
+        for jx in range(nx):
+            copies[jx].wait()
+            high, low = halves(strips[jx])
             span = slice(jx * 128, (jx + 1) * 128)
             right[0:depth, span] = high
             right[depth : 2 * depth, span] = low
             right[2 * depth : 3 * depth, span] = high
         for jy in range(ny):
-            at = lax.rem(place[1] + jy, ny) * high_rows
-            high, low = halves(rows[pl.ds(pl.multiple_of(at, high_rows), high_rows), :])
+            copies[nx + jy].wait()
+            high, low = halves(blocks[jy])
             left[:, 0:depth] = high
             left[:, depth : 2 * depth] = high
             left[:, 2 * depth : 3 * depth] = low
@@ -49,7 +64,7 @@
             for jx in range(nx):
                 block = value[:, jx * 128 : (jx + 1) * 128]
                 first, second = (jx, jy) if by_column else (jy, jx)
-                span = slice(second * high_rows, (second + 1) * high_rows)
+                span = slice(second * size, (second + 1) * size)
                 if has_received:
                     outs[first][span, :] = block + received[first, span, :]
                 else:
@@ -59,7 +74,7 @@
 
 
 def products(place, panel, rows, cols, received, by_column, nx, ny):
-    kernel = product_kernel(by_column, received is not None, nx, ny)
+    kernel = product_kernel(panel, by_column, received is not None, nx, ny)
     _, size, depth = rows.shape
     first = nx if by_column else ny
     if received is None:
@@ -71,15 +86,13 @@
     return pl.pallas_call(
         kernel,
         out_shape=shapes,
-        grid=(1,),
-        in_specs=[
-            SMEM,
-            pl.BlockSpec((pl.Squeezed(), size, depth), lambda i: (panel, 0, 0)),
-        ]
-        + [pl.BlockSpec()] * (len(args) - 2),
+        in_specs=[SMEM, FAR, FAR] + [pl.BlockSpec()] * (len(args) - 3),
         scratch_shapes=[
             pltpu.VMEM((size // ny, 3 * depth), BF16),
             pltpu.VMEM((3 * depth, nx * 128), BF16),
+            pltpu.VMEM((nx, depth, 128), F32),
+            pltpu.VMEM((ny, size // ny, depth), F32),
+            pltpu.SemaphoreType.DMA((nx + ny,)),
         ],
         compiler_params=pltpu.CompilerParams(vmem_limit_bytes=16 << 20),
         cost_estimate=pl.CostEstimate(
@@ -111,18 +124,47 @@
     )
 
 
-def chain_kernel(tiles, part0, part1, part2, part3, out):
-    total = (part0[...] + part1[...]) + (part2[...] + part3[...])
+def chain_kernel(tiles, part0, got1, got2, got3, out):
+    total = (part0[...] + got1[256:384, :]) + (got2[256:384, :] + got3[256:384, :])
     out[...] = jnp.dot(tiles[:, 128:256], total, precision=EXACT, preferred_element_type=F32)
 
 
-def apply_kernel(place, tiles, mix0, mix1, mix2, mix3, rest0, rest1, rest2, rest3, out, first, second):
+def gather_sums_kernel(a, b, c, d, rider, own, *outs):
+    size = own.shape[0]
+    for j, out in enumerate((own,) + outs):
+        span = slice(j * size, (j + 1) * size)
+        out[0:size, :] = (a[span, :] + b[span, :]) + (c[span, :] + d[span, :])
+        if j:
+            out[size:, :] = rider[...]
+
+
+def gather_sums(parts, rider, count):
+    size = parts[0].shape[0] // count
+    longer = jax.ShapeDtypeStruct((size + rider.shape[0], 128), F32)
+    return pl.pallas_call(
+        gather_sums_kernel,
+        out_shape=[jax.ShapeDtypeStruct((size, 128), F32)] + [longer] * (count - 1),
+        compiler_params=SMALL,
+    )(*parts, rider)
+
+
+def interleave_kernel(a0, a1, a2, a3, b0, b1, b2, b3, part, out, mix):
+    size = a0.shape[0]
+    low = (a0[...] + a1[0:size, :]) + (a2[0:size, :] + a3[0:size, :])
+    high = (b0[...] + b1[0:size, :]) + (b2[0:size, :] + b3[0:size, :])
+    for z in range(out.shape[0]):
+        out[z, 0:32, :] = low[z * 32 : (z + 1) * 32, :]
+        out[z, 32:64, :] = high[z * 32 : (z + 1) * 32, :]
+    mix[...] = (part[...] + b1[size:, :]) + (b2[size:, :] + b3[size:, :])
+
+
+def apply_kernel(place, tiles, mix0, mix1, rest0, rest1, rest2, rest3, out, first, second):
     ny = 4
     for step, rest in enumerate((rest0, rest1, rest2, rest3)):
         at = pl.multiple_of(lax.rem(place[1] + ny - step, ny) * 32, 32)
         first[pl.ds(at, 32), :] = rest[0:32, :]
         second[pl.ds(at, 32), :] = rest[32:64, :]
-    mix = (mix0[...] + mix1[...]) + (mix2[...] + mix3[...])
+    mix = mix0[...] + mix1[...]
     low = jnp.dot(tiles[:, 256:384], first[...], precision=EXACT, preferred_element_type=F32)
     high = jnp.dot(tiles[:, 384:512], second[...], precision=EXACT, preferred_element_type=F32)
     high = high - jnp.dot(mix, first[...], precision=EXACT, preferred_element_type=F32)
@@ -131,26 +173,11 @@
         out[z, 32:64, :] = high[z * 32 : (z + 1) * 32, :]
 
 
-def interleave_kernel(a0, a1, a2, a3, b0, b1, b2, b3, after, out):
-    low = (a0[...] + a1[...]) + (a2[...] + a3[...])
-    high = (b0[...] + b1[...]) + (b2[...] + b3[...])
-    for z in range(out.shape[0]):
-        out[z, 0:32, :] = low[z * 32 : (z + 1) * 32, :]
-        out[z, 32:64, :] = high[z * 32 : (z + 1) * 32, :]
-
-
-def summed_blocks(parts, count):
-    rows = parts[0].shape[0] // count
-    out = []
-    for j in range(count):
-        a, b, c, d = [part[j * rows : (j + 1) * rows] for part in parts]
-        out.append((a + b) + (c + d))
-    return out
-
-
 def steps(panel_rows, solved, right_side, coupling, inverses):
     nx, ny, nz, nc = (lax.axis_size(a) for a in ("x", "y", "z", "core"))
     x, y, core = lax.axis_index("x"), lax.axis_index("y"), lax.axis_index("core")
+    panel_rows = pltpu.with_memory_space_constraint(panel_rows, pltpu.HBM)
+    solved = pltpu.with_memory_space_constraint(solved, pltpu.HBM)
     own = jnp.stack([x, y, core]).astype(jnp.int32)
     other = jnp.stack([x, y, 1 - core]).astype(jnp.int32)
 
@@ -173,36 +200,34 @@
     coupled = pl.pallas_call(
         couple_kernel, out_shape=jax.ShapeDtypeStruct((128, 128), F32), compiler_params=SMALL
     )(tiles)
-    coupled_all = [coupled] + [shift(coupled, "y", j, ny) for j in range(1, ny)]
+
+    sums0 = gather_sums(got0, coupled, ny)
+    again0 = [sums0[0]] + [shift(sums0[j], "y", j, ny) for j in range(1, ny)]
     chained = pl.pallas_call(
         chain_kernel, out_shape=jax.ShapeDtypeStruct((256, 128), F32), compiler_params=SMALL
-    )(
-        tiles, *coupled_all
-    )
-    both = chained + shift(chained, "core", 1, nc)
-    mixes = [both] + [shift(both, "x", j, nx) for j in range(1, nx)]
-
-    sums0 = summed_blocks(got0, ny)
-    again0 = [sums0[0]] + [shift(sums0[j], "y", j, ny) for j in range(1, ny)]
-    sums1 = summed_blocks(got1, nx)
+    )(tiles, coupled, *again0[1:])
+    sums1 = gather_sums(got1, chained, nx)
     again1 = [sums1[0]] + [shift(sums1[j], "x", j, nx) for j in range(1, nx)]
-    by_z = pl.pallas_call(
+    by_z, mix = pl.pallas_call(
         interleave_kernel,
-        out_shape=jax.ShapeDtypeStruct((nz, 64, 128), F32),
-        in_specs=[pl.BlockSpec()] * 8 + [ORDER],
+        out_shape=(
+            jax.ShapeDtypeStruct((nz, 64, 128), F32),
+            jax.ShapeDtypeStruct((256, 128), F32),
+        ),
         compiler_params=SMALL,
     )(*again0, *again1, chained)
     old = lax.all_to_all(by_z, "z", 0, 0, tiled=True).sum(axis=0)
+    mix_of_partner = shift(mix, "core", 1, nc)
     rest = right_side.reshape(64, 128) - old
 
     rests = [rest] + [shift(rest, "y", j, ny) for j in range(1, ny)]
     solved_part = pl.pallas_call(
         apply_kernel,
         out_shape=jax.ShapeDtypeStruct((nz, 64, 128), F32),
-        in_specs=[SMEM] + [pl.BlockSpec()] * 9,
+        in_specs=[SMEM] + [pl.BlockSpec()] * 7,
         scratch_shapes=[pltpu.VMEM((128, 128), F32), pltpu.VMEM((128, 128), F32)],
         compiler_params=SMALL,
-    )(own, tiles, *mixes, *rests)
+    )(own, tiles, mix, mix_of_partner, *rests)
     panels = lax.all_to_all(solved_part, "z", 0, 0, tiled=True).sum(axis=0)
     return panels.reshape(right_side.shape)
 

time: 125 us -> 134 us (1.072)
  waiting for transfers between devices: 20.5 us -> 47.4 us
  starting transfers between devices: 55.9 us -> 41.4 us
  Pallas kernels: 22 us -> 27.2 us
  local copies, waits for them, and re-layouts: 7.91 us -> 2.92 us
  other arithmetic: 2.62 us -> 0.81 us
    ppermute x24 -> x18, waiting for transfers between devices: 15.6 us -> 35.4 us  [shift(): lax.ppermute(value, axis, [(i, (i + step) % size) for i in range(size)])]
    ppermute x24 -> x18, starting transfers between devices: 39.2 us -> 26 us  [shift(): lax.ppermute(value, axis, [(i, (i + step) % size) for i in range(size)])]
    all_to_all x1, waiting for transfers between devices: 4.89 us -> 11.9 us  [steps(): old = lax.all_to_all(by_z, 'z', 0, 0, tiled=True).sum(axis=0)]
    pallas_call x5 -> x7, Pallas kernels: 17 us -> 24 us  [the longest x4 21.8 us: products(): pl.pallas_call(kernel, out_shape=shapes, in_specs=[SMEM, FAR, FAR] + [pl....]
    unnamed x24 -> x14, local copies, waits for them, and re-layouts: 7.91 us -> 2.92 us
    add x3 -> x0, other arithmetic: 1.81 us -> none  [the longest x2 1.79 us: summed_blocks(): out.append(a + b + (c + d))]
  transfers between devices with their start and end apart: 26 -> 20, of which waited for: 9 -> 12; matrix products, arithmetic and copies ran while one was open for 2% -> 0% of each run, Pallas kernels for 13% -> 15%
where the time goes in v1:
time: 134 us; the launch traced here: 133 us
  waiting for transfers between devices  47.4 us (35%)
  starting transfers between devices  41.4 us (31%)
  Pallas kernels  27.2 us (20%)
  blocking collectives  12.9 us (10%)
  local copies, waits for them, and re-layouts  2.92 us (2%)
    ppermute x18, waiting for transfers between devices, shift(): lax.ppermute(value, axis, [(i, (i + step) % size) for i in range(size)])  35.4 us
    ppermute x18, starting transfers between devices, shift(): lax.ppermute(value, axis, [(i, (i + step) % size) for i in range(size)])  26 us
    pallas_call x4, Pallas kernels, products(): pl.pallas_call(kernel, out_shape=shapes, in_specs=[SMEM, FAR, FAR] + [pl....  21.8 us
    all_to_all x1, blocking collectives, steps(): panels = lax.all_to_all(solved_part, 'z', 0, 0, tiled=True).sum(axis=0)  12.9 us
    all_to_all x1, waiting for transfers between devices, steps(): old = lax.all_to_all(by_z, 'z', 0, 0, tiled=True).sum(axis=0)  11.9 us
    all_to_all x1, starting transfers between devices, steps(): tiles = lax.all_to_all(packed, 'z', 0, 0, tiled=True).reshape(nz * 32, 512)  8.47 us
    all_to_all x1, starting transfers between devices, steps(): old = lax.all_to_all(by_z, 'z', 0, 0, tiled=True).sum(axis=0)  6.95 us
    unnamed x14, local copies, waits for them, and re-layouts  2.92 us
  transfers between devices with their start and end apart: 20, of which 12 were waited for; matrix products, arithmetic and copies ran while one was open for 0% of the time, Pallas kernels for 15%

profile of v1, /device:TPU:2, one launch (start us, length us, event | category | flops | bytes accessed | tf_op | source)
XLA Modules:
  0.0 132.8 jit_solution(3170895345092911562)
XLA Ops:
  0.0 0.1 pad_add_fusion.2.place
  0.1 5.4 %shard_map.56 = f32[4,1024,128]{2,1,0:T(8,128)} custom-call(s32[3]{0:T(128)S(1)} %pad_add_fusion.2.place, f32[2,1024,384]{2,1,0:T(8,128)} %rows.7, f32[384,1024]{1,0:T(8,128)} %cols.7), custom_call_target="tpu_custom_call" | custom-call | flops 1207959552 | bytes 6291456 | tf_op jit(solution)/shard_map/pallas_call | solution.py:86
  5.5 0.0 copy-start.4
  5.5 0.0 copy-start.5
  5.5 0.1 collective-permute-start
  5.6 5.4 %shard_map.60 = f32[4,1024,128]{2,1,0:T(8,128)} custom-call(s32[3]{0:T(128)S(1)} %pad_add_fusion.2.place, f32[2,1024,384]{2,1,0:T(8,128)} %rows.7, f32[384,1024]{1,0:T(8,128)} %cols.7), custom_call_target="tpu_custom_call" | custom-call | flops 1207959552 | bytes 6291456 | tf_op jit(solution)/shard_map/pallas_call | solution.py:86
  11.0 0.6 collective-permute-start.7
  11.6 0.1 pad_add_fusion.place
  11.7 0.0 copy-done.4
  11.7 0.0 copy-done.5
  11.7 1.6 %shard_map.55 = f32[8,32,512]{2,1,0:T(8,128)} custom-call(s32[3]{0:T(128)S(1)} %pad_add_fusion.place, f32[2,32,1024]{2,1,0:T(8,128)S(1)} %copy-done.4, f32[32,1024]{1,0:T(8,128)S(1)} %bitcast.12), custom_call_target="tpu_custom_call" | custom-call | tf_op jit(solution)/shard_map/pallas_call | solution.py:193
  13.3 8.5 %all-to-all-start = ((f32[8,32,512]{2,1,0:T(8,128)}), f32[8,32,512]{2,1,0:T(8,128)S(1)}, u32[]{:S(2)}, u32[]{:S(2)}) async-start(f32[8,32,512]{2,1,0:T(8,128)} %shard_map.55), calls=%async_computation | async-start | bytes 1048576 | tf_op jit(solution)/shard_map/all_to_all | solution.py:199
  21.8 0.0 collective-permute-done.refs_0_
  21.8 6.1 %shard_map.57 = (f32[1024,128]{1,0:T(8,128)S(1)}, f32[1024,128]{1,0:T(8,128)S(1)}, f32[1024,128]{1,0:T(8,128)}, f32[1024,128]{1,0:T(8,128)}) custom-call(s32[3]{0:T(128)S(1)} %pad_add_fusion.place, f32[2,1024,384]{2,1,0:T(8,128)} %rows.7, f32[384,1024]{1,0:T(8,128)} %cols.7, f32[4,1024,128]{2,1,0:T(8,128)} %collective-permute-done.refs_0_), custom_call_target="tpu_custom_call" | custom-call | flops 1207959552 | bytes 6291456 | tf_op jit(solution)/shard_map/pallas_call | solution.py:86
  27.9 0.0 copy-start
  27.9 1.6 %collective-permute-start.1 = (f32[1024,128]{1,0:T(8,128)S(1)}, f32[1024,128]{1,0:T(8,128)S(1)}, u32[]{:S(2)}, u32[]{:S(2)}) collective-permute-start(f32[1024,128]{1,0:T(8,128)S(1)} %get-tuple-element.24), channel_id=1, source_target_pairs={{0,2},{2,4},{4,6},{6,0},{1,3},{3,5},{5,7},{7,1},{8,10},{10,12},{12... | collective-permute-start | bytes 1572872 | tf_op jit(solution)/shard_map/ppermute | solution.py:20
  29.5 1.1 collective-permute-start.2
  30.6 2.2 %collective-permute-start.3 = (f32[1024,128]{1,0:T(8,128)}, f32[1024,128]{1,0:T(8,128)}, u32[]{:S(2)}, u32[]{:S(2)}) collective-permute-start(f32[1024,128]{1,0:T(8,128)} %get-tuple-element.26), channel_id=1, source_target_pairs={{0,6},{2,0},{4,2},{6,4},{1,7},{3,1},{5,3},{7,5},{8,14},{10,8},{12,... | collective-permute-start | bytes 1572872 | tf_op jit(solution)/shard_map/ppermute | solution.py:20
  32.8 0.0 collective-permute-done.7.refs_0_
  32.8 4.8 %shard_map.61 = (f32[1024,128]{1,0:T(8,128)S(1)}, f32[1024,128]{1,0:T(8,128)}, f32[1024,128]{1,0:T(8,128)}, f32[1024,128]{1,0:T(8,128)}) custom-call(s32[3]{0:T(128)S(1)} %pad_add_fusion.place, f32[2,1024,384]{2,1,0:T(8,128)} %rows.7, f32[384,1024]{1,0:T(8,128)} %cols.7, f32[4,1024,128]{2,1,0:T(8,128)S(1)} %collective-permute-done.7.refs_0_), custom_call_target="tpu_custom_call" | custom-call | flops 1207959552 | bytes 6291456 | tf_op jit(solution)/shard_map/pallas_call | solution.py:86
  37.6 1.7 %collective-permute-start.8 = (f32[1024,128]{1,0:T(8,128)}, f32[1024,128]{1,0:T(8,128)S(1)}, u32[]{:S(2)}, u32[]{:S(2)}) collective-permute-start(f32[1024,128]{1,0:T(8,128)} %get-tuple-element.32), channel_id=1, source_target_pairs={{0,64},{64,128},{128,192},{192,0},{1,65},{65,129},{129,193},{193,1... | collective-permute-start | bytes 1572872 | tf_op jit(solution)/shard_map/ppermute | solution.py:20
  39.3 2.9 %collective-permute-start.9 = (f32[1024,128]{1,0:T(8,128)}, f32[1024,128]{1,0:T(8,128)S(1)}, u32[]{:S(2)}, u32[]{:S(2)}) collective-permute-start(f32[1024,128]{1,0:T(8,128)} %get-tuple-element.33), channel_id=1, source_target_pairs={{0,128},{64,192},{128,0},{192,64},{1,129},{65,193},{129,1},{193,65... | collective-permute-start | bytes 1572872 | tf_op jit(solution)/shard_map/ppermute | solution.py:20
  42.2 0.6 collective-permute-done.1.b
  42.8 0.8 copy-done.2
  43.6 3.0 %collective-permute-start.10 = (f32[1024,128]{1,0:T(8,128)}, f32[1024,128]{1,0:T(8,128)S(1)}, u32[]{:S(2)}, u32[]{:S(2)}) collective-permute-start(f32[1024,128]{1,0:T(8,128)} %get-tuple-element.34), channel_id=1, source_target_pairs={{0,192},{64,0},{128,64},{192,128},{1,193},{65,1},{129,65},{193,129... | collective-permute-start | bytes 1572872 | tf_op jit(solution)/shard_map/ppermute | solution.py:20
  46.6 0.0 all-to-all-done
  46.6 0.3 shard_map.58.rider.part0
  46.9 0.0 collective-permute-done.2.c
  47.0 8.2 %collective-permute-done.3.d = f32[1024,128]{1,0:T(8,128)} collective-permute-done((f32[1024,128]{1,0:T(8,128)}, f32[1024,128]{1,0:T(8,128)}, u32[]{:S(2)}, u32[]{:S(2)}) %collective-permute-start.3) | collective-permute-done | bytes 524320 | tf_op jit(solution)/shard_map/ppermute | solution.py:20
  55.2 1.0 copy-done.1
  56.2 1.0 copy-done.3
  57.3 1.3 shard_map.59
  58.6 1.7 %collective-permute-start.4 = (f32[384,128]{1,0:T(8,128)S(1)}, f32[384,128]{1,0:T(8,128)S(1)}, u32[]{:S(2)}, u32[]{:S(2)}) collective-permute-start(f32[384,128]{1,0:T(8,128)S(1)} %get-tuple-element.28), channel_id=1, source_target_pairs={{0,64},{64,128},{128,192},{192,0},{1,65},{65,129},{129,193},{193,1... | collective-permute-start | bytes 589832 | tf_op jit(solution)/shard_map/ppermute | solution.py:20
  60.2 2.9 %collective-permute-start.5 = (f32[384,128]{1,0:T(8,128)S(1)}, f32[384,128]{1,0:T(8,128)S(1)}, u32[]{:S(2)}, u32[]{:S(2)}) collective-permute-start(f32[384,128]{1,0:T(8,128)S(1)} %get-tuple-element.29), channel_id=1, source_target_pairs={{0,128},{64,192},{128,0},{192,64},{1,129},{65,193},{129,1},{193,65... | collective-permute-start | bytes 589832 | tf_op jit(solution)/shard_map/ppermute | solution.py:20
  63.1 6.7 %collective-permute-done.4.got1.a1 = f32[384,128]{1,0:T(8,128)S(1)} collective-permute-done((f32[384,128]{1,0:T(8,128)S(1)}, f32[384,128]{1,0:T(8,128)S(1)}, u32[]{:S(2)}, u32[]{:S(2)}) %collective-permute-start.4) | collective-permute-done | bytes 196640 | tf_op jit(solution)/shard_map/ppermute | solution.py:20
  69.8 0.6 collective-permute-start.6
  70.4 2.4 %collective-permute-done.5.got2.a2 = f32[384,128]{1,0:T(8,128)S(1)} collective-permute-done((f32[384,128]{1,0:T(8,128)S(1)}, f32[384,128]{1,0:T(8,128)S(1)}, u32[]{:S(2)}, u32[]{:S(2)}) %collective-permute-start.5) | collective-permute-done | bytes 196640 | tf_op jit(solution)/shard_map/ppermute | solution.py:20
  72.8 3.6 %collective-permute-done.6.got3.a3 = f32[384,128]{1,0:T(8,128)S(1)} collective-permute-done((f32[384,128]{1,0:T(8,128)S(1)}, f32[384,128]{1,0:T(8,128)S(1)}, u32[]{:S(2)}, u32[]{:S(2)}) %collective-permute-start.6) | collective-permute-done | bytes 196640 | tf_op jit(solution)/shard_map/ppermute | solution.py:20
  76.4 0.3 shard_map.62.rider.part
  76.6 0.0 collective-permute-done.8.b
  76.6 0.0 collective-permute-done.9.c
  76.7 0.0 collective-permute-done.10.d
  76.7 0.0 copy-start.6
  76.7 0.1 shard_map.63
  76.8 0.1 collective-permute-start.11
  76.9 4.4 %collective-permute-start.12 = (f32[512,128]{1,0:T(8,128)S(1)}, f32[512,128]{1,0:T(8,128)S(1)}, u32[]{:S(2)}, u32[]{:S(2)}) collective-permute-start(f32[512,128]{1,0:T(8,128)S(1)} %get-tuple-element.37), channel_id=1, source_target_pairs={{0,4},{2,6},{4,0},{6,2},{1,5},{3,7},{5,1},{7,3},{8,12},{10,14},{12... | collective-permute-start | bytes 786440 | tf_op jit(solution)/shard_map/ppermute | solution.py:20
  81.3 0.0 collective-permute-start.13
  81.3 5.1 %collective-permute-done.11.b1 = f32[512,128]{1,0:T(8,128)S(1)} collective-permute-done((f32[512,128]{1,0:T(8,128)S(1)}, f32[512,128]{1,0:T(8,128)S(1)}, u32[]{:S(2)}, u32[]{:S(2)}) %collective-permute-start.11) | collective-permute-done | bytes 262176 | tf_op jit(solution)/shard_map/ppermute | solution.py:20
  86.4 2.1 %collective-permute-done.12.b2 = f32[512,128]{1,0:T(8,128)S(1)} collective-permute-done((f32[512,128]{1,0:T(8,128)S(1)}, f32[512,128]{1,0:T(8,128)S(1)}, u32[]{:S(2)}, u32[]{:S(2)}) %collective-permute-start.12) | collective-permute-done | bytes 262176 | tf_op jit(solution)/shard_map/ppermute | solution.py:20
  88.5 3.6 %collective-permute-done.13.b3 = f32[512,128]{1,0:T(8,128)S(1)} collective-permute-done((f32[512,128]{1,0:T(8,128)S(1)}, f32[512,128]{1,0:T(8,128)S(1)}, u32[]{:S(2)}, u32[]{:S(2)}) %collective-permute-start.13) | collective-permute-done | bytes 262176 | tf_op jit(solution)/shard_map/ppermute | solution.py:20
  92.1 0.8 shard_map.64
  92.9 6.9 %all-to-all-start.1 = ((f32[8,64,128]{2,1,0:T(8,128)}), f32[8,64,128]{2,1,0:T(8,128)S(1)}, u32[]{:S(2)}, u32[]{:S(2)}) async-start(f32[8,64,128]{2,1,0:T(8,128)} %get-tuple-element.40), calls=%async_computation.1 | async-start | bytes 524288 | tf_op jit(solution)/shard_map/all_to_all | solution.py:219
  99.8 0.0 collective-permute-start.14
  99.8 11.9 %all-to-all-done.1 = f32[8,64,128]{2,1,0:T(8,128)S(1)} async-done(((f32[8,64,128]{2,1,0:T(8,128)}), f32[8,64,128]{2,1,0:T(8,128)S(1)}, u32[]{:S(2)}, u32[]{:S(2)}) %all-to-all-start.1) | async-done | bytes 262176 | tf_op jit(solution)/shard_map/all_to_all | solution.py:219
  111.8 0.1 collective-permute-start.15
  111.9 2.4 %collective-permute-start.16 = (f32[64,128]{1,0:T(8,128)S(1)}, f32[64,128]{1,0:T(8,128)S(1)}, u32[]{:S(2)}, u32[]{:S(2)}) collective-permute-start(f32[64,128]{1,0:T(8,128)S(1)} %bitcast_subtract_fusion.rest0), channel_id=1, source_target_pairs={{0,128},{64,192},{128,0},{192,64},{1,129},{65,193},{129,1},{193,65... | collective-permute-start | bytes 98312 | tf_op jit(solution)/shard_map/ppermute | solution.py:20
  114.2 0.9 collective-permute-start.17
  115.1 0.0 collective-permute-done.14.mix1
  115.1 1.9 %collective-permute-done.15.rest1 = f32[64,128]{1,0:T(8,128)S(1)} collective-permute-done((f32[64,128]{1,0:T(8,128)S(1)}, f32[64,128]{1,0:T(8,128)S(1)}, u32[]{:S(2)}, u32[]{:S(2)}) %collective-permute-start.15) | collective-permute-done | bytes 32800 | tf_op jit(solution)/shard_map/ppermute | solution.py:20
  117.0 0.4 collective-permute-done.16.rest2
  117.4 0.8 collective-permute-done.17.rest3
  118.2 1.0 shard_map.65
  119.2 12.9 %all_to_all.15 = f32[8,64,128]{2,1,0:T(8,128)S(1)} all-to-all(f32[8,64,128]{2,1,0:T(8,128)S(1)} %shard_map.65), channel_id=1, replica_groups=mesh['y'=4,'z'=8,'x'=4,'core'=2] {'z'}, dimensions={0} | all-to-all | bytes 524288 | tf_op jit(solution)/shard_map/all_to_all | solution.py:231
  132.1 0.6 reduce_sum.19
  (7 shorter events, 0.0 us)
Async XLA Ops:
  5.5 6.2 %copy-start.4 = (f32[2,32,1024]{2,1,0:T(8,128)S(1)}, f32[2,32,1024]{2,1,0:T(8,128)}, u32[]{:S(2)}) copy-start(f32[2,32,1024]{2,1,0:T(8,128)} %inverses.1) | copy-start | bytes 786436
  5.5 6.2 %copy-start.5 = (f32[1024,32]{0,1:T(8,128)S(1)}, f32[1024,32]{0,1:T(8,128)}, u32[]{:S(2)}) copy-start(f32[1024,32]{0,1:T(8,128)} %param.8) | copy-start | bytes 393220
  5.5 16.3 %collective-permute-start = (f32[4,1024,128]{2,1,0:T(8,128)}, f32[4,1024,128]{2,1,0:T(8,128)}, u32[]{:S(2)}, u32[]{:S(2)}) collective-permute-start(f32[4,1024,128]{2,1,0:T(8,128)} %shard_map.56), channel_id=1, source_target_pairs={{0,1},{1,0},{2,3},{3,2},{4,5},{5,4},{6,7},{7,6},{8,9},{9,8},{10,11... | collective-permute-start | bytes 6291464 | tf_op jit(solution)/shard_map/ppermute | solution.py:20
  11.0 21.8 %collective-permute-start.7 = (f32[4,1024,128]{2,1,0:T(8,128)}, f32[4,1024,128]{2,1,0:T(8,128)S(1)}, u32[]{:S(2)}, u32[]{:S(2)}) collective-permute-start(f32[4,1024,128]{2,1,0:T(8,128)} %shard_map.60), channel_id=1, source_target_pairs={{0,1},{1,0},{2,3},{3,2},{4,5},{5,4},{6,7},{7,6},{8,9},{9,8},{10,11... | collective-permute-start | bytes 6291464 | tf_op jit(solution)/shard_map/ppermute | solution.py:20
  13.3 33.3 %all-to-all-start = ((f32[8,32,512]{2,1,0:T(8,128)}), f32[8,32,512]{2,1,0:T(8,128)S(1)}, u32[]{:S(2)}, u32[]{:S(2)}) async-start(f32[8,32,512]{2,1,0:T(8,128)} %shard_map.55), calls=%async_computation | async-start | bytes 1048576 | tf_op jit(solution)/shard_map/all_to_all | solution.py:199
  27.9 9.7 %copy-start = (f32[1024,128]{1,0:T(8,128)}, f32[1024,128]{1,0:T(8,128)S(1)}, u32[]{:S(2)}) copy-start(f32[1024,128]{1,0:T(8,128)S(1)} %get-tuple-element.23.a) | copy-start | bytes 1572868
  27.9 14.9 %collective-permute-start.1 = (f32[1024,128]{1,0:T(8,128)S(1)}, f32[1024,128]{1,0:T(8,128)S(1)}, u32[]{:S(2)}, u32[]{:S(2)}) collective-permute-start(f32[1024,128]{1,0:T(8,128)S(1)} %get-tuple-element.24), channel_id=1, source_target_pairs={{0,2},{2,4},{4,6},{6,0},{1,3},{3,5},{5,7},{7,1},{8,10},{10,12},{12... | collective-permute-start | bytes 1572872 | tf_op jit(solution)/shard_map/ppermute | solution.py:20
  29.5 17.4 %collective-permute-start.2 = (f32[1024,128]{1,0:T(8,128)}, f32[1024,128]{1,0:T(8,128)}, u32[]{:S(2)}, u32[]{:S(2)}) collective-permute-start(f32[1024,128]{1,0:T(8,128)} %get-tuple-element.25), channel_id=1, source_target_pairs={{0,4},{2,6},{4,0},{6,2},{1,5},{3,7},{5,1},{7,3},{8,12},{10,14},{12... | collective-permute-start | bytes 1572872 | tf_op jit(solution)/shard_map/ppermute | solution.py:20
  30.6 24.6 %collective-permute-start.3 = (f32[1024,128]{1,0:T(8,128)}, f32[1024,128]{1,0:T(8,128)}, u32[]{:S(2)}, u32[]{:S(2)}) collective-permute-start(f32[1024,128]{1,0:T(8,128)} %get-tuple-element.26), channel_id=1, source_target_pairs={{0,6},{2,0},{4,2},{6,4},{1,7},{3,1},{5,3},{7,5},{8,14},{10,8},{12,... | collective-permute-start | bytes 1572872 | tf_op jit(solution)/shard_map/ppermute | solution.py:20
  37.6 39.0 %collective-permute-start.8 = (f32[1024,128]{1,0:T(8,128)}, f32[1024,128]{1,0:T(8,128)S(1)}, u32[]{:S(2)}, u32[]{:S(2)}) collective-permute-start(f32[1024,128]{1,0:T(8,128)} %get-tuple-element.32), channel_id=1, source_target_pairs={{0,64},{64,128},{128,192},{192,0},{1,65},{65,129},{129,193},{193,1... | collective-permute-start | bytes 1572872 | tf_op jit(solution)/shard_map/ppermute | solution.py:20
  39.3 37.4 %collective-permute-start.9 = (f32[1024,128]{1,0:T(8,128)}, f32[1024,128]{1,0:T(8,128)S(1)}, u32[]{:S(2)}, u32[]{:S(2)}) collective-permute-start(f32[1024,128]{1,0:T(8,128)} %get-tuple-element.33), channel_id=1, source_target_pairs={{0,128},{64,192},{128,0},{192,64},{1,129},{65,193},{129,1},{193,65... | collective-permute-start | bytes 1572872 | tf_op jit(solution)/shard_map/ppermute | solution.py:20
  42.8 0.8 copy-start.2
  43.6 33.0 %collective-permute-start.10 = (f32[1024,128]{1,0:T(8,128)}, f32[1024,128]{1,0:T(8,128)S(1)}, u32[]{:S(2)}, u32[]{:S(2)}) collective-permute-start(f32[1024,128]{1,0:T(8,128)} %get-tuple-element.34), channel_id=1, source_target_pairs={{0,192},{64,0},{128,64},{192,128},{1,193},{65,1},{129,65},{193,129... | collective-permute-start | bytes 1572872 | tf_op jit(solution)/shard_map/ppermute | solution.py:20
  55.2 1.0 copy-start.1
  56.2 1.0 copy-start.3
  58.6 11.3 %collective-permute-start.4 = (f32[384,128]{1,0:T(8,128)S(1)}, f32[384,128]{1,0:T(8,128)S(1)}, u32[]{:S(2)}, u32[]{:S(2)}) collective-permute-start(f32[384,128]{1,0:T(8,128)S(1)} %get-tuple-element.28), channel_id=1, source_target_pairs={{0,64},{64,128},{128,192},{192,0},{1,65},{65,129},{129,193},{193,1... | collective-permute-start | bytes 589832 | tf_op jit(solution)/shard_map/ppermute | solution.py:20
  60.2 12.5 %collective-permute-start.5 = (f32[384,128]{1,0:T(8,128)S(1)}, f32[384,128]{1,0:T(8,128)S(1)}, u32[]{:S(2)}, u32[]{:S(2)}) collective-permute-start(f32[384,128]{1,0:T(8,128)S(1)} %get-tuple-element.29), channel_id=1, source_target_pairs={{0,128},{64,192},{128,0},{192,64},{1,129},{65,193},{129,1},{193,65... | collective-permute-start | bytes 589832 | tf_op jit(solution)/shard_map/ppermute | solution.py:20
  69.8 6.5 %collective-permute-start.6 = (f32[384,128]{1,0:T(8,128)S(1)}, f32[384,128]{1,0:T(8,128)S(1)}, u32[]{:S(2)}, u32[]{:S(2)}) collective-permute-start(f32[384,128]{1,0:T(8,128)S(1)} %get-tuple-element.30), channel_id=1, source_target_pairs={{0,192},{64,0},{128,64},{192,128},{1,193},{65,1},{129,65},{193,129... | collective-permute-start | bytes 589832 | tf_op jit(solution)/shard_map/ppermute | solution.py:20
  76.7 35.1 %copy-start.6 = (f32[2,32,128]{2,1,0:T(8,128)S(1)}, f32[2,32,128]{2,1,0:T(8,128)}, u32[]{:S(2)}) copy-start(f32[2,32,128]{2,1,0:T(8,128)} %param.7) | copy-start | bytes 98308
  76.8 9.5 %collective-permute-start.11 = (f32[512,128]{1,0:T(8,128)S(1)}, f32[512,128]{1,0:T(8,128)S(1)}, u32[]{:S(2)}, u32[]{:S(2)}) collective-permute-start(f32[512,128]{1,0:T(8,128)S(1)} %get-tuple-element.36), channel_id=1, source_target_pairs={{0,2},{2,4},{4,6},{6,0},{1,3},{3,5},{5,7},{7,1},{8,10},{10,12},{12... | collective-permute-start | bytes 786440 | tf_op jit(solution)/shard_map/ppermute | solution.py:20
  76.9 11.6 %collective-permute-start.12 = (f32[512,128]{1,0:T(8,128)S(1)}, f32[512,128]{1,0:T(8,128)S(1)}, u32[]{:S(2)}, u32[]{:S(2)}) collective-permute-start(f32[512,128]{1,0:T(8,128)S(1)} %get-tuple-element.37), channel_id=1, source_target_pairs={{0,4},{2,6},{4,0},{6,2},{1,5},{3,7},{5,1},{7,3},{8,12},{10,14},{12... | collective-permute-start | bytes 786440 | tf_op jit(solution)/shard_map/ppermute | solution.py:20
  81.3 10.8 %collective-permute-start.13 = (f32[512,128]{1,0:T(8,128)S(1)}, f32[512,128]{1,0:T(8,128)S(1)}, u32[]{:S(2)}, u32[]{:S(2)}) collective-permute-start(f32[512,128]{1,0:T(8,128)S(1)} %get-tuple-element.38), channel_id=1, source_target_pairs={{0,6},{2,0},{4,2},{6,4},{1,7},{3,1},{5,3},{7,5},{8,14},{10,8},{12,... | collective-permute-start | bytes 786440 | tf_op jit(solution)/shard_map/ppermute | solution.py:20
  92.9 18.9 %all-to-all-start.1 = ((f32[8,64,128]{2,1,0:T(8,128)}), f32[8,64,128]{2,1,0:T(8,128)S(1)}, u32[]{:S(2)}, u32[]{:S(2)}) async-start(f32[8,64,128]{2,1,0:T(8,128)} %get-tuple-element.40), calls=%async_computation.1 | async-start | bytes 524288 | tf_op jit(solution)/shard_map/all_to_all | solution.py:219
  99.8 15.3 %collective-permute-start.14 = (f32[256,128]{1,0:T(8,128)S(1)}, f32[256,128]{1,0:T(8,128)S(1)}, u32[]{:S(2)}, u32[]{:S(2)}) collective-permute-start(f32[256,128]{1,0:T(8,128)S(1)} %get-tuple-element.39.mix0), channel_id=1, source_target_pairs={{0,1},{1,0},{2,3},{3,2},{4,5},{5,4},{6,7},{7,6},{8,9},{9,8},{10,11... | collective-permute-start | bytes 393224 | tf_op jit(solution)/shard_map/ppermute | solution.py:20
  111.8 5.2 %collective-permute-start.15 = (f32[64,128]{1,0:T(8,128)S(1)}, f32[64,128]{1,0:T(8,128)S(1)}, u32[]{:S(2)}, u32[]{:S(2)}) collective-permute-start(f32[64,128]{1,0:T(8,128)S(1)} %bitcast_subtract_fusion.rest0), channel_id=1, source_target_pairs={{0,64},{64,128},{128,192},{192,0},{1,65},{65,129},{129,193},{193,1... | collective-permute-start | bytes 98312 | tf_op jit(solution)/shard_map/ppermute | solution.py:20
  111.9 5.5 %collective-permute-start.16 = (f32[64,128]{1,0:T(8,128)S(1)}, f32[64,128]{1,0:T(8,128)S(1)}, u32[]{:S(2)}, u32[]{:S(2)}) collective-permute-start(f32[64,128]{1,0:T(8,128)S(1)} %bitcast_subtract_fusion.rest0), channel_id=1, source_target_pairs={{0,128},{64,192},{128,0},{192,64},{1,129},{65,193},{129,1},{193,65... | collective-permute-start | bytes 98312 | tf_op jit(solution)/shard_map/ppermute | solution.py:20
  114.2 4.0 %collective-permute-start.17 = (f32[64,128]{1,0:T(8,128)S(1)}, f32[64,128]{1,0:T(8,128)S(1)}, u32[]{:S(2)}, u32[]{:S(2)}) collective-permute-start(f32[64,128]{1,0:T(8,128)S(1)} %bitcast_subtract_fusion.rest0), channel_id=1, source_target_pairs={{0,192},{64,0},{128,64},{192,128},{1,193},{65,1},{129,65},{193,129... | collective-permute-start | bytes 98312 | tf_op jit(solution)/shard_map/ppermute | solution.py:20

commit v2 on v1

v2 whole, which is shorter than its diff:
```python
import jax
import jax.numpy as jnp
from jax import lax
from jax.experimental import pallas as pl
from jax.experimental.pallas import tpu as pltpu
from jax.sharding import Mesh
from jax.sharding import PartitionSpec as P


AXES = ("y", "z", "x", "core")
F32 = jnp.float32
BF16 = jnp.bfloat16
EXACT = lax.Precision.HIGHEST
SMEM = pl.BlockSpec(memory_space=pltpu.SMEM)
FAR = pl.BlockSpec(memory_space=pltpu.HBM)
SMALL = pltpu.CompilerParams(vmem_limit_bytes=6 << 20)


def far(value):
    return pltpu.with_memory_space_constraint(value, pltpu.HBM)


def shift(value, axis, step, size):
    return lax.ppermute(value, axis, [(i, (i + step) % size) for i in range(size)])


def halves(value):
    high = value.astype(BF16)
    return high, (value - high.astype(F32)).astype(BF16)


def product_kernel(panel, by_column, has_received, nx, ny):
    def kernel(place, rows, cols, *refs):
        received = refs[0] if has_received else None
        outs = refs[1:-4] if has_received else refs[:-4]
        left, right, blocks, sems = refs[-4:]
        depth = cols.shape[0]
        size = blocks.shape[1]
        copies = []
        for jy in range(ny):
            at = pl.multiple_of(lax.rem(place[1] + jy, ny) * size, size)
            copies.append(
                pltpu.make_async_copy(
                    rows.at[panel, pl.ds(at, size), :], blocks.at[jy], sems.at[jy]
                )
            )
        for copy in copies:
            copy.start()
        for jx in range(nx):
            at = lax.rem(place[0] + jx, nx) * 256 + place[2] * 128
            high, low = halves(cols[:, pl.ds(pl.multiple_of(at, 128), 128)])
            span = slice(jx * 128, (jx + 1) * 128)
            right[0:depth, span] = high
            right[depth : 2 * depth, span] = low
            right[2 * depth : 3 * depth, span] = high
        for jy in range(ny):
            copies[jy].wait()
            high, low = halves(blocks[jy])
            left[:, 0:depth] = high
            left[:, depth : 2 * depth] = high
            left[:, 2 * depth : 3 * depth] = low
            value = jnp.dot(left[...], right[...], preferred_element_type=F32)
            for jx in range(nx):
                block = value[:, jx * 128 : (jx + 1) * 128]
                first, second = (jx, jy) if by_column else (jy, jx)
                span = slice(second * size, (second + 1) * size)
                if has_received:
                    outs[first][span, :] = block + received[first, span, :]
                else:
                    outs[0][first, span, :] = block

    return kernel


def products(place, panel, rows, cols, received, by_column, nx, ny):
    kernel = product_kernel(panel, by_column, received is not None, nx, ny)
    _, size, depth = rows.shape
    first = nx if by_column else ny
    if received is None:
        shapes = jax.ShapeDtypeStruct((first, size, 128), F32)
        args = (place, rows, cols)
    else:
        shapes = [jax.ShapeDtypeStruct((size, 128), F32)] * first
        args = (place, rows, cols, received)
    return pl.pallas_call(
        kernel,
        out_shape=shapes,
        in_specs=[SMEM, FAR] + [pl.BlockSpec()] * (len(args) - 2),
        scratch_shapes=[
            pltpu.VMEM((size // ny, 3 * depth), BF16),
            pltpu.VMEM((3 * depth, nx * 128), BF16),
            pltpu.VMEM((ny, size // ny, depth), F32),
            pltpu.SemaphoreType.DMA((ny,)),
        ],
        compiler_params=pltpu.CompilerParams(vmem_limit_bytes=12 << 20),
        cost_estimate=pl.CostEstimate(
            flops=6 * size * depth * nx * 128, transcendentals=0, bytes_accessed=6 << 20
        ),
    )(*args)


def pack_kernel(place, inverses, across, out):
    at = pl.multiple_of(place[0] * 256 + place[2] * 128, 128)
    strip_of_coupling = across[:, pl.ds(at, 128)]
    strip_of_second = inverses[1, :, pl.ds(at, 128)]
    nz = out.shape[0]
    for z in range(nz):
        out[z, :, 0:128] = strip_of_coupling
        out[z, :, 128:256] = strip_of_second
        for panel in range(2):
            pieces = [inverses[panel, :, y * 256 + z * 32 : y * 256 + z * 32 + 32] for y in range(4)]
            out[z, :, 256 + panel * 128 : 384 + panel * 128] = jnp.concatenate(pieces, axis=1)


def couple_kernel(tiles, out):
    out[...] = lax.dot_general(
        tiles[:, 0:128],
        tiles[:, 256:384],
        (((0,), (0,)), ((), ())),
        precision=EXACT,
        preferred_element_type=F32,
    )


def chain_kernel(tiles, part0, part1, part2, part3, out):
    total = (part0[...] + part1[...]) + (part2[...] + part3[...])
    out[...] = jnp.dot(tiles[:, 128:256], total, precision=EXACT, preferred_element_type=F32)


def sum_kernel(a, b, out):
    out[...] = a[...] + b[...]


def gather_sums_kernel(a, b, c, d, *outs):
    size = outs[0].shape[0]
    for j, out in enumerate(outs):
        span = slice(j * size, (j + 1) * size)
        out[...] = (a[span, :] + b[span, :]) + (c[span, :] + d[span, :])


def gather_sums(parts, count):
    size = parts[0].shape[0] // count
    return pl.pallas_call(
        gather_sums_kernel,
        out_shape=[jax.ShapeDtypeStruct((size, 128), F32)] * count,
        compiler_params=SMALL,
    )(*parts)


def interleave_kernel(a0, a1, a2, a3, b0, b1, b2, b3, out):
    low = (a0[...] + a1[...]) + (a2[...] + a3[...])
    high = (b0[...] + b1[...]) + (b2[...] + b3[...])
    for z in range(out.shape[0]):
        out[z, 0:32, :] = low[z * 32 : (z + 1) * 32, :]
        out[z, 32:64, :] = high[z * 32 : (z + 1) * 32, :]


def apply_kernel(place, tiles, mix0, mix1, mix2, mix3, rest0, rest1, rest2, rest3, out, first, second):
    ny = 4
    for step, rest in enumerate((rest0, rest1, rest2, rest3)):
        at = pl.multiple_of(lax.rem(place[1] + ny - step, ny) * 32, 32)
        first[pl.ds(at, 32), :] = rest[0:32, :]
        second[pl.ds(at, 32), :] = rest[32:64, :]
    mix = (mix0[...] + mix1[...]) + (mix2[...] + mix3[...])
    low = jnp.dot(tiles[:, 256:384], first[...], precision=EXACT, preferred_element_type=F32)
    high = jnp.dot(tiles[:, 384:512], second[...], precision=EXACT, preferred_element_type=F32)
    high = high - jnp.dot(mix, first[...], precision=EXACT, preferred_element_type=F32)
    for z in range(out.shape[0]):
        out[z, 0:32, :] = low[z * 32 : (z + 1) * 32, :]
        out[z, 32:64, :] = high[z * 32 : (z + 1) * 32, :]


def steps(panel_rows, solved, right_side, coupling, inverses):
    nx, ny, nz, nc = (lax.axis_size(a) for a in ("x", "y", "z", "core"))
    x, y, core = lax.axis_index("x"), lax.axis_index("y"), lax.axis_index("core")
    panel_rows = far(panel_rows)
    own = jnp.stack([x, y, core]).astype(jnp.int32)
    other = jnp.stack([x, y, 1 - core]).astype(jnp.int32)

    packed = pl.pallas_call(
        pack_kernel,
        out_shape=jax.ShapeDtypeStruct((nz, 32, 512), F32),
        in_specs=[SMEM, pl.BlockSpec(), pl.BlockSpec()],
        compiler_params=SMALL,
    )(own, inverses, coupling.T)
    tiles = lax.all_to_all(packed, "z", 0, 0, tiled=True).reshape(nz * 32, 512)

    to_partner0 = products(other, 0, panel_rows, solved, None, True, nx, ny)
    from_partner0 = shift(to_partner0, "core", 1, nc)
    to_partner1 = products(other, 1, panel_rows, solved, None, False, nx, ny)
    from_partner1 = shift(to_partner1, "core", 1, nc)
    blocks0 = products(own, 0, panel_rows, solved, from_partner0, True, nx, ny)
    got0 = [blocks0[0]] + [shift(blocks0[j], "x", j, nx) for j in range(1, nx)]
    blocks1 = products(own, 1, panel_rows, solved, from_partner1, False, nx, ny)
    got1 = [blocks1[0]] + [shift(blocks1[j], "y", j, ny) for j in range(1, ny)]

    coupled = pl.pallas_call(
        couple_kernel, out_shape=jax.ShapeDtypeStruct((128, 128), F32), compiler_params=SMALL
    )(tiles)
    coupled_all = [coupled] + [shift(coupled, "y", j, ny) for j in range(1, ny)]
    chained = pl.pallas_call(
        chain_kernel, out_shape=jax.ShapeDtypeStruct((256, 128), F32), compiler_params=SMALL
    )(tiles, *coupled_all)
    mix = pl.pallas_call(
        sum_kernel, out_shape=jax.ShapeDtypeStruct((256, 128), F32), compiler_params=SMALL
    )(chained, shift(chained, "core", 1, nc))
    mixes = [mix] + [shift(mix, "x", j, nx) for j in range(1, nx)]

    sums0 = gather_sums(got0, ny)
    again0 = [sums0[0]] + [shift(sums0[j], "y", j, ny) for j in range(1, ny)]
    sums1 = gather_sums(got1, nx)
    again1 = [sums1[0]] + [shift(sums1[j], "x", j, nx) for j in range(1, nx)]
    by_z = pl.pallas_call(
        interleave_kernel, out_shape=jax.ShapeDtypeStruct((nz, 64, 128), F32), compiler_params=SMALL
    )(*again0, *again1)
    old = lax.all_to_all(by_z, "z", 0, 0, tiled=True).sum(axis=0)
    rest = right_side.reshape(64, 128) - old

    rests = [rest] + [shift(rest, "y", j, ny) for j in range(1, ny)]
    solved_part = pl.pallas_call(
        apply_kernel,
        out_shape=jax.ShapeDtypeStruct((nz, 64, 128), F32),
        in_specs=[SMEM] + [pl.BlockSpec()] * 9,
        scratch_shapes=[pltpu.VMEM((128, 128), F32), pltpu.VMEM((128, 128), F32)],
        compiler_params=SMALL,
    )(own, tiles, *mixes, *rests)
    panels = lax.all_to_all(solved_part, "z", 0, 0, tiled=True).sum(axis=0)
    return panels.reshape(right_side.shape)


def solution(mesh):
    finer = Mesh(mesh.devices.reshape(4, 8, 4, 2), AXES)
    prow, pcol = ("y", "z"), ("x", "core")
    return jax.shard_map(
        steps,
        mesh=finer,
        in_specs=(
            P(None, None, AXES),
            P(AXES, None),
            P(None, prow, pcol),
            P(None, prow),
            P(None, prow, None),
        ),
        out_specs=P(None, prow, pcol),
        check_vma=False,
    )
```

time: 134 us -> 129 us (0.963)
  the two profiles are of different devices: /device:TPU:2 before, /device:TPU:24 now
where the time goes in v2:
time: 129 us; the launch traced here: 128 us
  starting transfers between devices  43.5 us (34%)
  waiting for transfers between devices  41.8 us (32%)
  Pallas kernels  21.5 us (17%)
  blocking collectives  17.5 us (14%)
  local copies, waits for them, and re-layouts  3.03 us (2%)
    ppermute x24, waiting for transfers between devices, shift(): lax.ppermute(value, axis, [(i, (i + step) % size) for i in range(size)])  41.8 us
    ppermute x24, starting transfers between devices, shift(): lax.ppermute(value, axis, [(i, (i + step) % size) for i in range(size)])  29.8 us
    all_to_all x1, blocking collectives, steps(): panels = lax.all_to_all(solved_part, 'z', 0, 0, tiled=True).sum(axis=0)  17.5 us
    pallas_call x4, Pallas kernels, products(): pl.pallas_call(kernel, out_shape=shapes, in_specs=[SMEM, FAR] + [pl.Block...  17.3 us
    all_to_all x1, starting transfers between devices, steps(): old = lax.all_to_all(by_z, 'z', 0, 0, tiled=True).sum(axis=0)  6.93 us
    all_to_all x1, starting transfers between devices, steps(): tiles = lax.all_to_all(packed, 'z', 0, 0, tiled=True).reshape(nz * 32, 512)  6.76 us
    unnamed x14, local copies, waits for them, and re-layouts  3.03 us
  transfers between devices with their start and end apart: 26, of which 14 were waited for; matrix products, arithmetic and copies ran while one was open for 0% of the time, Pallas kernels for 13%

profile of v2, /device:TPU:24, one launch (start us, length us, event | category | flops | bytes accessed | tf_op | source)
XLA Modules:
  0.0 128.3 jit_solution(4822344931427900507)
XLA Ops:
  0.0 0.1 pad_add_fusion.2.place
  0.1 1.4 %copy-done = f32[384,1024]{1,0:T(8,128)S(1)} copy-done((f32[384,1024]{1,0:T(8,128)S(1)}, f32[384,1024]{1,0:T(8,128)}, u32[]{:S(2)}) %copy-start) | copy-done | bytes 1572888
  1.5 3.6 %shard_map.62 = f32[4,1024,128]{2,1,0:T(8,128)S(1)} custom-call(s32[3]{0:T(128)S(1)} %pad_add_fusion.2.place, f32[2,1024,384]{2,1,0:T(8,128)} %rows.7, f32[384,1024]{1,0:T(8,128)S(1)} %copy-done), custom_call_target="tpu_custom_call" | custom-call | flops 1207959552 | bytes 6291456 | tf_op jit(solution)/shard_map/pallas_call | solution.py:85
  5.1 0.1 collective-permute-start.14
  5.2 5.0 %shard_map.59 = f32[4,1024,128]{2,1,0:T(8,128)} custom-call(s32[3]{0:T(128)S(1)} %pad_add_fusion.2.place, f32[2,1024,384]{2,1,0:T(8,128)} %rows.7, f32[384,1024]{1,0:T(8,128)S(1)} %copy-done), custom_call_target="tpu_custom_call" | custom-call | flops 1207959552 | bytes 6291456 | tf_op jit(solution)/shard_map/pallas_call | solution.py:85
  10.2 0.6 collective-permute-start.7
  10.8 0.1 pad_add_fusion.place
  10.9 3.9 %shard_map.63 = (f32[1024,128]{1,0:T(8,128)S(1)}, f32[1024,128]{1,0:T(8,128)}, f32[1024,128]{1,0:T(8,128)S(1)}, f32[1024,128]{1,0:T(8,128)S(1)}) custom-call(s32[3]{0:T(128)S(1)} %pad_add_fusion.place, f32[2,1024,384]{2,1,0:T(8,128)} %rows.7, f32[384,1024]{1,0:T(8,128)S(1)} %copy-done, f32[4,1024,128]{2,1,0:T(8,128)S(1)} %collective-permute-done.14.refs_0_), custom_call_target="tpu_custom_call" | custom-call | flops 1207959552 | bytes 6291456 | tf_op jit(solution)/shard_map/pallas_call | solution.py:85
  14.9 0.8 copy-done.4
  15.7 0.8 copy-done.5
  16.5 1.9 %collective-permute-start.15 = (f32[1024,128]{1,0:T(8,128)}, f32[1024,128]{1,0:T(8,128)S(1)}, u32[]{:S(2)}, u32[]{:S(2)}) collective-permute-start(f32[1024,128]{1,0:T(8,128)} %get-tuple-element.30), channel_id=1, source_target_pairs={{0,64},{64,128},{128,192},{192,0},{1,65},{65,129},{129,193},{193,1... | collective-permute-start | bytes 1572872 | tf_op jit(solution)/shard_map/ppermute | solution.py:24
  18.4 1.6 %shard_map.55 = f32[8,32,512]{2,1,0:T(8,128)} custom-call(s32[3]{0:T(128)S(1)} %pad_add_fusion.place, f32[2,32,1024]{2,1,0:T(8,128)S(1)} %copy-done.2, f32[32,1024]{1,0:T(8,128)S(1)} %bitcast.12), custom_call_target="tpu_custom_call" | custom-call | tf_op jit(solution)/shard_map/pallas_call | solution.py:180
  20.0 6.8 %all-to-all-start = ((f32[8,32,512]{2,1,0:T(8,128)}), f32[8,32,512]{2,1,0:T(8,128)S(1)}, u32[]{:S(2)}, u32[]{:S(2)}) async-start(f32[8,32,512]{2,1,0:T(8,128)} %shard_map.55), calls=%async_computation | async-start | bytes 1048576 | tf_op jit(solution)/shard_map/all_to_all | solution.py:186
  26.8 2.6 %collective-permute-start.16 = (f32[1024,128]{1,0:T(8,128)}, f32[1024,128]{1,0:T(8,128)S(1)}, u32[]{:S(2)}, u32[]{:S(2)}) collective-permute-start(f32[1024,128]{1,0:T(8,128)} %copy-done.5), channel_id=1, source_target_pairs={{0,128},{64,192},{128,0},{192,64},{1,129},{65,193},{129,1},{193,65... | collective-permute-start | bytes 1572872 | tf_op jit(solution)/shard_map/ppermute | solution.py:24
  29.4 0.0 collective-permute-start.17
  29.4 0.0 collective-permute-done.7.refs_0_
  29.4 4.7 %shard_map.60 = (f32[1024,128]{1,0:T(8,128)S(1)}, f32[1024,128]{1,0:T(8,128)S(1)}, f32[1024,128]{1,0:T(8,128)S(1)}, f32[1024,128]{1,0:T(8,128)S(1)}) custom-call(s32[3]{0:T(128)S(1)} %pad_add_fusion.place, f32[2,1024,384]{2,1,0:T(8,128)} %rows.7, f32[384,1024]{1,0:T(8,128)S(1)} %copy-done.1, f32[4,1024,128]{2,1,0:T(8,128)} %collective-permute-done.7.refs_0_), custom_call_target="tpu_custom_call" | custom-call | flops 1207959552 | bytes 6291456 | tf_op jit(solution)/shard_map/pallas_call | solution.py:85
  34.1 2.8 %collective-permute-start.10 = (f32[1024,128]{1,0:T(8,128)S(1)}, f32[1024,128]{1,0:T(8,128)S(1)}, u32[]{:S(2)}, u32[]{:S(2)}) collective-permute-start(f32[1024,128]{1,0:T(8,128)S(1)} %get-tuple-element.24), channel_id=1, source_target_pairs={{0,6},{2,0},{4,2},{6,4},{1,7},{3,1},{5,3},{7,5},{8,14},{10,8},{12,... | collective-permute-start | bytes 1572872 | tf_op jit(solution)/shard_map/ppermute | solution.py:24
  37.0 4.4 %collective-permute-done.15.b = f32[1024,128]{1,0:T(8,128)S(1)} collective-permute-done((f32[1024,128]{1,0:T(8,128)}, f32[1024,128]{1,0:T(8,128)S(1)}, u32[]{:S(2)}, u32[]{:S(2)}) %collective-permute-start.15) | collective-permute-done | bytes 524320 | tf_op jit(solution)/shard_map/ppermute | solution.py:24
  41.4 0.0 collective-permute-start.9
  41.4 2.0 %collective-permute-done.16.c = f32[1024,128]{1,0:T(8,128)S(1)} collective-permute-done((f32[1024,128]{1,0:T(8,128)}, f32[1024,128]{1,0:T(8,128)S(1)}, u32[]{:S(2)}, u32[]{:S(2)}) %collective-permute-start.16) | collective-permute-done | bytes 524320 | tf_op jit(solution)/shard_map/ppermute | solution.py:24
  43.4 9.7 %collective-permute-done.17.d = f32[1024,128]{1,0:T(8,128)S(1)} collective-permute-done((f32[1024,128]{1,0:T(8,128)}, f32[1024,128]{1,0:T(8,128)S(1)}, u32[]{:S(2)}, u32[]{:S(2)}) %collective-permute-start.17) | collective-permute-done | bytes 524320 | tf_op jit(solution)/shard_map/ppermute | solution.py:24
  53.1 0.1 shard_map.64
  53.2 1.7 %collective-permute-start.18 = (f32[256,128]{1,0:T(8,128)S(1)}, f32[256,128]{1,0:T(8,128)S(1)}, u32[]{:S(2)}, u32[]{:S(2)}) collective-permute-start(f32[256,128]{1,0:T(8,128)S(1)} %get-tuple-element.34), channel_id=1, source_target_pairs={{0,2},{2,4},{4,6},{6,0},{1,3},{3,5},{5,7},{7,1},{8,10},{10,12},{12... | collective-permute-start | bytes 393224 | tf_op jit(solution)/shard_map/ppermute | solution.py:24
  55.0 2.7 %collective-permute-start.19 = (f32[256,128]{1,0:T(8,128)S(1)}, f32[256,128]{1,0:T(8,128)S(1)}, u32[]{:S(2)}, u32[]{:S(2)}) collective-permute-start(f32[256,128]{1,0:T(8,128)S(1)} %get-tuple-element.35), channel_id=1, source_target_pairs={{0,4},{2,6},{4,0},{6,2},{1,5},{3,7},{5,1},{7,3},{8,12},{10,14},{12... | collective-permute-start | bytes 393224 | tf_op jit(solution)/shard_map/ppermute | solution.py:24
  57.7 5.0 %collective-permute-done.10.d = f32[1024,128]{1,0:T(8,128)S(1)} collective-permute-done((f32[1024,128]{1,0:T(8,128)S(1)}, f32[1024,128]{1,0:T(8,128)S(1)}, u32[]{:S(2)}, u32[]{:S(2)}) %collective-permute-start.10) | collective-permute-done | bytes 524320 | tf_op jit(solution)/shard_map/ppermute | solution.py:24
  62.7 3.7 %collective-permute-start.20 = (f32[256,128]{1,0:T(8,128)S(1)}, f32[256,128]{1,0:T(8,128)S(1)}, u32[]{:S(2)}, u32[]{:S(2)}) collective-permute-start(f32[256,128]{1,0:T(8,128)S(1)} %get-tuple-element.36), channel_id=1, source_target_pairs={{0,6},{2,0},{4,2},{6,4},{1,7},{3,1},{5,3},{7,5},{8,14},{10,8},{12,... | collective-permute-start | bytes 393224 | tf_op jit(solution)/shard_map/ppermute | solution.py:24
  66.4 0.1 shard_map.61
  66.5 0.0 copy-start.6
  66.5 3.0 %collective-permute-start.11 = (f32[256,128]{1,0:T(8,128)S(1)}, f32[256,128]{1,0:T(8,128)S(1)}, u32[]{:S(2)}, u32[]{:S(2)}) collective-permute-start(f32[256,128]{1,0:T(8,128)S(1)} %get-tuple-element.26), channel_id=1, source_target_pairs={{0,64},{64,128},{128,192},{192,0},{1,65},{65,129},{129,193},{193,1... | collective-permute-start | bytes 393224 | tf_op jit(solution)/shard_map/ppermute | solution.py:24
  69.6 0.2 collective-permute-start.12
  69.8 0.0 collective-permute-done.18.b1
  69.8 1.3 %collective-permute-start.13 = (f32[256,128]{1,0:T(8,128)S(1)}, f32[256,128]{1,0:T(8,128)S(1)}, u32[]{:S(2)}, u32[]{:S(2)}) collective-permute-start(f32[256,128]{1,0:T(8,128)S(1)} %get-tuple-element.28), channel_id=1, source_target_pairs={{0,192},{64,0},{128,64},{192,128},{1,193},{65,1},{129,65},{193,129... | collective-permute-start | bytes 393224 | tf_op jit(solution)/shard_map/ppermute | solution.py:24
  71.1 2.4 %collective-permute-done.11.a1 = f32[256,128]{1,0:T(8,128)S(1)} collective-permute-done((f32[256,128]{1,0:T(8,128)S(1)}, f32[256,128]{1,0:T(8,128)S(1)}, u32[]{:S(2)}, u32[]{:S(2)}) %collective-permute-start.11) | collective-permute-done | bytes 131104 | tf_op jit(solution)/shard_map/ppermute | solution.py:24
  73.5 2.6 %collective-permute-done.12.a2 = f32[256,128]{1,0:T(8,128)S(1)} collective-permute-done((f32[256,128]{1,0:T(8,128)S(1)}, f32[256,128]{1,0:T(8,128)S(1)}, u32[]{:S(2)}, u32[]{:S(2)}) %collective-permute-start.12) | collective-permute-done | bytes 131104 | tf_op jit(solution)/shard_map/ppermute | solution.py:24
  76.1 1.2 collective-permute-done.13.a3
  77.4 0.7 shard_map.65
  78.1 0.0 all-to-all-done
  78.1 6.9 %all-to-all-start.1 = ((f32[8,64,128]{2,1,0:T(8,128)}), f32[8,64,128]{2,1,0:T(8,128)S(1)}, u32[]{:S(2)}, u32[]{:S(2)}) async-start(f32[8,64,128]{2,1,0:T(8,128)} %shard_map.65), calls=%async_computation.1 | async-start | bytes 524288 | tf_op jit(solution)/shard_map/all_to_all | solution.py:216
  85.0 0.3 shard_map.56.part0
  85.4 0.8 collective-permute-start
  86.1 0.2 collective-permute-start.1
  86.3 1.3 collective-permute-start.2
  87.6 2.1 %collective-permute-done.part1 = f32[128,128]{1,0:T(8,128)S(1)} collective-permute-done((f32[128,128]{1,0:T(8,128)S(1)}, f32[128,128]{1,0:T(8,128)S(1)}, u32[]{:S(2)}, u32[]{:S(2)}) %collective-permute-start) | collective-permute-done | bytes 65568 | tf_op jit(solution)/shard_map/ppermute | solution.py:24
  89.7 2.2 %collective-permute-done.1.part2 = f32[128,128]{1,0:T(8,128)S(1)} collective-permute-done((f32[128,128]{1,0:T(8,128)S(1)}, f32[128,128]{1,0:T(8,128)S(1)}, u32[]{:S(2)}, u32[]{:S(2)}) %collective-permute-start.1) | collective-permute-done | bytes 65568 | tf_op jit(solution)/shard_map/ppermute | solution.py:24
  91.9 0.7 collective-permute-done.2.part3
  92.6 0.3 shard_map.57.a
  92.9 0.1 collective-permute-start.3
  93.0 1.3 %collective-permute-done.3.b = f32[256,128]{1,0:T(8,128)S(1)} collective-permute-done((f32[256,128]{1,0:T(8,128)S(1)}, f32[256,128]{1,0:T(8,128)S(1)}, u32[]{:S(2)}, u32[]{:S(2)}) %collective-permute-start.3) | collective-permute-done | bytes 131104 | tf_op jit(solution)/shard_map/ppermute | solution.py:24
  94.3 0.1 collective-permute-start.4
  94.4 1.5 %collective-permute-start.5 = (f32[256,128]{1,0:T(8,128)S(1)}, f32[256,128]{1,0:T(8,128)S(1)}, u32[]{:S(2)}, u32[]{:S(2)}) collective-permute-start(f32[256,128]{1,0:T(8,128)S(1)} %shard_map.58.mix0), channel_id=1, source_target_pairs={{0,4},{2,6},{4,0},{6,2},{1,5},{3,7},{5,1},{7,3},{8,12},{10,14},{12... | collective-permute-start | bytes 393224 | tf_op jit(solution)/shard_map/ppermute | solution.py:24
  95.9 1.8 %collective-permute-start.6 = (f32[256,128]{1,0:T(8,128)S(1)}, f32[256,128]{1,0:T(8,128)S(1)}, u32[]{:S(2)}, u32[]{:S(2)}) collective-permute-start(f32[256,128]{1,0:T(8,128)S(1)} %shard_map.58.mix0), channel_id=1, source_target_pairs={{0,6},{2,0},{4,2},{6,4},{1,7},{3,1},{5,3},{7,5},{8,14},{10,8},{12,... | collective-permute-start | bytes 393224 | tf_op jit(solution)/shard_map/ppermute | solution.py:24
  97.6 0.0 all-to-all-done.1
  97.7 1.9 %collective-permute-start.21 = (f32[64,128]{1,0:T(8,128)S(1)}, f32[64,128]{1,0:T(8,128)S(1)}, u32[]{:S(2)}, u32[]{:S(2)}) collective-permute-start(f32[64,128]{1,0:T(8,128)S(1)} %bitcast_subtract_fusion.rest0), channel_id=1, source_target_pairs={{0,64},{64,128},{128,192},{192,0},{1,65},{65,129},{129,193},{193,1... | collective-permute-start | bytes 98312 | tf_op jit(solution)/shard_map/ppermute | solution.py:24
  99.6 0.9 collective-permute-start.22
  100.5 3.5 %collective-permute-done.4.mix1 = f32[256,128]{1,0:T(8,128)S(1)} collective-permute-done((f32[256,128]{1,0:T(8,128)S(1)}, f32[256,128]{1,0:T(8,128)S(1)}, u32[]{:S(2)}, u32[]{:S(2)}) %collective-permute-start.4) | collective-permute-done | bytes 131104 | tf_op jit(solution)/shard_map/ppermute | solution.py:24
  104.0 0.6 collective-permute-start.23
  104.6 0.0 collective-permute-done.5.mix2
  104.6 0.0 collective-permute-done.6.mix3
  104.6 0.4 collective-permute-done.22.rest2
  105.0 4.1 %collective-permute-done.23.rest3 = f32[64,128]{1,0:T(8,128)S(1)} collective-permute-done((f32[64,128]{1,0:T(8,128)S(1)}, f32[64,128]{1,0:T(8,128)S(1)}, u32[]{:S(2)}, u32[]{:S(2)}) %collective-permute-start.23) | collective-permute-done | bytes 32800 | tf_op jit(solution)/shard_map/ppermute | solution.py:24
  109.1 1.0 shard_map.66
  110.1 17.5 %all_to_all.15 = f32[8,64,128]{2,1,0:T(8,128)S(1)} all-to-all(f32[8,64,128]{2,1,0:T(8,128)S(1)} %shard_map.66), channel_id=1, replica_groups=mesh['y'=4,'z'=8,'x'=4,'core'=2] {'z'}, dimensions={0} | all-to-all | bytes 524288 | tf_op jit(solution)/shard_map/all_to_all | solution.py:227
  127.6 0.6 reduce_sum.19
  (20 shorter events, 0.1 us)
Async XLA Ops:
  0.1 1.4 %copy-start = (f32[384,1024]{1,0:T(8,128)S(1)}, f32[384,1024]{1,0:T(8,128)}, u32[]{:S(2)}) copy-start(f32[384,1024]{1,0:T(8,128)} %cols.7) | copy-start | bytes 4718596
  5.1 5.8 %collective-permute-start.14 = (f32[4,1024,128]{2,1,0:T(8,128)S(1)}, f32[4,1024,128]{2,1,0:T(8,128)S(1)}, u32[]{:S(2)}, u32[]{:S(2)}) collective-permute-start(f32[4,1024,128]{2,1,0:T(8,128)S(1)} %shard_map.62), channel_id=1, source_target_pairs={{0,1},{1,0},{2,3},{3,2},{4,5},{5,4},{6,7},{7,6},{8,9},{9,8},{10,11... | collective-permute-start | bytes 6291464 | tf_op jit(solution)/shard_map/ppermute | solution.py:24
  10.2 19.2 %collective-permute-start.7 = (f32[4,1024,128]{2,1,0:T(8,128)}, f32[4,1024,128]{2,1,0:T(8,128)}, u32[]{:S(2)}, u32[]{:S(2)}) collective-permute-start(f32[4,1024,128]{2,1,0:T(8,128)} %shard_map.59), channel_id=1, source_target_pairs={{0,1},{1,0},{2,3},{3,2},{4,5},{5,4},{6,7},{7,6},{8,9},{9,8},{10,11... | collective-permute-start | bytes 6291464 | tf_op jit(solution)/shard_map/ppermute | solution.py:24
  10.9 7.5 %copy-start.2 = (f32[2,32,1024]{2,1,0:T(8,128)S(1)}, f32[2,32,1024]{2,1,0:T(8,128)}, u32[]{:S(2)}) copy-start(f32[2,32,1024]{2,1,0:T(8,128)} %inverses.1) | copy-start | bytes 786436
  10.9 7.5 %copy-start.3 = (f32[1024,32]{0,1:T(8,128)S(1)}, f32[1024,32]{0,1:T(8,128)}, u32[]{:S(2)}) copy-start(f32[1024,32]{0,1:T(8,128)} %param.8) | copy-start | bytes 393220
  14.9 0.8 copy-start.4
  15.7 0.8 copy-start.5
  16.5 12.9 %copy-start.1 = (f32[384,1024]{1,0:T(8,128)S(1)}, f32[384,1024]{1,0:T(8,128)}, u32[]{:S(2)}) copy-start(f32[384,1024]{1,0:T(8,128)} %cols.7) | copy-start | bytes 4718596
  16.5 24.9 %collective-permute-start.15 = (f32[1024,128]{1,0:T(8,128)}, f32[1024,128]{1,0:T(8,128)S(1)}, u32[]{:S(2)}, u32[]{:S(2)}) collective-permute-start(f32[1024,128]{1,0:T(8,128)} %get-tuple-element.30), channel_id=1, source_target_pairs={{0,64},{64,128},{128,192},{192,0},{1,65},{65,129},{129,193},{193,1... | collective-permute-start | bytes 1572872 | tf_op jit(solution)/shard_map/ppermute | solution.py:24
  20.0 58.1 %all-to-all-start = ((f32[8,32,512]{2,1,0:T(8,128)}), f32[8,32,512]{2,1,0:T(8,128)S(1)}, u32[]{:S(2)}, u32[]{:S(2)}) async-start(f32[8,32,512]{2,1,0:T(8,128)} %shard_map.55), calls=%async_computation | async-start | bytes 1048576 | tf_op jit(solution)/shard_map/all_to_all | solution.py:186
  26.8 16.6 %collective-permute-start.16 = (f32[1024,128]{1,0:T(8,128)}, f32[1024,128]{1,0:T(8,128)S(1)}, u32[]{:S(2)}, u32[]{:S(2)}) collective-permute-start(f32[1024,128]{1,0:T(8,128)} %copy-done.5), channel_id=1, source_target_pairs={{0,128},{64,192},{128,0},{192,64},{1,129},{65,193},{129,1},{193,65... | collective-permute-start | bytes 1572872 | tf_op jit(solution)/shard_map/ppermute | solution.py:24
  29.4 23.7 %collective-permute-start.17 = (f32[1024,128]{1,0:T(8,128)}, f32[1024,128]{1,0:T(8,128)S(1)}, u32[]{:S(2)}, u32[]{:S(2)}) collective-permute-start(f32[1024,128]{1,0:T(8,128)} %copy-done.4), channel_id=1, source_target_pairs={{0,192},{64,0},{128,64},{192,128},{1,193},{65,1},{129,65},{193,129... | collective-permute-start | bytes 1572872 | tf_op jit(solution)/shard_map/ppermute | solution.py:24
  34.1 28.6 %collective-permute-start.10 = (f32[1024,128]{1,0:T(8,128)S(1)}, f32[1024,128]{1,0:T(8,128)S(1)}, u32[]{:S(2)}, u32[]{:S(2)}) collective-permute-start(f32[1024,128]{1,0:T(8,128)S(1)} %get-tuple-element.24), channel_id=1, source_target_pairs={{0,6},{2,0},{4,2},{6,4},{1,7},{3,1},{5,3},{7,5},{8,14},{10,8},{12,... | collective-permute-start | bytes 1572872 | tf_op jit(solution)/shard_map/ppermute | solution.py:24
  37.0 29.5 %collective-permute-start.8 = (f32[1024,128]{1,0:T(8,128)S(1)}, f32[1024,128]{1,0:T(8,128)S(1)}, u32[]{:S(2)}, u32[]{:S(2)}) collective-permute-start(f32[1024,128]{1,0:T(8,128)S(1)} %get-tuple-element.22), channel_id=1, source_target_pairs={{0,2},{2,4},{4,6},{6,0},{1,3},{3,5},{5,7},{7,1},{8,10},{10,12},{12... | collective-permute-start | bytes 1572872 | tf_op jit(solution)/shard_map/ppermute | solution.py:24
  41.4 25.1 %collective-permute-start.9 = (f32[1024,128]{1,0:T(8,128)S(1)}, f32[1024,128]{1,0:T(8,128)S(1)}, u32[]{:S(2)}, u32[]{:S(2)}) collective-permute-start(f32[1024,128]{1,0:T(8,128)S(1)} %get-tuple-element.23), channel_id=1, source_target_pairs={{0,4},{2,6},{4,0},{6,2},{1,5},{3,7},{5,1},{7,3},{8,12},{10,14},{12... | collective-permute-start | bytes 1572872 | tf_op jit(solution)/shard_map/ppermute | solution.py:24
  53.2 16.6 %collective-permute-start.18 = (f32[256,128]{1,0:T(8,128)S(1)}, f32[256,128]{1,0:T(8,128)S(1)}, u32[]{:S(2)}, u32[]{:S(2)}) collective-permute-start(f32[256,128]{1,0:T(8,128)S(1)} %get-tuple-element.34), channel_id=1, source_target_pairs={{0,2},{2,4},{4,6},{6,0},{1,3},{3,5},{5,7},{7,1},{8,10},{10,12},{12... | collective-permute-start | bytes 393224 | tf_op jit(solution)/shard_map/ppermute | solution.py:24
  55.0 16.2 %collective-permute-start.19 = (f32[256,128]{1,0:T(8,128)S(1)}, f32[256,128]{1,0:T(8,128)S(1)}, u32[]{:S(2)}, u32[]{:S(2)}) collective-permute-start(f32[256,128]{1,0:T(8,128)S(1)} %get-tuple-element.35), channel_id=1, source_target_pairs={{0,4},{2,6},{4,0},{6,2},{1,5},{3,7},{5,1},{7,3},{8,12},{10,14},{12... | collective-permute-start | bytes 393224 | tf_op jit(solution)/shard_map/ppermute | solution.py:24
  62.7 8.4 %collective-permute-start.20 = (f32[256,128]{1,0:T(8,128)S(1)}, f32[256,128]{1,0:T(8,128)S(1)}, u32[]{:S(2)}, u32[]{:S(2)}) collective-permute-start(f32[256,128]{1,0:T(8,128)S(1)} %get-tuple-element.36), channel_id=1, source_target_pairs={{0,6},{2,0},{4,2},{6,4},{1,7},{3,1},{5,3},{7,5},{8,14},{10,8},{12,... | collective-permute-start | bytes 393224 | tf_op jit(solution)/shard_map/ppermute | solution.py:24
  66.5 31.1 %copy-start.6 = (f32[2,32,128]{2,1,0:T(8,128)S(1)}, f32[2,32,128]{2,1,0:T(8,128)}, u32[]{:S(2)}) copy-start(f32[2,32,128]{2,1,0:T(8,128)} %param.7) | copy-start | bytes 98308
  66.5 7.0 %collective-permute-start.11 = (f32[256,128]{1,0:T(8,128)S(1)}, f32[256,128]{1,0:T(8,128)S(1)}, u32[]{:S(2)}, u32[]{:S(2)}) collective-permute-start(f32[256,128]{1,0:T(8,128)S(1)} %get-tuple-element.26), channel_id=1, source_target_pairs={{0,64},{64,128},{128,192},{192,0},{1,65},{65,129},{129,193},{193,1... | collective-permute-start | bytes 393224 | tf_op jit(solution)/shard_map/ppermute | solution.py:24
  69.6 6.6 %collective-permute-start.12 = (f32[256,128]{1,0:T(8,128)S(1)}, f32[256,128]{1,0:T(8,128)S(1)}, u32[]{:S(2)}, u32[]{:S(2)}) collective-permute-start(f32[256,128]{1,0:T(8,128)S(1)} %get-tuple-element.27), channel_id=1, source_target_pairs={{0,128},{64,192},{128,0},{192,64},{1,129},{65,193},{129,1},{193,65... | collective-permute-start | bytes 393224 | tf_op jit(solution)/shard_map/ppermute | solution.py:24
  69.8 7.6 %collective-permute-start.13 = (f32[256,128]{1,0:T(8,128)S(1)}, f32[256,128]{1,0:T(8,128)S(1)}, u32[]{:S(2)}, u32[]{:S(2)}) collective-permute-start(f32[256,128]{1,0:T(8,128)S(1)} %get-tuple-element.28), channel_id=1, source_target_pairs={{0,192},{64,0},{128,64},{192,128},{1,193},{65,1},{129,65},{193,129... | collective-permute-start | bytes 393224 | tf_op jit(solution)/shard_map/ppermute | solution.py:24
  78.1 19.5 %all-to-all-start.1 = ((f32[8,64,128]{2,1,0:T(8,128)}), f32[8,64,128]{2,1,0:T(8,128)S(1)}, u32[]{:S(2)}, u32[]{:S(2)}) async-start(f32[8,64,128]{2,1,0:T(8,128)} %shard_map.65), calls=%async_computation.1 | async-start | bytes 524288 | tf_op jit(solution)/shard_map/all_to_all | solution.py:216
  85.4 4.3 %collective-permute-start = (f32[128,128]{1,0:T(8,128)S(1)}, f32[128,128]{1,0:T(8,128)S(1)}, u32[]{:S(2)}, u32[]{:S(2)}) collective-permute-start(f32[128,128]{1,0:T(8,128)S(1)} %shard_map.56.part0), channel_id=1, source_target_pairs={{0,64},{64,128},{128,192},{192,0},{1,65},{65,129},{129,193},{193,1... | collective-permute-start | bytes 196616 | tf_op jit(solution)/shard_map/ppermute | solution.py:24
  86.1 5.8 %collective-permute-start.1 = (f32[128,128]{1,0:T(8,128)S(1)}, f32[128,128]{1,0:T(8,128)S(1)}, u32[]{:S(2)}, u32[]{:S(2)}) collective-permute-start(f32[128,128]{1,0:T(8,128)S(1)} %shard_map.56.part0), channel_id=1, source_target_pairs={{0,128},{64,192},{128,0},{192,64},{1,129},{65,193},{129,1},{193,65... | collective-permute-start | bytes 196616 | tf_op jit(solution)/shard_map/ppermute | solution.py:24
  86.3 6.3 %collective-permute-start.2 = (f32[128,128]{1,0:T(8,128)S(1)}, f32[128,128]{1,0:T(8,128)S(1)}, u32[]{:S(2)}, u32[]{:S(2)}) collective-permute-start(f32[128,128]{1,0:T(8,128)S(1)} %shard_map.56.part0), channel_id=1, source_target_pairs={{0,192},{64,0},{128,64},{192,128},{1,193},{65,1},{129,65},{193,129... | collective-permute-start | bytes 196616 | tf_op jit(solution)/shard_map/ppermute | solution.py:24
  92.9 1.4 %collective-permute-start.3 = (f32[256,128]{1,0:T(8,128)S(1)}, f32[256,128]{1,0:T(8,128)S(1)}, u32[]{:S(2)}, u32[]{:S(2)}) collective-permute-start(f32[256,128]{1,0:T(8,128)S(1)} %shard_map.57.a), channel_id=1, source_target_pairs={{0,1},{1,0},{2,3},{3,2},{4,5},{5,4},{6,7},{7,6},{8,9},{9,8},{10,11... | collective-permute-start | bytes 393224 | tf_op jit(solution)/shard_map/ppermute | solution.py:24
  94.3 9.6 %collective-permute-start.4 = (f32[256,128]{1,0:T(8,128)S(1)}, f32[256,128]{1,0:T(8,128)S(1)}, u32[]{:S(2)}, u32[]{:S(2)}) collective-permute-start(f32[256,128]{1,0:T(8,128)S(1)} %shard_map.58.mix0), channel_id=1, source_target_pairs={{0,2},{2,4},{4,6},{6,0},{1,3},{3,5},{5,7},{7,1},{8,10},{10,12},{12... | collective-permute-start | bytes 393224 | tf_op jit(solution)/shard_map/ppermute | solution.py:24
  94.4 10.2 %collective-permute-start.5 = (f32[256,128]{1,0:T(8,128)S(1)}, f32[256,128]{1,0:T(8,128)S(1)}, u32[]{:S(2)}, u32[]{:S(2)}) collective-permute-start(f32[256,128]{1,0:T(8,128)S(1)} %shard_map.58.mix0), channel_id=1, source_target_pairs={{0,4},{2,6},{4,0},{6,2},{1,5},{3,7},{5,1},{7,3},{8,12},{10,14},{12... | collective-permute-start | bytes 393224 | tf_op jit(solution)/shard_map/ppermute | solution.py:24
  95.9 8.8 %collective-permute-start.6 = (f32[256,128]{1,0:T(8,128)S(1)}, f32[256,128]{1,0:T(8,128)S(1)}, u32[]{:S(2)}, u32[]{:S(2)}) collective-permute-start(f32[256,128]{1,0:T(8,128)S(1)} %shard_map.58.mix0), channel_id=1, source_target_pairs={{0,6},{2,0},{4,2},{6,4},{1,7},{3,1},{5,3},{7,5},{8,14},{10,8},{12,... | collective-permute-start | bytes 393224 | tf_op jit(solution)/shard_map/ppermute | solution.py:24
  97.7 6.9 %collective-permute-start.21 = (f32[64,128]{1,0:T(8,128)S(1)}, f32[64,128]{1,0:T(8,128)S(1)}, u32[]{:S(2)}, u32[]{:S(2)}) collective-permute-start(f32[64,128]{1,0:T(8,128)S(1)} %bitcast_subtract_fusion.rest0), channel_id=1, source_target_pairs={{0,64},{64,128},{128,192},{192,0},{1,65},{65,129},{129,193},{193,1... | collective-permute-start | bytes 98312 | tf_op jit(solution)/shard_map/ppermute | solution.py:24
  99.6 5.4 %collective-permute-start.22 = (f32[64,128]{1,0:T(8,128)S(1)}, f32[64,128]{1,0:T(8,128)S(1)}, u32[]{:S(2)}, u32[]{:S(2)}) collective-permute-start(f32[64,128]{1,0:T(8,128)S(1)} %bitcast_subtract_fusion.rest0), channel_id=1, source_target_pairs={{0,128},{64,192},{128,0},{192,64},{1,129},{65,193},{129,1},{193,65... | collective-permute-start | bytes 98312 | tf_op jit(solution)/shard_map/ppermute | solution.py:24
  104.0 5.1 %collective-permute-start.23 = (f32[64,128]{1,0:T(8,128)S(1)}, f32[64,128]{1,0:T(8,128)S(1)}, u32[]{:S(2)}, u32[]{:S(2)}) collective-permute-start(f32[64,128]{1,0:T(8,128)S(1)} %bitcast_subtract_fusion.rest0), channel_id=1, source_target_pairs={{0,192},{64,0},{128,64},{192,128},{1,193},{65,1},{129,65},{193,129... | collective-permute-start | bytes 98312 | tf_op jit(solution)/shard_map/ppermute | solution.py:24

commit v3 on v2

--- a/solution.py
+++ b/solution.py
@@ -13,6 +13,8 @@
 EXACT = lax.Precision.HIGHEST
 SMEM = pl.BlockSpec(memory_space=pltpu.SMEM)
 FAR = pl.BlockSpec(memory_space=pltpu.HBM)
+PRODUCT = pltpu.CompilerParams(vmem_limit_bytes=16 << 20)
+ORDER = pl.BlockSpec(memory_space=pl.ANY)
 SMALL = pltpu.CompilerParams(vmem_limit_bytes=6 << 20)
 
 
@@ -29,37 +31,39 @@
     return high, (value - high.astype(F32)).astype(BF16)
 
 
+def split_columns(place, cols, right, nx):
+    depth = cols.shape[0]
+    for jx in range(nx):
+        at = lax.rem(place[0] + jx, nx) * 256 + place[2] * 128
+        high, low = halves(cols[:, pl.ds(pl.multiple_of(at, 128), 128)])
+        span = slice(jx * 128, (jx + 1) * 128)
+        right[0:depth, span] = high
+        right[depth : 2 * depth, span] = low
+        right[2 * depth : 3 * depth, span] = high
+
+
+def multiply(block, left, right):
+    depth = block.shape[1]
+    high, low = halves(block)
+    left[:, 0:depth] = high
+    left[:, depth : 2 * depth] = high
+    left[:, 2 * depth : 3 * depth] = low
+    return jnp.dot(left[...], right[...], preferred_element_type=F32)
+
+
+def rows_at(place, jy, ny, size):
+    return pl.ds(pl.multiple_of(lax.rem(place[1] + jy, ny) * size, size), size)
+
+
 def product_kernel(panel, by_column, has_received, nx, ny):
     def kernel(place, rows, cols, *refs):
         received = refs[0] if has_received else None
-        outs = refs[1:-4] if has_received else refs[:-4]
-        left, right, blocks, sems = refs[-4:]
-        depth = cols.shape[0]
-        size = blocks.shape[1]
-        copies = []
+        outs = refs[1:-2] if has_received else refs[:-2]
+        left, right = refs[-2:]
+        size = left.shape[0]
+        split_columns(place, cols, right, nx)
         for jy in range(ny):
-            at = pl.multiple_of(lax.rem(place[1] + jy, ny) * size, size)
-            copies.append(
-                pltpu.make_async_copy(
-                    rows.at[panel, pl.ds(at, size), :], blocks.at[jy], sems.at[jy]
-                )
-            )
-        for copy in copies:
-            copy.start()
-        for jx in range(nx):
-            at = lax.rem(place[0] + jx, nx) * 256 + place[2] * 128
-            high, low = halves(cols[:, pl.ds(pl.multiple_of(at, 128), 128)])
-            span = slice(jx * 128, (jx + 1) * 128)
-            right[0:depth, span] = high
-            right[depth : 2 * depth, span] = low
-            right[2 * depth : 3 * depth, span] = high
-        for jy in range(ny):
-            copies[jy].wait()
-            high, low = halves(blocks[jy])
-            left[:, 0:depth] = high
-            left[:, depth : 2 * depth] = high
-            left[:, 2 * depth : 3 * depth] = low
-            value = jnp.dot(left[...], right[...], preferred_element_type=F32)
+            value = multiply(rows[panel, rows_at(place, jy, ny, size), :], left, right)
             for jx in range(nx):
                 block = value[:, jx * 128 : (jx + 1) * 128]
                 first, second = (jx, jy) if by_column else (jy, jx)
@@ -70,6 +74,62 @@
                     outs[0][first, span, :] = block
 
     return kernel
+
+
+def first_kernel(nx, ny):
+    def kernel(place, far_rows, far_cols, out, rows, cols, left, right, sems):
+        size = left.shape[0]
+        load_cols = pltpu.make_async_copy(far_cols, cols, sems.at[0])
+        load_cols.start()
+        loads = []
+        for panel in range(2):
+            for jy in range(ny):
+                at = rows_at(place, jy, ny, size)
+                loads.append(
+                    pltpu.make_async_copy(
+                        far_rows.at[panel, at, :], rows.at[panel, at, :], sems.at[1 + panel * ny + jy]
+                    )
+                )
+        for load in loads:
+            load.start()
+        load_cols.wait()
+        split_columns(place, cols, right, nx)
+        for jy in range(ny):
+            loads[jy].wait()
+            value = multiply(rows[0, rows_at(place, jy, ny, size), :], left, right)
+            for jx in range(nx):
+                out[jx, jy * size : (jy + 1) * size, :] = value[:, jx * 128 : (jx + 1) * 128]
+        for load in loads[ny:]:
+            load.wait()
+
+    return kernel
+
+
+def product_scratch(size, depth, nx, ny):
+    return [pltpu.VMEM((size // ny, 3 * depth), BF16), pltpu.VMEM((3 * depth, nx * 128), BF16)]
+
+
+def product_cost(size, depth, nx):
+    return pl.CostEstimate(
+        flops=6 * size * depth * nx * 128, transcendentals=0, bytes_accessed=6 << 20
+    )
+
+
+def first_products(place, rows, cols, nx, ny):
+    _, size, depth = rows.shape
+    return pl.pallas_call(
+        first_kernel(nx, ny),
+        out_shape=(
+            jax.ShapeDtypeStruct((nx, size, 128), F32),
+            jax.ShapeDtypeStruct(rows.shape, F32),
+            jax.ShapeDtypeStruct(cols.shape, F32),
+        ),
+        in_specs=[SMEM, FAR, FAR],
+        scratch_shapes=product_scratch(size, depth, nx, ny)
+        + [pltpu.SemaphoreType.DMA((1 + 2 * ny,))],
+        compiler_params=PRODUCT,
+        cost_estimate=product_cost(size, depth, nx),
+    )(place, far(rows), far(cols))
 
 
 def products(place, panel, rows, cols, received, by_column, nx, ny):
@@ -85,17 +145,10 @@
     return pl.pallas_call(
         kernel,
         out_shape=shapes,
-        in_specs=[SMEM, FAR] + [pl.BlockSpec()] * (len(args) - 2),
-        scratch_shapes=[
-            pltpu.VMEM((size // ny, 3 * depth), BF16),
-            pltpu.VMEM((3 * depth, nx * 128), BF16),
-            pltpu.VMEM((ny, size // ny, depth), F32),
-            pltpu.SemaphoreType.DMA((ny,)),
-        ],
-        compiler_params=pltpu.CompilerParams(vmem_limit_bytes=12 << 20),
-        cost_estimate=pl.CostEstimate(
-            flops=6 * size * depth * nx * 128, transcendentals=0, bytes_accessed=6 << 20
-        ),
+        in_specs=[SMEM] + [pl.BlockSpec()] * (len(args) - 1),
+        scratch_shapes=product_scratch(size, depth, nx, ny),
+        compiler_params=PRODUCT,
+        cost_estimate=product_cost(size, depth, nx),
     )(*args)
 
 
@@ -131,20 +184,21 @@
     out[...] = a[...] + b[...]
 
 
-def gather_sums_kernel(a, b, c, d, *outs):
+def gather_sums_kernel(a, b, c, d, after, *outs):
     size = outs[0].shape[0]
     for j, out in enumerate(outs):
         span = slice(j * size, (j + 1) * size)
         out[...] = (a[span, :] + b[span, :]) + (c[span, :] + d[span, :])
 
 
-def gather_sums(parts, count):
+def gather_sums(parts, after, count):
     size = parts[0].shape[0] // count
     return pl.pallas_call(
         gather_sums_kernel,
         out_shape=[jax.ShapeDtypeStruct((size, 128), F32)] * count,
+        in_specs=[pl.BlockSpec()] * len(parts) + [ORDER],
         compiler_params=SMALL,
-    )(*parts)
+    )(*parts, after)
 
 
 def interleave_kernel(a0, a1, a2, a3, b0, b1, b2, b3, out):
@@ -173,9 +227,17 @@
 def steps(panel_rows, solved, right_side, coupling, inverses):
     nx, ny, nz, nc = (lax.axis_size(a) for a in ("x", "y", "z", "core"))
     x, y, core = lax.axis_index("x"), lax.axis_index("y"), lax.axis_index("core")
-    panel_rows = far(panel_rows)
     own = jnp.stack([x, y, core]).astype(jnp.int32)
     other = jnp.stack([x, y, 1 - core]).astype(jnp.int32)
+
+    to_partner0, panel_rows, solved = first_products(other, panel_rows, solved, nx, ny)
+    from_partner0 = shift(to_partner0, "core", 1, nc)
+    to_partner1 = products(other, 1, panel_rows, solved, None, False, nx, ny)
+    from_partner1 = shift(to_partner1, "core", 1, nc)
+    blocks0 = products(own, 0, panel_rows, solved, from_partner0, True, nx, ny)
+    got0 = [blocks0[0]] + [shift(blocks0[j], "x", j, nx) for j in range(1, nx)]
+    blocks1 = products(own, 1, panel_rows, solved, from_partner1, False, nx, ny)
+    got1 = [blocks1[0]] + [shift(blocks1[j], "y", j, ny) for j in range(1, ny)]
 
     packed = pl.pallas_call(
         pack_kernel,
@@ -184,15 +246,6 @@
         compiler_params=SMALL,
     )(own, inverses, coupling.T)
     tiles = lax.all_to_all(packed, "z", 0, 0, tiled=True).reshape(nz * 32, 512)
-
-    to_partner0 = products(other, 0, panel_rows, solved, None, True, nx, ny)
-    from_partner0 = shift(to_partner0, "core", 1, nc)
-    to_partner1 = products(other, 1, panel_rows, solved, None, False, nx, ny)
-    from_partner1 = shift(to_partner1, "core", 1, nc)
-    blocks0 = products(own, 0, panel_rows, solved, from_partner0, True, nx, ny)
-    got0 = [blocks0[0]] + [shift(blocks0[j], "x", j, nx) for j in range(1, nx)]
-    blocks1 = products(own, 1, panel_rows, solved, from_partner1, False, nx, ny)
-    got1 = [blocks1[0]] + [shift(blocks1[j], "y", j, ny) for j in range(1, ny)]
 
     coupled = pl.pallas_call(
         couple_kernel, out_shape=jax.ShapeDtypeStruct((128, 128), F32), compiler_params=SMALL
@@ -206,12 +259,14 @@
     )(chained, shift(chained, "core", 1, nc))
     mixes = [mix] + [shift(mix, "x", j, nx) for j in range(1, nx)]
 
-    sums0 = gather_sums(got0, ny)
+    sums0 = gather_sums(got0, coupled, ny)
     again0 = [sums0[0]] + [shift(sums0[j], "y", j, ny) for j in range(1, ny)]
-    sums1 = gather_sums(got1, nx)
+    sums1 = gather_sums(got1, coupled, nx)
     again1 = [sums1[0]] + [shift(sums1[j], "x", j, nx) for j in range(1, nx)]
     by_z = pl.pallas_call(
-        interleave_kernel, out_shape=jax.ShapeDtypeStruct((nz, 64, 128), F32), compiler_params=SMALL
+        interleave_kernel,
+        out_shape=jax.ShapeDtypeStruct((nz, 64, 128), F32),
+        compiler_params=SMALL,
     )(*again0, *again1)
     old = lax.all_to_all(by_z, "z", 0, 0, tiled=True).sum(axis=0)
     rest = right_side.reshape(64, 128) - old

time: 129 us -> 126 us (0.977)
  the two profiles are of different devices: /device:TPU:24 before, /device:TPU:2 now
where the time goes in v3:
time: 126 us; the launch traced here: 125 us
  starting transfers between devices  51.5 us (41%)
  waiting for transfers between devices  26.1 us (21%)
  Pallas kernels  22.8 us (18%)
  blocking collectives  17.5 us (14%)
  local copies, waits for them, and re-layouts  6.49 us (5%)
    ppermute x24, starting transfers between devices, shift(): lax.ppermute(value, axis, [(i, (i + step) % size) for i in range(size)])  36.1 us
    ppermute x24, waiting for transfers between devices, shift(): lax.ppermute(value, axis, [(i, (i + step) % size) for i in range(size)])  24 us
    all_to_all x1, blocking collectives, steps(): panels = lax.all_to_all(solved_part, 'z', 0, 0, tiled=True).sum(axis=0)  17.5 us
    pallas_call x3, Pallas kernels, products(): pl.pallas_call(kernel, out_shape=shapes, in_specs=[SMEM] + [pl.BlockSpec(...  11.1 us
    all_to_all x1, starting transfers between devices, steps(): tiles = lax.all_to_all(packed, 'z', 0, 0, tiled=True).reshape(nz * 32, 512)  8.47 us
    all_to_all x1, starting transfers between devices, steps(): old = lax.all_to_all(by_z, 'z', 0, 0, tiled=True).sum(axis=0)  6.93 us
    unnamed x24, local copies, waits for them, and re-layouts  6.49 us
    pallas_call x1, Pallas kernels, first_products(): pl.pallas_call(first_kernel(nx, ny), out_shape=(jax.ShapeDtypeStruct((nx,...  4.38 us
  transfers between devices with their start and end apart: 26, of which 14 were waited for; matrix products, arithmetic and copies ran while one was open for 0% of the time, Pallas kernels for 13%

profile of v3, /device:TPU:2, one launch (start us, length us, event | category | flops | bytes accessed | tf_op | source)
XLA Modules:
  0.0 125.3 jit_solution(9478426844142739034)
XLA Ops:
  0.0 0.1 pad_add_fusion.2.place
  0.1 4.4 %shard_map.59 = (f32[4,1024,128]{2,1,0:T(8,128)S(1)}, f32[2,1024,384]{2,1,0:T(8,128)S(1)}, f32[384,1024]{1,0:T(8,128)S(1)}) custom-call(s32[3]{0:T(128)S(1)} %pad_add_fusion.2.place, f32[2,1024,384]{2,1,0:T(8,128)} %far_rows.1, f32[384,1024]{1,0:T(8,128)} %far_cols.1), custom_call_target="tpu_custom_call" | custom-call | flops 1207959552 | bytes 6291456 | tf_op jit(solution)/shard_map/pallas_call | solution.py:120
  4.5 0.1 collective-permute-start.7
  4.6 0.0 copy-start.7
  4.6 0.0 copy-start.8
  4.6 3.7 %shard_map.62 = f32[4,1024,128]{2,1,0:T(8,128)} custom-call(s32[3]{0:T(128)S(1)} %pad_add_fusion.2.place, f32[2,1024,384]{2,1,0:T(8,128)S(1)} %get-tuple-element.24.rows, f32[384,1024]{1,0:T(8,128)S(1)} %get-tuple-element.25.cols), custom_call_target="tpu_custom_call" | custom-call | flops 1207959552 | bytes 6291456 | tf_op jit(solution)/shard_map/pallas_call | solution.py:145
  8.3 0.5 collective-permute-start.14
  8.7 0.1 pad_add_fusion.place
  8.8 0.8 shard_map.55
  9.7 0.8 copy-done.2
  10.4 3.2 %shard_map.60 = (f32[1024,128]{1,0:T(8,128)S(1)}, f32[1024,128]{1,0:T(8,128)}, f32[1024,128]{1,0:T(8,128)S(1)}, f32[1024,128]{1,0:T(8,128)S(1)}) custom-call(s32[3]{0:T(128)S(1)} %pad_add_fusion.place, f32[2,1024,384]{2,1,0:T(8,128)S(1)} %get-tuple-element.24.rows, f32[384,1024]{1,0:T(8,128)S(1)} %get-tuple-element.25.cols, ...), custom_call_target="tpu_custom_call" | custom-call | flops 1207959552 | bytes 6291456 | tf_op jit(solution)/shard_map/pallas_call | solution.py:145
  13.6 0.8 copy-done.5
  14.4 0.8 copy-done.9
  15.3 0.8 copy-done.10
  16.1 1.5 %collective-permute-start.8 = (f32[1024,128]{1,0:T(8,128)}, f32[1024,128]{1,0:T(8,128)}, u32[]{:S(2)}, u32[]{:S(2)}) collective-permute-start(f32[1024,128]{1,0:T(8,128)} %get-tuple-element.28), channel_id=1, source_target_pairs={{0,2},{2,4},{4,6},{6,0},{1,3},{3,5},{5,7},{7,1},{8,10},{10,12},{12... | collective-permute-start | bytes 1572872 | tf_op jit(solution)/shard_map/ppermute | solution.py:26
  17.6 8.5 %all-to-all-start = ((f32[8,32,512]{2,1,0:T(8,128)}), f32[8,32,512]{2,1,0:T(8,128)}, u32[]{:S(2)}, u32[]{:S(2)}) async-start(f32[8,32,512]{2,1,0:T(8,128)} %copy-done.2), calls=%async_computation | async-start | bytes 1048576 | tf_op jit(solution)/shard_map/all_to_all | solution.py:248
  26.0 1.1 collective-permute-start.9
  27.2 2.1 %collective-permute-start.10 = (f32[1024,128]{1,0:T(8,128)}, f32[1024,128]{1,0:T(8,128)}, u32[]{:S(2)}, u32[]{:S(2)}) collective-permute-start(f32[1024,128]{1,0:T(8,128)} %copy-done.9), channel_id=1, source_target_pairs={{0,6},{2,0},{4,2},{6,4},{1,7},{3,1},{5,3},{7,5},{8,14},{10,8},{12,... | collective-permute-start | bytes 1572872 | tf_op jit(solution)/shard_map/ppermute | solution.py:26
  29.3 1.4 %copy-done.1 = f32[384,1024]{1,0:T(8,128)S(1)} copy-done((f32[384,1024]{1,0:T(8,128)S(1)}, f32[384,1024]{1,0:T(8,128)}, u32[]{:S(2)}) %copy-start.1) | copy-done | bytes 1572888
  30.7 4.2 %shard_map.63 = (f32[1024,128]{1,0:T(8,128)S(1)}, f32[1024,128]{1,0:T(8,128)}, f32[1024,128]{1,0:T(8,128)}, f32[1024,128]{1,0:T(8,128)}) custom-call(s32[3]{0:T(128)S(1)} %pad_add_fusion.place, f32[2,1024,384]{2,1,0:T(8,128)S(1)} %get-tuple-element.24.rows, f32[384,1024]{1,0:T(8,128)S(1)} %copy-done.1, f32[4,1024,128]{2,1,0:T(8,128)} %collective-permute-done.14.refs_0_), custom_call_target="tpu_custom_call" | custom-call | flops 1207959552 | bytes 6291456 | tf_op jit(solution)/shard_map/pallas_call | solution.py:145
  34.9 0.8 copy-done.3
  35.7 1.6 %collective-permute-start.15 = (f32[1024,128]{1,0:T(8,128)}, f32[1024,128]{1,0:T(8,128)S(1)}, u32[]{:S(2)}, u32[]{:S(2)}) collective-permute-start(f32[1024,128]{1,0:T(8,128)} %get-tuple-element.36), channel_id=1, source_target_pairs={{0,64},{64,128},{128,192},{192,0},{1,65},{65,129},{129,193},{193,1... | collective-permute-start | bytes 1572872 | tf_op jit(solution)/shard_map/ppermute | solution.py:26
  37.3 2.9 %collective-permute-start.16 = (f32[1024,128]{1,0:T(8,128)}, f32[1024,128]{1,0:T(8,128)S(1)}, u32[]{:S(2)}, u32[]{:S(2)}) collective-permute-start(f32[1024,128]{1,0:T(8,128)} %get-tuple-element.37), channel_id=1, source_target_pairs={{0,128},{64,192},{128,0},{192,64},{1,129},{65,193},{129,1},{193,65... | collective-permute-start | bytes 1572872 | tf_op jit(solution)/shard_map/ppermute | solution.py:26
  40.2 1.3 %collective-permute-start.17 = (f32[1024,128]{1,0:T(8,128)}, f32[1024,128]{1,0:T(8,128)S(1)}, u32[]{:S(2)}, u32[]{:S(2)}) collective-permute-start(f32[1024,128]{1,0:T(8,128)} %get-tuple-element.38), channel_id=1, source_target_pairs={{0,192},{64,0},{128,64},{192,128},{1,193},{65,1},{129,65},{193,129... | collective-permute-start | bytes 1572872 | tf_op jit(solution)/shard_map/ppermute | solution.py:26
  41.5 2.1 %all-to-all-done = f32[8,32,512]{2,1,0:T(8,128)} async-done(((f32[8,32,512]{2,1,0:T(8,128)}), f32[8,32,512]{2,1,0:T(8,128)}, u32[]{:S(2)}, u32[]{:S(2)}) %all-to-all-start) | async-done | bytes 524320 | tf_op jit(solution)/shard_map/all_to_all | solution.py:248
  43.6 1.3 %shard_map.56.part0.after = f32[128,128]{1,0:T(8,128)S(1)} custom-call(f32[256,512]{1,0:T(8,128)} %bitcast.4.tiles), custom_call_target="tpu_custom_call" | custom-call | tf_op jit(solution)/shard_map/pallas_call | solution.py:250
  44.9 6.8 %collective-permute-done.10.d = f32[1024,128]{1,0:T(8,128)} collective-permute-done((f32[1024,128]{1,0:T(8,128)}, f32[1024,128]{1,0:T(8,128)}, u32[]{:S(2)}, u32[]{:S(2)}) %collective-permute-start.10) | collective-permute-done | bytes 524320 | tf_op jit(solution)/shard_map/ppermute | solution.py:26
  51.8 1.0 copy-done.6
  52.8 1.5 %shard_map.61 = (f32[256,128]{1,0:T(8,128)S(1)}, f32[256,128]{1,0:T(8,128)S(1)}, f32[256,128]{1,0:T(8,128)S(1)}, f32[256,128]{1,0:T(8,128)S(1)}) custom-call(f32[1024,128]{1,0:T(8,128)S(1)} %copy-done.6, f32[1024,128]{1,0:T(8,128)} %collective-permute-done.8.b, f32[1024,128]{1,0:T(8,128)} %collective-permute-done.9.c, ...), custom_call_target="tpu_custom_call" | custom-call | tf_op jit(solution)/shard_map/pallas_call | solution.py:196
  54.3 1.8 %collective-permute-start.11 = (f32[256,128]{1,0:T(8,128)S(1)}, f32[256,128]{1,0:T(8,128)S(1)}, u32[]{:S(2)}, u32[]{:S(2)}) collective-permute-start(f32[256,128]{1,0:T(8,128)S(1)} %get-tuple-element.32), channel_id=1, source_target_pairs={{0,64},{64,128},{128,192},{192,0},{1,65},{65,129},{129,193},{193,1... | collective-permute-start | bytes 393224 | tf_op jit(solution)/shard_map/ppermute | solution.py:26
  56.1 2.9 %collective-permute-start.12 = (f32[256,128]{1,0:T(8,128)S(1)}, f32[256,128]{1,0:T(8,128)S(1)}, u32[]{:S(2)}, u32[]{:S(2)}) collective-permute-start(f32[256,128]{1,0:T(8,128)S(1)} %get-tuple-element.33), channel_id=1, source_target_pairs={{0,128},{64,192},{128,0},{192,64},{1,129},{65,193},{129,1},{193,65... | collective-permute-start | bytes 393224 | tf_op jit(solution)/shard_map/ppermute | solution.py:26
  59.0 1.3 %collective-permute-start.13 = (f32[256,128]{1,0:T(8,128)S(1)}, f32[256,128]{1,0:T(8,128)S(1)}, u32[]{:S(2)}, u32[]{:S(2)}) collective-permute-start(f32[256,128]{1,0:T(8,128)S(1)} %get-tuple-element.34), channel_id=1, source_target_pairs={{0,192},{64,0},{128,64},{192,128},{1,193},{65,1},{129,65},{193,129... | collective-permute-start | bytes 393224 | tf_op jit(solution)/shard_map/ppermute | solution.py:26
  60.3 4.1 %collective-permute-done.16.c = f32[1024,128]{1,0:T(8,128)S(1)} collective-permute-done((f32[1024,128]{1,0:T(8,128)}, f32[1024,128]{1,0:T(8,128)S(1)}, u32[]{:S(2)}, u32[]{:S(2)}) %collective-permute-start.16) | collective-permute-done | bytes 524320 | tf_op jit(solution)/shard_map/ppermute | solution.py:26
  64.4 0.1 shard_map.64
  64.5 0.0 copy-start.11
  64.6 0.1 collective-permute-start.18
  64.6 3.5 %collective-permute-start.19 = (f32[256,128]{1,0:T(8,128)S(1)}, f32[256,128]{1,0:T(8,128)S(1)}, u32[]{:S(2)}, u32[]{:S(2)}) collective-permute-start(f32[256,128]{1,0:T(8,128)S(1)} %get-tuple-element.41), channel_id=1, source_target_pairs={{0,4},{2,6},{4,0},{6,2},{1,5},{3,7},{5,1},{7,3},{8,12},{10,14},{12... | collective-permute-start | bytes 393224 | tf_op jit(solution)/shard_map/ppermute | solution.py:26
  68.2 1.4 %collective-permute-done.18.b1 = f32[256,128]{1,0:T(8,128)S(1)} collective-permute-done((f32[256,128]{1,0:T(8,128)S(1)}, f32[256,128]{1,0:T(8,128)S(1)}, u32[]{:S(2)}, u32[]{:S(2)}) %collective-permute-start.18) | collective-permute-done | bytes 131104 | tf_op jit(solution)/shard_map/ppermute | solution.py:26
  69.6 1.7 %collective-permute-done.19.b2 = f32[256,128]{1,0:T(8,128)S(1)} collective-permute-done((f32[256,128]{1,0:T(8,128)S(1)}, f32[256,128]{1,0:T(8,128)S(1)}, u32[]{:S(2)}, u32[]{:S(2)}) %collective-permute-start.19) | collective-permute-done | bytes 131104 | tf_op jit(solution)/shard_map/ppermute | solution.py:26
  71.3 2.1 %collective-permute-done.20.b3 = f32[256,128]{1,0:T(8,128)S(1)} collective-permute-done((f32[256,128]{1,0:T(8,128)S(1)}, f32[256,128]{1,0:T(8,128)S(1)}, u32[]{:S(2)}, u32[]{:S(2)}) %collective-permute-start.20) | collective-permute-done | bytes 131104 | tf_op jit(solution)/shard_map/ppermute | solution.py:26
  73.4 0.7 shard_map.65
  74.2 6.9 %all-to-all-start.1 = ((f32[8,64,128]{2,1,0:T(8,128)}), f32[8,64,128]{2,1,0:T(8,128)S(1)}, u32[]{:S(2)}, u32[]{:S(2)}) async-start(f32[8,64,128]{2,1,0:T(8,128)} %shard_map.65), calls=%async_computation.1 | async-start | bytes 524288 | tf_op jit(solution)/shard_map/all_to_all | solution.py:271
  81.1 1.1 collective-permute-start
  82.2 2.9 %collective-permute-start.1 = (f32[128,128]{1,0:T(8,128)S(1)}, f32[128,128]{1,0:T(8,128)S(1)}, u32[]{:S(2)}, u32[]{:S(2)}) collective-permute-start(f32[128,128]{1,0:T(8,128)S(1)} %shard_map.56.part0.after), channel_id=1, source_target_pairs={{0,128},{64,192},{128,0},{192,64},{1,129},{65,193},{129,1},{193,65... | collective-permute-start | bytes 196616 | tf_op jit(solution)/shard_map/ppermute | solution.py:26
  85.0 1.4 %collective-permute-start.2 = (f32[128,128]{1,0:T(8,128)S(1)}, f32[128,128]{1,0:T(8,128)S(1)}, u32[]{:S(2)}, u32[]{:S(2)}) collective-permute-start(f32[128,128]{1,0:T(8,128)S(1)} %shard_map.56.part0.after), channel_id=1, source_target_pairs={{0,192},{64,0},{128,64},{192,128},{1,193},{65,1},{129,65},{193,129... | collective-permute-start | bytes 196616 | tf_op jit(solution)/shard_map/ppermute | solution.py:26
  86.5 0.5 collective-permute-done.part1
  86.9 1.0 collective-permute-done.1.part2
  88.0 1.3 %collective-permute-done.2.part3 = f32[128,128]{1,0:T(8,128)S(1)} collective-permute-done((f32[128,128]{1,0:T(8,128)S(1)}, f32[128,128]{1,0:T(8,128)S(1)}, u32[]{:S(2)}, u32[]{:S(2)}) %collective-permute-start.2) | collective-permute-done | bytes 65568 | tf_op jit(solution)/shard_map/ppermute | solution.py:26
  89.3 1.3 %shard_map.57.a = f32[256,128]{1,0:T(8,128)S(1)} custom-call(f32[256,512]{1,0:T(8,128)} %bitcast.4.tiles, f32[128,128]{1,0:T(8,128)S(1)} %shard_map.56.part0.after, f32[128,128]{1,0:T(8,128)S(1)} %collective-permute-done.part1, f32[128,128]{1,0:T(8,128)S(1)} %collective-permute-done.1.part2, f32[128,128]{1,0:T(8,128)S(1)} %collective-permute-done.2.part3), custom_call_target="tpu_custom_call" | custom-call | tf_op jit(solution)/shard_map/pallas_call | solution.py:254
  90.6 0.1 collective-permute-start.3
  90.7 1.3 %collective-permute-done.3.b = f32[256,128]{1,0:T(8,128)S(1)} collective-permute-done((f32[256,128]{1,0:T(8,128)S(1)}, f32[256,128]{1,0:T(8,128)S(1)}, u32[]{:S(2)}, u32[]{:S(2)}) %collective-permute-start.3) | collective-permute-done | bytes 131104 | tf_op jit(solution)/shard_map/ppermute | solution.py:26
  92.1 0.6 collective-permute-start.4
  92.7 3.2 %collective-permute-start.5 = (f32[256,128]{1,0:T(8,128)S(1)}, f32[256,128]{1,0:T(8,128)S(1)}, u32[]{:S(2)}, u32[]{:S(2)}) collective-permute-start(f32[256,128]{1,0:T(8,128)S(1)} %shard_map.58.mix0), channel_id=1, source_target_pairs={{0,4},{2,6},{4,0},{6,2},{1,5},{3,7},{5,1},{7,3},{8,12},{10,14},{12... | collective-permute-start | bytes 393224 | tf_op jit(solution)/shard_map/ppermute | solution.py:26
  95.9 1.9 %collective-permute-start.6 = (f32[256,128]{1,0:T(8,128)S(1)}, f32[256,128]{1,0:T(8,128)S(1)}, u32[]{:S(2)}, u32[]{:S(2)}) collective-permute-start(f32[256,128]{1,0:T(8,128)S(1)} %shard_map.58.mix0), channel_id=1, source_target_pairs={{0,6},{2,0},{4,2},{6,4},{1,7},{3,1},{5,3},{7,5},{8,14},{10,8},{12,... | collective-permute-start | bytes 393224 | tf_op jit(solution)/shard_map/ppermute | solution.py:26
  97.8 0.7 collective-permute-start.21
  98.5 3.3 %collective-permute-start.22 = (f32[64,128]{1,0:T(8,128)S(1)}, f32[64,128]{1,0:T(8,128)S(1)}, u32[]{:S(2)}, u32[]{:S(2)}) collective-permute-start(f32[64,128]{1,0:T(8,128)S(1)} %bitcast_subtract_fusion.rest0), channel_id=1, source_target_pairs={{0,128},{64,192},{128,0},{192,64},{1,129},{65,193},{129,1},{193,65... | collective-permute-start | bytes 98312 | tf_op jit(solution)/shard_map/ppermute | solution.py:26
  101.8 0.2 collective-permute-start.23
  102.0 0.3 collective-permute-done.6.mix3
  102.3 0.7 collective-permute-done.21.rest1
  103.0 1.0 collective-permute-done.22.rest2
  104.0 1.7 %collective-permute-done.23.rest3 = f32[64,128]{1,0:T(8,128)S(1)} collective-permute-done((f32[64,128]{1,0:T(8,128)S(1)}, f32[64,128]{1,0:T(8,128)S(1)}, u32[]{:S(2)}, u32[]{:S(2)}) %collective-permute-start.23) | collective-permute-done | bytes 32800 | tf_op jit(solution)/shard_map/ppermute | solution.py:26
  105.7 1.5 %shard_map.66 = f32[8,64,128]{2,1,0:T(8,128)S(1)} custom-call(s32[3]{0:T(128)S(1)} %pad_add_fusion.place, f32[256,512]{1,0:T(8,128)} %bitcast.4.tiles, f32[256,128]{1,0:T(8,128)S(1)} %shard_map.58.mix0, f32[256,128]{1,0:T(8,128)S(1)} %collective-permute-done.4.mix1, f32[256,128]{1,0:T(8,128)S(1)} %collective-permute-done.5.mix2, ...), custom_call_target="tpu_custom_call" | custom-call | tf_op jit(solution)/shard_map/pallas_call | solution.py:275
  107.2 17.5 %all_to_all.15 = f32[8,64,128]{2,1,0:T(8,128)S(1)} all-to-all(f32[8,64,128]{2,1,0:T(8,128)S(1)} %shard_map.66), channel_id=1, replica_groups=mesh['y'=4,'z'=8,'x'=4,'core'=2] {'z'}, dimensions={0} | all-to-all | bytes 524288 | tf_op jit(solution)/shard_map/all_to_all | solution.py:282
  124.7 0.6 reduce_sum.19
  (30 shorter events, 0.1 us)
Async XLA Ops:
  4.5 6.0 %copy-start = (f32[384,1024]{1,0:T(8,128)}, f32[384,1024]{1,0:T(8,128)S(1)}, u32[]{:S(2)}) copy-start(f32[384,1024]{1,0:T(8,128)S(1)} %get-tuple-element.25.cols) | copy-start | bytes 4718596
  4.5 6.0 %collective-permute-start.7 = (f32[4,1024,128]{2,1,0:T(8,128)S(1)}, f32[4,1024,128]{2,1,0:T(8,128)S(1)}, u32[]{:S(2)}, u32[]{:S(2)}) collective-permute-start(f32[4,1024,128]{2,1,0:T(8,128)S(1)} %get-tuple-element.26), channel_id=1, source_target_pairs={{0,1},{1,0},{2,3},{3,2},{4,5},{5,4},{6,7},{7,6},{8,9},{9,8},{10,11... | collective-permute-start | bytes 6291464 | tf_op jit(solution)/shard_map/ppermute | solution.py:26
  4.6 4.2 %copy-start.7 = (f32[2,32,1024]{2,1,0:T(8,128)S(1)}, f32[2,32,1024]{2,1,0:T(8,128)}, u32[]{:S(2)}) copy-start(f32[2,32,1024]{2,1,0:T(8,128)} %inverses.1) | copy-start | bytes 786436
  4.6 4.2 %copy-start.8 = (f32[1024,32]{0,1:T(8,128)S(1)}, f32[1024,32]{0,1:T(8,128)}, u32[]{:S(2)}) copy-start(f32[1024,32]{0,1:T(8,128)} %param.8) | copy-start | bytes 393220
  8.3 21.0 %collective-permute-start.14 = (f32[4,1024,128]{2,1,0:T(8,128)}, f32[4,1024,128]{2,1,0:T(8,128)}, u32[]{:S(2)}, u32[]{:S(2)}) collective-permute-start(f32[4,1024,128]{2,1,0:T(8,128)} %shard_map.62), channel_id=1, source_target_pairs={{0,1},{1,0},{2,3},{3,2},{4,5},{5,4},{6,7},{7,6},{8,9},{9,8},{10,11... | collective-permute-start | bytes 6291464 | tf_op jit(solution)/shard_map/ppermute | solution.py:26
  9.6 0.8 copy-start.2
  13.6 0.8 copy-start.5
  14.4 0.8 copy-start.9
  15.2 0.8 copy-start.10
  16.1 24.1 %collective-permute-start.8 = (f32[1024,128]{1,0:T(8,128)}, f32[1024,128]{1,0:T(8,128)}, u32[]{:S(2)}, u32[]{:S(2)}) collective-permute-start(f32[1024,128]{1,0:T(8,128)} %get-tuple-element.28), channel_id=1, source_target_pairs={{0,2},{2,4},{4,6},{6,0},{1,3},{3,5},{5,7},{7,1},{8,10},{10,12},{12... | collective-permute-start | bytes 1572872 | tf_op jit(solution)/shard_map/ppermute | solution.py:26
  17.6 26.0 %all-to-all-start = ((f32[8,32,512]{2,1,0:T(8,128)}), f32[8,32,512]{2,1,0:T(8,128)}, u32[]{:S(2)}, u32[]{:S(2)}) async-start(f32[8,32,512]{2,1,0:T(8,128)} %copy-done.2), calls=%async_computation | async-start | bytes 1048576 | tf_op jit(solution)/shard_map/all_to_all | solution.py:248
  26.0 18.9 %collective-permute-start.9 = (f32[1024,128]{1,0:T(8,128)}, f32[1024,128]{1,0:T(8,128)}, u32[]{:S(2)}, u32[]{:S(2)}) collective-permute-start(f32[1024,128]{1,0:T(8,128)} %copy-done.10), channel_id=1, source_target_pairs={{0,4},{2,6},{4,0},{6,2},{1,5},{3,7},{5,1},{7,3},{8,12},{10,14},{12... | collective-permute-start | bytes 1572872 | tf_op jit(solution)/shard_map/ppermute | solution.py:26
  27.2 24.6 %collective-permute-start.10 = (f32[1024,128]{1,0:T(8,128)}, f32[1024,128]{1,0:T(8,128)}, u32[]{:S(2)}, u32[]{:S(2)}) collective-permute-start(f32[1024,128]{1,0:T(8,128)} %copy-done.9), channel_id=1, source_target_pairs={{0,6},{2,0},{4,2},{6,4},{1,7},{3,1},{5,3},{7,5},{8,14},{10,8},{12,... | collective-permute-start | bytes 1572872 | tf_op jit(solution)/shard_map/ppermute | solution.py:26
  29.3 1.4 %copy-start.1 = (f32[384,1024]{1,0:T(8,128)S(1)}, f32[384,1024]{1,0:T(8,128)}, u32[]{:S(2)}) copy-start(f32[384,1024]{1,0:T(8,128)} %copy-done) | copy-start | bytes 4718596
  34.9 0.8 copy-start.3
  35.7 28.7 %copy-start.4 = (f32[1024,128]{1,0:T(8,128)S(1)}, f32[1024,128]{1,0:T(8,128)}, u32[]{:S(2)}) copy-start(f32[1024,128]{1,0:T(8,128)} %copy-done.3) | copy-start | bytes 1572868
  35.7 23.3 %collective-permute-start.15 = (f32[1024,128]{1,0:T(8,128)}, f32[1024,128]{1,0:T(8,128)S(1)}, u32[]{:S(2)}, u32[]{:S(2)}) collective-permute-start(f32[1024,128]{1,0:T(8,128)} %get-tuple-element.36), channel_id=1, source_target_pairs={{0,64},{64,128},{128,192},{192,0},{1,65},{65,129},{129,193},{193,1... | collective-permute-start | bytes 1572872 | tf_op jit(solution)/shard_map/ppermute | solution.py:26
  37.3 27.2 %collective-permute-start.16 = (f32[1024,128]{1,0:T(8,128)}, f32[1024,128]{1,0:T(8,128)S(1)}, u32[]{:S(2)}, u32[]{:S(2)}) collective-permute-start(f32[1024,128]{1,0:T(8,128)} %get-tuple-element.37), channel_id=1, source_target_pairs={{0,128},{64,192},{128,0},{192,64},{1,129},{65,193},{129,1},{193,65... | collective-permute-start | bytes 1572872 | tf_op jit(solution)/shard_map/ppermute | solution.py:26
  40.2 24.3 %collective-permute-start.17 = (f32[1024,128]{1,0:T(8,128)}, f32[1024,128]{1,0:T(8,128)S(1)}, u32[]{:S(2)}, u32[]{:S(2)}) collective-permute-start(f32[1024,128]{1,0:T(8,128)} %get-tuple-element.38), channel_id=1, source_target_pairs={{0,192},{64,0},{128,64},{192,128},{1,193},{65,1},{129,65},{193,129... | collective-permute-start | bytes 1572872 | tf_op jit(solution)/shard_map/ppermute | solution.py:26
  51.8 1.0 copy-start.6
  54.3 13.9 %collective-permute-start.11 = (f32[256,128]{1,0:T(8,128)S(1)}, f32[256,128]{1,0:T(8,128)S(1)}, u32[]{:S(2)}, u32[]{:S(2)}) collective-permute-start(f32[256,128]{1,0:T(8,128)S(1)} %get-tuple-element.32), channel_id=1, source_target_pairs={{0,64},{64,128},{128,192},{192,0},{1,65},{65,129},{129,193},{193,1... | collective-permute-start | bytes 393224 | tf_op jit(solution)/shard_map/ppermute | solution.py:26
  56.1 12.1 %collective-permute-start.12 = (f32[256,128]{1,0:T(8,128)S(1)}, f32[256,128]{1,0:T(8,128)S(1)}, u32[]{:S(2)}, u32[]{:S(2)}) collective-permute-start(f32[256,128]{1,0:T(8,128)S(1)} %get-tuple-element.33), channel_id=1, source_target_pairs={{0,128},{64,192},{128,0},{192,64},{1,129},{65,193},{129,1},{193,65... | collective-permute-start | bytes 393224 | tf_op jit(solution)/shard_map/ppermute | solution.py:26
  59.0 9.2 %collective-permute-start.13 = (f32[256,128]{1,0:T(8,128)S(1)}, f32[256,128]{1,0:T(8,128)S(1)}, u32[]{:S(2)}, u32[]{:S(2)}) collective-permute-start(f32[256,128]{1,0:T(8,128)S(1)} %get-tuple-element.34), channel_id=1, source_target_pairs={{0,192},{64,0},{128,64},{192,128},{1,193},{65,1},{129,65},{193,129... | collective-permute-start | bytes 393224 | tf_op jit(solution)/shard_map/ppermute | solution.py:26
  64.5 33.2 %copy-start.11 = (f32[2,32,128]{2,1,0:T(8,128)S(1)}, f32[2,32,128]{2,1,0:T(8,128)}, u32[]{:S(2)}) copy-start(f32[2,32,128]{2,1,0:T(8,128)} %param.7) | copy-start | bytes 98308
  64.6 5.0 %collective-permute-start.18 = (f32[256,128]{1,0:T(8,128)S(1)}, f32[256,128]{1,0:T(8,128)S(1)}, u32[]{:S(2)}, u32[]{:S(2)}) collective-permute-start(f32[256,128]{1,0:T(8,128)S(1)} %get-tuple-element.40), channel_id=1, source_target_pairs={{0,2},{2,4},{4,6},{6,0},{1,3},{3,5},{5,7},{7,1},{8,10},{10,12},{12... | collective-permute-start | bytes 393224 | tf_op jit(solution)/shard_map/ppermute | solution.py:26
  64.6 6.7 %collective-permute-start.19 = (f32[256,128]{1,0:T(8,128)S(1)}, f32[256,128]{1,0:T(8,128)S(1)}, u32[]{:S(2)}, u32[]{:S(2)}) collective-permute-start(f32[256,128]{1,0:T(8,128)S(1)} %get-tuple-element.41), channel_id=1, source_target_pairs={{0,4},{2,6},{4,0},{6,2},{1,5},{3,7},{5,1},{7,3},{8,12},{10,14},{12... | collective-permute-start | bytes 393224 | tf_op jit(solution)/shard_map/ppermute | solution.py:26
  68.2 5.3 %collective-permute-start.20 = (f32[256,128]{1,0:T(8,128)S(1)}, f32[256,128]{1,0:T(8,128)S(1)}, u32[]{:S(2)}, u32[]{:S(2)}) collective-permute-start(f32[256,128]{1,0:T(8,128)S(1)} %get-tuple-element.42), channel_id=1, source_target_pairs={{0,6},{2,0},{4,2},{6,4},{1,7},{3,1},{5,3},{7,5},{8,14},{10,8},{12,... | collective-permute-start | bytes 393224 | tf_op jit(solution)/shard_map/ppermute | solution.py:26
  74.2 23.6 %all-to-all-start.1 = ((f32[8,64,128]{2,1,0:T(8,128)}), f32[8,64,128]{2,1,0:T(8,128)S(1)}, u32[]{:S(2)}, u32[]{:S(2)}) async-start(f32[8,64,128]{2,1,0:T(8,128)} %shard_map.65), calls=%async_computation.1 | async-start | bytes 524288 | tf_op jit(solution)/shard_map/all_to_all | solution.py:271
  81.1 5.8 %collective-permute-start = (f32[128,128]{1,0:T(8,128)S(1)}, f32[128,128]{1,0:T(8,128)S(1)}, u32[]{:S(2)}, u32[]{:S(2)}) collective-permute-start(f32[128,128]{1,0:T(8,128)S(1)} %shard_map.56.part0.after), channel_id=1, source_target_pairs={{0,64},{64,128},{128,192},{192,0},{1,65},{65,129},{129,193},{193,1... | collective-permute-start | bytes 196616 | tf_op jit(solution)/shard_map/ppermute | solution.py:26
  82.2 5.8 %collective-permute-start.1 = (f32[128,128]{1,0:T(8,128)S(1)}, f32[128,128]{1,0:T(8,128)S(1)}, u32[]{:S(2)}, u32[]{:S(2)}) collective-permute-start(f32[128,128]{1,0:T(8,128)S(1)} %shard_map.56.part0.after), channel_id=1, source_target_pairs={{0,128},{64,192},{128,0},{192,64},{1,129},{65,193},{129,1},{193,65... | collective-permute-start | bytes 196616 | tf_op jit(solution)/shard_map/ppermute | solution.py:26
  85.0 4.3 %collective-permute-start.2 = (f32[128,128]{1,0:T(8,128)S(1)}, f32[128,128]{1,0:T(8,128)S(1)}, u32[]{:S(2)}, u32[]{:S(2)}) collective-permute-start(f32[128,128]{1,0:T(8,128)S(1)} %shard_map.56.part0.after), channel_id=1, source_target_pairs={{0,192},{64,0},{128,64},{192,128},{1,193},{65,1},{129,65},{193,129... | collective-permute-start | bytes 196616 | tf_op jit(solution)/shard_map/ppermute | solution.py:26
  90.6 1.4 %collective-permute-start.3 = (f32[256,128]{1,0:T(8,128)S(1)}, f32[256,128]{1,0:T(8,128)S(1)}, u32[]{:S(2)}, u32[]{:S(2)}) collective-permute-start(f32[256,128]{1,0:T(8,128)S(1)} %shard_map.57.a), channel_id=1, source_target_pairs={{0,1},{1,0},{2,3},{3,2},{4,5},{5,4},{6,7},{7,6},{8,9},{9,8},{10,11... | collective-permute-start | bytes 393224 | tf_op jit(solution)/shard_map/ppermute | solution.py:26
  92.1 9.7 %collective-permute-start.4 = (f32[256,128]{1,0:T(8,128)S(1)}, f32[256,128]{1,0:T(8,128)S(1)}, u32[]{:S(2)}, u32[]{:S(2)}) collective-permute-start(f32[256,128]{1,0:T(8,128)S(1)} %shard_map.58.mix0), channel_id=1, source_target_pairs={{0,2},{2,4},{4,6},{6,0},{1,3},{3,5},{5,7},{7,1},{8,10},{10,12},{12... | collective-permute-start | bytes 393224 | tf_op jit(solution)/shard_map/ppermute | solution.py:26
  92.7 9.3 %collective-permute-start.5 = (f32[256,128]{1,0:T(8,128)S(1)}, f32[256,128]{1,0:T(8,128)S(1)}, u32[]{:S(2)}, u32[]{:S(2)}) collective-permute-start(f32[256,128]{1,0:T(8,128)S(1)} %shard_map.58.mix0), channel_id=1, source_target_pairs={{0,4},{2,6},{4,0},{6,2},{1,5},{3,7},{5,1},{7,3},{8,12},{10,14},{12... | collective-permute-start | bytes 393224 | tf_op jit(solution)/shard_map/ppermute | solution.py:26
  95.9 6.4 %collective-permute-start.6 = (f32[256,128]{1,0:T(8,128)S(1)}, f32[256,128]{1,0:T(8,128)S(1)}, u32[]{:S(2)}, u32[]{:S(2)}) collective-permute-start(f32[256,128]{1,0:T(8,128)S(1)} %shard_map.58.mix0), channel_id=1, source_target_pairs={{0,6},{2,0},{4,2},{6,4},{1,7},{3,1},{5,3},{7,5},{8,14},{10,8},{12,... | collective-permute-start | bytes 393224 | tf_op jit(solution)/shard_map/ppermute | solution.py:26
  97.8 5.2 %collective-permute-start.21 = (f32[64,128]{1,0:T(8,128)S(1)}, f32[64,128]{1,0:T(8,128)S(1)}, u32[]{:S(2)}, u32[]{:S(2)}) collective-permute-start(f32[64,128]{1,0:T(8,128)S(1)} %bitcast_subtract_fusion.rest0), channel_id=1, source_target_pairs={{0,64},{64,128},{128,192},{192,0},{1,65},{65,129},{129,193},{193,1... | collective-permute-start | bytes 98312 | tf_op jit(solution)/shard_map/ppermute | solution.py:26
  98.5 5.5 %collective-permute-start.22 = (f32[64,128]{1,0:T(8,128)S(1)}, f32[64,128]{1,0:T(8,128)S(1)}, u32[]{:S(2)}, u32[]{:S(2)}) collective-permute-start(f32[64,128]{1,0:T(8,128)S(1)} %bitcast_subtract_fusion.rest0), channel_id=1, source_target_pairs={{0,128},{64,192},{128,0},{192,64},{1,129},{65,193},{129,1},{193,65... | collective-permute-start | bytes 98312 | tf_op jit(solution)/shard_map/ppermute | solution.py:26
  101.8 3.9 %collective-permute-start.23 = (f32[64,128]{1,0:T(8,128)S(1)}, f32[64,128]{1,0:T(8,128)S(1)}, u32[]{:S(2)}, u32[]{:S(2)}) collective-permute-start(f32[64,128]{1,0:T(8,128)S(1)} %bitcast_subtract_fusion.rest0), channel_id=1, source_target_pairs={{0,192},{64,0},{128,64},{192,128},{1,193},{65,1},{129,65},{193,129... | collective-permute-start | bytes 98312 | tf_op jit(solution)/shard_map/ppermute | solution.py:26

commit v4 on v3

--- a/solution.py
+++ b/solution.py
@@ -79,20 +79,26 @@
 def first_kernel(nx, ny):
     def kernel(place, far_rows, far_cols, out, rows, cols, left, right, sems):
         size = left.shape[0]
-        load_cols = pltpu.make_async_copy(far_cols, cols, sems.at[0])
-        load_cols.start()
+        part = cols.shape[0] // ny
+        first_loads = []
+        for k in range(ny):
+            at = slice(k * part, (k + 1) * part)
+            first_loads.append(
+                pltpu.make_async_copy(far_cols.at[at, :], cols.at[at, :], sems.at[2 * ny + k])
+            )
         loads = []
         for panel in range(2):
             for jy in range(ny):
                 at = rows_at(place, jy, ny, size)
                 loads.append(
                     pltpu.make_async_copy(
-                        far_rows.at[panel, at, :], rows.at[panel, at, :], sems.at[1 + panel * ny + jy]
+                        far_rows.at[panel, at, :], rows.at[panel, at, :], sems.at[panel * ny + jy]
                     )
                 )
-        for load in loads:
+        for load in first_loads + loads:
             load.start()
-        load_cols.wait()
+        for load in first_loads:
+            load.wait()
         split_columns(place, cols, right, nx)
         for jy in range(ny):
             loads[jy].wait()
@@ -126,7 +132,7 @@
         ),
         in_specs=[SMEM, FAR, FAR],
         scratch_shapes=product_scratch(size, depth, nx, ny)
-        + [pltpu.SemaphoreType.DMA((1 + 2 * ny,))],
+        + [pltpu.SemaphoreType.DMA((3 * ny,))],
         compiler_params=PRODUCT,
         cost_estimate=product_cost(size, depth, nx),
     )(place, far(rows), far(cols))
@@ -175,8 +181,9 @@
     )
 
 
-def chain_kernel(tiles, part0, part1, part2, part3, out):
-    total = (part0[...] + part1[...]) + (part2[...] + part3[...])
+def chain_kernel(tiles, part0, got1, got2, got3, out):
+    at = got1.shape[0] - 128
+    total = (part0[...] + got1[at:, :]) + (got2[at:, :] + got3[at:, :])
     out[...] = jnp.dot(tiles[:, 128:256], total, precision=EXACT, preferred_element_type=F32)
 
 
@@ -184,25 +191,29 @@
     out[...] = a[...] + b[...]
 
 
-def gather_sums_kernel(a, b, c, d, after, *outs):
-    size = outs[0].shape[0]
-    for j, out in enumerate(outs):
+def gather_sums_kernel(a, b, c, d, rider, own, *outs):
+    size = own.shape[0]
+    for j, out in enumerate((own,) + outs):
         span = slice(j * size, (j + 1) * size)
-        out[...] = (a[span, :] + b[span, :]) + (c[span, :] + d[span, :])
-
-
-def gather_sums(parts, after, count):
+        out[0:size, :] = (a[span, :] + b[span, :]) + (c[span, :] + d[span, :])
+        if j and out.shape[0] > size:
+            out[size:, :] = rider[...]
+
+
+def gather_sums(parts, rider, count, carried):
     size = parts[0].shape[0] // count
+    longer = jax.ShapeDtypeStruct((size + (rider.shape[0] if carried else 0), 128), F32)
     return pl.pallas_call(
         gather_sums_kernel,
-        out_shape=[jax.ShapeDtypeStruct((size, 128), F32)] * count,
-        in_specs=[pl.BlockSpec()] * len(parts) + [ORDER],
+        out_shape=[jax.ShapeDtypeStruct((size, 128), F32)] + [longer] * (count - 1),
+        in_specs=[pl.BlockSpec()] * len(parts) + [pl.BlockSpec() if carried else ORDER],
         compiler_params=SMALL,
-    )(*parts, after)
+    )(*parts, rider)
 
 
 def interleave_kernel(a0, a1, a2, a3, b0, b1, b2, b3, out):
-    low = (a0[...] + a1[...]) + (a2[...] + a3[...])
+    size = a0.shape[0]
+    low = (a0[...] + a1[0:size, :]) + (a2[0:size, :] + a3[0:size, :])
     high = (b0[...] + b1[...]) + (b2[...] + b3[...])
     for z in range(out.shape[0]):
         out[z, 0:32, :] = low[z * 32 : (z + 1) * 32, :]
@@ -250,24 +261,22 @@
     coupled = pl.pallas_call(
         couple_kernel, out_shape=jax.ShapeDtypeStruct((128, 128), F32), compiler_params=SMALL
     )(tiles)
-    coupled_all = [coupled] + [shift(coupled, "y", j, ny) for j in range(1, ny)]
-    chained = pl.pallas_call(
-        chain_kernel, out_shape=jax.ShapeDtypeStruct((256, 128), F32), compiler_params=SMALL
-    )(tiles, *coupled_all)
-    mix = pl.pallas_call(
-        sum_kernel, out_shape=jax.ShapeDtypeStruct((256, 128), F32), compiler_params=SMALL
-    )(chained, shift(chained, "core", 1, nc))
-    mixes = [mix] + [shift(mix, "x", j, nx) for j in range(1, nx)]
-
-    sums0 = gather_sums(got0, coupled, ny)
+    sums0 = gather_sums(got0, coupled, ny, True)
     again0 = [sums0[0]] + [shift(sums0[j], "y", j, ny) for j in range(1, ny)]
-    sums1 = gather_sums(got1, coupled, nx)
+    sums1 = gather_sums(got1, coupled, nx, False)
     again1 = [sums1[0]] + [shift(sums1[j], "x", j, nx) for j in range(1, nx)]
     by_z = pl.pallas_call(
         interleave_kernel,
         out_shape=jax.ShapeDtypeStruct((nz, 64, 128), F32),
         compiler_params=SMALL,
     )(*again0, *again1)
+    chained = pl.pallas_call(
+        chain_kernel, out_shape=jax.ShapeDtypeStruct((256, 128), F32), compiler_params=SMALL
+    )(tiles, coupled, *again0[1:])
+    mix = pl.pallas_call(
+        sum_kernel, out_shape=jax.ShapeDtypeStruct((256, 128), F32), compiler_params=SMALL
+    )(chained, shift(chained, "core", 1, nc))
+    mixes = [mix] + [shift(mix, "x", j, nx) for j in range(1, nx)]
     old = lax.all_to_all(by_z, "z", 0, 0, tiled=True).sum(axis=0)
     rest = right_side.reshape(64, 128) - old
 

time: 126 us -> 123 us (0.976)
  waiting for transfers between devices: 26.1 us -> 31.8 us
  starting transfers between devices: 51.5 us -> 46.9 us
  blocking collectives: 17.5 us -> 13.4 us
    ppermute x24 -> x21, starting transfers between devices: 36.1 us -> 31.5 us  [shift(): lax.ppermute(value, axis, [(i, (i + step) % size) for i in range(size)])]
    ppermute x24 -> x21, waiting for transfers between devices: 24 us -> 28.3 us  [shift(): lax.ppermute(value, axis, [(i, (i + step) % size) for i in range(size)])]
    all_to_all x1, blocking collectives: 17.5 us -> 13.4 us  [steps(): panels = lax.all_to_all(solved_part, 'z', 0, 0, tiled=True).sum(axis=0)]
    all_to_all x1, waiting for transfers between devices: 0.01 us -> 3.11 us  [steps(): old = lax.all_to_all(by_z, 'z', 0, 0, tiled=True).sum(axis=0)]
    all_to_all x1, waiting for transfers between devices: 2.05 us -> 0.34 us  [steps(): tiles = lax.all_to_all(packed, 'z', 0, 0, tiled=True).reshape(nz * 32, 512)]
    pallas_call x1, Pallas kernels: 4.38 us -> 5.71 us  [first_products(): pl.pallas_call(first_kernel(nx, ny), out_shape=(jax.ShapeDtypeStruct((nx,...]
  transfers between devices with their start and end apart: 26 -> 23, of which waited for: 14 -> 12; matrix products, arithmetic and copies ran while one was open for 0% -> 0% of each run, Pallas kernels for 13% -> 10%
where the time goes in v4:
time: 123 us; the launch traced here: 122 us
  starting transfers between devices  46.9 us (38%)
  waiting for transfers between devices  31.8 us (26%)
  Pallas kernels  22.9 us (19%)
  blocking collectives  13.4 us (11%)
  local copies, waits for them, and re-layouts  6.53 us (5%)
    ppermute x21, starting transfers between devices, shift(): lax.ppermute(value, axis, [(i, (i + step) % size) for i in range(size)])  31.5 us
    ppermute x21, waiting for transfers between devices, shift(): lax.ppermute(value, axis, [(i, (i + step) % size) for i in range(size)])  28.3 us
    all_to_all x1, blocking collectives, steps(): panels = lax.all_to_all(solved_part, 'z', 0, 0, tiled=True).sum(axis=0)  13.4 us
    pallas_call x3, Pallas kernels, products(): pl.pallas_call(kernel, out_shape=shapes, in_specs=[SMEM] + [pl.BlockSpec(...  9.81 us
    all_to_all x1, starting transfers between devices, steps(): tiles = lax.all_to_all(packed, 'z', 0, 0, tiled=True).reshape(nz * 32, 512)  8.46 us
    all_to_all x1, starting transfers between devices, steps(): old = lax.all_to_all(by_z, 'z', 0, 0, tiled=True).sum(axis=0)  6.93 us
    unnamed x24, local copies, waits for them, and re-layouts  6.53 us
    pallas_call x1, Pallas kernels, first_products(): pl.pallas_call(first_kernel(nx, ny), out_shape=(jax.ShapeDtypeStruct((nx,...  5.71 us
  transfers between devices with their start and end apart: 23, of which 12 were waited for; matrix products, arithmetic and copies ran while one was open for 0% of the time, Pallas kernels for 10%

profile of v4, /device:TPU:2, one launch (start us, length us, event | category | flops | bytes accessed | tf_op | source)
XLA Modules:
  0.0 122.5 jit_solution(5396014365457652093)
XLA Ops:
  0.0 0.1 pad_add_fusion.2.place
  0.1 5.7 %shard_map.57 = (f32[4,1024,128]{2,1,0:T(8,128)}, f32[2,1024,384]{2,1,0:T(8,128)S(1)}, f32[384,1024]{1,0:T(8,128)S(1)}) custom-call(s32[3]{0:T(128)S(1)} %pad_add_fusion.2.place, f32[2,1024,384]{2,1,0:T(8,128)} %far_rows.1, f32[384,1024]{1,0:T(8,128)} %far_cols.1), custom_call_target="tpu_custom_call" | custom-call | flops 1207959552 | bytes 6291456 | tf_op jit(solution)/shard_map/pallas_call | solution.py:126
  5.8 2.3 %shard_map.62 = f32[4,1024,128]{2,1,0:T(8,128)S(1)} custom-call(s32[3]{0:T(128)S(1)} %pad_add_fusion.2.place, f32[2,1024,384]{2,1,0:T(8,128)S(1)} %get-tuple-element.24.rows, f32[384,1024]{1,0:T(8,128)S(1)} %get-tuple-element.25.cols), custom_call_target="tpu_custom_call" | custom-call | flops 1207959552 | bytes 6291456 | tf_op jit(solution)/shard_map/pallas_call | solution.py:151
  8.1 0.1 collective-permute-start.11
  8.2 0.5 collective-permute-start
  8.7 0.1 pad_add_fusion.place
  8.8 3.6 %collective-permute-done.11.refs_0_ = f32[4,1024,128]{2,1,0:T(8,128)S(1)} collective-permute-done((f32[4,1024,128]{2,1,0:T(8,128)S(1)}, f32[4,1024,128]{2,1,0:T(8,128)S(1)}, u32[]{:S(2)}, u32[]{:S(2)}) %collective-permute-start.11) | collective-permute-done | bytes 2097184 | tf_op jit(solution)/shard_map/ppermute | solution.py:26
  12.4 2.9 %shard_map.63 = (f32[1024,128]{1,0:T(8,128)S(1)}, f32[1024,128]{1,0:T(8,128)}, f32[1024,128]{1,0:T(8,128)S(1)}, f32[1024,128]{1,0:T(8,128)S(1)}) custom-call(s32[3]{0:T(128)S(1)} %pad_add_fusion.place, f32[2,1024,384]{2,1,0:T(8,128)S(1)} %get-tuple-element.24.rows, f32[384,1024]{1,0:T(8,128)S(1)} %get-tuple-element.25.cols, ...), custom_call_target="tpu_custom_call" | custom-call | flops 1207959552 | bytes 6291456 | tf_op jit(solution)/shard_map/pallas_call | solution.py:151
  15.3 0.8 copy-done.3
  16.1 0.8 copy-done.9
  17.0 0.8 copy-done.10
  17.8 1.6 %collective-permute-start.12 = (f32[1024,128]{1,0:T(8,128)}, f32[1024,128]{1,0:T(8,128)}, u32[]{:S(2)}, u32[]{:S(2)}) collective-permute-start(f32[1024,128]{1,0:T(8,128)} %get-tuple-element.36), channel_id=1, source_target_pairs={{0,64},{64,128},{128,192},{192,0},{1,65},{65,129},{129,193},{193,1... | collective-permute-start | bytes 1572872 | tf_op jit(solution)/shard_map/ppermute | solution.py:26
  19.4 0.8 shard_map.55
  20.2 0.8 copy-done.2
  21.0 8.5 %all-to-all-start = ((f32[8,32,512]{2,1,0:T(8,128)}), f32[8,32,512]{2,1,0:T(8,128)}, u32[]{:S(2)}, u32[]{:S(2)}) async-start(f32[8,32,512]{2,1,0:T(8,128)} %copy-done.2), calls=%async_computation | async-start | bytes 1048576 | tf_op jit(solution)/shard_map/all_to_all | solution.py:259
  29.5 2.9 %collective-permute-start.13 = (f32[1024,128]{1,0:T(8,128)}, f32[1024,128]{1,0:T(8,128)}, u32[]{:S(2)}, u32[]{:S(2)}) collective-permute-start(f32[1024,128]{1,0:T(8,128)} %copy-done.10), channel_id=1, source_target_pairs={{0,128},{64,192},{128,0},{192,64},{1,129},{65,193},{129,1},{193,65... | collective-permute-start | bytes 1572872 | tf_op jit(solution)/shard_map/ppermute | solution.py:26
  32.4 1.3 %collective-permute-start.14 = (f32[1024,128]{1,0:T(8,128)}, f32[1024,128]{1,0:T(8,128)}, u32[]{:S(2)}, u32[]{:S(2)}) collective-permute-start(f32[1024,128]{1,0:T(8,128)} %copy-done.9), channel_id=1, source_target_pairs={{0,192},{64,0},{128,64},{192,128},{1,193},{65,1},{129,65},{193,129... | collective-permute-start | bytes 1572872 | tf_op jit(solution)/shard_map/ppermute | solution.py:26
  33.7 0.0 collective-permute-done.refs_0_
  33.7 1.4 %copy-done.1 = f32[384,1024]{1,0:T(8,128)S(1)} copy-done((f32[384,1024]{1,0:T(8,128)S(1)}, f32[384,1024]{1,0:T(8,128)}, u32[]{:S(2)}) %copy-start.1) | copy-done | bytes 1572888
  35.1 4.5 %shard_map.58 = (f32[1024,128]{1,0:T(8,128)S(1)}, f32[1024,128]{1,0:T(8,128)}, f32[1024,128]{1,0:T(8,128)}, f32[1024,128]{1,0:T(8,128)}) custom-call(s32[3]{0:T(128)S(1)} %pad_add_fusion.place, f32[2,1024,384]{2,1,0:T(8,128)S(1)} %get-tuple-element.24.rows, f32[384,1024]{1,0:T(8,128)S(1)} %copy-done.1, f32[4,1024,128]{2,1,0:T(8,128)} %collective-permute-done.refs_0_), custom_call_target="tpu_custom_call" | custom-call | flops 1207959552 | bytes 6291456 | tf_op jit(solution)/shard_map/pallas_call | solution.py:151
  39.7 0.8 copy-done.5
  40.5 1.5 %collective-permute-start.1 = (f32[1024,128]{1,0:T(8,128)}, f32[1024,128]{1,0:T(8,128)S(1)}, u32[]{:S(2)}, u32[]{:S(2)}) collective-permute-start(f32[1024,128]{1,0:T(8,128)} %get-tuple-element.28), channel_id=1, source_target_pairs={{0,2},{2,4},{4,6},{6,0},{1,3},{3,5},{5,7},{7,1},{8,10},{10,12},{12... | collective-permute-start | bytes 1572872 | tf_op jit(solution)/shard_map/ppermute | solution.py:26
  41.9 1.1 collective-permute-start.2
  43.1 0.0 collective-permute-done.12.b
  43.1 3.6 %collective-permute-start.3 = (f32[1024,128]{1,0:T(8,128)}, f32[1024,128]{1,0:T(8,128)S(1)}, u32[]{:S(2)}, u32[]{:S(2)}) collective-permute-start(f32[1024,128]{1,0:T(8,128)} %get-tuple-element.30), channel_id=1, source_target_pairs={{0,6},{2,0},{4,2},{6,4},{1,7},{3,1},{5,3},{7,5},{8,14},{10,8},{12,... | collective-permute-start | bytes 1572872 | tf_op jit(solution)/shard_map/ppermute | solution.py:26
  46.7 0.3 all-to-all-done
  47.1 1.3 %shard_map.56.rider.part0 = f32[128,128]{1,0:T(8,128)S(1)} custom-call(f32[256,512]{1,0:T(8,128)} %bitcast.4.tiles), custom_call_target="tpu_custom_call" | custom-call | tf_op jit(solution)/shard_map/pallas_call | solution.py:261
  48.4 6.6 %collective-permute-done.14.d = f32[1024,128]{1,0:T(8,128)} collective-permute-done((f32[1024,128]{1,0:T(8,128)}, f32[1024,128]{1,0:T(8,128)}, u32[]{:S(2)}, u32[]{:S(2)}) %collective-permute-start.14) | collective-permute-done | bytes 524320 | tf_op jit(solution)/shard_map/ppermute | solution.py:26
  55.0 1.0 copy-done.4
  56.0 1.5 %shard_map.64 = (f32[256,128]{1,0:T(8,128)S(1)}, f32[256,128]{1,0:T(8,128)S(1)}, f32[256,128]{1,0:T(8,128)S(1)}, f32[256,128]{1,0:T(8,128)S(1)}) custom-call(f32[1024,128]{1,0:T(8,128)S(1)} %copy-done.4, f32[1024,128]{1,0:T(8,128)} %collective-permute-done.12.b, f32[1024,128]{1,0:T(8,128)} %collective-permute-done.13.c, ...), custom_call_target="tpu_custom_call" | custom-call | tf_op jit(solution)/shard_map/pallas_call | solution.py:206
  57.5 1.7 %collective-permute-start.15 = (f32[256,128]{1,0:T(8,128)S(1)}, f32[256,128]{1,0:T(8,128)S(1)}, u32[]{:S(2)}, u32[]{:S(2)}) collective-permute-start(f32[256,128]{1,0:T(8,128)S(1)} %get-tuple-element.40), channel_id=1, source_target_pairs={{0,2},{2,4},{4,6},{6,0},{1,3},{3,5},{5,7},{7,1},{8,10},{10,12},{12... | collective-permute-start | bytes 393224 | tf_op jit(solution)/shard_map/ppermute | solution.py:26
  59.3 0.0 collective-permute-done.1.b
  59.3 0.0 collective-permute-done.2.c
  59.3 7.5 %collective-permute-done.3.d = f32[1024,128]{1,0:T(8,128)S(1)} collective-permute-done((f32[1024,128]{1,0:T(8,128)}, f32[1024,128]{1,0:T(8,128)S(1)}, u32[]{:S(2)}, u32[]{:S(2)}) %collective-permute-start.3) | collective-permute-done | bytes 524320 | tf_op jit(solution)/shard_map/ppermute | solution.py:26
  66.8 0.1 shard_map.59
  66.9 0.0 copy-start.11
  66.9 0.8 collective-permute-start.4
  67.6 1.1 collective-permute-start.5
  68.7 1.7 %collective-permute-start.6 = (f32[384,128]{1,0:T(8,128)S(1)}, f32[384,128]{1,0:T(8,128)S(1)}, u32[]{:S(2)}, u32[]{:S(2)}) collective-permute-start(f32[384,128]{1,0:T(8,128)S(1)} %get-tuple-element.33), channel_id=1, source_target_pairs={{0,192},{64,0},{128,64},{192,128},{1,193},{65,1},{129,65},{193,129... | collective-permute-start | bytes 589832 | tf_op jit(solution)/shard_map/ppermute | solution.py:26
  70.4 1.8 %collective-permute-start.16 = (f32[256,128]{1,0:T(8,128)S(1)}, f32[256,128]{1,0:T(8,128)S(1)}, u32[]{:S(2)}, u32[]{:S(2)}) collective-permute-start(f32[256,128]{1,0:T(8,128)S(1)} %get-tuple-element.41), channel_id=1, source_target_pairs={{0,4},{2,6},{4,0},{6,2},{1,5},{3,7},{5,1},{7,3},{8,12},{10,14},{12... | collective-permute-start | bytes 393224 | tf_op jit(solution)/shard_map/ppermute | solution.py:26
  72.2 1.6 %collective-permute-start.17 = (f32[256,128]{1,0:T(8,128)S(1)}, f32[256,128]{1,0:T(8,128)S(1)}, u32[]{:S(2)}, u32[]{:S(2)}) collective-permute-start(f32[256,128]{1,0:T(8,128)S(1)} %get-tuple-element.42), channel_id=1, source_target_pairs={{0,6},{2,0},{4,2},{6,4},{1,7},{3,1},{5,3},{7,5},{8,14},{10,8},{12,... | collective-permute-start | bytes 393224 | tf_op jit(solution)/shard_map/ppermute | solution.py:26
  73.8 3.9 %collective-permute-done.16.b2 = f32[256,128]{1,0:T(8,128)S(1)} collective-permute-done((f32[256,128]{1,0:T(8,128)S(1)}, f32[256,128]{1,0:T(8,128)S(1)}, u32[]{:S(2)}, u32[]{:S(2)}) %collective-permute-start.16) | collective-permute-done | bytes 131104 | tf_op jit(solution)/shard_map/ppermute | solution.py:26
  77.6 1.3 %collective-permute-done.17.b3 = f32[256,128]{1,0:T(8,128)S(1)} collective-permute-done((f32[256,128]{1,0:T(8,128)S(1)}, f32[256,128]{1,0:T(8,128)S(1)}, u32[]{:S(2)}, u32[]{:S(2)}) %collective-permute-start.17) | collective-permute-done | bytes 131104 | tf_op jit(solution)/shard_map/ppermute | solution.py:26
  78.9 0.0 collective-permute-done.4.got1.a1
  78.9 0.0 collective-permute-done.5.got2.a2
  78.9 0.2 collective-permute-done.6.got3.a3
  79.2 0.7 shard_map.65
  79.9 6.9 %all-to-all-start.1 = ((f32[8,64,128]{2,1,0:T(8,128)}), f32[8,64,128]{2,1,0:T(8,128)S(1)}, u32[]{:S(2)}, u32[]{:S(2)}) async-start(f32[8,64,128]{2,1,0:T(8,128)} %shard_map.65), calls=%async_computation.1 | async-start | bytes 524288 | tf_op jit(solution)/shard_map/all_to_all | solution.py:280
  86.9 1.3 %shard_map.60.a = f32[256,128]{1,0:T(8,128)S(1)} custom-call(f32[256,512]{1,0:T(8,128)} %bitcast.4.tiles, f32[128,128]{1,0:T(8,128)S(1)} %shard_map.56.rider.part0, f32[384,128]{1,0:T(8,128)S(1)} %collective-permute-done.4.got1.a1, f32[384,128]{1,0:T(8,128)S(1)} %collective-permute-done.5.got2.a2, f32[384,128]{1,0:T(8,128)S(1)} %collective-permute-done.6.got3.a3), custom_call_target="tpu_custom_call" | custom-call | tf_op jit(solution)/shard_map/pallas_call | solution.py:273
  88.2 0.1 collective-permute-start.7
  88.3 1.3 %collective-permute-done.7.b = f32[256,128]{1,0:T(8,128)S(1)} collective-permute-done((f32[256,128]{1,0:T(8,128)S(1)}, f32[256,128]{1,0:T(8,128)S(1)}, u32[]{:S(2)}, u32[]{:S(2)}) %collective-permute-start.7) | collective-permute-done | bytes 131104 | tf_op jit(solution)/shard_map/ppermute | solution.py:26
  89.6 0.4 collective-permute-start.8
  90.0 2.4 %collective-permute-start.9 = (f32[256,128]{1,0:T(8,128)S(1)}, f32[256,128]{1,0:T(8,128)S(1)}, u32[]{:S(2)}, u32[]{:S(2)}) collective-permute-start(f32[256,128]{1,0:T(8,128)S(1)} %shard_map.61.mix0), channel_id=1, source_target_pairs={{0,4},{2,6},{4,0},{6,2},{1,5},{3,7},{5,1},{7,3},{8,12},{10,14},{12... | collective-permute-start | bytes 393224 | tf_op jit(solution)/shard_map/ppermute | solution.py:26
  92.5 2.3 %collective-permute-start.10 = (f32[256,128]{1,0:T(8,128)S(1)}, f32[256,128]{1,0:T(8,128)S(1)}, u32[]{:S(2)}, u32[]{:S(2)}) collective-permute-start(f32[256,128]{1,0:T(8,128)S(1)} %shard_map.61.mix0), channel_id=1, source_target_pairs={{0,6},{2,0},{4,2},{6,4},{1,7},{3,1},{5,3},{7,5},{8,14},{10,8},{12,... | collective-permute-start | bytes 393224 | tf_op jit(solution)/shard_map/ppermute | solution.py:26
  94.8 3.1 %all-to-all-done.1 = f32[8,64,128]{2,1,0:T(8,128)S(1)} async-done(((f32[8,64,128]{2,1,0:T(8,128)}), f32[8,64,128]{2,1,0:T(8,128)S(1)}, u32[]{:S(2)}, u32[]{:S(2)}) %all-to-all-start.1) | async-done | bytes 262176 | tf_op jit(solution)/shard_map/all_to_all | solution.py:280
  97.9 1.3 %collective-permute-start.18 = (f32[64,128]{1,0:T(8,128)S(1)}, f32[64,128]{1,0:T(8,128)S(1)}, u32[]{:S(2)}, u32[]{:S(2)}) collective-permute-start(f32[64,128]{1,0:T(8,128)S(1)} %bitcast_subtract_fusion.rest0), channel_id=1, source_target_pairs={{0,64},{64,128},{128,192},{192,0},{1,65},{65,129},{129,193},{193,1... | collective-permute-start | bytes 98312 | tf_op jit(solution)/shard_map/ppermute | solution.py:26
  99.2 3.8 %collective-permute-start.19 = (f32[64,128]{1,0:T(8,128)S(1)}, f32[64,128]{1,0:T(8,128)S(1)}, u32[]{:S(2)}, u32[]{:S(2)}) collective-permute-start(f32[64,128]{1,0:T(8,128)S(1)} %bitcast_subtract_fusion.rest0), channel_id=1, source_target_pairs={{0,128},{64,192},{128,0},{192,64},{1,129},{65,193},{129,1},{193,65... | collective-permute-start | bytes 98312 | tf_op jit(solution)/shard_map/ppermute | solution.py:26
  103.0 0.0 collective-permute-done.8.mix1
  103.0 0.4 collective-permute-done.18.rest1
  103.4 1.8 %collective-permute-done.19.rest2 = f32[64,128]{1,0:T(8,128)S(1)} collective-permute-done((f32[64,128]{1,0:T(8,128)S(1)}, f32[64,128]{1,0:T(8,128)S(1)}, u32[]{:S(2)}, u32[]{:S(2)}) %collective-permute-start.19) | collective-permute-done | bytes 32800 | tf_op jit(solution)/shard_map/ppermute | solution.py:26
  105.2 1.7 %collective-permute-done.20.rest3 = f32[64,128]{1,0:T(8,128)S(1)} collective-permute-done((f32[64,128]{1,0:T(8,128)S(1)}, f32[64,128]{1,0:T(8,128)S(1)}, u32[]{:S(2)}, u32[]{:S(2)}) %collective-permute-start.20) | collective-permute-done | bytes 32800 | tf_op jit(solution)/shard_map/ppermute | solution.py:26
  106.9 1.5 %shard_map.66 = f32[8,64,128]{2,1,0:T(8,128)S(1)} custom-call(s32[3]{0:T(128)S(1)} %pad_add_fusion.place, f32[256,512]{1,0:T(8,128)} %bitcast.4.tiles, f32[256,128]{1,0:T(8,128)S(1)} %shard_map.61.mix0, f32[256,128]{1,0:T(8,128)S(1)} %collective-permute-done.8.mix1, f32[256,128]{1,0:T(8,128)S(1)} %collective-permute-done.9.mix2, ...), custom_call_target="tpu_custom_call" | custom-call | tf_op jit(solution)/shard_map/pallas_call | solution.py:284
  108.4 13.4 %all_to_all.15 = f32[8,64,128]{2,1,0:T(8,128)S(1)} all-to-all(f32[8,64,128]{2,1,0:T(8,128)S(1)} %shard_map.66), channel_id=1, replica_groups=mesh['y'=4,'z'=8,'x'=4,'core'=2] {'z'}, dimensions={0} | all-to-all | bytes 524288 | tf_op jit(solution)/shard_map/all_to_all | solution.py:291
  121.9 0.6 reduce_sum.19
  (24 shorter events, 0.1 us)
Async XLA Ops:
  5.8 6.6 %copy-start = (f32[384,1024]{1,0:T(8,128)}, f32[384,1024]{1,0:T(8,128)S(1)}, u32[]{:S(2)}) copy-start(f32[384,1024]{1,0:T(8,128)S(1)} %get-tuple-element.25.cols) | copy-start | bytes 4718596
  8.1 4.2 %collective-permute-start.11 = (f32[4,1024,128]{2,1,0:T(8,128)S(1)}, f32[4,1024,128]{2,1,0:T(8,128)S(1)}, u32[]{:S(2)}, u32[]{:S(2)}) collective-permute-start(f32[4,1024,128]{2,1,0:T(8,128)S(1)} %shard_map.62), channel_id=1, source_target_pairs={{0,1},{1,0},{2,3},{3,2},{4,5},{5,4},{6,7},{7,6},{8,9},{9,8},{10,11... | collective-permute-start | bytes 6291464 | tf_op jit(solution)/shard_map/ppermute | solution.py:26
  8.2 25.5 %collective-permute-start = (f32[4,1024,128]{2,1,0:T(8,128)}, f32[4,1024,128]{2,1,0:T(8,128)}, u32[]{:S(2)}, u32[]{:S(2)}) collective-permute-start(f32[4,1024,128]{2,1,0:T(8,128)} %get-tuple-element.26), channel_id=1, source_target_pairs={{0,1},{1,0},{2,3},{3,2},{4,5},{5,4},{6,7},{7,6},{8,9},{9,8},{10,11... | collective-permute-start | bytes 6291464 | tf_op jit(solution)/shard_map/ppermute | solution.py:26
  8.8 10.6 %copy-start.7 = (f32[2,32,1024]{2,1,0:T(8,128)S(1)}, f32[2,32,1024]{2,1,0:T(8,128)}, u32[]{:S(2)}) copy-start(f32[2,32,1024]{2,1,0:T(8,128)} %inverses.1) | copy-start | bytes 786436
  8.8 10.6 %copy-start.8 = (f32[1024,32]{0,1:T(8,128)S(1)}, f32[1024,32]{0,1:T(8,128)}, u32[]{:S(2)}) copy-start(f32[1024,32]{0,1:T(8,128)} %param.8) | copy-start | bytes 393220
  15.3 0.8 copy-start.3
  16.1 0.8 copy-start.9
  17.0 0.8 copy-start.10
  17.8 25.3 %collective-permute-start.12 = (f32[1024,128]{1,0:T(8,128)}, f32[1024,128]{1,0:T(8,128)}, u32[]{:S(2)}, u32[]{:S(2)}) collective-permute-start(f32[1024,128]{1,0:T(8,128)} %get-tuple-element.36), channel_id=1, source_target_pairs={{0,64},{64,128},{128,192},{192,0},{1,65},{65,129},{129,193},{193,1... | collective-permute-start | bytes 1572872 | tf_op jit(solution)/shard_map/ppermute | solution.py:26
  20.2 0.8 copy-start.2
  21.0 26.0 %all-to-all-start = ((f32[8,32,512]{2,1,0:T(8,128)}), f32[8,32,512]{2,1,0:T(8,128)}, u32[]{:S(2)}, u32[]{:S(2)}) async-start(f32[8,32,512]{2,1,0:T(8,128)} %copy-done.2), calls=%async_computation | async-start | bytes 1048576 | tf_op jit(solution)/shard_map/all_to_all | solution.py:259
  29.5 18.9 %collective-permute-start.13 = (f32[1024,128]{1,0:T(8,128)}, f32[1024,128]{1,0:T(8,128)}, u32[]{:S(2)}, u32[]{:S(2)}) collective-permute-start(f32[1024,128]{1,0:T(8,128)} %copy-done.10), channel_id=1, source_target_pairs={{0,128},{64,192},{128,0},{192,64},{1,129},{65,193},{129,1},{193,65... | collective-permute-start | bytes 1572872 | tf_op jit(solution)/shard_map/ppermute | solution.py:26
  32.4 22.6 %collective-permute-start.14 = (f32[1024,128]{1,0:T(8,128)}, f32[1024,128]{1,0:T(8,128)}, u32[]{:S(2)}, u32[]{:S(2)}) collective-permute-start(f32[1024,128]{1,0:T(8,128)} %copy-done.9), channel_id=1, source_target_pairs={{0,192},{64,0},{128,64},{192,128},{1,193},{65,1},{129,65},{193,129... | collective-permute-start | bytes 1572872 | tf_op jit(solution)/shard_map/ppermute | solution.py:26
  33.7 1.4 %copy-start.1 = (f32[384,1024]{1,0:T(8,128)S(1)}, f32[384,1024]{1,0:T(8,128)}, u32[]{:S(2)}) copy-start(f32[384,1024]{1,0:T(8,128)} %copy-done) | copy-start | bytes 4718596
  39.7 0.8 copy-start.5
  40.5 26.3 %copy-start.6 = (f32[1024,128]{1,0:T(8,128)S(1)}, f32[1024,128]{1,0:T(8,128)}, u32[]{:S(2)}) copy-start(f32[1024,128]{1,0:T(8,128)} %copy-done.5) | copy-start | bytes 1572868
  40.5 18.8 %collective-permute-start.1 = (f32[1024,128]{1,0:T(8,128)}, f32[1024,128]{1,0:T(8,128)S(1)}, u32[]{:S(2)}, u32[]{:S(2)}) collective-permute-start(f32[1024,128]{1,0:T(8,128)} %get-tuple-element.28), channel_id=1, source_target_pairs={{0,2},{2,4},{4,6},{6,0},{1,3},{3,5},{5,7},{7,1},{8,10},{10,12},{12... | collective-permute-start | bytes 1572872 | tf_op jit(solution)/shard_map/ppermute | solution.py:26
  41.9 17.3 %collective-permute-start.2 = (f32[1024,128]{1,0:T(8,128)}, f32[1024,128]{1,0:T(8,128)S(1)}, u32[]{:S(2)}, u32[]{:S(2)}) collective-permute-start(f32[1024,128]{1,0:T(8,128)} %get-tuple-element.29), channel_id=1, source_target_pairs={{0,4},{2,6},{4,0},{6,2},{1,5},{3,7},{5,1},{7,3},{8,12},{10,14},{12... | collective-permute-start | bytes 1572872 | tf_op jit(solution)/shard_map/ppermute | solution.py:26
  43.1 23.7 %collective-permute-start.3 = (f32[1024,128]{1,0:T(8,128)}, f32[1024,128]{1,0:T(8,128)S(1)}, u32[]{:S(2)}, u32[]{:S(2)}) collective-permute-start(f32[1024,128]{1,0:T(8,128)} %get-tuple-element.30), channel_id=1, source_target_pairs={{0,6},{2,0},{4,2},{6,4},{1,7},{3,1},{5,3},{7,5},{8,14},{10,8},{12,... | collective-permute-start | bytes 1572872 | tf_op jit(solution)/shard_map/ppermute | solution.py:26
  55.0 1.0 copy-start.4
  57.5 14.7 %collective-permute-start.15 = (f32[256,128]{1,0:T(8,128)S(1)}, f32[256,128]{1,0:T(8,128)S(1)}, u32[]{:S(2)}, u32[]{:S(2)}) collective-permute-start(f32[256,128]{1,0:T(8,128)S(1)} %get-tuple-element.40), channel_id=1, source_target_pairs={{0,2},{2,4},{4,6},{6,0},{1,3},{3,5},{5,7},{7,1},{8,10},{10,12},{12... | collective-permute-start | bytes 393224 | tf_op jit(solution)/shard_map/ppermute | solution.py:26
  66.9 31.0 %copy-start.11 = (f32[2,32,128]{2,1,0:T(8,128)S(1)}, f32[2,32,128]{2,1,0:T(8,128)}, u32[]{:S(2)}) copy-start(f32[2,32,128]{2,1,0:T(8,128)} %param.7) | copy-start | bytes 98308
  66.9 12.0 %collective-permute-start.4 = (f32[384,128]{1,0:T(8,128)S(1)}, f32[384,128]{1,0:T(8,128)S(1)}, u32[]{:S(2)}, u32[]{:S(2)}) collective-permute-start(f32[384,128]{1,0:T(8,128)S(1)} %get-tuple-element.31), channel_id=1, source_target_pairs={{0,64},{64,128},{128,192},{192,0},{1,65},{65,129},{129,193},{193,1... | collective-permute-start | bytes 589832 | tf_op jit(solution)/shard_map/ppermute | solution.py:26
  67.6 11.3 %collective-permute-start.5 = (f32[384,128]{1,0:T(8,128)S(1)}, f32[384,128]{1,0:T(8,128)S(1)}, u32[]{:S(2)}, u32[]{:S(2)}) collective-permute-start(f32[384,128]{1,0:T(8,128)S(1)} %get-tuple-element.32), channel_id=1, source_target_pairs={{0,128},{64,192},{128,0},{192,64},{1,129},{65,193},{129,1},{193,65... | collective-permute-start | bytes 589832 | tf_op jit(solution)/shard_map/ppermute | solution.py:26
  68.7 10.5 %collective-permute-start.6 = (f32[384,128]{1,0:T(8,128)S(1)}, f32[384,128]{1,0:T(8,128)S(1)}, u32[]{:S(2)}, u32[]{:S(2)}) collective-permute-start(f32[384,128]{1,0:T(8,128)S(1)} %get-tuple-element.33), channel_id=1, source_target_pairs={{0,192},{64,0},{128,64},{192,128},{1,193},{65,1},{129,65},{193,129... | collective-permute-start | bytes 589832 | tf_op jit(solution)/shard_map/ppermute | solution.py:26
  70.4 7.2 %collective-permute-start.16 = (f32[256,128]{1,0:T(8,128)S(1)}, f32[256,128]{1,0:T(8,128)S(1)}, u32[]{:S(2)}, u32[]{:S(2)}) collective-permute-start(f32[256,128]{1,0:T(8,128)S(1)} %get-tuple-element.41), channel_id=1, source_target_pairs={{0,4},{2,6},{4,0},{6,2},{1,5},{3,7},{5,1},{7,3},{8,12},{10,14},{12... | collective-permute-start | bytes 393224 | tf_op jit(solution)/shard_map/ppermute | solution.py:26
  72.2 6.7 %collective-permute-start.17 = (f32[256,128]{1,0:T(8,128)S(1)}, f32[256,128]{1,0:T(8,128)S(1)}, u32[]{:S(2)}, u32[]{:S(2)}) collective-permute-start(f32[256,128]{1,0:T(8,128)S(1)} %get-tuple-element.42), channel_id=1, source_target_pairs={{0,6},{2,0},{4,2},{6,4},{1,7},{3,1},{5,3},{7,5},{8,14},{10,8},{12,... | collective-permute-start | bytes 393224 | tf_op jit(solution)/shard_map/ppermute | solution.py:26
  79.9 17.9 %all-to-all-start.1 = ((f32[8,64,128]{2,1,0:T(8,128)}), f32[8,64,128]{2,1,0:T(8,128)S(1)}, u32[]{:S(2)}, u32[]{:S(2)}) async-start(f32[8,64,128]{2,1,0:T(8,128)} %shard_map.65), calls=%async_computation.1 | async-start | bytes 524288 | tf_op jit(solution)/shard_map/all_to_all | solution.py:280
  88.2 1.4 %collective-permute-start.7 = (f32[256,128]{1,0:T(8,128)S(1)}, f32[256,128]{1,0:T(8,128)S(1)}, u32[]{:S(2)}, u32[]{:S(2)}) collective-permute-start(f32[256,128]{1,0:T(8,128)S(1)} %shard_map.60.a), channel_id=1, source_target_pairs={{0,1},{1,0},{2,3},{3,2},{4,5},{5,4},{6,7},{7,6},{8,9},{9,8},{10,11... | collective-permute-start | bytes 393224 | tf_op jit(solution)/shard_map/ppermute | solution.py:26
  89.6 13.3 %collective-permute-start.8 = (f32[256,128]{1,0:T(8,128)S(1)}, f32[256,128]{1,0:T(8,128)S(1)}, u32[]{:S(2)}, u32[]{:S(2)}) collective-permute-start(f32[256,128]{1,0:T(8,128)S(1)} %shard_map.61.mix0), channel_id=1, source_target_pairs={{0,2},{2,4},{4,6},{6,0},{1,3},{3,5},{5,7},{7,1},{8,10},{10,12},{12... | collective-permute-start | bytes 393224 | tf_op jit(solution)/shard_map/ppermute | solution.py:26
  90.0 12.9 %collective-permute-start.9 = (f32[256,128]{1,0:T(8,128)S(1)}, f32[256,128]{1,0:T(8,128)S(1)}, u32[]{:S(2)}, u32[]{:S(2)}) collective-permute-start(f32[256,128]{1,0:T(8,128)S(1)} %shard_map.61.mix0), channel_id=1, source_target_pairs={{0,4},{2,6},{4,0},{6,2},{1,5},{3,7},{5,1},{7,3},{8,12},{10,14},{12... | collective-permute-start | bytes 393224 | tf_op jit(solution)/shard_map/ppermute | solution.py:26
  92.5 10.5 %collective-permute-start.10 = (f32[256,128]{1,0:T(8,128)S(1)}, f32[256,128]{1,0:T(8,128)S(1)}, u32[]{:S(2)}, u32[]{:S(2)}) collective-permute-start(f32[256,128]{1,0:T(8,128)S(1)} %shard_map.61.mix0), channel_id=1, source_target_pairs={{0,6},{2,0},{4,2},{6,4},{1,7},{3,1},{5,3},{7,5},{8,14},{10,8},{12,... | collective-permute-start | bytes 393224 | tf_op jit(solution)/shard_map/ppermute | solution.py:26
  97.9 5.5 %collective-permute-start.18 = (f32[64,128]{1,0:T(8,128)S(1)}, f32[64,128]{1,0:T(8,128)S(1)}, u32[]{:S(2)}, u32[]{:S(2)}) collective-permute-start(f32[64,128]{1,0:T(8,128)S(1)} %bitcast_subtract_fusion.rest0), channel_id=1, source_target_pairs={{0,64},{64,128},{128,192},{192,0},{1,65},{65,129},{129,193},{193,1... | collective-permute-start | bytes 98312 | tf_op jit(solution)/shard_map/ppermute | solution.py:26
  99.2 6.0 %collective-permute-start.19 = (f32[64,128]{1,0:T(8,128)S(1)}, f32[64,128]{1,0:T(8,128)S(1)}, u32[]{:S(2)}, u32[]{:S(2)}) collective-permute-start(f32[64,128]{1,0:T(8,128)S(1)} %bitcast_subtract_fusion.rest0), channel_id=1, source_target_pairs={{0,128},{64,192},{128,0},{192,64},{1,129},{65,193},{129,1},{193,65... | collective-permute-start | bytes 98312 | tf_op jit(solution)/shard_map/ppermute | solution.py:26
  103.0 3.9 %collective-permute-start.20 = (f32[64,128]{1,0:T(8,128)S(1)}, f32[64,128]{1,0:T(8,128)S(1)}, u32[]{:S(2)}, u32[]{:S(2)}) collective-permute-start(f32[64,128]{1,0:T(8,128)S(1)} %bitcast_subtract_fusion.rest0), channel_id=1, source_target_pairs={{0,192},{64,0},{128,64},{192,128},{1,193},{65,1},{129,65},{193,129... | collective-permute-start | bytes 98312 | tf_op jit(solution)/shard_map/ppermute | solution.py:26

commit v5 on v4

--- a/solution.py
+++ b/solution.py
@@ -95,13 +95,16 @@
                         far_rows.at[panel, at, :], rows.at[panel, at, :], sems.at[panel * ny + jy]
                     )
                 )
-        for load in first_loads + loads:
+        for load in first_loads + loads[:ny]:
             load.start()
         for load in first_loads:
             load.wait()
         split_columns(place, cols, right, nx)
         for jy in range(ny):
             loads[jy].wait()
+            if jy == 0:
+                for load in loads[ny:]:
+                    load.start()
             value = multiply(rows[0, rows_at(place, jy, ny, size), :], left, right)
             for jx in range(nx):
                 out[jx, jy * size : (jy + 1) * size, :] = value[:, jx * 128 : (jx + 1) * 128]
@@ -158,17 +161,19 @@
     )(*args)
 
 
-def pack_kernel(place, inverses, across, out):
+def pack_kernel(place, inverses, across, out, late):
     at = pl.multiple_of(place[0] * 256 + place[2] * 128, 128)
     strip_of_coupling = across[:, pl.ds(at, 128)]
     strip_of_second = inverses[1, :, pl.ds(at, 128)]
-    nz = out.shape[0]
-    for z in range(nz):
+    for z in range(out.shape[0]):
         out[z, :, 0:128] = strip_of_coupling
         out[z, :, 128:256] = strip_of_second
+        slabs = []
         for panel in range(2):
             pieces = [inverses[panel, :, y * 256 + z * 32 : y * 256 + z * 32 + 32] for y in range(4)]
-            out[z, :, 256 + panel * 128 : 384 + panel * 128] = jnp.concatenate(pieces, axis=1)
+            slabs.append(jnp.concatenate(pieces, axis=1))
+        out[z, :, 256:384] = slabs[0]
+        late[z] = slabs[1]
 
 
 def couple_kernel(tiles, out):
@@ -211,26 +216,36 @@
     )(*parts, rider)
 
 
-def interleave_kernel(a0, a1, a2, a3, b0, b1, b2, b3, out):
+def interleave_kernel(a0, a1, a2, a3, b0, b1, b2, b3, late, out):
     size = a0.shape[0]
     low = (a0[...] + a1[0:size, :]) + (a2[0:size, :] + a3[0:size, :])
     high = (b0[...] + b1[...]) + (b2[...] + b3[...])
     for z in range(out.shape[0]):
         out[z, 0:32, :] = low[z * 32 : (z + 1) * 32, :]
         out[z, 32:64, :] = high[z * 32 : (z + 1) * 32, :]
-
-
-def apply_kernel(place, tiles, mix0, mix1, mix2, mix3, rest0, rest1, rest2, rest3, out, first, second):
+        out[z, 64:96, :] = late[z]
+
+
+def rest_kernel(got, right_side, out):
+    total = [got[z, 0:64, :] for z in range(got.shape[0])]
+    while len(total) > 1:
+        total = [a + b for a, b in zip(total[::2], total[1::2])]
+    out[...] = right_side[...] - total[0]
+
+
+def apply_kernel(place, tiles, got, mix0, mix1, mix2, mix3, rest0, rest1, rest2, rest3, out, first, second):
     ny = 4
+    nz = out.shape[0]
     for step, rest in enumerate((rest0, rest1, rest2, rest3)):
         at = pl.multiple_of(lax.rem(place[1] + ny - step, ny) * 32, 32)
         first[pl.ds(at, 32), :] = rest[0:32, :]
         second[pl.ds(at, 32), :] = rest[32:64, :]
     mix = (mix0[...] + mix1[...]) + (mix2[...] + mix3[...])
+    slab = got[:, 64:96, :].reshape(nz * 32, 128)
     low = jnp.dot(tiles[:, 256:384], first[...], precision=EXACT, preferred_element_type=F32)
-    high = jnp.dot(tiles[:, 384:512], second[...], precision=EXACT, preferred_element_type=F32)
+    high = jnp.dot(slab, second[...], precision=EXACT, preferred_element_type=F32)
     high = high - jnp.dot(mix, first[...], precision=EXACT, preferred_element_type=F32)
-    for z in range(out.shape[0]):
+    for z in range(nz):
         out[z, 0:32, :] = low[z * 32 : (z + 1) * 32, :]
         out[z, 32:64, :] = high[z * 32 : (z + 1) * 32, :]
 
@@ -250,13 +265,16 @@
     blocks1 = products(own, 1, panel_rows, solved, from_partner1, False, nx, ny)
     got1 = [blocks1[0]] + [shift(blocks1[j], "y", j, ny) for j in range(1, ny)]
 
-    packed = pl.pallas_call(
+    packed, late = pl.pallas_call(
         pack_kernel,
-        out_shape=jax.ShapeDtypeStruct((nz, 32, 512), F32),
+        out_shape=(
+            jax.ShapeDtypeStruct((nz, 32, 384), F32),
+            jax.ShapeDtypeStruct((nz, 32, 128), F32),
+        ),
         in_specs=[SMEM, pl.BlockSpec(), pl.BlockSpec()],
         compiler_params=SMALL,
     )(own, inverses, coupling.T)
-    tiles = lax.all_to_all(packed, "z", 0, 0, tiled=True).reshape(nz * 32, 512)
+    tiles = lax.all_to_all(packed, "z", 0, 0, tiled=True).reshape(nz * 32, 384)
 
     coupled = pl.pallas_call(
         couple_kernel, out_shape=jax.ShapeDtypeStruct((128, 128), F32), compiler_params=SMALL
@@ -267,9 +285,9 @@
     again1 = [sums1[0]] + [shift(sums1[j], "x", j, nx) for j in range(1, nx)]
     by_z = pl.pallas_call(
         interleave_kernel,
-        out_shape=jax.ShapeDtypeStruct((nz, 64, 128), F32),
+        out_shape=jax.ShapeDtypeStruct((nz, 96, 128), F32),
         compiler_params=SMALL,
-    )(*again0, *again1)
+    )(*again0, *again1, late)
     chained = pl.pallas_call(
         chain_kernel, out_shape=jax.ShapeDtypeStruct((256, 128), F32), compiler_params=SMALL
     )(tiles, coupled, *again0[1:])
@@ -277,17 +295,19 @@
         sum_kernel, out_shape=jax.ShapeDtypeStruct((256, 128), F32), compiler_params=SMALL
     )(chained, shift(chained, "core", 1, nc))
     mixes = [mix] + [shift(mix, "x", j, nx) for j in range(1, nx)]
-    old = lax.all_to_all(by_z, "z", 0, 0, tiled=True).sum(axis=0)
-    rest = right_side.reshape(64, 128) - old
+    by_source = lax.all_to_all(by_z, "z", 0, 0, tiled=True)
+    rest = pl.pallas_call(
+        rest_kernel, out_shape=jax.ShapeDtypeStruct((64, 128), F32), compiler_params=SMALL
+    )(by_source, right_side.reshape(64, 128))
 
     rests = [rest] + [shift(rest, "y", j, ny) for j in range(1, ny)]
     solved_part = pl.pallas_call(
         apply_kernel,
         out_shape=jax.ShapeDtypeStruct((nz, 64, 128), F32),
-        in_specs=[SMEM] + [pl.BlockSpec()] * 9,
+        in_specs=[SMEM] + [pl.BlockSpec()] * 10,
         scratch_shapes=[pltpu.VMEM((128, 128), F32), pltpu.VMEM((128, 128), F32)],
         compiler_params=SMALL,
-    )(own, tiles, *mixes, *rests)
+    )(own, tiles, by_source, *mixes, *rests)
     panels = lax.all_to_all(solved_part, "z", 0, 0, tiled=True).sum(axis=0)
     return panels.reshape(right_side.shape)
 

time: 123 us -> 126 us (1.024)
  waiting for transfers between devices: 31.8 us -> 37 us
  Pallas kernels: 22.9 us -> 20.4 us
    all_to_all x2, waiting for transfers between devices: 3.45 us -> 6.92 us  [the longest x1 6.92 us: steps(): by_source = lax.all_to_all(by_z, 'z', 0, 0, tiled=True)]
    ppermute x21, waiting for transfers between devices: 28.3 us -> 30.1 us  [shift(): lax.ppermute(value, axis, [(i, (i + step) % size) for i in range(size)])]
    unnamed x24 -> x28, local copies, waits for them, and re-layouts: 6.53 us -> 7.11 us
  transfers between devices with their start and end apart: 23 -> 23, of which waited for: 12 -> 11; matrix products, arithmetic and copies ran while one was open for 0% -> 0% of each run, Pallas kernels for 10% -> 8%
where the time goes in v5:
time: 126 us; the launch traced here: 125 us
  starting transfers between devices  46.5 us (37%)
  waiting for transfers between devices  37 us (29%)
  Pallas kernels  20.4 us (16%)
  blocking collectives  13.2 us (10%)
  local copies, waits for them, and re-layouts  7.11 us (6%)
    ppermute x21, starting transfers between devices, shift(): lax.ppermute(value, axis, [(i, (i + step) % size) for i in range(size)])  31 us
    ppermute x21, waiting for transfers between devices, shift(): lax.ppermute(value, axis, [(i, (i + step) % size) for i in range(size)])  30.1 us
    all_to_all x1, blocking collectives, steps(): panels = lax.all_to_all(solved_part, 'z', 0, 0, tiled=True).sum(axis=0)  13.2 us
    pallas_call x3, Pallas kernels, products(): pl.pallas_call(kernel, out_shape=shapes, in_specs=[SMEM] + [pl.BlockSpec(...  9.83 us
    all_to_all x1, starting transfers between devices, steps(): tiles = lax.all_to_all(packed, 'z', 0, 0, tiled=True).reshape(nz * 32, 384)  8.49 us
    unnamed x28, local copies, waits for them, and re-layouts  7.11 us
    all_to_all x1, starting transfers between devices, steps(): by_source = lax.all_to_all(by_z, 'z', 0, 0, tiled=True)  6.93 us
    all_to_all x1, waiting for transfers between devices, steps(): by_source = lax.all_to_all(by_z, 'z', 0, 0, tiled=True)  6.92 us
  transfers between devices with their start and end apart: 23, of which 11 were waited for; matrix products, arithmetic and copies ran while one was open for 0% of the time, Pallas kernels for 8%

profile of v5, /device:TPU:2, one launch (start us, length us, event | category | flops | bytes accessed | tf_op | source)
XLA Modules:
  0.0 125.1 jit_solution(10345194240419257421)
XLA Ops:
  0.0 0.1 pad_add_fusion.2.place
  0.1 5.7 %shard_map.56 = (f32[4,1024,128]{2,1,0:T(8,128)}, f32[2,1024,384]{2,1,0:T(8,128)S(1)}, f32[384,1024]{1,0:T(8,128)S(1)}) custom-call(s32[3]{0:T(128)S(1)} %pad_add_fusion.2.place, f32[2,1024,384]{2,1,0:T(8,128)} %far_rows.1, f32[384,1024]{1,0:T(8,128)} %far_cols.1), custom_call_target="tpu_custom_call" | custom-call | flops 1207959552 | bytes 6291456 | tf_op jit(solution)/shard_map/pallas_call | solution.py:129
  5.8 2.3 %shard_map.60 = f32[4,1024,128]{2,1,0:T(8,128)S(1)} custom-call(s32[3]{0:T(128)S(1)} %pad_add_fusion.2.place, f32[2,1024,384]{2,1,0:T(8,128)S(1)} %get-tuple-element.27.rows, f32[384,1024]{1,0:T(8,128)S(1)} %get-tuple-element.28.cols), custom_call_target="tpu_custom_call" | custom-call | flops 1207959552 | bytes 6291456 | tf_op jit(solution)/shard_map/pallas_call | solution.py:154
  8.1 0.1 collective-permute-start.7
  8.2 0.5 collective-permute-start
  8.7 0.1 pad_add_fusion.place
  8.8 3.6 %collective-permute-done.7.refs_0_ = f32[4,1024,128]{2,1,0:T(8,128)S(1)} collective-permute-done((f32[4,1024,128]{2,1,0:T(8,128)S(1)}, f32[4,1024,128]{2,1,0:T(8,128)S(1)}, u32[]{:S(2)}, u32[]{:S(2)}) %collective-permute-start.7) | collective-permute-done | bytes 2097184 | tf_op jit(solution)/shard_map/ppermute | solution.py:26
  12.4 2.9 %shard_map.61 = (f32[1024,128]{1,0:T(8,128)S(1)}, f32[1024,128]{1,0:T(8,128)}, f32[1024,128]{1,0:T(8,128)S(1)}, f32[1024,128]{1,0:T(8,128)S(1)}) custom-call(s32[3]{0:T(128)S(1)} %pad_add_fusion.place, f32[2,1024,384]{2,1,0:T(8,128)S(1)} %get-tuple-element.27.rows, f32[384,1024]{1,0:T(8,128)S(1)} %get-tuple-element.28.cols, ...), custom_call_target="tpu_custom_call" | custom-call | flops 1207959552 | bytes 6291456 | tf_op jit(solution)/shard_map/pallas_call | solution.py:154
  15.3 0.8 copy-done.2
  16.1 0.8 copy-done.12
  16.9 0.8 copy-done.13
  17.8 1.6 %collective-permute-start.8 = (f32[1024,128]{1,0:T(8,128)}, f32[1024,128]{1,0:T(8,128)}, u32[]{:S(2)}, u32[]{:S(2)}) collective-permute-start(f32[1024,128]{1,0:T(8,128)} %get-tuple-element.39), channel_id=1, source_target_pairs={{0,64},{64,128},{128,192},{192,0},{1,65},{65,129},{129,193},{193,1... | collective-permute-start | bytes 1572872 | tf_op jit(solution)/shard_map/ppermute | solution.py:26
  19.4 0.8 shard_map.55
  20.2 0.7 copy-done.6
  20.9 0.7 copy-done.8
  21.6 8.5 %all-to-all-start = ((f32[8,32,384]{2,1,0:T(8,128)}), f32[8,32,384]{2,1,0:T(8,128)S(1)}, u32[]{:S(2)}, u32[]{:S(2)}) async-start(f32[8,32,384]{2,1,0:T(8,128)} %copy-done.6), calls=%async_computation | async-start | bytes 786432 | tf_op jit(solution)/shard_map/all_to_all | solution.py:277
  30.1 2.9 %collective-permute-start.9 = (f32[1024,128]{1,0:T(8,128)}, f32[1024,128]{1,0:T(8,128)}, u32[]{:S(2)}, u32[]{:S(2)}) collective-permute-start(f32[1024,128]{1,0:T(8,128)} %copy-done.13), channel_id=1, source_target_pairs={{0,128},{64,192},{128,0},{192,64},{1,129},{65,193},{129,1},{193,65... | collective-permute-start | bytes 1572872 | tf_op jit(solution)/shard_map/ppermute | solution.py:26
  32.9 1.3 %collective-permute-start.10 = (f32[1024,128]{1,0:T(8,128)}, f32[1024,128]{1,0:T(8,128)}, u32[]{:S(2)}, u32[]{:S(2)}) collective-permute-start(f32[1024,128]{1,0:T(8,128)} %copy-done.12), channel_id=1, source_target_pairs={{0,192},{64,0},{128,64},{192,128},{1,193},{65,1},{129,65},{193,129... | collective-permute-start | bytes 1572872 | tf_op jit(solution)/shard_map/ppermute | solution.py:26
  34.3 1.4 %copy-done.1 = f32[384,1024]{1,0:T(8,128)S(1)} copy-done((f32[384,1024]{1,0:T(8,128)S(1)}, f32[384,1024]{1,0:T(8,128)}, u32[]{:S(2)}) %copy-start.1) | copy-done | bytes 1572888
  35.7 4.6 %shard_map.57 = (f32[1024,128]{1,0:T(8,128)S(1)}, f32[1024,128]{1,0:T(8,128)}, f32[1024,128]{1,0:T(8,128)}, f32[1024,128]{1,0:T(8,128)}) custom-call(s32[3]{0:T(128)S(1)} %pad_add_fusion.place, f32[2,1024,384]{2,1,0:T(8,128)S(1)} %get-tuple-element.27.rows, f32[384,1024]{1,0:T(8,128)S(1)} %copy-done.1, f32[4,1024,128]{2,1,0:T(8,128)} %collective-permute-done.refs_0_), custom_call_target="tpu_custom_call" | custom-call | flops 1207959552 | bytes 6291456 | tf_op jit(solution)/shard_map/pallas_call | solution.py:154
  40.3 0.8 copy-done.4
  41.0 1.5 %collective-permute-start.1 = (f32[1024,128]{1,0:T(8,128)}, f32[1024,128]{1,0:T(8,128)S(1)}, u32[]{:S(2)}, u32[]{:S(2)}) collective-permute-start(f32[1024,128]{1,0:T(8,128)} %get-tuple-element.31), channel_id=1, source_target_pairs={{0,2},{2,4},{4,6},{6,0},{1,3},{3,5},{5,7},{7,1},{8,10},{10,12},{12... | collective-permute-start | bytes 1572872 | tf_op jit(solution)/shard_map/ppermute | solution.py:26
  42.6 1.1 collective-permute-start.2
  43.7 0.0 collective-permute-done.8.b
  43.7 3.1 %collective-permute-start.3 = (f32[1024,128]{1,0:T(8,128)}, f32[1024,128]{1,0:T(8,128)S(1)}, u32[]{:S(2)}, u32[]{:S(2)}) collective-permute-start(f32[1024,128]{1,0:T(8,128)} %get-tuple-element.33), channel_id=1, source_target_pairs={{0,6},{2,0},{4,2},{6,4},{1,7},{3,1},{5,3},{7,5},{8,14},{10,8},{12,... | collective-permute-start | bytes 1572872 | tf_op jit(solution)/shard_map/ppermute | solution.py:26
  46.7 0.3 shard_map.58.rider.part0
  47.0 0.0 collective-permute-done.9.c
  47.0 8.5 %collective-permute-done.10.d = f32[1024,128]{1,0:T(8,128)} collective-permute-done((f32[1024,128]{1,0:T(8,128)}, f32[1024,128]{1,0:T(8,128)}, u32[]{:S(2)}, u32[]{:S(2)}) %collective-permute-start.10) | collective-permute-done | bytes 524320 | tf_op jit(solution)/shard_map/ppermute | solution.py:26
  55.6 1.0 copy-done.3
  56.6 1.6 %shard_map.62 = (f32[256,128]{1,0:T(8,128)S(1)}, f32[256,128]{1,0:T(8,128)S(1)}, f32[256,128]{1,0:T(8,128)S(1)}, f32[256,128]{1,0:T(8,128)S(1)}) custom-call(f32[1024,128]{1,0:T(8,128)S(1)} %copy-done.3, f32[1024,128]{1,0:T(8,128)} %collective-permute-done.8.b, f32[1024,128]{1,0:T(8,128)} %collective-permute-done.9.c, ...), custom_call_target="tpu_custom_call" | custom-call | tf_op jit(solution)/shard_map/pallas_call | solution.py:211
  58.2 1.8 %collective-permute-start.11 = (f32[256,128]{1,0:T(8,128)S(1)}, f32[256,128]{1,0:T(8,128)S(1)}, u32[]{:S(2)}, u32[]{:S(2)}) collective-permute-start(f32[256,128]{1,0:T(8,128)S(1)} %get-tuple-element.43), channel_id=1, source_target_pairs={{0,2},{2,4},{4,6},{6,0},{1,3},{3,5},{5,7},{7,1},{8,10},{10,12},{12... | collective-permute-start | bytes 393224 | tf_op jit(solution)/shard_map/ppermute | solution.py:26
  60.0 0.0 collective-permute-done.2.c
  60.0 7.4 %collective-permute-done.3.d = f32[1024,128]{1,0:T(8,128)S(1)} collective-permute-done((f32[1024,128]{1,0:T(8,128)}, f32[1024,128]{1,0:T(8,128)S(1)}, u32[]{:S(2)}, u32[]{:S(2)}) %collective-permute-start.3) | collective-permute-done | bytes 524320 | tf_op jit(solution)/shard_map/ppermute | solution.py:26
  67.3 0.1 shard_map.59
  67.5 0.0 copy-start.11
  67.5 0.8 collective-permute-start.4
  68.2 1.1 collective-permute-start.5
  69.3 1.7 %collective-permute-start.6 = (f32[384,128]{1,0:T(8,128)S(1)}, f32[384,128]{1,0:T(8,128)S(1)}, u32[]{:S(2)}, u32[]{:S(2)}) collective-permute-start(f32[384,128]{1,0:T(8,128)S(1)} %get-tuple-element.37), channel_id=1, source_target_pairs={{0,192},{64,0},{128,64},{192,128},{1,193},{65,1},{129,65},{193,129... | collective-permute-start | bytes 589832 | tf_op jit(solution)/shard_map/ppermute | solution.py:26
  71.0 1.8 %collective-permute-start.12 = (f32[256,128]{1,0:T(8,128)S(1)}, f32[256,128]{1,0:T(8,128)S(1)}, u32[]{:S(2)}, u32[]{:S(2)}) collective-permute-start(f32[256,128]{1,0:T(8,128)S(1)} %get-tuple-element.44), channel_id=1, source_target_pairs={{0,4},{2,6},{4,0},{6,2},{1,5},{3,7},{5,1},{7,3},{8,12},{10,14},{12... | collective-permute-start | bytes 393224 | tf_op jit(solution)/shard_map/ppermute | solution.py:26
  72.8 0.0 collective-permute-done.11.b1
  72.8 1.6 %collective-permute-start.13 = (f32[256,128]{1,0:T(8,128)S(1)}, f32[256,128]{1,0:T(8,128)S(1)}, u32[]{:S(2)}, u32[]{:S(2)}) collective-permute-start(f32[256,128]{1,0:T(8,128)S(1)} %get-tuple-element.45), channel_id=1, source_target_pairs={{0,6},{2,0},{4,2},{6,4},{1,7},{3,1},{5,3},{7,5},{8,14},{10,8},{12,... | collective-permute-start | bytes 393224 | tf_op jit(solution)/shard_map/ppermute | solution.py:26
  74.4 3.8 %collective-permute-done.12.b2 = f32[256,128]{1,0:T(8,128)S(1)} collective-permute-done((f32[256,128]{1,0:T(8,128)S(1)}, f32[256,128]{1,0:T(8,128)S(1)}, u32[]{:S(2)}, u32[]{:S(2)}) %collective-permute-start.12) | collective-permute-done | bytes 131104 | tf_op jit(solution)/shard_map/ppermute | solution.py:26
  78.2 1.3 %collective-permute-done.13.b3 = f32[256,128]{1,0:T(8,128)S(1)} collective-permute-done((f32[256,128]{1,0:T(8,128)S(1)}, f32[256,128]{1,0:T(8,128)S(1)}, u32[]{:S(2)}, u32[]{:S(2)}) %collective-permute-start.13) | collective-permute-done | bytes 131104 | tf_op jit(solution)/shard_map/ppermute | solution.py:26
  79.5 0.0 collective-permute-done.4.a1.got1
  79.5 0.0 collective-permute-done.5.a2.got2
  79.5 0.2 collective-permute-done.6.a3.got3
  79.7 0.8 shard_map.63
  80.5 6.9 %all-to-all-start.1 = ((f32[8,96,128]{2,1,0:T(8,128)}), f32[8,96,128]{2,1,0:T(8,128)S(1)}, u32[]{:S(2)}, u32[]{:S(2)}) async-start(f32[8,96,128]{2,1,0:T(8,128)} %shard_map.63), calls=%async_computation.1 | async-start | bytes 786432 | tf_op jit(solution)/shard_map/all_to_all | solution.py:298
  87.5 0.3 shard_map.64.a
  87.7 0.1 collective-permute-start.14
  87.8 1.3 %collective-permute-done.14.b = f32[256,128]{1,0:T(8,128)S(1)} collective-permute-done((f32[256,128]{1,0:T(8,128)S(1)}, f32[256,128]{1,0:T(8,128)S(1)}, u32[]{:S(2)}, u32[]{:S(2)}) %collective-permute-start.14) | collective-permute-done | bytes 131104 | tf_op jit(solution)/shard_map/ppermute | solution.py:26
  89.2 0.4 collective-permute-start.15
  89.6 2.5 %collective-permute-start.16 = (f32[256,128]{1,0:T(8,128)S(1)}, f32[256,128]{1,0:T(8,128)S(1)}, u32[]{:S(2)}, u32[]{:S(2)}) collective-permute-start(f32[256,128]{1,0:T(8,128)S(1)} %shard_map.65.mix0), channel_id=1, source_target_pairs={{0,4},{2,6},{4,0},{6,2},{1,5},{3,7},{5,1},{7,3},{8,12},{10,14},{12... | collective-permute-start | bytes 393224 | tf_op jit(solution)/shard_map/ppermute | solution.py:26
  92.1 2.3 %collective-permute-start.17 = (f32[256,128]{1,0:T(8,128)S(1)}, f32[256,128]{1,0:T(8,128)S(1)}, u32[]{:S(2)}, u32[]{:S(2)}) collective-permute-start(f32[256,128]{1,0:T(8,128)S(1)} %shard_map.65.mix0), channel_id=1, source_target_pairs={{0,6},{2,0},{4,2},{6,4},{1,7},{3,1},{5,3},{7,5},{8,14},{10,8},{12,... | collective-permute-start | bytes 393224 | tf_op jit(solution)/shard_map/ppermute | solution.py:26
  94.4 6.9 %all-to-all-done.1.got = f32[8,96,128]{2,1,0:T(8,128)S(1)} async-done(((f32[8,96,128]{2,1,0:T(8,128)}), f32[8,96,128]{2,1,0:T(8,128)S(1)}, u32[]{:S(2)}, u32[]{:S(2)}) %all-to-all-start.1) | async-done | bytes 393248 | tf_op jit(solution)/shard_map/all_to_all | solution.py:298
  101.3 1.2 collective-permute-start.18
  102.6 3.8 %collective-permute-start.19 = (f32[64,128]{1,0:T(8,128)S(1)}, f32[64,128]{1,0:T(8,128)S(1)}, u32[]{:S(2)}, u32[]{:S(2)}) collective-permute-start(f32[64,128]{1,0:T(8,128)S(1)} %shard_map.66.rest0), channel_id=1, source_target_pairs={{0,128},{64,192},{128,0},{192,64},{1,129},{65,193},{129,1},{193,65... | collective-permute-start | bytes 98312 | tf_op jit(solution)/shard_map/ppermute | solution.py:26
  106.4 0.0 collective-permute-done.16.mix2
  106.4 0.4 collective-permute-done.18.rest1
  106.8 1.8 %collective-permute-done.19.rest2 = f32[64,128]{1,0:T(8,128)S(1)} collective-permute-done((f32[64,128]{1,0:T(8,128)S(1)}, f32[64,128]{1,0:T(8,128)S(1)}, u32[]{:S(2)}, u32[]{:S(2)}) %collective-permute-start.19) | collective-permute-done | bytes 32800 | tf_op jit(solution)/shard_map/ppermute | solution.py:26
  108.6 1.7 %collective-permute-done.20.rest3 = f32[64,128]{1,0:T(8,128)S(1)} collective-permute-done((f32[64,128]{1,0:T(8,128)S(1)}, f32[64,128]{1,0:T(8,128)S(1)}, u32[]{:S(2)}, u32[]{:S(2)}) %collective-permute-start.20) | collective-permute-done | bytes 32800 | tf_op jit(solution)/shard_map/ppermute | solution.py:26
  110.3 1.0 shard_map.67
  111.3 13.2 %all_to_all.15 = f32[8,64,128]{2,1,0:T(8,128)S(1)} all-to-all(f32[8,64,128]{2,1,0:T(8,128)S(1)} %shard_map.67), channel_id=1, replica_groups=mesh['y'=4,'z'=8,'x'=4,'core'=2] {'z'}, dimensions={0} | all-to-all | bytes 524288 | tf_op jit(solution)/shard_map/all_to_all | solution.py:311
  124.5 0.6 reduce_sum.9
  (27 shorter events, 0.1 us)
Async XLA Ops:
  5.8 6.6 %copy-start = (f32[384,1024]{1,0:T(8,128)}, f32[384,1024]{1,0:T(8,128)S(1)}, u32[]{:S(2)}) copy-start(f32[384,1024]{1,0:T(8,128)S(1)} %get-tuple-element.28.cols) | copy-start | bytes 4718596
  8.1 4.2 %collective-permute-start.7 = (f32[4,1024,128]{2,1,0:T(8,128)S(1)}, f32[4,1024,128]{2,1,0:T(8,128)S(1)}, u32[]{:S(2)}, u32[]{:S(2)}) collective-permute-start(f32[4,1024,128]{2,1,0:T(8,128)S(1)} %shard_map.60), channel_id=1, source_target_pairs={{0,1},{1,0},{2,3},{3,2},{4,5},{5,4},{6,7},{7,6},{8,9},{9,8},{10,11... | collective-permute-start | bytes 6291464 | tf_op jit(solution)/shard_map/ppermute | solution.py:26
  8.2 26.1 %collective-permute-start = (f32[4,1024,128]{2,1,0:T(8,128)}, f32[4,1024,128]{2,1,0:T(8,128)}, u32[]{:S(2)}, u32[]{:S(2)}) collective-permute-start(f32[4,1024,128]{2,1,0:T(8,128)} %get-tuple-element.29), channel_id=1, source_target_pairs={{0,1},{1,0},{2,3},{3,2},{4,5},{5,4},{6,7},{7,6},{8,9},{9,8},{10,11... | collective-permute-start | bytes 6291464 | tf_op jit(solution)/shard_map/ppermute | solution.py:26
  8.8 10.6 %copy-start.7 = (f32[2,32,1024]{2,1,0:T(8,128)S(1)}, f32[2,32,1024]{2,1,0:T(8,128)}, u32[]{:S(2)}) copy-start(f32[2,32,1024]{2,1,0:T(8,128)} %inverses.1) | copy-start | bytes 786436
  8.8 10.6 %copy-start.10 = (f32[1024,32]{0,1:T(8,128)S(1)}, f32[1024,32]{0,1:T(8,128)}, u32[]{:S(2)}) copy-start(f32[1024,32]{0,1:T(8,128)} %param.8) | copy-start | bytes 393220
  15.3 0.8 copy-start.2
  16.1 0.8 copy-start.12
  16.9 0.8 copy-start.13
  17.8 25.9 %collective-permute-start.8 = (f32[1024,128]{1,0:T(8,128)}, f32[1024,128]{1,0:T(8,128)}, u32[]{:S(2)}, u32[]{:S(2)}) collective-permute-start(f32[1024,128]{1,0:T(8,128)} %get-tuple-element.39), channel_id=1, source_target_pairs={{0,64},{64,128},{128,192},{192,0},{1,65},{65,129},{129,193},{193,1... | collective-permute-start | bytes 1572872 | tf_op jit(solution)/shard_map/ppermute | solution.py:26
  20.2 0.7 copy-start.6
  20.9 0.7 copy-start.8
  21.6 25.1 %all-to-all-start = ((f32[8,32,384]{2,1,0:T(8,128)}), f32[8,32,384]{2,1,0:T(8,128)S(1)}, u32[]{:S(2)}, u32[]{:S(2)}) async-start(f32[8,32,384]{2,1,0:T(8,128)} %copy-done.6), calls=%async_computation | async-start | bytes 786432 | tf_op jit(solution)/shard_map/all_to_all | solution.py:277
  30.1 17.0 %collective-permute-start.9 = (f32[1024,128]{1,0:T(8,128)}, f32[1024,128]{1,0:T(8,128)}, u32[]{:S(2)}, u32[]{:S(2)}) collective-permute-start(f32[1024,128]{1,0:T(8,128)} %copy-done.13), channel_id=1, source_target_pairs={{0,128},{64,192},{128,0},{192,64},{1,129},{65,193},{129,1},{193,65... | collective-permute-start | bytes 1572872 | tf_op jit(solution)/shard_map/ppermute | solution.py:26
  32.9 22.6 %collective-permute-start.10 = (f32[1024,128]{1,0:T(8,128)}, f32[1024,128]{1,0:T(8,128)}, u32[]{:S(2)}, u32[]{:S(2)}) collective-permute-start(f32[1024,128]{1,0:T(8,128)} %copy-done.12), channel_id=1, source_target_pairs={{0,192},{64,0},{128,64},{192,128},{1,193},{65,1},{129,65},{193,129... | collective-permute-start | bytes 1572872 | tf_op jit(solution)/shard_map/ppermute | solution.py:26
  34.3 1.4 %copy-start.1 = (f32[384,1024]{1,0:T(8,128)S(1)}, f32[384,1024]{1,0:T(8,128)}, u32[]{:S(2)}) copy-start(f32[384,1024]{1,0:T(8,128)} %copy-done) | copy-start | bytes 4718596
  40.3 0.8 copy-start.4
  41.0 18.9 %collective-permute-start.1 = (f32[1024,128]{1,0:T(8,128)}, f32[1024,128]{1,0:T(8,128)S(1)}, u32[]{:S(2)}, u32[]{:S(2)}) collective-permute-start(f32[1024,128]{1,0:T(8,128)} %get-tuple-element.31), channel_id=1, source_target_pairs={{0,2},{2,4},{4,6},{6,0},{1,3},{3,5},{5,7},{7,1},{8,10},{10,12},{12... | collective-permute-start | bytes 1572872 | tf_op jit(solution)/shard_map/ppermute | solution.py:26
  42.6 17.4 %collective-permute-start.2 = (f32[1024,128]{1,0:T(8,128)}, f32[1024,128]{1,0:T(8,128)S(1)}, u32[]{:S(2)}, u32[]{:S(2)}) collective-permute-start(f32[1024,128]{1,0:T(8,128)} %get-tuple-element.32), channel_id=1, source_target_pairs={{0,4},{2,6},{4,0},{6,2},{1,5},{3,7},{5,1},{7,3},{8,12},{10,14},{12... | collective-permute-start | bytes 1572872 | tf_op jit(solution)/shard_map/ppermute | solution.py:26
  43.7 23.7 %collective-permute-start.3 = (f32[1024,128]{1,0:T(8,128)}, f32[1024,128]{1,0:T(8,128)S(1)}, u32[]{:S(2)}, u32[]{:S(2)}) collective-permute-start(f32[1024,128]{1,0:T(8,128)} %get-tuple-element.33), channel_id=1, source_target_pairs={{0,6},{2,0},{4,2},{6,4},{1,7},{3,1},{5,3},{7,5},{8,14},{10,8},{12,... | collective-permute-start | bytes 1572872 | tf_op jit(solution)/shard_map/ppermute | solution.py:26
  55.6 1.0 copy-start.3
  56.6 10.7 %copy-start.5 = (f32[1024,128]{1,0:T(8,128)S(1)}, f32[1024,128]{1,0:T(8,128)}, u32[]{:S(2)}) copy-start(f32[1024,128]{1,0:T(8,128)} %copy-done.4) | copy-start | bytes 1572868
  56.6 23.1 %copy-start.9 = (f32[8,32,128]{2,1,0:T(8,128)S(1)}, f32[8,32,128]{2,1,0:T(8,128)}, u32[]{:S(2)}) copy-start(f32[8,32,128]{2,1,0:T(8,128)} %copy-done.8) | copy-start | bytes 393220
  58.2 14.6 %collective-permute-start.11 = (f32[256,128]{1,0:T(8,128)S(1)}, f32[256,128]{1,0:T(8,128)S(1)}, u32[]{:S(2)}, u32[]{:S(2)}) collective-permute-start(f32[256,128]{1,0:T(8,128)S(1)} %get-tuple-element.43), channel_id=1, source_target_pairs={{0,2},{2,4},{4,6},{6,0},{1,3},{3,5},{5,7},{7,1},{8,10},{10,12},{12... | collective-permute-start | bytes 393224 | tf_op jit(solution)/shard_map/ppermute | solution.py:26
  67.5 33.8 %copy-start.11 = (f32[2,32,128]{2,1,0:T(8,128)S(1)}, f32[2,32,128]{2,1,0:T(8,128)}, u32[]{:S(2)}) copy-start(f32[2,32,128]{2,1,0:T(8,128)} %param.7) | copy-start | bytes 98308
  67.5 12.0 %collective-permute-start.4 = (f32[384,128]{1,0:T(8,128)S(1)}, f32[384,128]{1,0:T(8,128)S(1)}, u32[]{:S(2)}, u32[]{:S(2)}) collective-permute-start(f32[384,128]{1,0:T(8,128)S(1)} %get-tuple-element.35), channel_id=1, source_target_pairs={{0,64},{64,128},{128,192},{192,0},{1,65},{65,129},{129,193},{193,1... | collective-permute-start | bytes 589832 | tf_op jit(solution)/shard_map/ppermute | solution.py:26
  68.2 11.3 %collective-permute-start.5 = (f32[384,128]{1,0:T(8,128)S(1)}, f32[384,128]{1,0:T(8,128)S(1)}, u32[]{:S(2)}, u32[]{:S(2)}) collective-permute-start(f32[384,128]{1,0:T(8,128)S(1)} %get-tuple-element.36), channel_id=1, source_target_pairs={{0,128},{64,192},{128,0},{192,64},{1,129},{65,193},{129,1},{193,65... | collective-permute-start | bytes 589832 | tf_op jit(solution)/shard_map/ppermute | solution.py:26
  69.3 10.4 %collective-permute-start.6 = (f32[384,128]{1,0:T(8,128)S(1)}, f32[384,128]{1,0:T(8,128)S(1)}, u32[]{:S(2)}, u32[]{:S(2)}) collective-permute-start(f32[384,128]{1,0:T(8,128)S(1)} %get-tuple-element.37), channel_id=1, source_target_pairs={{0,192},{64,0},{128,64},{192,128},{1,193},{65,1},{129,65},{193,129... | collective-permute-start | bytes 589832 | tf_op jit(solution)/shard_map/ppermute | solution.py:26
  71.0 7.2 %collective-permute-start.12 = (f32[256,128]{1,0:T(8,128)S(1)}, f32[256,128]{1,0:T(8,128)S(1)}, u32[]{:S(2)}, u32[]{:S(2)}) collective-permute-start(f32[256,128]{1,0:T(8,128)S(1)} %get-tuple-element.44), channel_id=1, source_target_pairs={{0,4},{2,6},{4,0},{6,2},{1,5},{3,7},{5,1},{7,3},{8,12},{10,14},{12... | collective-permute-start | bytes 393224 | tf_op jit(solution)/shard_map/ppermute | solution.py:26
  72.8 6.7 %collective-permute-start.13 = (f32[256,128]{1,0:T(8,128)S(1)}, f32[256,128]{1,0:T(8,128)S(1)}, u32[]{:S(2)}, u32[]{:S(2)}) collective-permute-start(f32[256,128]{1,0:T(8,128)S(1)} %get-tuple-element.45), channel_id=1, source_target_pairs={{0,6},{2,0},{4,2},{6,4},{1,7},{3,1},{5,3},{7,5},{8,14},{10,8},{12,... | collective-permute-start | bytes 393224 | tf_op jit(solution)/shard_map/ppermute | solution.py:26
  80.5 20.7 %all-to-all-start.1 = ((f32[8,96,128]{2,1,0:T(8,128)}), f32[8,96,128]{2,1,0:T(8,128)S(1)}, u32[]{:S(2)}, u32[]{:S(2)}) async-start(f32[8,96,128]{2,1,0:T(8,128)} %shard_map.63), calls=%async_computation.1 | async-start | bytes 786432 | tf_op jit(solution)/shard_map/all_to_all | solution.py:298
  87.7 1.4 %collective-permute-start.14 = (f32[256,128]{1,0:T(8,128)S(1)}, f32[256,128]{1,0:T(8,128)S(1)}, u32[]{:S(2)}, u32[]{:S(2)}) collective-permute-start(f32[256,128]{1,0:T(8,128)S(1)} %shard_map.64.a), channel_id=1, source_target_pairs={{0,1},{1,0},{2,3},{3,2},{4,5},{5,4},{6,7},{7,6},{8,9},{9,8},{10,11... | collective-permute-start | bytes 393224 | tf_op jit(solution)/shard_map/ppermute | solution.py:26
  89.2 17.2 %collective-permute-start.15 = (f32[256,128]{1,0:T(8,128)S(1)}, f32[256,128]{1,0:T(8,128)S(1)}, u32[]{:S(2)}, u32[]{:S(2)}) collective-permute-start(f32[256,128]{1,0:T(8,128)S(1)} %shard_map.65.mix0), channel_id=1, source_target_pairs={{0,2},{2,4},{4,6},{6,0},{1,3},{3,5},{5,7},{7,1},{8,10},{10,12},{12... | collective-permute-start | bytes 393224 | tf_op jit(solution)/shard_map/ppermute | solution.py:26
  89.6 16.8 %collective-permute-start.16 = (f32[256,128]{1,0:T(8,128)S(1)}, f32[256,128]{1,0:T(8,128)S(1)}, u32[]{:S(2)}, u32[]{:S(2)}) collective-permute-start(f32[256,128]{1,0:T(8,128)S(1)} %shard_map.65.mix0), channel_id=1, source_target_pairs={{0,4},{2,6},{4,0},{6,2},{1,5},{3,7},{5,1},{7,3},{8,12},{10,14},{12... | collective-permute-start | bytes 393224 | tf_op jit(solution)/shard_map/ppermute | solution.py:26
  92.1 14.3 %collective-permute-start.17 = (f32[256,128]{1,0:T(8,128)S(1)}, f32[256,128]{1,0:T(8,128)S(1)}, u32[]{:S(2)}, u32[]{:S(2)}) collective-permute-start(f32[256,128]{1,0:T(8,128)S(1)} %shard_map.65.mix0), channel_id=1, source_target_pairs={{0,6},{2,0},{4,2},{6,4},{1,7},{3,1},{5,3},{7,5},{8,14},{10,8},{12,... | collective-permute-start | bytes 393224 | tf_op jit(solution)/shard_map/ppermute | solution.py:26
  101.3 5.5 %collective-permute-start.18 = (f32[64,128]{1,0:T(8,128)S(1)}, f32[64,128]{1,0:T(8,128)S(1)}, u32[]{:S(2)}, u32[]{:S(2)}) collective-permute-start(f32[64,128]{1,0:T(8,128)S(1)} %shard_map.66.rest0), channel_id=1, source_target_pairs={{0,64},{64,128},{128,192},{192,0},{1,65},{65,129},{129,193},{193,1... | collective-permute-start | bytes 98312 | tf_op jit(solution)/shard_map/ppermute | solution.py:26
  102.6 6.1 %collective-permute-start.19 = (f32[64,128]{1,0:T(8,128)S(1)}, f32[64,128]{1,0:T(8,128)S(1)}, u32[]{:S(2)}, u32[]{:S(2)}) collective-permute-start(f32[64,128]{1,0:T(8,128)S(1)} %shard_map.66.rest0), channel_id=1, source_target_pairs={{0,128},{64,192},{128,0},{192,64},{1,129},{65,193},{129,1},{193,65... | collective-permute-start | bytes 98312 | tf_op jit(solution)/shard_map/ppermute | solution.py:26
  106.4 3.9 %collective-permute-start.20 = (f32[64,128]{1,0:T(8,128)S(1)}, f32[64,128]{1,0:T(8,128)S(1)}, u32[]{:S(2)}, u32[]{:S(2)}) collective-permute-start(f32[64,128]{1,0:T(8,128)S(1)} %shard_map.66.rest0), channel_id=1, source_target_pairs={{0,192},{64,0},{128,64},{192,128},{1,193},{65,1},{129,65},{193,129... | collective-permute-start | bytes 98312 | tf_op jit(solution)/shard_map/ppermute | solution.py:26

commit v6 on v3

--- a/solution.py
+++ b/solution.py
@@ -14,7 +14,6 @@
 SMEM = pl.BlockSpec(memory_space=pltpu.SMEM)
 FAR = pl.BlockSpec(memory_space=pltpu.HBM)
 PRODUCT = pltpu.CompilerParams(vmem_limit_bytes=16 << 20)
-ORDER = pl.BlockSpec(memory_space=pl.ANY)
 SMALL = pltpu.CompilerParams(vmem_limit_bytes=6 << 20)
 
 
@@ -79,23 +78,32 @@
 def first_kernel(nx, ny):
     def kernel(place, far_rows, far_cols, out, rows, cols, left, right, sems):
         size = left.shape[0]
-        load_cols = pltpu.make_async_copy(far_cols, cols, sems.at[0])
-        load_cols.start()
+        part = cols.shape[0] // ny
+        first_loads = []
+        for k in range(ny):
+            at = slice(k * part, (k + 1) * part)
+            first_loads.append(
+                pltpu.make_async_copy(far_cols.at[at, :], cols.at[at, :], sems.at[2 * ny + k])
+            )
         loads = []
         for panel in range(2):
             for jy in range(ny):
                 at = rows_at(place, jy, ny, size)
                 loads.append(
                     pltpu.make_async_copy(
-                        far_rows.at[panel, at, :], rows.at[panel, at, :], sems.at[1 + panel * ny + jy]
+                        far_rows.at[panel, at, :], rows.at[panel, at, :], sems.at[panel * ny + jy]
                     )
                 )
-        for load in loads:
+        for load in first_loads + loads[:ny]:
             load.start()
-        load_cols.wait()
+        for load in first_loads:
+            load.wait()
         split_columns(place, cols, right, nx)
         for jy in range(ny):
             loads[jy].wait()
+            if jy == 0:
+                for load in loads[ny:]:
+                    load.start()
             value = multiply(rows[0, rows_at(place, jy, ny, size), :], left, right)
             for jx in range(nx):
                 out[jx, jy * size : (jy + 1) * size, :] = value[:, jx * 128 : (jx + 1) * 128]
@@ -126,7 +134,7 @@
         ),
         in_specs=[SMEM, FAR, FAR],
         scratch_shapes=product_scratch(size, depth, nx, ny)
-        + [pltpu.SemaphoreType.DMA((1 + 2 * ny,))],
+        + [pltpu.SemaphoreType.DMA((3 * ny,))],
         compiler_params=PRODUCT,
         cost_estimate=product_cost(size, depth, nx),
     )(place, far(rows), far(cols))
@@ -184,21 +192,20 @@
     out[...] = a[...] + b[...]
 
 
-def gather_sums_kernel(a, b, c, d, after, *outs):
+def gather_sums_kernel(a, b, c, d, *outs):
     size = outs[0].shape[0]
     for j, out in enumerate(outs):
         span = slice(j * size, (j + 1) * size)
         out[...] = (a[span, :] + b[span, :]) + (c[span, :] + d[span, :])
 
 
-def gather_sums(parts, after, count):
+def gather_sums(parts, count):
     size = parts[0].shape[0] // count
     return pl.pallas_call(
         gather_sums_kernel,
         out_shape=[jax.ShapeDtypeStruct((size, 128), F32)] * count,
-        in_specs=[pl.BlockSpec()] * len(parts) + [ORDER],
         compiler_params=SMALL,
-    )(*parts, after)
+    )(*parts)
 
 
 def interleave_kernel(a0, a1, a2, a3, b0, b1, b2, b3, out):
@@ -259,9 +266,9 @@
     )(chained, shift(chained, "core", 1, nc))
     mixes = [mix] + [shift(mix, "x", j, nx) for j in range(1, nx)]
 
-    sums0 = gather_sums(got0, coupled, ny)
+    sums0 = gather_sums(got0, ny)
     again0 = [sums0[0]] + [shift(sums0[j], "y", j, ny) for j in range(1, ny)]
-    sums1 = gather_sums(got1, coupled, nx)
+    sums1 = gather_sums(got1, nx)
     again1 = [sums1[0]] + [shift(sums1[j], "x", j, nx) for j in range(1, nx)]
     by_z = pl.pallas_call(
         interleave_kernel,

time: 126 us -> 126 us (level)
  waiting for transfers between devices: 26.1 us -> 28.5 us
  local copies, waits for them, and re-layouts: 6.49 us -> 4.61 us
    ppermute x24, waiting for transfers between devices: 24 us -> 28.5 us  [shift(): lax.ppermute(value, axis, [(i, (i + step) % size) for i in range(size)])]
    all_to_all x1, waiting for transfers between devices: 2.05 us -> 0.01 us  [steps(): tiles = lax.all_to_all(packed, 'z', 0, 0, tiled=True).reshape(nz * 32, 512)]
    unnamed x24 -> x20, local copies, waits for them, and re-layouts: 6.49 us -> 4.61 us
where the time goes in v6:
time: 126 us; the launch traced here: 125 us
  starting transfers between devices  51.8 us (41%)
  waiting for transfers between devices  28.5 us (23%)
  Pallas kernels  21.9 us (17%)
  blocking collectives  17.5 us (14%)
  local copies, waits for them, and re-layouts  4.61 us (4%)
    ppermute x24, starting transfers between devices, shift(): lax.ppermute(value, axis, [(i, (i + step) % size) for i in range(size)])  36.4 us
    ppermute x24, waiting for transfers between devices, shift(): lax.ppermute(value, axis, [(i, (i + step) % size) for i in range(size)])  28.5 us
    all_to_all x1, blocking collectives, steps(): panels = lax.all_to_all(solved_part, 'z', 0, 0, tiled=True).sum(axis=0)  17.5 us
    pallas_call x3, Pallas kernels, products(): pl.pallas_call(kernel, out_shape=shapes, in_specs=[SMEM] + [pl.BlockSpec(...  10.4 us
    all_to_all x1, starting transfers between devices, steps(): tiles = lax.all_to_all(packed, 'z', 0, 0, tiled=True).reshape(nz * 32, 512)  8.46 us
    all_to_all x1, starting transfers between devices, steps(): old = lax.all_to_all(by_z, 'z', 0, 0, tiled=True).sum(axis=0)  7 us
    unnamed x20, local copies, waits for them, and re-layouts  4.61 us
    pallas_call x1, Pallas kernels, first_products(): pl.pallas_call(first_kernel(nx, ny), out_shape=(jax.ShapeDtypeStruct((nx,...  4.38 us
  transfers between devices with their start and end apart: 26, of which 14 were waited for; matrix products, arithmetic and copies ran while one was open for 0% of the time, Pallas kernels for 13%

profile of v6, /device:TPU:2, one launch (start us, length us, event | category | flops | bytes accessed | tf_op | source)
XLA Modules:
  0.0 125.2 jit_solution(6333938174881027885)
XLA Ops:
  0.0 0.1 pad_add_fusion.2.place
  0.1 4.4 %shard_map.59 = (f32[4,1024,128]{2,1,0:T(8,128)S(1)}, f32[2,1024,384]{2,1,0:T(8,128)S(1)}, f32[384,1024]{1,0:T(8,128)S(1)}) custom-call(s32[3]{0:T(128)S(1)} %pad_add_fusion.2.place, f32[2,1024,384]{2,1,0:T(8,128)} %far_rows.1, f32[384,1024]{1,0:T(8,128)} %far_cols.1), custom_call_target="tpu_custom_call" | custom-call | flops 1207959552 | bytes 6291456 | tf_op jit(solution)/shard_map/pallas_call | solution.py:128
  4.5 0.1 collective-permute-start.7
  4.6 3.7 %shard_map.62 = f32[4,1024,128]{2,1,0:T(8,128)} custom-call(s32[3]{0:T(128)S(1)} %pad_add_fusion.2.place, f32[2,1024,384]{2,1,0:T(8,128)S(1)} %get-tuple-element.24.rows, f32[384,1024]{1,0:T(8,128)S(1)} %get-tuple-element.25.cols), custom_call_target="tpu_custom_call" | custom-call | flops 1207959552 | bytes 6291456 | tf_op jit(solution)/shard_map/pallas_call | solution.py:153
  8.2 0.5 collective-permute-start.14
  8.8 0.1 pad_add_fusion.place
  8.8 0.0 collective-permute-done.7.refs_0_
  8.9 3.3 %shard_map.60 = (f32[1024,128]{1,0:T(8,128)S(1)}, f32[1024,128]{1,0:T(8,128)}, f32[1024,128]{1,0:T(8,128)S(1)}, f32[1024,128]{1,0:T(8,128)S(1)}) custom-call(s32[3]{0:T(128)S(1)} %pad_add_fusion.place, f32[2,1024,384]{2,1,0:T(8,128)S(1)} %get-tuple-element.24.rows, f32[384,1024]{1,0:T(8,128)S(1)} %get-tuple-element.25.cols, ...), custom_call_target="tpu_custom_call" | custom-call | flops 1207959552 | bytes 6291456 | tf_op jit(solution)/shard_map/pallas_call | solution.py:153
  12.1 0.8 copy-done.3
  12.9 0.8 copy-done.7
  13.8 0.8 copy-done.8
  14.5 1.5 %collective-permute-start.8 = (f32[1024,128]{1,0:T(8,128)}, f32[1024,128]{1,0:T(8,128)}, u32[]{:S(2)}, u32[]{:S(2)}) collective-permute-start(f32[1024,128]{1,0:T(8,128)} %get-tuple-element.28), channel_id=1, source_target_pairs={{0,2},{2,4},{4,6},{6,0},{1,3},{3,5},{5,7},{7,1},{8,10},{10,12},{12... | collective-permute-start | bytes 1572872 | tf_op jit(solution)/shard_map/ppermute | solution.py:25
  16.0 0.8 shard_map.55
  16.8 0.8 copy-done.2
  17.6 8.5 %all-to-all-start = ((f32[8,32,512]{2,1,0:T(8,128)}), f32[8,32,512]{2,1,0:T(8,128)}, u32[]{:S(2)}, u32[]{:S(2)}) async-start(f32[8,32,512]{2,1,0:T(8,128)} %copy-done.2), calls=%async_computation | async-start | bytes 1048576 | tf_op jit(solution)/shard_map/all_to_all | solution.py:255
  26.1 1.1 collective-permute-start.9
  27.2 2.2 %collective-permute-start.10 = (f32[1024,128]{1,0:T(8,128)}, f32[1024,128]{1,0:T(8,128)S(1)}, u32[]{:S(2)}, u32[]{:S(2)}) collective-permute-start(f32[1024,128]{1,0:T(8,128)} %copy-done.7), channel_id=1, source_target_pairs={{0,6},{2,0},{4,2},{6,4},{1,7},{3,1},{5,3},{7,5},{8,14},{10,8},{12,... | collective-permute-start | bytes 1572872 | tf_op jit(solution)/shard_map/ppermute | solution.py:25
  29.3 0.0 collective-permute-done.14.refs_0_
  29.4 1.4 %copy-done.1 = f32[384,1024]{1,0:T(8,128)S(1)} copy-done((f32[384,1024]{1,0:T(8,128)S(1)}, f32[384,1024]{1,0:T(8,128)}, u32[]{:S(2)}) %copy-start.1) | copy-done | bytes 1572888
  30.8 3.5 %shard_map.63 = (f32[1024,128]{1,0:T(8,128)S(1)}, f32[1024,128]{1,0:T(8,128)S(1)}, f32[1024,128]{1,0:T(8,128)S(1)}, f32[1024,128]{1,0:T(8,128)S(1)}) custom-call(s32[3]{0:T(128)S(1)} %pad_add_fusion.place, f32[2,1024,384]{2,1,0:T(8,128)S(1)} %get-tuple-element.24.rows, f32[384,1024]{1,0:T(8,128)S(1)} %copy-done.1, ...), custom_call_target="tpu_custom_call" | custom-call | flops 1207959552 | bytes 6291456 | tf_op jit(solution)/shard_map/pallas_call | solution.py:153
  34.2 1.7 %collective-permute-start.15 = (f32[1024,128]{1,0:T(8,128)S(1)}, f32[1024,128]{1,0:T(8,128)S(1)}, u32[]{:S(2)}, u32[]{:S(2)}) collective-permute-start(f32[1024,128]{1,0:T(8,128)S(1)} %get-tuple-element.36), channel_id=1, source_target_pairs={{0,64},{64,128},{128,192},{192,0},{1,65},{65,129},{129,193},{193,1... | collective-permute-start | bytes 1572872 | tf_op jit(solution)/shard_map/ppermute | solution.py:25
  35.9 2.9 %collective-permute-start.16 = (f32[1024,128]{1,0:T(8,128)S(1)}, f32[1024,128]{1,0:T(8,128)S(1)}, u32[]{:S(2)}, u32[]{:S(2)}) collective-permute-start(f32[1024,128]{1,0:T(8,128)S(1)} %get-tuple-element.37), channel_id=1, source_target_pairs={{0,128},{64,192},{128,0},{192,64},{1,129},{65,193},{129,1},{193,65... | collective-permute-start | bytes 1572872 | tf_op jit(solution)/shard_map/ppermute | solution.py:25
  38.8 1.3 %collective-permute-start.17 = (f32[1024,128]{1,0:T(8,128)S(1)}, f32[1024,128]{1,0:T(8,128)S(1)}, u32[]{:S(2)}, u32[]{:S(2)}) collective-permute-start(f32[1024,128]{1,0:T(8,128)S(1)} %get-tuple-element.38), channel_id=1, source_target_pairs={{0,192},{64,0},{128,64},{192,128},{1,193},{65,1},{129,65},{193,129... | collective-permute-start | bytes 1572872 | tf_op jit(solution)/shard_map/ppermute | solution.py:25
  40.2 2.4 %collective-permute-done.9.c = f32[1024,128]{1,0:T(8,128)S(1)} collective-permute-done((f32[1024,128]{1,0:T(8,128)}, f32[1024,128]{1,0:T(8,128)S(1)}, u32[]{:S(2)}, u32[]{:S(2)}) %collective-permute-start.9) | collective-permute-done | bytes 524320 | tf_op jit(solution)/shard_map/ppermute | solution.py:25
  42.6 9.0 %collective-permute-done.10.d = f32[1024,128]{1,0:T(8,128)S(1)} collective-permute-done((f32[1024,128]{1,0:T(8,128)}, f32[1024,128]{1,0:T(8,128)S(1)}, u32[]{:S(2)}, u32[]{:S(2)}) %collective-permute-start.10) | collective-permute-done | bytes 524320 | tf_op jit(solution)/shard_map/ppermute | solution.py:25
  51.6 1.2 shard_map.61
  52.8 1.8 %collective-permute-start.11 = (f32[256,128]{1,0:T(8,128)S(1)}, f32[256,128]{1,0:T(8,128)S(1)}, u32[]{:S(2)}, u32[]{:S(2)}) collective-permute-start(f32[256,128]{1,0:T(8,128)S(1)} %get-tuple-element.32), channel_id=1, source_target_pairs={{0,64},{64,128},{128,192},{192,0},{1,65},{65,129},{129,193},{193,1... | collective-permute-start | bytes 393224 | tf_op jit(solution)/shard_map/ppermute | solution.py:25
  54.7 2.9 %collective-permute-start.12 = (f32[256,128]{1,0:T(8,128)S(1)}, f32[256,128]{1,0:T(8,128)S(1)}, u32[]{:S(2)}, u32[]{:S(2)}) collective-permute-start(f32[256,128]{1,0:T(8,128)S(1)} %get-tuple-element.33), channel_id=1, source_target_pairs={{0,128},{64,192},{128,0},{192,64},{1,129},{65,193},{129,1},{193,65... | collective-permute-start | bytes 393224 | tf_op jit(solution)/shard_map/ppermute | solution.py:25
  57.5 0.0 collective-permute-done.15.b
  57.6 1.3 %collective-permute-start.13 = (f32[256,128]{1,0:T(8,128)S(1)}, f32[256,128]{1,0:T(8,128)S(1)}, u32[]{:S(2)}, u32[]{:S(2)}) collective-permute-start(f32[256,128]{1,0:T(8,128)S(1)} %get-tuple-element.34), channel_id=1, source_target_pairs={{0,192},{64,0},{128,64},{192,128},{1,193},{65,1},{129,65},{193,129... | collective-permute-start | bytes 393224 | tf_op jit(solution)/shard_map/ppermute | solution.py:25
  58.9 4.0 %collective-permute-done.16.c = f32[1024,128]{1,0:T(8,128)S(1)} collective-permute-done((f32[1024,128]{1,0:T(8,128)S(1)}, f32[1024,128]{1,0:T(8,128)S(1)}, u32[]{:S(2)}, u32[]{:S(2)}) %collective-permute-start.16) | collective-permute-done | bytes 524320 | tf_op jit(solution)/shard_map/ppermute | solution.py:25
  62.9 0.0 collective-permute-done.17.d
  62.9 0.1 shard_map.64
  63.0 0.0 copy-start.9
  63.0 0.1 collective-permute-start.18
  63.1 3.5 %collective-permute-start.19 = (f32[256,128]{1,0:T(8,128)S(1)}, f32[256,128]{1,0:T(8,128)S(1)}, u32[]{:S(2)}, u32[]{:S(2)}) collective-permute-start(f32[256,128]{1,0:T(8,128)S(1)} %get-tuple-element.41), channel_id=1, source_target_pairs={{0,4},{2,6},{4,0},{6,2},{1,5},{3,7},{5,1},{7,3},{8,12},{10,14},{12... | collective-permute-start | bytes 393224 | tf_op jit(solution)/shard_map/ppermute | solution.py:25
  66.6 1.5 %collective-permute-done.18.b1 = f32[256,128]{1,0:T(8,128)S(1)} collective-permute-done((f32[256,128]{1,0:T(8,128)S(1)}, f32[256,128]{1,0:T(8,128)S(1)}, u32[]{:S(2)}, u32[]{:S(2)}) %collective-permute-start.18) | collective-permute-done | bytes 131104 | tf_op jit(solution)/shard_map/ppermute | solution.py:25
  68.0 1.7 %collective-permute-done.19.b2 = f32[256,128]{1,0:T(8,128)S(1)} collective-permute-done((f32[256,128]{1,0:T(8,128)S(1)}, f32[256,128]{1,0:T(8,128)S(1)}, u32[]{:S(2)}, u32[]{:S(2)}) %collective-permute-start.19) | collective-permute-done | bytes 131104 | tf_op jit(solution)/shard_map/ppermute | solution.py:25
  69.7 2.0 %collective-permute-done.20.b3 = f32[256,128]{1,0:T(8,128)S(1)} collective-permute-done((f32[256,128]{1,0:T(8,128)S(1)}, f32[256,128]{1,0:T(8,128)S(1)}, u32[]{:S(2)}, u32[]{:S(2)}) %collective-permute-start.20) | collective-permute-done | bytes 131104 | tf_op jit(solution)/shard_map/ppermute | solution.py:25
  71.7 0.8 shard_map.65
  72.5 7.0 %all-to-all-start.1 = ((f32[8,64,128]{2,1,0:T(8,128)}), f32[8,64,128]{2,1,0:T(8,128)S(1)}, u32[]{:S(2)}, u32[]{:S(2)}) async-start(f32[8,64,128]{2,1,0:T(8,128)} %shard_map.65), calls=%async_computation.1 | async-start | bytes 524288 | tf_op jit(solution)/shard_map/all_to_all | solution.py:278
  79.5 1.3 %shard_map.56.part0 = f32[128,128]{1,0:T(8,128)S(1)} custom-call(f32[256,512]{1,0:T(8,128)} %bitcast.4.tiles), custom_call_target="tpu_custom_call" | custom-call | tf_op jit(solution)/shard_map/pallas_call | solution.py:257
  80.8 1.1 collective-permute-start
  81.9 3.0 %collective-permute-start.1 = (f32[128,128]{1,0:T(8,128)S(1)}, f32[128,128]{1,0:T(8,128)S(1)}, u32[]{:S(2)}, u32[]{:S(2)}) collective-permute-start(f32[128,128]{1,0:T(8,128)S(1)} %shard_map.56.part0), channel_id=1, source_target_pairs={{0,128},{64,192},{128,0},{192,64},{1,129},{65,193},{129,1},{193,65... | collective-permute-start | bytes 196616 | tf_op jit(solution)/shard_map/ppermute | solution.py:25
  84.9 1.4 %collective-permute-start.2 = (f32[128,128]{1,0:T(8,128)S(1)}, f32[128,128]{1,0:T(8,128)S(1)}, u32[]{:S(2)}, u32[]{:S(2)}) collective-permute-start(f32[128,128]{1,0:T(8,128)S(1)} %shard_map.56.part0), channel_id=1, source_target_pairs={{0,192},{64,0},{128,64},{192,128},{1,193},{65,1},{129,65},{193,129... | collective-permute-start | bytes 196616 | tf_op jit(solution)/shard_map/ppermute | solution.py:25
  86.3 0.5 collective-permute-done.part1
  86.8 1.0 collective-permute-done.1.part2
  87.8 1.3 %collective-permute-done.2.part3 = f32[128,128]{1,0:T(8,128)S(1)} collective-permute-done((f32[128,128]{1,0:T(8,128)S(1)}, f32[128,128]{1,0:T(8,128)S(1)}, u32[]{:S(2)}, u32[]{:S(2)}) %collective-permute-start.2) | collective-permute-done | bytes 65568 | tf_op jit(solution)/shard_map/ppermute | solution.py:25
  89.1 1.3 %shard_map.57.a = f32[256,128]{1,0:T(8,128)S(1)} custom-call(f32[256,512]{1,0:T(8,128)} %bitcast.4.tiles, f32[128,128]{1,0:T(8,128)S(1)} %shard_map.56.part0, f32[128,128]{1,0:T(8,128)S(1)} %collective-permute-done.part1, f32[128,128]{1,0:T(8,128)S(1)} %collective-permute-done.1.part2, f32[128,128]{1,0:T(8,128)S(1)} %collective-permute-done.2.part3), custom_call_target="tpu_custom_call" | custom-call | tf_op jit(solution)/shard_map/pallas_call | solution.py:261
  90.4 0.1 collective-permute-start.3
  90.5 1.3 %collective-permute-done.3.b = f32[256,128]{1,0:T(8,128)S(1)} collective-permute-done((f32[256,128]{1,0:T(8,128)S(1)}, f32[256,128]{1,0:T(8,128)S(1)}, u32[]{:S(2)}, u32[]{:S(2)}) %collective-permute-start.3) | collective-permute-done | bytes 131104 | tf_op jit(solution)/shard_map/ppermute | solution.py:25
  91.9 0.6 collective-permute-start.4
  92.5 3.2 %collective-permute-start.5 = (f32[256,128]{1,0:T(8,128)S(1)}, f32[256,128]{1,0:T(8,128)S(1)}, u32[]{:S(2)}, u32[]{:S(2)}) collective-permute-start(f32[256,128]{1,0:T(8,128)S(1)} %shard_map.58.mix0), channel_id=1, source_target_pairs={{0,4},{2,6},{4,0},{6,2},{1,5},{3,7},{5,1},{7,3},{8,12},{10,14},{12... | collective-permute-start | bytes 393224 | tf_op jit(solution)/shard_map/ppermute | solution.py:25
  95.7 1.9 %collective-permute-start.6 = (f32[256,128]{1,0:T(8,128)S(1)}, f32[256,128]{1,0:T(8,128)S(1)}, u32[]{:S(2)}, u32[]{:S(2)}) collective-permute-start(f32[256,128]{1,0:T(8,128)S(1)} %shard_map.58.mix0), channel_id=1, source_target_pairs={{0,6},{2,0},{4,2},{6,4},{1,7},{3,1},{5,3},{7,5},{8,14},{10,8},{12,... | collective-permute-start | bytes 393224 | tf_op jit(solution)/shard_map/ppermute | solution.py:25
  97.6 0.7 collective-permute-start.21
  98.3 3.3 %collective-permute-start.22 = (f32[64,128]{1,0:T(8,128)S(1)}, f32[64,128]{1,0:T(8,128)S(1)}, u32[]{:S(2)}, u32[]{:S(2)}) collective-permute-start(f32[64,128]{1,0:T(8,128)S(1)} %bitcast_subtract_fusion.rest0), channel_id=1, source_target_pairs={{0,128},{64,192},{128,0},{192,64},{1,129},{65,193},{129,1},{193,65... | collective-permute-start | bytes 98312 | tf_op jit(solution)/shard_map/ppermute | solution.py:25
  101.6 0.2 collective-permute-start.23
  101.8 0.3 collective-permute-done.6.mix3
  102.1 0.7 collective-permute-done.21.rest1
  102.8 1.0 collective-permute-done.22.rest2
  103.9 1.7 %collective-permute-done.23.rest3 = f32[64,128]{1,0:T(8,128)S(1)} collective-permute-done((f32[64,128]{1,0:T(8,128)S(1)}, f32[64,128]{1,0:T(8,128)S(1)}, u32[]{:S(2)}, u32[]{:S(2)}) %collective-permute-start.23) | collective-permute-done | bytes 32800 | tf_op jit(solution)/shard_map/ppermute | solution.py:25
  105.5 1.5 %shard_map.66 = f32[8,64,128]{2,1,0:T(8,128)S(1)} custom-call(s32[3]{0:T(128)S(1)} %pad_add_fusion.place, f32[256,512]{1,0:T(8,128)} %bitcast.4.tiles, f32[256,128]{1,0:T(8,128)S(1)} %shard_map.58.mix0, f32[256,128]{1,0:T(8,128)S(1)} %collective-permute-done.4.mix1, f32[256,128]{1,0:T(8,128)S(1)} %collective-permute-done.5.mix2, ...), custom_call_target="tpu_custom_call" | custom-call | tf_op jit(solution)/shard_map/pallas_call | solution.py:282
  107.1 17.5 %all_to_all.15 = f32[8,64,128]{2,1,0:T(8,128)S(1)} all-to-all(f32[8,64,128]{2,1,0:T(8,128)S(1)} %shard_map.66), channel_id=1, replica_groups=mesh['y'=4,'z'=8,'x'=4,'core'=2] {'z'}, dimensions={0} | all-to-all | bytes 524288 | tf_op jit(solution)/shard_map/all_to_all | solution.py:289
  124.6 0.6 reduce_sum.19
  (26 shorter events, 0.1 us)
Async XLA Ops:
  4.5 4.4 %copy-start = (f32[384,1024]{1,0:T(8,128)}, f32[384,1024]{1,0:T(8,128)S(1)}, u32[]{:S(2)}) copy-start(f32[384,1024]{1,0:T(8,128)S(1)} %get-tuple-element.25.cols) | copy-start | bytes 4718596
  4.5 4.4 %collective-permute-start.7 = (f32[4,1024,128]{2,1,0:T(8,128)S(1)}, f32[4,1024,128]{2,1,0:T(8,128)S(1)}, u32[]{:S(2)}, u32[]{:S(2)}) collective-permute-start(f32[4,1024,128]{2,1,0:T(8,128)S(1)} %get-tuple-element.26), channel_id=1, source_target_pairs={{0,1},{1,0},{2,3},{3,2},{4,5},{5,4},{6,7},{7,6},{8,9},{9,8},{10,11... | collective-permute-start | bytes 6291464 | tf_op jit(solution)/shard_map/ppermute | solution.py:25
  8.2 21.1 %collective-permute-start.14 = (f32[4,1024,128]{2,1,0:T(8,128)}, f32[4,1024,128]{2,1,0:T(8,128)}, u32[]{:S(2)}, u32[]{:S(2)}) collective-permute-start(f32[4,1024,128]{2,1,0:T(8,128)} %shard_map.62), channel_id=1, source_target_pairs={{0,1},{1,0},{2,3},{3,2},{4,5},{5,4},{6,7},{7,6},{8,9},{9,8},{10,11... | collective-permute-start | bytes 6291464 | tf_op jit(solution)/shard_map/ppermute | solution.py:25
  8.8 7.2 %copy-start.5 = (f32[2,32,1024]{2,1,0:T(8,128)S(1)}, f32[2,32,1024]{2,1,0:T(8,128)}, u32[]{:S(2)}) copy-start(f32[2,32,1024]{2,1,0:T(8,128)} %inverses.1) | copy-start | bytes 786436
  8.8 7.2 %copy-start.6 = (f32[1024,32]{0,1:T(8,128)S(1)}, f32[1024,32]{0,1:T(8,128)}, u32[]{:S(2)}) copy-start(f32[1024,32]{0,1:T(8,128)} %param.8) | copy-start | bytes 393220
  12.1 0.8 copy-start.3
  12.9 0.8 copy-start.7
  13.8 0.8 copy-start.8
  14.5 24.3 %collective-permute-start.8 = (f32[1024,128]{1,0:T(8,128)}, f32[1024,128]{1,0:T(8,128)}, u32[]{:S(2)}, u32[]{:S(2)}) collective-permute-start(f32[1024,128]{1,0:T(8,128)} %get-tuple-element.28), channel_id=1, source_target_pairs={{0,2},{2,4},{4,6},{6,0},{1,3},{3,5},{5,7},{7,1},{8,10},{10,12},{12... | collective-permute-start | bytes 1572872 | tf_op jit(solution)/shard_map/ppermute | solution.py:25
  16.8 0.8 copy-start.2
  17.6 54.9 %all-to-all-start = ((f32[8,32,512]{2,1,0:T(8,128)}), f32[8,32,512]{2,1,0:T(8,128)}, u32[]{:S(2)}, u32[]{:S(2)}) async-start(f32[8,32,512]{2,1,0:T(8,128)} %copy-done.2), calls=%async_computation | async-start | bytes 1048576 | tf_op jit(solution)/shard_map/all_to_all | solution.py:255
  26.1 16.5 %collective-permute-start.9 = (f32[1024,128]{1,0:T(8,128)}, f32[1024,128]{1,0:T(8,128)S(1)}, u32[]{:S(2)}, u32[]{:S(2)}) collective-permute-start(f32[1024,128]{1,0:T(8,128)} %copy-done.8), channel_id=1, source_target_pairs={{0,4},{2,6},{4,0},{6,2},{1,5},{3,7},{5,1},{7,3},{8,12},{10,14},{12... | collective-permute-start | bytes 1572872 | tf_op jit(solution)/shard_map/ppermute | solution.py:25
  27.2 24.4 %collective-permute-start.10 = (f32[1024,128]{1,0:T(8,128)}, f32[1024,128]{1,0:T(8,128)S(1)}, u32[]{:S(2)}, u32[]{:S(2)}) collective-permute-start(f32[1024,128]{1,0:T(8,128)} %copy-done.7), channel_id=1, source_target_pairs={{0,6},{2,0},{4,2},{6,4},{1,7},{3,1},{5,3},{7,5},{8,14},{10,8},{12,... | collective-permute-start | bytes 1572872 | tf_op jit(solution)/shard_map/ppermute | solution.py:25
  29.4 1.4 %copy-start.1 = (f32[384,1024]{1,0:T(8,128)S(1)}, f32[384,1024]{1,0:T(8,128)}, u32[]{:S(2)}) copy-start(f32[384,1024]{1,0:T(8,128)} %copy-done) | copy-start | bytes 4718596
  30.8 20.9 %copy-start.4 = (f32[1024,128]{1,0:T(8,128)S(1)}, f32[1024,128]{1,0:T(8,128)}, u32[]{:S(2)}) copy-start(f32[1024,128]{1,0:T(8,128)} %copy-done.3) | copy-start | bytes 1572868
  34.2 23.3 %collective-permute-start.15 = (f32[1024,128]{1,0:T(8,128)S(1)}, f32[1024,128]{1,0:T(8,128)S(1)}, u32[]{:S(2)}, u32[]{:S(2)}) collective-permute-start(f32[1024,128]{1,0:T(8,128)S(1)} %get-tuple-element.36), channel_id=1, source_target_pairs={{0,64},{64,128},{128,192},{192,0},{1,65},{65,129},{129,193},{193,1... | collective-permute-start | bytes 1572872 | tf_op jit(solution)/shard_map/ppermute | solution.py:25
  35.9 27.0 %collective-permute-start.16 = (f32[1024,128]{1,0:T(8,128)S(1)}, f32[1024,128]{1,0:T(8,128)S(1)}, u32[]{:S(2)}, u32[]{:S(2)}) collective-permute-start(f32[1024,128]{1,0:T(8,128)S(1)} %get-tuple-element.37), channel_id=1, source_target_pairs={{0,128},{64,192},{128,0},{192,64},{1,129},{65,193},{129,1},{193,65... | collective-permute-start | bytes 1572872 | tf_op jit(solution)/shard_map/ppermute | solution.py:25
  38.8 24.0 %collective-permute-start.17 = (f32[1024,128]{1,0:T(8,128)S(1)}, f32[1024,128]{1,0:T(8,128)S(1)}, u32[]{:S(2)}, u32[]{:S(2)}) collective-permute-start(f32[1024,128]{1,0:T(8,128)S(1)} %get-tuple-element.38), channel_id=1, source_target_pairs={{0,192},{64,0},{128,64},{192,128},{1,193},{65,1},{129,65},{193,129... | collective-permute-start | bytes 1572872 | tf_op jit(solution)/shard_map/ppermute | solution.py:25
  52.8 13.7 %collective-permute-start.11 = (f32[256,128]{1,0:T(8,128)S(1)}, f32[256,128]{1,0:T(8,128)S(1)}, u32[]{:S(2)}, u32[]{:S(2)}) collective-permute-start(f32[256,128]{1,0:T(8,128)S(1)} %get-tuple-element.32), channel_id=1, source_target_pairs={{0,64},{64,128},{128,192},{192,0},{1,65},{65,129},{129,193},{193,1... | collective-permute-start | bytes 393224 | tf_op jit(solution)/shard_map/ppermute | solution.py:25
  54.7 11.9 %collective-permute-start.12 = (f32[256,128]{1,0:T(8,128)S(1)}, f32[256,128]{1,0:T(8,128)S(1)}, u32[]{:S(2)}, u32[]{:S(2)}) collective-permute-start(f32[256,128]{1,0:T(8,128)S(1)} %get-tuple-element.33), channel_id=1, source_target_pairs={{0,128},{64,192},{128,0},{192,64},{1,129},{65,193},{129,1},{193,65... | collective-permute-start | bytes 393224 | tf_op jit(solution)/shard_map/ppermute | solution.py:25
  57.6 9.0 %collective-permute-start.13 = (f32[256,128]{1,0:T(8,128)S(1)}, f32[256,128]{1,0:T(8,128)S(1)}, u32[]{:S(2)}, u32[]{:S(2)}) collective-permute-start(f32[256,128]{1,0:T(8,128)S(1)} %get-tuple-element.34), channel_id=1, source_target_pairs={{0,192},{64,0},{128,64},{192,128},{1,193},{65,1},{129,65},{193,129... | collective-permute-start | bytes 393224 | tf_op jit(solution)/shard_map/ppermute | solution.py:25
  63.0 34.6 %copy-start.9 = (f32[2,32,128]{2,1,0:T(8,128)S(1)}, f32[2,32,128]{2,1,0:T(8,128)}, u32[]{:S(2)}) copy-start(f32[2,32,128]{2,1,0:T(8,128)} %param.7) | copy-start | bytes 98308
  63.0 5.0 %collective-permute-start.18 = (f32[256,128]{1,0:T(8,128)S(1)}, f32[256,128]{1,0:T(8,128)S(1)}, u32[]{:S(2)}, u32[]{:S(2)}) collective-permute-start(f32[256,128]{1,0:T(8,128)S(1)} %get-tuple-element.40), channel_id=1, source_target_pairs={{0,2},{2,4},{4,6},{6,0},{1,3},{3,5},{5,7},{7,1},{8,10},{10,12},{12... | collective-permute-start | bytes 393224 | tf_op jit(solution)/shard_map/ppermute | solution.py:25
  63.1 6.7 %collective-permute-start.19 = (f32[256,128]{1,0:T(8,128)S(1)}, f32[256,128]{1,0:T(8,128)S(1)}, u32[]{:S(2)}, u32[]{:S(2)}) collective-permute-start(f32[256,128]{1,0:T(8,128)S(1)} %get-tuple-element.41), channel_id=1, source_target_pairs={{0,4},{2,6},{4,0},{6,2},{1,5},{3,7},{5,1},{7,3},{8,12},{10,14},{12... | collective-permute-start | bytes 393224 | tf_op jit(solution)/shard_map/ppermute | solution.py:25
  66.5 5.2 %collective-permute-start.20 = (f32[256,128]{1,0:T(8,128)S(1)}, f32[256,128]{1,0:T(8,128)S(1)}, u32[]{:S(2)}, u32[]{:S(2)}) collective-permute-start(f32[256,128]{1,0:T(8,128)S(1)} %get-tuple-element.42), channel_id=1, source_target_pairs={{0,6},{2,0},{4,2},{6,4},{1,7},{3,1},{5,3},{7,5},{8,14},{10,8},{12,... | collective-permute-start | bytes 393224 | tf_op jit(solution)/shard_map/ppermute | solution.py:25
  72.5 25.1 %all-to-all-start.1 = ((f32[8,64,128]{2,1,0:T(8,128)}), f32[8,64,128]{2,1,0:T(8,128)S(1)}, u32[]{:S(2)}, u32[]{:S(2)}) async-start(f32[8,64,128]{2,1,0:T(8,128)} %shard_map.65), calls=%async_computation.1 | async-start | bytes 524288 | tf_op jit(solution)/shard_map/all_to_all | solution.py:278
  80.8 6.0 %collective-permute-start = (f32[128,128]{1,0:T(8,128)S(1)}, f32[128,128]{1,0:T(8,128)S(1)}, u32[]{:S(2)}, u32[]{:S(2)}) collective-permute-start(f32[128,128]{1,0:T(8,128)S(1)} %shard_map.56.part0), channel_id=1, source_target_pairs={{0,64},{64,128},{128,192},{192,0},{1,65},{65,129},{129,193},{193,1... | collective-permute-start | bytes 196616 | tf_op jit(solution)/shard_map/ppermute | solution.py:25
  81.9 5.9 %collective-permute-start.1 = (f32[128,128]{1,0:T(8,128)S(1)}, f32[128,128]{1,0:T(8,128)S(1)}, u32[]{:S(2)}, u32[]{:S(2)}) collective-permute-start(f32[128,128]{1,0:T(8,128)S(1)} %shard_map.56.part0), channel_id=1, source_target_pairs={{0,128},{64,192},{128,0},{192,64},{1,129},{65,193},{129,1},{193,65... | collective-permute-start | bytes 196616 | tf_op jit(solution)/shard_map/ppermute | solution.py:25
  84.9 4.3 %collective-permute-start.2 = (f32[128,128]{1,0:T(8,128)S(1)}, f32[128,128]{1,0:T(8,128)S(1)}, u32[]{:S(2)}, u32[]{:S(2)}) collective-permute-start(f32[128,128]{1,0:T(8,128)S(1)} %shard_map.56.part0), channel_id=1, source_target_pairs={{0,192},{64,0},{128,64},{192,128},{1,193},{65,1},{129,65},{193,129... | collective-permute-start | bytes 196616 | tf_op jit(solution)/shard_map/ppermute | solution.py:25
  90.4 1.4 %collective-permute-start.3 = (f32[256,128]{1,0:T(8,128)S(1)}, f32[256,128]{1,0:T(8,128)S(1)}, u32[]{:S(2)}, u32[]{:S(2)}) collective-permute-start(f32[256,128]{1,0:T(8,128)S(1)} %shard_map.57.a), channel_id=1, source_target_pairs={{0,1},{1,0},{2,3},{3,2},{4,5},{5,4},{6,7},{7,6},{8,9},{9,8},{10,11... | collective-permute-start | bytes 393224 | tf_op jit(solution)/shard_map/ppermute | solution.py:25
  91.9 9.7 %collective-permute-start.4 = (f32[256,128]{1,0:T(8,128)S(1)}, f32[256,128]{1,0:T(8,128)S(1)}, u32[]{:S(2)}, u32[]{:S(2)}) collective-permute-start(f32[256,128]{1,0:T(8,128)S(1)} %shard_map.58.mix0), channel_id=1, source_target_pairs={{0,2},{2,4},{4,6},{6,0},{1,3},{3,5},{5,7},{7,1},{8,10},{10,12},{12... | collective-permute-start | bytes 393224 | tf_op jit(solution)/shard_map/ppermute | solution.py:25
  92.5 9.3 %collective-permute-start.5 = (f32[256,128]{1,0:T(8,128)S(1)}, f32[256,128]{1,0:T(8,128)S(1)}, u32[]{:S(2)}, u32[]{:S(2)}) collective-permute-start(f32[256,128]{1,0:T(8,128)S(1)} %shard_map.58.mix0), channel_id=1, source_target_pairs={{0,4},{2,6},{4,0},{6,2},{1,5},{3,7},{5,1},{7,3},{8,12},{10,14},{12... | collective-permute-start | bytes 393224 | tf_op jit(solution)/shard_map/ppermute | solution.py:25
  95.7 6.4 %collective-permute-start.6 = (f32[256,128]{1,0:T(8,128)S(1)}, f32[256,128]{1,0:T(8,128)S(1)}, u32[]{:S(2)}, u32[]{:S(2)}) collective-permute-start(f32[256,128]{1,0:T(8,128)S(1)} %shard_map.58.mix0), channel_id=1, source_target_pairs={{0,6},{2,0},{4,2},{6,4},{1,7},{3,1},{5,3},{7,5},{8,14},{10,8},{12,... | collective-permute-start | bytes 393224 | tf_op jit(solution)/shard_map/ppermute | solution.py:25
  97.6 5.2 %collective-permute-start.21 = (f32[64,128]{1,0:T(8,128)S(1)}, f32[64,128]{1,0:T(8,128)S(1)}, u32[]{:S(2)}, u32[]{:S(2)}) collective-permute-start(f32[64,128]{1,0:T(8,128)S(1)} %bitcast_subtract_fusion.rest0), channel_id=1, source_target_pairs={{0,64},{64,128},{128,192},{192,0},{1,65},{65,129},{129,193},{193,1... | collective-permute-start | bytes 98312 | tf_op jit(solution)/shard_map/ppermute | solution.py:25
  98.3 5.5 %collective-permute-start.22 = (f32[64,128]{1,0:T(8,128)S(1)}, f32[64,128]{1,0:T(8,128)S(1)}, u32[]{:S(2)}, u32[]{:S(2)}) collective-permute-start(f32[64,128]{1,0:T(8,128)S(1)} %bitcast_subtract_fusion.rest0), channel_id=1, source_target_pairs={{0,128},{64,192},{128,0},{192,64},{1,129},{65,193},{129,1},{193,65... | collective-permute-start | bytes 98312 | tf_op jit(solution)/shard_map/ppermute | solution.py:25
  101.6 3.9 %collective-permute-start.23 = (f32[64,128]{1,0:T(8,128)S(1)}, f32[64,128]{1,0:T(8,128)S(1)}, u32[]{:S(2)}, u32[]{:S(2)}) collective-permute-start(f32[64,128]{1,0:T(8,128)S(1)} %bitcast_subtract_fusion.rest0), channel_id=1, source_target_pairs={{0,192},{64,0},{128,64},{192,128},{1,193},{65,1},{129,65},{193,129... | collective-permute-start | bytes 98312 | tf_op jit(solution)/shard_map/ppermute | solution.py:25

commit v7 on v4

--- a/solution.py
+++ b/solution.py
@@ -79,33 +79,38 @@
 def first_kernel(nx, ny):
     def kernel(place, far_rows, far_cols, out, rows, cols, left, right, sems):
         size = left.shape[0]
-        part = cols.shape[0] // ny
-        first_loads = []
-        for k in range(ny):
-            at = slice(k * part, (k + 1) * part)
-            first_loads.append(
-                pltpu.make_async_copy(far_cols.at[at, :], cols.at[at, :], sems.at[2 * ny + k])
+
+        def strip(jx, core, sem):
+            at = lax.rem(place[0] + jx, nx) * 256 + core * 128
+            at = pl.ds(pl.multiple_of(at, 128), 128)
+            return pltpu.make_async_copy(far_cols.at[:, at], cols.at[:, at], sems.at[sem])
+
+        def block(panel, jy, sem):
+            at = rows_at(place, jy, ny, size)
+            return pltpu.make_async_copy(
+                far_rows.at[panel, at, :], rows.at[panel, at, :], sems.at[sem]
             )
-        loads = []
-        for panel in range(2):
-            for jy in range(ny):
-                at = rows_at(place, jy, ny, size)
-                loads.append(
-                    pltpu.make_async_copy(
-                        far_rows.at[panel, at, :], rows.at[panel, at, :], sems.at[panel * ny + jy]
-                    )
-                )
-        for load in first_loads + loads:
+
+        strips = [strip(jx, place[2], jx) for jx in range(nx)]
+        blocks = [block(0, jy, nx + jy) for jy in range(ny)]
+        later = [strip(jx, 1 - place[2], nx + ny + jx) for jx in range(nx)]
+        later += [block(1, jy, 2 * nx + ny + jy) for jy in range(ny)]
+        for load in strips + blocks[:2]:
             load.start()
-        for load in first_loads:
+        for load in strips:
             load.wait()
+        for load in blocks[2:]:
+            load.start()
         split_columns(place, cols, right, nx)
         for jy in range(ny):
-            loads[jy].wait()
+            blocks[jy].wait()
+            if jy == 0:
+                for load in later:
+                    load.start()
             value = multiply(rows[0, rows_at(place, jy, ny, size), :], left, right)
             for jx in range(nx):
                 out[jx, jy * size : (jy + 1) * size, :] = value[:, jx * 128 : (jx + 1) * 128]
-        for load in loads[ny:]:
+        for load in later:
             load.wait()
 
     return kernel
@@ -132,7 +137,7 @@
         ),
         in_specs=[SMEM, FAR, FAR],
         scratch_shapes=product_scratch(size, depth, nx, ny)
-        + [pltpu.SemaphoreType.DMA((3 * ny,))],
+        + [pltpu.SemaphoreType.DMA((2 * nx + 2 * ny,))],
         compiler_params=PRODUCT,
         cost_estimate=product_cost(size, depth, nx),
     )(place, far(rows), far(cols))
@@ -265,17 +270,18 @@
     again0 = [sums0[0]] + [shift(sums0[j], "y", j, ny) for j in range(1, ny)]
     sums1 = gather_sums(got1, coupled, nx, False)
     again1 = [sums1[0]] + [shift(sums1[j], "x", j, nx) for j in range(1, nx)]
+    chained = pl.pallas_call(
+        chain_kernel, out_shape=jax.ShapeDtypeStruct((256, 128), F32), compiler_params=SMALL
+    )(tiles, coupled, *again0[1:])
+    chained_of_partner = shift(chained, "core", 1, nc)
     by_z = pl.pallas_call(
         interleave_kernel,
         out_shape=jax.ShapeDtypeStruct((nz, 64, 128), F32),
         compiler_params=SMALL,
     )(*again0, *again1)
-    chained = pl.pallas_call(
-        chain_kernel, out_shape=jax.ShapeDtypeStruct((256, 128), F32), compiler_params=SMALL
-    )(tiles, coupled, *again0[1:])
     mix = pl.pallas_call(
         sum_kernel, out_shape=jax.ShapeDtypeStruct((256, 128), F32), compiler_params=SMALL
-    )(chained, shift(chained, "core", 1, nc))
+    )(chained, chained_of_partner)
     mixes = [mix] + [shift(mix, "x", j, nx) for j in range(1, nx)]
     old = lax.all_to_all(by_z, "z", 0, 0, tiled=True).sum(axis=0)
     rest = right_side.reshape(64, 128) - old

time: 123 us -> 123 us (level)
  no operation moved by 1% of the time
where the time goes in v7:
time: 123 us; the launch traced here: 122 us
  starting transfers between devices  47.1 us (38%)
  waiting for transfers between devices  31.5 us (26%)
  Pallas kernels  22.8 us (19%)
  blocking collectives  13.5 us (11%)
  local copies, waits for them, and re-layouts  6.53 us (5%)
    ppermute x21, starting transfers between devices, shift(): lax.ppermute(value, axis, [(i, (i + step) % size) for i in range(size)])  31.7 us
    ppermute x21, waiting for transfers between devices, shift(): lax.ppermute(value, axis, [(i, (i + step) % size) for i in range(size)])  28.2 us
    all_to_all x1, blocking collectives, steps(): panels = lax.all_to_all(solved_part, 'z', 0, 0, tiled=True).sum(axis=0)  13.5 us
    pallas_call x3, Pallas kernels, products(): pl.pallas_call(kernel, out_shape=shapes, in_specs=[SMEM] + [pl.BlockSpec(...  9.81 us
    all_to_all x1, starting transfers between devices, steps(): tiles = lax.all_to_all(packed, 'z', 0, 0, tiled=True).reshape(nz * 32, 512)  8.46 us
    all_to_all x1, starting transfers between devices, steps(): old = lax.all_to_all(by_z, 'z', 0, 0, tiled=True).sum(axis=0)  6.93 us
    unnamed x24, local copies, waits for them, and re-layouts  6.53 us
    pallas_call x1, Pallas kernels, first_products(): pl.pallas_call(first_kernel(nx, ny), out_shape=(jax.ShapeDtypeStruct((nx,...  5.62 us
  transfers between devices with their start and end apart: 23, of which 12 were waited for; matrix products, arithmetic and copies ran while one was open for 0% of the time, Pallas kernels for 10%

profile of v7, /device:TPU:2, one launch (start us, length us, event | category | flops | bytes accessed | tf_op | source)
XLA Modules:
  0.0 122.4 jit_solution(14651464951476767001)
XLA Ops:
  0.0 0.1 pad_add_fusion.2.place
  0.1 5.6 %shard_map.57 = (f32[4,1024,128]{2,1,0:T(8,128)}, f32[2,1024,384]{2,1,0:T(8,128)S(1)}, f32[384,1024]{1,0:T(8,128)S(1)}) custom-call(s32[3]{0:T(128)S(1)} %pad_add_fusion.2.place, f32[2,1024,384]{2,1,0:T(8,128)} %far_rows.1, f32[384,1024]{1,0:T(8,128)} %far_cols.1), custom_call_target="tpu_custom_call" | custom-call | flops 1207959552 | bytes 6291456 | tf_op jit(solution)/shard_map/pallas_call | solution.py:131
  5.7 2.3 %shard_map.62 = f32[4,1024,128]{2,1,0:T(8,128)S(1)} custom-call(s32[3]{0:T(128)S(1)} %pad_add_fusion.2.place, f32[2,1024,384]{2,1,0:T(8,128)S(1)} %get-tuple-element.24.rows, f32[384,1024]{1,0:T(8,128)S(1)} %get-tuple-element.25.cols), custom_call_target="tpu_custom_call" | custom-call | flops 1207959552 | bytes 6291456 | tf_op jit(solution)/shard_map/pallas_call | solution.py:156
  8.0 0.1 collective-permute-start.11
  8.1 0.5 collective-permute-start
  8.6 0.1 pad_add_fusion.place
  8.7 3.6 %collective-permute-done.11.refs_0_ = f32[4,1024,128]{2,1,0:T(8,128)S(1)} collective-permute-done((f32[4,1024,128]{2,1,0:T(8,128)S(1)}, f32[4,1024,128]{2,1,0:T(8,128)S(1)}, u32[]{:S(2)}, u32[]{:S(2)}) %collective-permute-start.11) | collective-permute-done | bytes 2097184 | tf_op jit(solution)/shard_map/ppermute | solution.py:26
  12.3 2.9 %shard_map.63 = (f32[1024,128]{1,0:T(8,128)S(1)}, f32[1024,128]{1,0:T(8,128)}, f32[1024,128]{1,0:T(8,128)S(1)}, f32[1024,128]{1,0:T(8,128)S(1)}) custom-call(s32[3]{0:T(128)S(1)} %pad_add_fusion.place, f32[2,1024,384]{2,1,0:T(8,128)S(1)} %get-tuple-element.24.rows, f32[384,1024]{1,0:T(8,128)S(1)} %get-tuple-element.25.cols, ...), custom_call_target="tpu_custom_call" | custom-call | flops 1207959552 | bytes 6291456 | tf_op jit(solution)/shard_map/pallas_call | solution.py:156
  15.2 0.8 copy-done.3
  16.0 0.8 copy-done.9
  16.9 0.8 copy-done.10
  17.7 1.6 %collective-permute-start.12 = (f32[1024,128]{1,0:T(8,128)}, f32[1024,128]{1,0:T(8,128)}, u32[]{:S(2)}, u32[]{:S(2)}) collective-permute-start(f32[1024,128]{1,0:T(8,128)} %get-tuple-element.36), channel_id=1, source_target_pairs={{0,64},{64,128},{128,192},{192,0},{1,65},{65,129},{129,193},{193,1... | collective-permute-start | bytes 1572872 | tf_op jit(solution)/shard_map/ppermute | solution.py:26
  19.3 0.8 shard_map.55
  20.1 0.8 copy-done.2
  20.9 8.5 %all-to-all-start = ((f32[8,32,512]{2,1,0:T(8,128)}), f32[8,32,512]{2,1,0:T(8,128)}, u32[]{:S(2)}, u32[]{:S(2)}) async-start(f32[8,32,512]{2,1,0:T(8,128)} %copy-done.2), calls=%async_computation | async-start | bytes 1048576 | tf_op jit(solution)/shard_map/all_to_all | solution.py:264
  29.4 2.9 %collective-permute-start.13 = (f32[1024,128]{1,0:T(8,128)}, f32[1024,128]{1,0:T(8,128)}, u32[]{:S(2)}, u32[]{:S(2)}) collective-permute-start(f32[1024,128]{1,0:T(8,128)} %copy-done.10), channel_id=1, source_target_pairs={{0,128},{64,192},{128,0},{192,64},{1,129},{65,193},{129,1},{193,65... | collective-permute-start | bytes 1572872 | tf_op jit(solution)/shard_map/ppermute | solution.py:26
  32.3 1.3 %collective-permute-start.14 = (f32[1024,128]{1,0:T(8,128)}, f32[1024,128]{1,0:T(8,128)}, u32[]{:S(2)}, u32[]{:S(2)}) collective-permute-start(f32[1024,128]{1,0:T(8,128)} %copy-done.9), channel_id=1, source_target_pairs={{0,192},{64,0},{128,64},{192,128},{1,193},{65,1},{129,65},{193,129... | collective-permute-start | bytes 1572872 | tf_op jit(solution)/shard_map/ppermute | solution.py:26
  33.6 0.0 collective-permute-done.refs_0_
  33.6 1.4 %copy-done.1 = f32[384,1024]{1,0:T(8,128)S(1)} copy-done((f32[384,1024]{1,0:T(8,128)S(1)}, f32[384,1024]{1,0:T(8,128)}, u32[]{:S(2)}) %copy-start.1) | copy-done | bytes 1572888
  35.0 4.5 %shard_map.58 = (f32[1024,128]{1,0:T(8,128)S(1)}, f32[1024,128]{1,0:T(8,128)}, f32[1024,128]{1,0:T(8,128)}, f32[1024,128]{1,0:T(8,128)}) custom-call(s32[3]{0:T(128)S(1)} %pad_add_fusion.place, f32[2,1024,384]{2,1,0:T(8,128)S(1)} %get-tuple-element.24.rows, f32[384,1024]{1,0:T(8,128)S(1)} %copy-done.1, f32[4,1024,128]{2,1,0:T(8,128)} %collective-permute-done.refs_0_), custom_call_target="tpu_custom_call" | custom-call | flops 1207959552 | bytes 6291456 | tf_op jit(solution)/shard_map/pallas_call | solution.py:156
  39.6 0.8 copy-done.5
  40.4 1.5 %collective-permute-start.1 = (f32[1024,128]{1,0:T(8,128)}, f32[1024,128]{1,0:T(8,128)S(1)}, u32[]{:S(2)}, u32[]{:S(2)}) collective-permute-start(f32[1024,128]{1,0:T(8,128)} %get-tuple-element.28), channel_id=1, source_target_pairs={{0,2},{2,4},{4,6},{6,0},{1,3},{3,5},{5,7},{7,1},{8,10},{10,12},{12... | collective-permute-start | bytes 1572872 | tf_op jit(solution)/shard_map/ppermute | solution.py:26
  41.9 1.1 collective-permute-start.2
  43.0 0.0 collective-permute-done.12.b
  43.0 3.7 %collective-permute-start.3 = (f32[1024,128]{1,0:T(8,128)}, f32[1024,128]{1,0:T(8,128)S(1)}, u32[]{:S(2)}, u32[]{:S(2)}) collective-permute-start(f32[1024,128]{1,0:T(8,128)} %get-tuple-element.30), channel_id=1, source_target_pairs={{0,6},{2,0},{4,2},{6,4},{1,7},{3,1},{5,3},{7,5},{8,14},{10,8},{12,... | collective-permute-start | bytes 1572872 | tf_op jit(solution)/shard_map/ppermute | solution.py:26
  46.7 0.3 all-to-all-done
  47.0 1.3 %shard_map.56.rider.part0 = f32[128,128]{1,0:T(8,128)S(1)} custom-call(f32[256,512]{1,0:T(8,128)} %bitcast.4.tiles), custom_call_target="tpu_custom_call" | custom-call | tf_op jit(solution)/shard_map/pallas_call | solution.py:266
  48.3 0.0 collective-permute-done.13.c
  48.3 6.6 %collective-permute-done.14.d = f32[1024,128]{1,0:T(8,128)} collective-permute-done((f32[1024,128]{1,0:T(8,128)}, f32[1024,128]{1,0:T(8,128)}, u32[]{:S(2)}, u32[]{:S(2)}) %collective-permute-start.14) | collective-permute-done | bytes 524320 | tf_op jit(solution)/shard_map/ppermute | solution.py:26
  54.9 1.0 copy-done.4
  55.9 1.5 %shard_map.64 = (f32[256,128]{1,0:T(8,128)S(1)}, f32[256,128]{1,0:T(8,128)S(1)}, f32[256,128]{1,0:T(8,128)S(1)}, f32[256,128]{1,0:T(8,128)S(1)}) custom-call(f32[1024,128]{1,0:T(8,128)S(1)} %copy-done.4, f32[1024,128]{1,0:T(8,128)} %collective-permute-done.12.b, f32[1024,128]{1,0:T(8,128)} %collective-permute-done.13.c, ...), custom_call_target="tpu_custom_call" | custom-call | tf_op jit(solution)/shard_map/pallas_call | solution.py:211
  57.4 1.8 %collective-permute-start.15 = (f32[256,128]{1,0:T(8,128)S(1)}, f32[256,128]{1,0:T(8,128)S(1)}, u32[]{:S(2)}, u32[]{:S(2)}) collective-permute-start(f32[256,128]{1,0:T(8,128)S(1)} %get-tuple-element.40), channel_id=1, source_target_pairs={{0,2},{2,4},{4,6},{6,0},{1,3},{3,5},{5,7},{7,1},{8,10},{10,12},{12... | collective-permute-start | bytes 393224 | tf_op jit(solution)/shard_map/ppermute | solution.py:26
  59.2 0.0 collective-permute-done.1.b
  59.2 0.0 collective-permute-done.2.c
  59.2 7.4 %collective-permute-done.3.d = f32[1024,128]{1,0:T(8,128)S(1)} collective-permute-done((f32[1024,128]{1,0:T(8,128)}, f32[1024,128]{1,0:T(8,128)S(1)}, u32[]{:S(2)}, u32[]{:S(2)}) %collective-permute-start.3) | collective-permute-done | bytes 524320 | tf_op jit(solution)/shard_map/ppermute | solution.py:26
  66.7 0.1 shard_map.59
  66.8 0.0 copy-start.11
  66.8 0.8 collective-permute-start.4
  67.6 1.1 collective-permute-start.5
  68.6 1.7 %collective-permute-start.6 = (f32[384,128]{1,0:T(8,128)S(1)}, f32[384,128]{1,0:T(8,128)S(1)}, u32[]{:S(2)}, u32[]{:S(2)}) collective-permute-start(f32[384,128]{1,0:T(8,128)S(1)} %get-tuple-element.33), channel_id=1, source_target_pairs={{0,192},{64,0},{128,64},{192,128},{1,193},{65,1},{129,65},{193,129... | collective-permute-start | bytes 589832 | tf_op jit(solution)/shard_map/ppermute | solution.py:26
  70.3 1.8 %collective-permute-start.16 = (f32[256,128]{1,0:T(8,128)S(1)}, f32[256,128]{1,0:T(8,128)S(1)}, u32[]{:S(2)}, u32[]{:S(2)}) collective-permute-start(f32[256,128]{1,0:T(8,128)S(1)} %get-tuple-element.41), channel_id=1, source_target_pairs={{0,4},{2,6},{4,0},{6,2},{1,5},{3,7},{5,1},{7,3},{8,12},{10,14},{12... | collective-permute-start | bytes 393224 | tf_op jit(solution)/shard_map/ppermute | solution.py:26
  72.1 0.0 collective-permute-done.15.b1
  72.1 1.6 %collective-permute-start.17 = (f32[256,128]{1,0:T(8,128)S(1)}, f32[256,128]{1,0:T(8,128)S(1)}, u32[]{:S(2)}, u32[]{:S(2)}) collective-permute-start(f32[256,128]{1,0:T(8,128)S(1)} %get-tuple-element.42), channel_id=1, source_target_pairs={{0,6},{2,0},{4,2},{6,4},{1,7},{3,1},{5,3},{7,5},{8,14},{10,8},{12,... | collective-permute-start | bytes 393224 | tf_op jit(solution)/shard_map/ppermute | solution.py:26
  73.7 3.8 %collective-permute-done.16.b2 = f32[256,128]{1,0:T(8,128)S(1)} collective-permute-done((f32[256,128]{1,0:T(8,128)S(1)}, f32[256,128]{1,0:T(8,128)S(1)}, u32[]{:S(2)}, u32[]{:S(2)}) %collective-permute-start.16) | collective-permute-done | bytes 131104 | tf_op jit(solution)/shard_map/ppermute | solution.py:26
  77.5 1.3 %collective-permute-done.17.b3 = f32[256,128]{1,0:T(8,128)S(1)} collective-permute-done((f32[256,128]{1,0:T(8,128)S(1)}, f32[256,128]{1,0:T(8,128)S(1)}, u32[]{:S(2)}, u32[]{:S(2)}) %collective-permute-start.17) | collective-permute-done | bytes 131104 | tf_op jit(solution)/shard_map/ppermute | solution.py:26
  78.8 0.2 collective-permute-done.6.got3.a3
  79.1 0.7 shard_map.65
  79.8 6.9 %all-to-all-start.1 = ((f32[8,64,128]{2,1,0:T(8,128)}), f32[8,64,128]{2,1,0:T(8,128)S(1)}, u32[]{:S(2)}, u32[]{:S(2)}) async-start(f32[8,64,128]{2,1,0:T(8,128)} %shard_map.65), calls=%async_computation.1 | async-start | bytes 524288 | tf_op jit(solution)/shard_map/all_to_all | solution.py:286
  86.7 1.3 %shard_map.60.a = f32[256,128]{1,0:T(8,128)S(1)} custom-call(f32[256,512]{1,0:T(8,128)} %bitcast.4.tiles, f32[128,128]{1,0:T(8,128)S(1)} %shard_map.56.rider.part0, f32[384,128]{1,0:T(8,128)S(1)} %collective-permute-done.4.got1.a1, f32[384,128]{1,0:T(8,128)S(1)} %collective-permute-done.5.got2.a2, f32[384,128]{1,0:T(8,128)S(1)} %collective-permute-done.6.got3.a3), custom_call_target="tpu_custom_call" | custom-call | tf_op jit(solution)/shard_map/pallas_call | solution.py:273
  88.0 0.1 collective-permute-start.7
  88.1 1.3 %collective-permute-done.7.b = f32[256,128]{1,0:T(8,128)S(1)} collective-permute-done((f32[256,128]{1,0:T(8,128)S(1)}, f32[256,128]{1,0:T(8,128)S(1)}, u32[]{:S(2)}, u32[]{:S(2)}) %collective-permute-start.7) | collective-permute-done | bytes 131104 | tf_op jit(solution)/shard_map/ppermute | solution.py:26
  89.5 0.4 collective-permute-start.8
  89.9 2.5 %collective-permute-start.9 = (f32[256,128]{1,0:T(8,128)S(1)}, f32[256,128]{1,0:T(8,128)S(1)}, u32[]{:S(2)}, u32[]{:S(2)}) collective-permute-start(f32[256,128]{1,0:T(8,128)S(1)} %shard_map.61.mix0), channel_id=1, source_target_pairs={{0,4},{2,6},{4,0},{6,2},{1,5},{3,7},{5,1},{7,3},{8,12},{10,14},{12... | collective-permute-start | bytes 393224 | tf_op jit(solution)/shard_map/ppermute | solution.py:26
  92.4 2.3 %collective-permute-start.10 = (f32[256,128]{1,0:T(8,128)S(1)}, f32[256,128]{1,0:T(8,128)S(1)}, u32[]{:S(2)}, u32[]{:S(2)}) collective-permute-start(f32[256,128]{1,0:T(8,128)S(1)} %shard_map.61.mix0), channel_id=1, source_target_pairs={{0,6},{2,0},{4,2},{6,4},{1,7},{3,1},{5,3},{7,5},{8,14},{10,8},{12,... | collective-permute-start | bytes 393224 | tf_op jit(solution)/shard_map/ppermute | solution.py:26
  94.7 3.0 %all-to-all-done.1 = f32[8,64,128]{2,1,0:T(8,128)S(1)} async-done(((f32[8,64,128]{2,1,0:T(8,128)}), f32[8,64,128]{2,1,0:T(8,128)S(1)}, u32[]{:S(2)}, u32[]{:S(2)}) %all-to-all-start.1) | async-done | bytes 262176 | tf_op jit(solution)/shard_map/all_to_all | solution.py:286
  97.8 1.3 %collective-permute-start.18 = (f32[64,128]{1,0:T(8,128)S(1)}, f32[64,128]{1,0:T(8,128)S(1)}, u32[]{:S(2)}, u32[]{:S(2)}) collective-permute-start(f32[64,128]{1,0:T(8,128)S(1)} %bitcast_subtract_fusion.rest0), channel_id=1, source_target_pairs={{0,64},{64,128},{128,192},{192,0},{1,65},{65,129},{129,193},{193,1... | collective-permute-start | bytes 98312 | tf_op jit(solution)/shard_map/ppermute | solution.py:26
  99.0 3.8 %collective-permute-start.19 = (f32[64,128]{1,0:T(8,128)S(1)}, f32[64,128]{1,0:T(8,128)S(1)}, u32[]{:S(2)}, u32[]{:S(2)}) collective-permute-start(f32[64,128]{1,0:T(8,128)S(1)} %bitcast_subtract_fusion.rest0), channel_id=1, source_target_pairs={{0,128},{64,192},{128,0},{192,64},{1,129},{65,193},{129,1},{193,65... | collective-permute-start | bytes 98312 | tf_op jit(solution)/shard_map/ppermute | solution.py:26
  102.9 0.0 collective-permute-done.10.mix3
  102.9 0.4 collective-permute-done.18.rest1
  103.3 1.8 %collective-permute-done.19.rest2 = f32[64,128]{1,0:T(8,128)S(1)} collective-permute-done((f32[64,128]{1,0:T(8,128)S(1)}, f32[64,128]{1,0:T(8,128)S(1)}, u32[]{:S(2)}, u32[]{:S(2)}) %collective-permute-start.19) | collective-permute-done | bytes 32800 | tf_op jit(solution)/shard_map/ppermute | solution.py:26
  105.1 1.7 %collective-permute-done.20.rest3 = f32[64,128]{1,0:T(8,128)S(1)} collective-permute-done((f32[64,128]{1,0:T(8,128)S(1)}, f32[64,128]{1,0:T(8,128)S(1)}, u32[]{:S(2)}, u32[]{:S(2)}) %collective-permute-start.20) | collective-permute-done | bytes 32800 | tf_op jit(solution)/shard_map/ppermute | solution.py:26
  106.8 1.5 %shard_map.66 = f32[8,64,128]{2,1,0:T(8,128)S(1)} custom-call(s32[3]{0:T(128)S(1)} %pad_add_fusion.place, f32[256,512]{1,0:T(8,128)} %bitcast.4.tiles, f32[256,128]{1,0:T(8,128)S(1)} %shard_map.61.mix0, f32[256,128]{1,0:T(8,128)S(1)} %collective-permute-done.8.mix1, f32[256,128]{1,0:T(8,128)S(1)} %collective-permute-done.9.mix2, ...), custom_call_target="tpu_custom_call" | custom-call | tf_op jit(solution)/shard_map/pallas_call | solution.py:290
  108.3 13.5 %all_to_all.15 = f32[8,64,128]{2,1,0:T(8,128)S(1)} all-to-all(f32[8,64,128]{2,1,0:T(8,128)S(1)} %shard_map.66), channel_id=1, replica_groups=mesh['y'=4,'z'=8,'x'=4,'core'=2] {'z'}, dimensions={0} | all-to-all | bytes 524288 | tf_op jit(solution)/shard_map/all_to_all | solution.py:297
  121.8 0.6 reduce_sum.19
  (24 shorter events, 0.1 us)
Async XLA Ops:
  5.7 6.6 %copy-start = (f32[384,1024]{1,0:T(8,128)}, f32[384,1024]{1,0:T(8,128)S(1)}, u32[]{:S(2)}) copy-start(f32[384,1024]{1,0:T(8,128)S(1)} %get-tuple-element.25.cols) | copy-start | bytes 4718596
  8.0 4.2 %collective-permute-start.11 = (f32[4,1024,128]{2,1,0:T(8,128)S(1)}, f32[4,1024,128]{2,1,0:T(8,128)S(1)}, u32[]{:S(2)}, u32[]{:S(2)}) collective-permute-start(f32[4,1024,128]{2,1,0:T(8,128)S(1)} %shard_map.62), channel_id=1, source_target_pairs={{0,1},{1,0},{2,3},{3,2},{4,5},{5,4},{6,7},{7,6},{8,9},{9,8},{10,11... | collective-permute-start | bytes 6291464 | tf_op jit(solution)/shard_map/ppermute | solution.py:26
  8.1 25.5 %collective-permute-start = (f32[4,1024,128]{2,1,0:T(8,128)}, f32[4,1024,128]{2,1,0:T(8,128)}, u32[]{:S(2)}, u32[]{:S(2)}) collective-permute-start(f32[4,1024,128]{2,1,0:T(8,128)} %get-tuple-element.26), channel_id=1, source_target_pairs={{0,1},{1,0},{2,3},{3,2},{4,5},{5,4},{6,7},{7,6},{8,9},{9,8},{10,11... | collective-permute-start | bytes 6291464 | tf_op jit(solution)/shard_map/ppermute | solution.py:26
  8.7 10.6 %copy-start.7 = (f32[2,32,1024]{2,1,0:T(8,128)S(1)}, f32[2,32,1024]{2,1,0:T(8,128)}, u32[]{:S(2)}) copy-start(f32[2,32,1024]{2,1,0:T(8,128)} %inverses.1) | copy-start | bytes 786436
  8.7 10.6 %copy-start.8 = (f32[1024,32]{0,1:T(8,128)S(1)}, f32[1024,32]{0,1:T(8,128)}, u32[]{:S(2)}) copy-start(f32[1024,32]{0,1:T(8,128)} %param.8) | copy-start | bytes 393220
  15.2 0.8 copy-start.3
  16.0 0.8 copy-start.9
  16.9 0.8 copy-start.10
  17.7 25.3 %collective-permute-start.12 = (f32[1024,128]{1,0:T(8,128)}, f32[1024,128]{1,0:T(8,128)}, u32[]{:S(2)}, u32[]{:S(2)}) collective-permute-start(f32[1024,128]{1,0:T(8,128)} %get-tuple-element.36), channel_id=1, source_target_pairs={{0,64},{64,128},{128,192},{192,0},{1,65},{65,129},{129,193},{193,1... | collective-permute-start | bytes 1572872 | tf_op jit(solution)/shard_map/ppermute | solution.py:26
  20.1 0.8 copy-start.2
  20.9 26.0 %all-to-all-start = ((f32[8,32,512]{2,1,0:T(8,128)}), f32[8,32,512]{2,1,0:T(8,128)}, u32[]{:S(2)}, u32[]{:S(2)}) async-start(f32[8,32,512]{2,1,0:T(8,128)} %copy-done.2), calls=%async_computation | async-start | bytes 1048576 | tf_op jit(solution)/shard_map/all_to_all | solution.py:264
  29.4 18.9 %collective-permute-start.13 = (f32[1024,128]{1,0:T(8,128)}, f32[1024,128]{1,0:T(8,128)}, u32[]{:S(2)}, u32[]{:S(2)}) collective-permute-start(f32[1024,128]{1,0:T(8,128)} %copy-done.10), channel_id=1, source_target_pairs={{0,128},{64,192},{128,0},{192,64},{1,129},{65,193},{129,1},{193,65... | collective-permute-start | bytes 1572872 | tf_op jit(solution)/shard_map/ppermute | solution.py:26
  32.3 22.6 %collective-permute-start.14 = (f32[1024,128]{1,0:T(8,128)}, f32[1024,128]{1,0:T(8,128)}, u32[]{:S(2)}, u32[]{:S(2)}) collective-permute-start(f32[1024,128]{1,0:T(8,128)} %copy-done.9), channel_id=1, source_target_pairs={{0,192},{64,0},{128,64},{192,128},{1,193},{65,1},{129,65},{193,129... | collective-permute-start | bytes 1572872 | tf_op jit(solution)/shard_map/ppermute | solution.py:26
  33.6 1.4 %copy-start.1 = (f32[384,1024]{1,0:T(8,128)S(1)}, f32[384,1024]{1,0:T(8,128)}, u32[]{:S(2)}) copy-start(f32[384,1024]{1,0:T(8,128)} %copy-done) | copy-start | bytes 4718596
  39.6 0.8 copy-start.5
  40.4 26.3 %copy-start.6 = (f32[1024,128]{1,0:T(8,128)S(1)}, f32[1024,128]{1,0:T(8,128)}, u32[]{:S(2)}) copy-start(f32[1024,128]{1,0:T(8,128)} %copy-done.5) | copy-start | bytes 1572868
  40.4 18.8 %collective-permute-start.1 = (f32[1024,128]{1,0:T(8,128)}, f32[1024,128]{1,0:T(8,128)S(1)}, u32[]{:S(2)}, u32[]{:S(2)}) collective-permute-start(f32[1024,128]{1,0:T(8,128)} %get-tuple-element.28), channel_id=1, source_target_pairs={{0,2},{2,4},{4,6},{6,0},{1,3},{3,5},{5,7},{7,1},{8,10},{10,12},{12... | collective-permute-start | bytes 1572872 | tf_op jit(solution)/shard_map/ppermute | solution.py:26
  41.9 17.3 %collective-permute-start.2 = (f32[1024,128]{1,0:T(8,128)}, f32[1024,128]{1,0:T(8,128)S(1)}, u32[]{:S(2)}, u32[]{:S(2)}) collective-permute-start(f32[1024,128]{1,0:T(8,128)} %get-tuple-element.29), channel_id=1, source_target_pairs={{0,4},{2,6},{4,0},{6,2},{1,5},{3,7},{5,1},{7,3},{8,12},{10,14},{12... | collective-permute-start | bytes 1572872 | tf_op jit(solution)/shard_map/ppermute | solution.py:26
  43.0 23.7 %collective-permute-start.3 = (f32[1024,128]{1,0:T(8,128)}, f32[1024,128]{1,0:T(8,128)S(1)}, u32[]{:S(2)}, u32[]{:S(2)}) collective-permute-start(f32[1024,128]{1,0:T(8,128)} %get-tuple-element.30), channel_id=1, source_target_pairs={{0,6},{2,0},{4,2},{6,4},{1,7},{3,1},{5,3},{7,5},{8,14},{10,8},{12,... | collective-permute-start | bytes 1572872 | tf_op jit(solution)/shard_map/ppermute | solution.py:26
  54.9 1.0 copy-start.4
  57.4 14.7 %collective-permute-start.15 = (f32[256,128]{1,0:T(8,128)S(1)}, f32[256,128]{1,0:T(8,128)S(1)}, u32[]{:S(2)}, u32[]{:S(2)}) collective-permute-start(f32[256,128]{1,0:T(8,128)S(1)} %get-tuple-element.40), channel_id=1, source_target_pairs={{0,2},{2,4},{4,6},{6,0},{1,3},{3,5},{5,7},{7,1},{8,10},{10,12},{12... | collective-permute-start | bytes 393224 | tf_op jit(solution)/shard_map/ppermute | solution.py:26
  66.8 31.0 %copy-start.11 = (f32[2,32,128]{2,1,0:T(8,128)S(1)}, f32[2,32,128]{2,1,0:T(8,128)}, u32[]{:S(2)}) copy-start(f32[2,32,128]{2,1,0:T(8,128)} %param.7) | copy-start | bytes 98308
  66.8 12.0 %collective-permute-start.4 = (f32[384,128]{1,0:T(8,128)S(1)}, f32[384,128]{1,0:T(8,128)S(1)}, u32[]{:S(2)}, u32[]{:S(2)}) collective-permute-start(f32[384,128]{1,0:T(8,128)S(1)} %get-tuple-element.31), channel_id=1, source_target_pairs={{0,64},{64,128},{128,192},{192,0},{1,65},{65,129},{129,193},{193,1... | collective-permute-start | bytes 589832 | tf_op jit(solution)/shard_map/ppermute | solution.py:26
  67.6 11.3 %collective-permute-start.5 = (f32[384,128]{1,0:T(8,128)S(1)}, f32[384,128]{1,0:T(8,128)S(1)}, u32[]{:S(2)}, u32[]{:S(2)}) collective-permute-start(f32[384,128]{1,0:T(8,128)S(1)} %get-tuple-element.32), channel_id=1, source_target_pairs={{0,128},{64,192},{128,0},{192,64},{1,129},{65,193},{129,1},{193,65... | collective-permute-start | bytes 589832 | tf_op jit(solution)/shard_map/ppermute | solution.py:26
  68.6 10.4 %collective-permute-start.6 = (f32[384,128]{1,0:T(8,128)S(1)}, f32[384,128]{1,0:T(8,128)S(1)}, u32[]{:S(2)}, u32[]{:S(2)}) collective-permute-start(f32[384,128]{1,0:T(8,128)S(1)} %get-tuple-element.33), channel_id=1, source_target_pairs={{0,192},{64,0},{128,64},{192,128},{1,193},{65,1},{129,65},{193,129... | collective-permute-start | bytes 589832 | tf_op jit(solution)/shard_map/ppermute | solution.py:26
  70.3 7.2 %collective-permute-start.16 = (f32[256,128]{1,0:T(8,128)S(1)}, f32[256,128]{1,0:T(8,128)S(1)}, u32[]{:S(2)}, u32[]{:S(2)}) collective-permute-start(f32[256,128]{1,0:T(8,128)S(1)} %get-tuple-element.41), channel_id=1, source_target_pairs={{0,4},{2,6},{4,0},{6,2},{1,5},{3,7},{5,1},{7,3},{8,12},{10,14},{12... | collective-permute-start | bytes 393224 | tf_op jit(solution)/shard_map/ppermute | solution.py:26
  72.1 6.7 %collective-permute-start.17 = (f32[256,128]{1,0:T(8,128)S(1)}, f32[256,128]{1,0:T(8,128)S(1)}, u32[]{:S(2)}, u32[]{:S(2)}) collective-permute-start(f32[256,128]{1,0:T(8,128)S(1)} %get-tuple-element.42), channel_id=1, source_target_pairs={{0,6},{2,0},{4,2},{6,4},{1,7},{3,1},{5,3},{7,5},{8,14},{10,8},{12,... | collective-permute-start | bytes 393224 | tf_op jit(solution)/shard_map/ppermute | solution.py:26
  79.8 17.9 %all-to-all-start.1 = ((f32[8,64,128]{2,1,0:T(8,128)}), f32[8,64,128]{2,1,0:T(8,128)S(1)}, u32[]{:S(2)}, u32[]{:S(2)}) async-start(f32[8,64,128]{2,1,0:T(8,128)} %shard_map.65), calls=%async_computation.1 | async-start | bytes 524288 | tf_op jit(solution)/shard_map/all_to_all | solution.py:286
  88.0 1.4 %collective-permute-start.7 = (f32[256,128]{1,0:T(8,128)S(1)}, f32[256,128]{1,0:T(8,128)S(1)}, u32[]{:S(2)}, u32[]{:S(2)}) collective-permute-start(f32[256,128]{1,0:T(8,128)S(1)} %shard_map.60.a), channel_id=1, source_target_pairs={{0,1},{1,0},{2,3},{3,2},{4,5},{5,4},{6,7},{7,6},{8,9},{9,8},{10,11... | collective-permute-start | bytes 393224 | tf_op jit(solution)/shard_map/ppermute | solution.py:26
  89.5 13.3 %collective-permute-start.8 = (f32[256,128]{1,0:T(8,128)S(1)}, f32[256,128]{1,0:T(8,128)S(1)}, u32[]{:S(2)}, u32[]{:S(2)}) collective-permute-start(f32[256,128]{1,0:T(8,128)S(1)} %shard_map.61.mix0), channel_id=1, source_target_pairs={{0,2},{2,4},{4,6},{6,0},{1,3},{3,5},{5,7},{7,1},{8,10},{10,12},{12... | collective-permute-start | bytes 393224 | tf_op jit(solution)/shard_map/ppermute | solution.py:26
  89.9 12.9 %collective-permute-start.9 = (f32[256,128]{1,0:T(8,128)S(1)}, f32[256,128]{1,0:T(8,128)S(1)}, u32[]{:S(2)}, u32[]{:S(2)}) collective-permute-start(f32[256,128]{1,0:T(8,128)S(1)} %shard_map.61.mix0), channel_id=1, source_target_pairs={{0,4},{2,6},{4,0},{6,2},{1,5},{3,7},{5,1},{7,3},{8,12},{10,14},{12... | collective-permute-start | bytes 393224 | tf_op jit(solution)/shard_map/ppermute | solution.py:26
  92.4 10.5 %collective-permute-start.10 = (f32[256,128]{1,0:T(8,128)S(1)}, f32[256,128]{1,0:T(8,128)S(1)}, u32[]{:S(2)}, u32[]{:S(2)}) collective-permute-start(f32[256,128]{1,0:T(8,128)S(1)} %shard_map.61.mix0), channel_id=1, source_target_pairs={{0,6},{2,0},{4,2},{6,4},{1,7},{3,1},{5,3},{7,5},{8,14},{10,8},{12,... | collective-permute-start | bytes 393224 | tf_op jit(solution)/shard_map/ppermute | solution.py:26
  97.8 5.5 %collective-permute-start.18 = (f32[64,128]{1,0:T(8,128)S(1)}, f32[64,128]{1,0:T(8,128)S(1)}, u32[]{:S(2)}, u32[]{:S(2)}) collective-permute-start(f32[64,128]{1,0:T(8,128)S(1)} %bitcast_subtract_fusion.rest0), channel_id=1, source_target_pairs={{0,64},{64,128},{128,192},{192,0},{1,65},{65,129},{129,193},{193,1... | collective-permute-start | bytes 98312 | tf_op jit(solution)/shard_map/ppermute | solution.py:26
  99.0 6.1 %collective-permute-start.19 = (f32[64,128]{1,0:T(8,128)S(1)}, f32[64,128]{1,0:T(8,128)S(1)}, u32[]{:S(2)}, u32[]{:S(2)}) collective-permute-start(f32[64,128]{1,0:T(8,128)S(1)} %bitcast_subtract_fusion.rest0), channel_id=1, source_target_pairs={{0,128},{64,192},{128,0},{192,64},{1,129},{65,193},{129,1},{193,65... | collective-permute-start | bytes 98312 | tf_op jit(solution)/shard_map/ppermute | solution.py:26
  102.8 3.9 %collective-permute-start.20 = (f32[64,128]{1,0:T(8,128)S(1)}, f32[64,128]{1,0:T(8,128)S(1)}, u32[]{:S(2)}, u32[]{:S(2)}) collective-permute-start(f32[64,128]{1,0:T(8,128)S(1)} %bitcast_subtract_fusion.rest0), channel_id=1, source_target_pairs={{0,192},{64,0},{128,64},{192,128},{1,193},{65,1},{129,65},{193,129... | collective-permute-start | bytes 98312 | tf_op jit(solution)/shard_map/ppermute | solution.py:26

commit v8 on v7

--- a/solution.py
+++ b/solution.py
@@ -42,20 +42,36 @@
         right[2 * depth : 3 * depth, span] = high
 
 
-def multiply(block, left, right):
-    depth = block.shape[1]
-    high, low = halves(block)
-    left[:, 0:depth] = high
-    left[:, depth : 2 * depth] = high
-    left[:, 2 * depth : 3 * depth] = low
+def pieces_of(group, ny, nz, tile_rows):
+    block = tile_rows // ny
+    end = block // nz
+    return ((0, 0, block), (1, block - end, end)) if group == 0 else ((1, 0, block - end),)
+
+
+def rows_of(group, ny, nz, tile_rows):
+    return sum(piece[2] for piece in pieces_of(group, ny, nz, tile_rows))
+
+
+def rows_at(place, jy, ny, tile_rows, first, count):
+    block = tile_rows // ny
+    at = lax.rem(place[1] + jy, ny) * block + first
+    return pl.ds(pl.multiple_of(at, 32), count)
+
+
+def multiply(place, rows, pieces, jy, ny, left, right):
+    _, tile_rows, depth = rows.shape
+    at = 0
+    for panel, first, count in pieces:
+        high, low = halves(rows[panel, rows_at(place, jy, ny, tile_rows, first, count), :])
+        span = slice(at, at + count)
+        left[span, 0:depth] = high
+        left[span, depth : 2 * depth] = high
+        left[span, 2 * depth : 3 * depth] = low
+        at += count
     return jnp.dot(left[...], right[...], preferred_element_type=F32)
 
 
-def rows_at(place, jy, ny, size):
-    return pl.ds(pl.multiple_of(lax.rem(place[1] + jy, ny) * size, size), size)
-
-
-def product_kernel(panel, by_column, has_received, nx, ny):
+def product_kernel(pieces, by_column, has_received, nx, ny):
     def kernel(place, rows, cols, *refs):
         received = refs[0] if has_received else None
         outs = refs[1:-2] if has_received else refs[:-2]
@@ -63,7 +79,7 @@
         size = left.shape[0]
         split_columns(place, cols, right, nx)
         for jy in range(ny):
-            value = multiply(rows[panel, rows_at(place, jy, ny, size), :], left, right)
+            value = multiply(place, rows, pieces, jy, ny, left, right)
             for jx in range(nx):
                 block = value[:, jx * 128 : (jx + 1) * 128]
                 first, second = (jx, jy) if by_column else (jy, jx)
@@ -76,38 +92,49 @@
     return kernel
 
 
-def first_kernel(nx, ny):
+def first_kernel(pieces, rest, nx, ny):
     def kernel(place, far_rows, far_cols, out, rows, cols, left, right, sems):
         size = left.shape[0]
+        tile_rows = rows.shape[1]
 
         def strip(jx, core, sem):
             at = lax.rem(place[0] + jx, nx) * 256 + core * 128
             at = pl.ds(pl.multiple_of(at, 128), 128)
             return pltpu.make_async_copy(far_cols.at[:, at], cols.at[:, at], sems.at[sem])
 
-        def block(panel, jy, sem):
-            at = rows_at(place, jy, ny, size)
+        def load_of(piece, jy, sem):
+            panel, first, count = piece
+            at = rows_at(place, jy, ny, tile_rows, first, count)
             return pltpu.make_async_copy(
                 far_rows.at[panel, at, :], rows.at[panel, at, :], sems.at[sem]
             )
 
         strips = [strip(jx, place[2], jx) for jx in range(nx)]
-        blocks = [block(0, jy, nx + jy) for jy in range(ny)]
-        later = [strip(jx, 1 - place[2], nx + ny + jx) for jx in range(nx)]
-        later += [block(1, jy, 2 * nx + ny + jy) for jy in range(ny)]
-        for load in strips + blocks[:2]:
+        sem = nx
+        blocks = []
+        for jy in range(ny):
+            blocks.append([load_of(piece, jy, sem + k) for k, piece in enumerate(pieces)])
+            sem += len(pieces)
+        later = [strip(jx, 1 - place[2], sem + jx) for jx in range(nx)]
+        sem += nx
+        for jy in range(ny):
+            later += [load_of(piece, jy, sem + k) for k, piece in enumerate(rest)]
+            sem += len(rest)
+        for load in strips + blocks[0] + blocks[1]:
             load.start()
         for load in strips:
             load.wait()
-        for load in blocks[2:]:
-            load.start()
+        for block in blocks[2:]:
+            for load in block:
+                load.start()
         split_columns(place, cols, right, nx)
         for jy in range(ny):
-            blocks[jy].wait()
+            for load in blocks[jy]:
+                load.wait()
             if jy == 0:
                 for load in later:
                     load.start()
-            value = multiply(rows[0, rows_at(place, jy, ny, size), :], left, right)
+            value = multiply(place, rows, pieces, jy, ny, left, right)
             for jx in range(nx):
                 out[jx, jy * size : (jy + 1) * size, :] = value[:, jx * 128 : (jx + 1) * 128]
         for load in later:
@@ -116,8 +143,8 @@
     return kernel
 
 
-def product_scratch(size, depth, nx, ny):
-    return [pltpu.VMEM((size // ny, 3 * depth), BF16), pltpu.VMEM((3 * depth, nx * 128), BF16)]
+def product_scratch(size, depth, nx):
+    return [pltpu.VMEM((size, 3 * depth), BF16), pltpu.VMEM((3 * depth, nx * 128), BF16)]
 
 
 def product_cost(size, depth, nx):
@@ -126,40 +153,44 @@
     )
 
 
-def first_products(place, rows, cols, nx, ny):
-    _, size, depth = rows.shape
+def first_products(place, rows, cols, nx, ny, nz):
+    _, tile_rows, depth = rows.shape
+    pieces, rest = (pieces_of(group, ny, nz, tile_rows) for group in (0, 1))
+    size = rows_of(0, ny, nz, tile_rows)
+    copies = 2 * nx + ny * (len(pieces) + len(rest))
     return pl.pallas_call(
-        first_kernel(nx, ny),
+        first_kernel(pieces, rest, nx, ny),
         out_shape=(
-            jax.ShapeDtypeStruct((nx, size, 128), F32),
+            jax.ShapeDtypeStruct((nx, ny * size, 128), F32),
             jax.ShapeDtypeStruct(rows.shape, F32),
             jax.ShapeDtypeStruct(cols.shape, F32),
         ),
         in_specs=[SMEM, FAR, FAR],
-        scratch_shapes=product_scratch(size, depth, nx, ny)
-        + [pltpu.SemaphoreType.DMA((2 * nx + 2 * ny,))],
+        scratch_shapes=product_scratch(size, depth, nx) + [pltpu.SemaphoreType.DMA((copies,))],
         compiler_params=PRODUCT,
-        cost_estimate=product_cost(size, depth, nx),
+        cost_estimate=product_cost(ny * size, depth, nx),
     )(place, far(rows), far(cols))
 
 
-def products(place, panel, rows, cols, received, by_column, nx, ny):
-    kernel = product_kernel(panel, by_column, received is not None, nx, ny)
-    _, size, depth = rows.shape
-    first = nx if by_column else ny
+def products(place, group, rows, cols, received, by_column, nx, ny, nz):
+    _, tile_rows, depth = rows.shape
+    size = rows_of(group, ny, nz, tile_rows)
+    pieces = pieces_of(group, ny, nz, tile_rows)
+    kernel = product_kernel(pieces, by_column, received is not None, nx, ny)
+    first, second = (nx, ny) if by_column else (ny, nx)
     if received is None:
-        shapes = jax.ShapeDtypeStruct((first, size, 128), F32)
+        shapes = jax.ShapeDtypeStruct((first, second * size, 128), F32)
         args = (place, rows, cols)
     else:
-        shapes = [jax.ShapeDtypeStruct((size, 128), F32)] * first
+        shapes = [jax.ShapeDtypeStruct((second * size, 128), F32)] * first
         args = (place, rows, cols, received)
     return pl.pallas_call(
         kernel,
         out_shape=shapes,
         in_specs=[SMEM] + [pl.BlockSpec()] * (len(args) - 1),
-        scratch_shapes=product_scratch(size, depth, nx, ny),
+        scratch_shapes=product_scratch(size, depth, nx),
         compiler_params=PRODUCT,
-        cost_estimate=product_cost(size, depth, nx),
+        cost_estimate=product_cost(second * size, depth, nx),
     )(*args)
 
 
@@ -220,9 +251,11 @@
     size = a0.shape[0]
     low = (a0[...] + a1[0:size, :]) + (a2[0:size, :] + a3[0:size, :])
     high = (b0[...] + b1[...]) + (b2[...] + b3[...])
-    for z in range(out.shape[0]):
-        out[z, 0:32, :] = low[z * 32 : (z + 1) * 32, :]
-        out[z, 32:64, :] = high[z * 32 : (z + 1) * 32, :]
+    nz = out.shape[0]
+    for z in range(nz):
+        span = slice(z * 32, (z + 1) * 32)
+        out[z, 0:32, :] = low[span, :]
+        out[z, 32:64, :] = high[span, :] if z < nz - 1 else low[nz * 32 :, :]
 
 
 def apply_kernel(place, tiles, mix0, mix1, mix2, mix3, rest0, rest1, rest2, rest3, out, first, second):
@@ -246,13 +279,13 @@
     own = jnp.stack([x, y, core]).astype(jnp.int32)
     other = jnp.stack([x, y, 1 - core]).astype(jnp.int32)
 
-    to_partner0, panel_rows, solved = first_products(other, panel_rows, solved, nx, ny)
+    to_partner0, panel_rows, solved = first_products(other, panel_rows, solved, nx, ny, nz)
     from_partner0 = shift(to_partner0, "core", 1, nc)
-    to_partner1 = products(other, 1, panel_rows, solved, None, False, nx, ny)
+    to_partner1 = products(other, 1, panel_rows, solved, None, False, nx, ny, nz)
     from_partner1 = shift(to_partner1, "core", 1, nc)
-    blocks0 = products(own, 0, panel_rows, solved, from_partner0, True, nx, ny)
+    blocks0 = products(own, 0, panel_rows, solved, from_partner0, True, nx, ny, nz)
     got0 = [blocks0[0]] + [shift(blocks0[j], "x", j, nx) for j in range(1, nx)]
-    blocks1 = products(own, 1, panel_rows, solved, from_partner1, False, nx, ny)
+    blocks1 = products(own, 1, panel_rows, solved, from_partner1, False, nx, ny, nz)
     got1 = [blocks1[0]] + [shift(blocks1[j], "y", j, ny) for j in range(1, ny)]
 
     packed = pl.pallas_call(

time: 123 us -> 121 us (0.984)
  waiting for transfers between devices: 31.5 us -> 27.8 us
    ppermute x21, waiting for transfers between devices: 28.2 us -> 25.2 us  [shift(): lax.ppermute(value, axis, [(i, (i + step) % size) for i in range(size)])]
    pallas_call x3, Pallas kernels: 9.81 us -> 12.1 us  [products(): pl.pallas_call(kernel, out_shape=shapes, in_specs=[SMEM] + [pl.BlockSpec(...]
    pallas_call x2, Pallas kernels: 1.6 us -> 0.21 us  [gather_sums(): pl.pallas_call(gather_sums_kernel, out_shape=[jax.ShapeDtypeStruct((size,...]
  transfers between devices with their start and end apart: 23 -> 23, of which waited for: 12 -> 10; matrix products, arithmetic and copies ran while one was open for 0% -> 0% of each run, Pallas kernels for 10% -> 13%
where the time goes in v8:
time: 121 us; the launch traced here: 120 us
  starting transfers between devices  46.4 us (38%)
  waiting for transfers between devices  27.8 us (23%)
  Pallas kernels  23.9 us (20%)
  blocking collectives  14.4 us (12%)
  local copies, waits for them, and re-layouts  6.65 us (5%)
    ppermute x21, starting transfers between devices, shift(): lax.ppermute(value, axis, [(i, (i + step) % size) for i in range(size)])  31 us
    ppermute x21, waiting for transfers between devices, shift(): lax.ppermute(value, axis, [(i, (i + step) % size) for i in range(size)])  25.2 us
    all_to_all x1, blocking collectives, steps(): panels = lax.all_to_all(solved_part, 'z', 0, 0, tiled=True).sum(axis=0)  14.4 us
    pallas_call x3, Pallas kernels, products(): pl.pallas_call(kernel, out_shape=shapes, in_specs=[SMEM] + [pl.BlockSpec(...  12.1 us
    all_to_all x1, starting transfers between devices, steps(): tiles = lax.all_to_all(packed, 'z', 0, 0, tiled=True).reshape(nz * 32, 512)  8.47 us
    all_to_all x1, starting transfers between devices, steps(): old = lax.all_to_all(by_z, 'z', 0, 0, tiled=True).sum(axis=0)  6.93 us
    unnamed x24, local copies, waits for them, and re-layouts  6.65 us
    pallas_call x1, Pallas kernels, first_products(): pl.pallas_call(first_kernel(pieces, rest, nx, ny), out_shape=(jax.ShapeDt...  5.86 us
  transfers between devices with their start and end apart: 23, of which 10 were waited for; matrix products, arithmetic and copies ran while one was open for 0% of the time, Pallas kernels for 13%

profile of v8, /device:TPU:2, one launch (start us, length us, event | category | flops | bytes accessed | tf_op | source)
XLA Modules:
  0.0 120.1 jit_solution(13004803102384456578)
XLA Ops:
  0.0 0.1 pad_add_fusion.2.place
  0.1 5.9 %shard_map.57 = (f32[4,1152,128]{2,1,0:T(8,128)}, f32[2,1024,384]{2,1,0:T(8,128)S(1)}, f32[384,1024]{1,0:T(8,128)S(1)}) custom-call(s32[3]{0:T(128)S(1)} %pad_add_fusion.2.place, f32[2,1024,384]{2,1,0:T(8,128)} %far_rows.1, f32[384,1024]{1,0:T(8,128)} %far_cols.1), custom_call_target="tpu_custom_call" | custom-call | flops 1358954496 | bytes 6291456 | tf_op jit(solution)/shard_map/pallas_call | solution.py:161
  6.0 0.1 collective-permute-start
  6.1 0.0 copy-start.9
  6.1 0.0 copy-start.10
  6.1 3.5 %shard_map.62 = f32[4,896,128]{2,1,0:T(8,128)} custom-call(s32[3]{0:T(128)S(1)} %pad_add_fusion.2.place, f32[2,1024,384]{2,1,0:T(8,128)S(1)} %get-tuple-element.24.rows, f32[384,1024]{1,0:T(8,128)S(1)} %get-tuple-element.25.cols), custom_call_target="tpu_custom_call" | custom-call | flops 1056964608 | bytes 6291456 | tf_op jit(solution)/shard_map/pallas_call | solution.py:187
  9.5 0.5 collective-permute-start.11
  10.0 0.1 pad_add_fusion.place
  10.1 0.8 shard_map.55
  10.9 0.8 copy-done.2
  11.7 8.5 %all-to-all-start = ((f32[8,32,512]{2,1,0:T(8,128)}), f32[8,32,512]{2,1,0:T(8,128)}, u32[]{:S(2)}, u32[]{:S(2)}) async-start(f32[8,32,512]{2,1,0:T(8,128)} %copy-done.2), calls=%async_computation | async-start | bytes 1048576 | tf_op jit(solution)/shard_map/all_to_all | solution.py:297
  20.2 1.4 %copy-done.1 = f32[384,1024]{1,0:T(8,128)S(1)} copy-done((f32[384,1024]{1,0:T(8,128)S(1)}, f32[384,1024]{1,0:T(8,128)}, u32[]{:S(2)}) %copy-start.1) | copy-done | bytes 1572888
  21.6 3.9 %shard_map.63 = (f32[896,128]{1,0:T(8,128)S(1)}, f32[896,128]{1,0:T(8,128)S(1)}, f32[896,128]{1,0:T(8,128)}, f32[896,128]{1,0:T(8,128)}) custom-call(s32[3]{0:T(128)S(1)} %pad_add_fusion.place, f32[2,1024,384]{2,1,0:T(8,128)S(1)} %get-tuple-element.24.rows, f32[384,1024]{1,0:T(8,128)S(1)} %copy-done.1, f32[4,896,128]{2,1,0:T(8,128)} %collective-permute-done.11.refs_0_), custom_call_target="tpu_custom_call" | custom-call | flops 1056964608 | bytes 6291456 | tf_op jit(solution)/shard_map/pallas_call | solution.py:187
  25.5 0.8 copy-done.5
  26.2 1.6 %collective-permute-start.12 = (f32[896,128]{1,0:T(8,128)S(1)}, f32[896,128]{1,0:T(8,128)S(1)}, u32[]{:S(2)}, u32[]{:S(2)}) collective-permute-start(f32[896,128]{1,0:T(8,128)S(1)} %get-tuple-element.36), channel_id=1, source_target_pairs={{0,64},{64,128},{128,192},{192,0},{1,65},{65,129},{129,193},{193,1... | collective-permute-start | bytes 1376264 | tf_op jit(solution)/shard_map/ppermute | solution.py:26
  27.8 0.0 collective-permute-done.refs_0_
  27.8 4.8 %shard_map.58 = (f32[1152,128]{1,0:T(8,128)S(1)}, f32[1152,128]{1,0:T(8,128)}, f32[1152,128]{1,0:T(8,128)}, f32[1152,128]{1,0:T(8,128)}) custom-call(s32[3]{0:T(128)S(1)} %pad_add_fusion.place, f32[2,1024,384]{2,1,0:T(8,128)S(1)} %get-tuple-element.24.rows, f32[384,1024]{1,0:T(8,128)S(1)} %copy-done.1, f32[4,1152,128]{2,1,0:T(8,128)} %collective-permute-done.refs_0_), custom_call_target="tpu_custom_call" | custom-call | flops 1358954496 | bytes 6291456 | tf_op jit(solution)/shard_map/pallas_call | solution.py:187
  32.6 0.8 copy-done.3
  33.4 1.5 %collective-permute-start.1 = (f32[1152,128]{1,0:T(8,128)}, f32[1152,128]{1,0:T(8,128)S(1)}, u32[]{:S(2)}, u32[]{:S(2)}) collective-permute-start(f32[1152,128]{1,0:T(8,128)} %get-tuple-element.28), channel_id=1, source_target_pairs={{0,2},{2,4},{4,6},{6,0},{1,3},{3,5},{5,7},{7,1},{8,10},{10,12},{12... | collective-permute-start | bytes 1769480 | tf_op jit(solution)/shard_map/ppermute | solution.py:26
  34.9 1.1 collective-permute-start.2
  36.0 2.1 %collective-permute-start.3 = (f32[1152,128]{1,0:T(8,128)}, f32[1152,128]{1,0:T(8,128)S(1)}, u32[]{:S(2)}, u32[]{:S(2)}) collective-permute-start(f32[1152,128]{1,0:T(8,128)} %get-tuple-element.30), channel_id=1, source_target_pairs={{0,6},{2,0},{4,2},{6,4},{1,7},{3,1},{5,3},{7,5},{8,14},{10,8},{12,... | collective-permute-start | bytes 1769480 | tf_op jit(solution)/shard_map/ppermute | solution.py:26
  38.2 2.9 %collective-permute-start.13 = (f32[896,128]{1,0:T(8,128)}, f32[896,128]{1,0:T(8,128)S(1)}, u32[]{:S(2)}, u32[]{:S(2)}) collective-permute-start(f32[896,128]{1,0:T(8,128)} %get-tuple-element.37), channel_id=1, source_target_pairs={{0,128},{64,192},{128,0},{192,64},{1,129},{65,193},{129,1},{193,65... | collective-permute-start | bytes 1376264 | tf_op jit(solution)/shard_map/ppermute | solution.py:26
  41.1 0.8 copy-done.7
  41.9 1.3 %collective-permute-start.14 = (f32[896,128]{1,0:T(8,128)}, f32[896,128]{1,0:T(8,128)S(1)}, u32[]{:S(2)}, u32[]{:S(2)}) collective-permute-start(f32[896,128]{1,0:T(8,128)} %get-tuple-element.38), channel_id=1, source_target_pairs={{0,192},{64,0},{128,64},{192,128},{1,193},{65,1},{129,65},{193,129... | collective-permute-start | bytes 1376264 | tf_op jit(solution)/shard_map/ppermute | solution.py:26
  43.2 0.0 all-to-all-done
  43.2 1.3 %shard_map.56.rider.part0 = f32[128,128]{1,0:T(8,128)S(1)} custom-call(f32[256,512]{1,0:T(8,128)} %bitcast.4.tiles), custom_call_target="tpu_custom_call" | custom-call | tf_op jit(solution)/shard_map/pallas_call | solution.py:299
  44.6 6.4 %collective-permute-done.13.c = f32[896,128]{1,0:T(8,128)S(1)} collective-permute-done((f32[896,128]{1,0:T(8,128)}, f32[896,128]{1,0:T(8,128)S(1)}, u32[]{:S(2)}, u32[]{:S(2)}) %collective-permute-start.13) | collective-permute-done | bytes 458784 | tf_op jit(solution)/shard_map/ppermute | solution.py:26
  51.0 8.9 %collective-permute-done.14.d = f32[896,128]{1,0:T(8,128)S(1)} collective-permute-done((f32[896,128]{1,0:T(8,128)}, f32[896,128]{1,0:T(8,128)S(1)}, u32[]{:S(2)}, u32[]{:S(2)}) %collective-permute-start.14) | collective-permute-done | bytes 458784 | tf_op jit(solution)/shard_map/ppermute | solution.py:26
  59.9 1.0 copy-done.6
  61.0 1.0 copy-done.8
  62.0 0.1 shard_map.64
  62.1 0.3 collective-permute-start.15
  62.3 0.0 collective-permute-done.1.b
  62.4 0.0 collective-permute-done.2.c
  62.4 0.7 collective-permute-done.3.d
  63.1 0.1 shard_map.59
  63.2 0.0 copy-start.11
  63.2 1.9 %collective-permute-start.4 = (f32[416,128]{1,0:T(8,128)S(1)}, f32[416,128]{1,0:T(8,128)S(1)}, u32[]{:S(2)}, u32[]{:S(2)}) collective-permute-start(f32[416,128]{1,0:T(8,128)S(1)} %get-tuple-element.31), channel_id=1, source_target_pairs={{0,64},{64,128},{128,192},{192,0},{1,65},{65,129},{129,193},{193,1... | collective-permute-start | bytes 638984 | tf_op jit(solution)/shard_map/ppermute | solution.py:26
  65.1 1.6 %collective-permute-start.5 = (f32[416,128]{1,0:T(8,128)S(1)}, f32[416,128]{1,0:T(8,128)S(1)}, u32[]{:S(2)}, u32[]{:S(2)}) collective-permute-start(f32[416,128]{1,0:T(8,128)S(1)} %get-tuple-element.32), channel_id=1, source_target_pairs={{0,128},{64,192},{128,0},{192,64},{1,129},{65,193},{129,1},{193,65... | collective-permute-start | bytes 638984 | tf_op jit(solution)/shard_map/ppermute | solution.py:26
  66.7 2.1 %collective-permute-start.6 = (f32[416,128]{1,0:T(8,128)S(1)}, f32[416,128]{1,0:T(8,128)S(1)}, u32[]{:S(2)}, u32[]{:S(2)}) collective-permute-start(f32[416,128]{1,0:T(8,128)S(1)} %get-tuple-element.33), channel_id=1, source_target_pairs={{0,192},{64,0},{128,64},{192,128},{1,193},{65,1},{129,65},{193,129... | collective-permute-start | bytes 638984 | tf_op jit(solution)/shard_map/ppermute | solution.py:26
  68.8 3.0 %collective-permute-start.16 = (f32[224,128]{1,0:T(8,128)S(1)}, f32[224,128]{1,0:T(8,128)S(1)}, u32[]{:S(2)}, u32[]{:S(2)}) collective-permute-start(f32[224,128]{1,0:T(8,128)S(1)} %get-tuple-element.41), channel_id=1, source_target_pairs={{0,4},{2,6},{4,0},{6,2},{1,5},{3,7},{5,1},{7,3},{8,12},{10,14},{12... | collective-permute-start | bytes 344072 | tf_op jit(solution)/shard_map/ppermute | solution.py:26
  71.8 0.3 collective-permute-start.17
  72.2 3.1 %collective-permute-done.16.b2 = f32[224,128]{1,0:T(8,128)S(1)} collective-permute-done((f32[224,128]{1,0:T(8,128)S(1)}, f32[224,128]{1,0:T(8,128)S(1)}, u32[]{:S(2)}, u32[]{:S(2)}) %collective-permute-start.16) | collective-permute-done | bytes 114720 | tf_op jit(solution)/shard_map/ppermute | solution.py:26
  75.2 1.4 %collective-permute-done.17.b3 = f32[224,128]{1,0:T(8,128)S(1)} collective-permute-done((f32[224,128]{1,0:T(8,128)S(1)}, f32[224,128]{1,0:T(8,128)S(1)}, u32[]{:S(2)}, u32[]{:S(2)}) %collective-permute-start.17) | collective-permute-done | bytes 114720 | tf_op jit(solution)/shard_map/ppermute | solution.py:26
  76.6 0.0 collective-permute-done.5.got2.a2
  76.6 0.0 collective-permute-done.6.got3.a3
  76.6 0.7 shard_map.65
  77.4 6.9 %all-to-all-start.1 = ((f32[8,64,128]{2,1,0:T(8,128)}), f32[8,64,128]{2,1,0:T(8,128)S(1)}, u32[]{:S(2)}, u32[]{:S(2)}) async-start(f32[8,64,128]{2,1,0:T(8,128)} %shard_map.65), calls=%async_computation.1 | async-start | bytes 524288 | tf_op jit(solution)/shard_map/all_to_all | solution.py:319
  84.3 1.3 %shard_map.60.a = f32[256,128]{1,0:T(8,128)S(1)} custom-call(f32[256,512]{1,0:T(8,128)} %bitcast.4.tiles, f32[128,128]{1,0:T(8,128)S(1)} %shard_map.56.rider.part0, f32[416,128]{1,0:T(8,128)S(1)} %collective-permute-done.4.got1.a1, f32[416,128]{1,0:T(8,128)S(1)} %collective-permute-done.5.got2.a2, f32[416,128]{1,0:T(8,128)S(1)} %collective-permute-done.6.got3.a3), custom_call_target="tpu_custom_call" | custom-call | tf_op jit(solution)/shard_map/pallas_call | solution.py:306
  85.6 0.1 collective-permute-start.7
  85.7 1.3 %collective-permute-done.7.b = f32[256,128]{1,0:T(8,128)S(1)} collective-permute-done((f32[256,128]{1,0:T(8,128)S(1)}, f32[256,128]{1,0:T(8,128)S(1)}, u32[]{:S(2)}, u32[]{:S(2)}) %collective-permute-start.7) | collective-permute-done | bytes 131104 | tf_op jit(solution)/shard_map/ppermute | solution.py:26
  87.1 0.6 collective-permute-start.8
  87.7 3.0 %collective-permute-start.9 = (f32[256,128]{1,0:T(8,128)S(1)}, f32[256,128]{1,0:T(8,128)S(1)}, u32[]{:S(2)}, u32[]{:S(2)}) collective-permute-start(f32[256,128]{1,0:T(8,128)S(1)} %shard_map.61.mix0), channel_id=1, source_target_pairs={{0,4},{2,6},{4,0},{6,2},{1,5},{3,7},{5,1},{7,3},{8,12},{10,14},{12... | collective-permute-start | bytes 393224 | tf_op jit(solution)/shard_map/ppermute | solution.py:26
  90.7 2.0 %collective-permute-start.10 = (f32[256,128]{1,0:T(8,128)S(1)}, f32[256,128]{1,0:T(8,128)S(1)}, u32[]{:S(2)}, u32[]{:S(2)}) collective-permute-start(f32[256,128]{1,0:T(8,128)S(1)} %shard_map.61.mix0), channel_id=1, source_target_pairs={{0,6},{2,0},{4,2},{6,4},{1,7},{3,1},{5,3},{7,5},{8,14},{10,8},{12,... | collective-permute-start | bytes 393224 | tf_op jit(solution)/shard_map/ppermute | solution.py:26
  92.7 2.6 %all-to-all-done.1 = f32[8,64,128]{2,1,0:T(8,128)S(1)} async-done(((f32[8,64,128]{2,1,0:T(8,128)}), f32[8,64,128]{2,1,0:T(8,128)S(1)}, u32[]{:S(2)}, u32[]{:S(2)}) %all-to-all-start.1) | async-done | bytes 262176 | tf_op jit(solution)/shard_map/all_to_all | solution.py:319
  95.3 2.1 %collective-permute-start.18 = (f32[64,128]{1,0:T(8,128)S(1)}, f32[64,128]{1,0:T(8,128)S(1)}, u32[]{:S(2)}, u32[]{:S(2)}) collective-permute-start(f32[64,128]{1,0:T(8,128)S(1)} %bitcast_subtract_fusion.rest0), channel_id=1, source_target_pairs={{0,64},{64,128},{128,192},{192,0},{1,65},{65,129},{129,193},{193,1... | collective-permute-start | bytes 98312 | tf_op jit(solution)/shard_map/ppermute | solution.py:26
  97.4 2.2 %collective-permute-start.19 = (f32[64,128]{1,0:T(8,128)S(1)}, f32[64,128]{1,0:T(8,128)S(1)}, u32[]{:S(2)}, u32[]{:S(2)}) collective-permute-start(f32[64,128]{1,0:T(8,128)S(1)} %bitcast_subtract_fusion.rest0), channel_id=1, source_target_pairs={{0,128},{64,192},{128,0},{192,64},{1,129},{65,193},{129,1},{193,65... | collective-permute-start | bytes 98312 | tf_op jit(solution)/shard_map/ppermute | solution.py:26
  99.6 0.6 collective-permute-start.20
  100.2 0.3 collective-permute-done.18.rest1
  100.5 2.3 %collective-permute-done.19.rest2 = f32[64,128]{1,0:T(8,128)S(1)} collective-permute-done((f32[64,128]{1,0:T(8,128)S(1)}, f32[64,128]{1,0:T(8,128)S(1)}, u32[]{:S(2)}, u32[]{:S(2)}) %collective-permute-start.19) | collective-permute-done | bytes 32800 | tf_op jit(solution)/shard_map/ppermute | solution.py:26
  102.8 0.7 collective-permute-done.20.rest3
  103.5 1.5 %shard_map.66 = f32[8,64,128]{2,1,0:T(8,128)S(1)} custom-call(s32[3]{0:T(128)S(1)} %pad_add_fusion.place, f32[256,512]{1,0:T(8,128)} %bitcast.4.tiles, f32[256,128]{1,0:T(8,128)S(1)} %shard_map.61.mix0, f32[256,128]{1,0:T(8,128)S(1)} %collective-permute-done.8.mix1, f32[256,128]{1,0:T(8,128)S(1)} %collective-permute-done.9.mix2, ...), custom_call_target="tpu_custom_call" | custom-call | tf_op jit(solution)/shard_map/pallas_call | solution.py:323
  105.1 14.4 %all_to_all.15 = f32[8,64,128]{2,1,0:T(8,128)S(1)} all-to-all(f32[8,64,128]{2,1,0:T(8,128)S(1)} %shard_map.66), channel_id=1, replica_groups=mesh['y'=4,'z'=8,'x'=4,'core'=2] {'z'}, dimensions={0} | all-to-all | bytes 524288 | tf_op jit(solution)/shard_map/all_to_all | solution.py:330
  119.4 0.6 reduce_sum.19
  (24 shorter events, 0.1 us)
Async XLA Ops:
  5.9 3.6 %copy-start = (f32[384,1024]{1,0:T(8,128)}, f32[384,1024]{1,0:T(8,128)S(1)}, u32[]{:S(2)}) copy-start(f32[384,1024]{1,0:T(8,128)S(1)} %get-tuple-element.25.cols) | copy-start | bytes 4718596
  6.0 21.9 %collective-permute-start = (f32[4,1152,128]{2,1,0:T(8,128)}, f32[4,1152,128]{2,1,0:T(8,128)}, u32[]{:S(2)}, u32[]{:S(2)}) collective-permute-start(f32[4,1152,128]{2,1,0:T(8,128)} %get-tuple-element.26), channel_id=1, source_target_pairs={{0,1},{1,0},{2,3},{3,2},{4,5},{5,4},{6,7},{7,6},{8,9},{9,8},{10,11... | collective-permute-start | bytes 7077896 | tf_op jit(solution)/shard_map/ppermute | solution.py:26
  6.1 4.0 %copy-start.9 = (f32[2,32,1024]{2,1,0:T(8,128)S(1)}, f32[2,32,1024]{2,1,0:T(8,128)}, u32[]{:S(2)}) copy-start(f32[2,32,1024]{2,1,0:T(8,128)} %inverses.1) | copy-start | bytes 786436
  6.1 4.0 %copy-start.10 = (f32[1024,32]{0,1:T(8,128)S(1)}, f32[1024,32]{0,1:T(8,128)}, u32[]{:S(2)}) copy-start(f32[1024,32]{0,1:T(8,128)} %param.8) | copy-start | bytes 393220
  9.5 10.6 %collective-permute-start.11 = (f32[4,896,128]{2,1,0:T(8,128)}, f32[4,896,128]{2,1,0:T(8,128)}, u32[]{:S(2)}, u32[]{:S(2)}) collective-permute-start(f32[4,896,128]{2,1,0:T(8,128)} %shard_map.62), channel_id=1, source_target_pairs={{0,1},{1,0},{2,3},{3,2},{4,5},{5,4},{6,7},{7,6},{8,9},{9,8},{10,11... | collective-permute-start | bytes 5505032 | tf_op jit(solution)/shard_map/ppermute | solution.py:26
  10.9 0.8 copy-start.2
  11.7 31.5 %all-to-all-start = ((f32[8,32,512]{2,1,0:T(8,128)}), f32[8,32,512]{2,1,0:T(8,128)}, u32[]{:S(2)}, u32[]{:S(2)}) async-start(f32[8,32,512]{2,1,0:T(8,128)} %copy-done.2), calls=%async_computation | async-start | bytes 1048576 | tf_op jit(solution)/shard_map/all_to_all | solution.py:297
  20.2 1.4 %copy-start.1 = (f32[384,1024]{1,0:T(8,128)S(1)}, f32[384,1024]{1,0:T(8,128)}, u32[]{:S(2)}) copy-start(f32[384,1024]{1,0:T(8,128)} %copy-done) | copy-start | bytes 4718596
  25.5 0.8 copy-start.5
  26.2 14.9 %collective-permute-start.12 = (f32[896,128]{1,0:T(8,128)S(1)}, f32[896,128]{1,0:T(8,128)S(1)}, u32[]{:S(2)}, u32[]{:S(2)}) collective-permute-start(f32[896,128]{1,0:T(8,128)S(1)} %get-tuple-element.36), channel_id=1, source_target_pairs={{0,64},{64,128},{128,192},{192,0},{1,65},{65,129},{129,193},{193,1... | collective-permute-start | bytes 1376264 | tf_op jit(solution)/shard_map/ppermute | solution.py:26
  32.6 0.8 copy-start.3
  33.4 29.7 %copy-start.4 = (f32[1152,128]{1,0:T(8,128)S(1)}, f32[1152,128]{1,0:T(8,128)}, u32[]{:S(2)}) copy-start(f32[1152,128]{1,0:T(8,128)} %copy-done.3) | copy-start | bytes 1769476
  33.4 28.9 %collective-permute-start.1 = (f32[1152,128]{1,0:T(8,128)}, f32[1152,128]{1,0:T(8,128)S(1)}, u32[]{:S(2)}, u32[]{:S(2)}) collective-permute-start(f32[1152,128]{1,0:T(8,128)} %get-tuple-element.28), channel_id=1, source_target_pairs={{0,2},{2,4},{4,6},{6,0},{1,3},{3,5},{5,7},{7,1},{8,10},{10,12},{12... | collective-permute-start | bytes 1769480 | tf_op jit(solution)/shard_map/ppermute | solution.py:26
  34.9 27.4 %collective-permute-start.2 = (f32[1152,128]{1,0:T(8,128)}, f32[1152,128]{1,0:T(8,128)S(1)}, u32[]{:S(2)}, u32[]{:S(2)}) collective-permute-start(f32[1152,128]{1,0:T(8,128)} %get-tuple-element.29), channel_id=1, source_target_pairs={{0,4},{2,6},{4,0},{6,2},{1,5},{3,7},{5,1},{7,3},{8,12},{10,14},{12... | collective-permute-start | bytes 1769480 | tf_op jit(solution)/shard_map/ppermute | solution.py:26
  36.0 27.0 %collective-permute-start.3 = (f32[1152,128]{1,0:T(8,128)}, f32[1152,128]{1,0:T(8,128)S(1)}, u32[]{:S(2)}, u32[]{:S(2)}) collective-permute-start(f32[1152,128]{1,0:T(8,128)} %get-tuple-element.30), channel_id=1, source_target_pairs={{0,6},{2,0},{4,2},{6,4},{1,7},{3,1},{5,3},{7,5},{8,14},{10,8},{12,... | collective-permute-start | bytes 1769480 | tf_op jit(solution)/shard_map/ppermute | solution.py:26
  38.2 12.8 %collective-permute-start.13 = (f32[896,128]{1,0:T(8,128)}, f32[896,128]{1,0:T(8,128)S(1)}, u32[]{:S(2)}, u32[]{:S(2)}) collective-permute-start(f32[896,128]{1,0:T(8,128)} %get-tuple-element.37), channel_id=1, source_target_pairs={{0,128},{64,192},{128,0},{192,64},{1,129},{65,193},{129,1},{193,65... | collective-permute-start | bytes 1376264 | tf_op jit(solution)/shard_map/ppermute | solution.py:26
  41.1 0.8 copy-start.7
  41.9 18.1 %collective-permute-start.14 = (f32[896,128]{1,0:T(8,128)}, f32[896,128]{1,0:T(8,128)S(1)}, u32[]{:S(2)}, u32[]{:S(2)}) collective-permute-start(f32[896,128]{1,0:T(8,128)} %get-tuple-element.38), channel_id=1, source_target_pairs={{0,192},{64,0},{128,64},{192,128},{1,193},{65,1},{129,65},{193,129... | collective-permute-start | bytes 1376264 | tf_op jit(solution)/shard_map/ppermute | solution.py:26
  59.9 1.0 copy-start.6
  61.0 1.0 copy-start.8
  62.1 9.8 %collective-permute-start.15 = (f32[224,128]{1,0:T(8,128)S(1)}, f32[224,128]{1,0:T(8,128)S(1)}, u32[]{:S(2)}, u32[]{:S(2)}) collective-permute-start(f32[224,128]{1,0:T(8,128)S(1)} %get-tuple-element.40), channel_id=1, source_target_pairs={{0,2},{2,4},{4,6},{6,0},{1,3},{3,5},{5,7},{7,1},{8,10},{10,12},{12... | collective-permute-start | bytes 344072 | tf_op jit(solution)/shard_map/ppermute | solution.py:26
  63.2 32.1 %copy-start.11 = (f32[2,32,128]{2,1,0:T(8,128)S(1)}, f32[2,32,128]{2,1,0:T(8,128)}, u32[]{:S(2)}) copy-start(f32[2,32,128]{2,1,0:T(8,128)} %param.7) | copy-start | bytes 98308
  63.2 13.4 %collective-permute-start.4 = (f32[416,128]{1,0:T(8,128)S(1)}, f32[416,128]{1,0:T(8,128)S(1)}, u32[]{:S(2)}, u32[]{:S(2)}) collective-permute-start(f32[416,128]{1,0:T(8,128)S(1)} %get-tuple-element.31), channel_id=1, source_target_pairs={{0,64},{64,128},{128,192},{192,0},{1,65},{65,129},{129,193},{193,1... | collective-permute-start | bytes 638984 | tf_op jit(solution)/shard_map/ppermute | solution.py:26
  65.1 11.5 %collective-permute-start.5 = (f32[416,128]{1,0:T(8,128)S(1)}, f32[416,128]{1,0:T(8,128)S(1)}, u32[]{:S(2)}, u32[]{:S(2)}) collective-permute-start(f32[416,128]{1,0:T(8,128)S(1)} %get-tuple-element.32), channel_id=1, source_target_pairs={{0,128},{64,192},{128,0},{192,64},{1,129},{65,193},{129,1},{193,65... | collective-permute-start | bytes 638984 | tf_op jit(solution)/shard_map/ppermute | solution.py:26
  66.7 9.9 %collective-permute-start.6 = (f32[416,128]{1,0:T(8,128)S(1)}, f32[416,128]{1,0:T(8,128)S(1)}, u32[]{:S(2)}, u32[]{:S(2)}) collective-permute-start(f32[416,128]{1,0:T(8,128)S(1)} %get-tuple-element.33), channel_id=1, source_target_pairs={{0,192},{64,0},{128,64},{192,128},{1,193},{65,1},{129,65},{193,129... | collective-permute-start | bytes 638984 | tf_op jit(solution)/shard_map/ppermute | solution.py:26
  68.8 6.4 %collective-permute-start.16 = (f32[224,128]{1,0:T(8,128)S(1)}, f32[224,128]{1,0:T(8,128)S(1)}, u32[]{:S(2)}, u32[]{:S(2)}) collective-permute-start(f32[224,128]{1,0:T(8,128)S(1)} %get-tuple-element.41), channel_id=1, source_target_pairs={{0,4},{2,6},{4,0},{6,2},{1,5},{3,7},{5,1},{7,3},{8,12},{10,14},{12... | collective-permute-start | bytes 344072 | tf_op jit(solution)/shard_map/ppermute | solution.py:26
  71.8 4.8 %collective-permute-start.17 = (f32[224,128]{1,0:T(8,128)S(1)}, f32[224,128]{1,0:T(8,128)S(1)}, u32[]{:S(2)}, u32[]{:S(2)}) collective-permute-start(f32[224,128]{1,0:T(8,128)S(1)} %get-tuple-element.42), channel_id=1, source_target_pairs={{0,6},{2,0},{4,2},{6,4},{1,7},{3,1},{5,3},{7,5},{8,14},{10,8},{12,... | collective-permute-start | bytes 344072 | tf_op jit(solution)/shard_map/ppermute | solution.py:26
  77.4 17.9 %all-to-all-start.1 = ((f32[8,64,128]{2,1,0:T(8,128)}), f32[8,64,128]{2,1,0:T(8,128)S(1)}, u32[]{:S(2)}, u32[]{:S(2)}) async-start(f32[8,64,128]{2,1,0:T(8,128)} %shard_map.65), calls=%async_computation.1 | async-start | bytes 524288 | tf_op jit(solution)/shard_map/all_to_all | solution.py:319
  85.6 1.4 %collective-permute-start.7 = (f32[256,128]{1,0:T(8,128)S(1)}, f32[256,128]{1,0:T(8,128)S(1)}, u32[]{:S(2)}, u32[]{:S(2)}) collective-permute-start(f32[256,128]{1,0:T(8,128)S(1)} %shard_map.60.a), channel_id=1, source_target_pairs={{0,1},{1,0},{2,3},{3,2},{4,5},{5,4},{6,7},{7,6},{8,9},{9,8},{10,11... | collective-permute-start | bytes 393224 | tf_op jit(solution)/shard_map/ppermute | solution.py:26
  87.1 12.6 %collective-permute-start.8 = (f32[256,128]{1,0:T(8,128)S(1)}, f32[256,128]{1,0:T(8,128)S(1)}, u32[]{:S(2)}, u32[]{:S(2)}) collective-permute-start(f32[256,128]{1,0:T(8,128)S(1)} %shard_map.61.mix0), channel_id=1, source_target_pairs={{0,2},{2,4},{4,6},{6,0},{1,3},{3,5},{5,7},{7,1},{8,10},{10,12},{12... | collective-permute-start | bytes 393224 | tf_op jit(solution)/shard_map/ppermute | solution.py:26
  87.7 12.5 %collective-permute-start.9 = (f32[256,128]{1,0:T(8,128)S(1)}, f32[256,128]{1,0:T(8,128)S(1)}, u32[]{:S(2)}, u32[]{:S(2)}) collective-permute-start(f32[256,128]{1,0:T(8,128)S(1)} %shard_map.61.mix0), channel_id=1, source_target_pairs={{0,4},{2,6},{4,0},{6,2},{1,5},{3,7},{5,1},{7,3},{8,12},{10,14},{12... | collective-permute-start | bytes 393224 | tf_op jit(solution)/shard_map/ppermute | solution.py:26
  90.7 9.5 %collective-permute-start.10 = (f32[256,128]{1,0:T(8,128)S(1)}, f32[256,128]{1,0:T(8,128)S(1)}, u32[]{:S(2)}, u32[]{:S(2)}) collective-permute-start(f32[256,128]{1,0:T(8,128)S(1)} %shard_map.61.mix0), channel_id=1, source_target_pairs={{0,6},{2,0},{4,2},{6,4},{1,7},{3,1},{5,3},{7,5},{8,14},{10,8},{12,... | collective-permute-start | bytes 393224 | tf_op jit(solution)/shard_map/ppermute | solution.py:26
  95.3 5.2 %collective-permute-start.18 = (f32[64,128]{1,0:T(8,128)S(1)}, f32[64,128]{1,0:T(8,128)S(1)}, u32[]{:S(2)}, u32[]{:S(2)}) collective-permute-start(f32[64,128]{1,0:T(8,128)S(1)} %bitcast_subtract_fusion.rest0), channel_id=1, source_target_pairs={{0,64},{64,128},{128,192},{192,0},{1,65},{65,129},{129,193},{193,1... | collective-permute-start | bytes 98312 | tf_op jit(solution)/shard_map/ppermute | solution.py:26
  97.4 5.4 %collective-permute-start.19 = (f32[64,128]{1,0:T(8,128)S(1)}, f32[64,128]{1,0:T(8,128)S(1)}, u32[]{:S(2)}, u32[]{:S(2)}) collective-permute-start(f32[64,128]{1,0:T(8,128)S(1)} %bitcast_subtract_fusion.rest0), channel_id=1, source_target_pairs={{0,128},{64,192},{128,0},{192,64},{1,129},{65,193},{129,1},{193,65... | collective-permute-start | bytes 98312 | tf_op jit(solution)/shard_map/ppermute | solution.py:26
  99.6 3.9 %collective-permute-start.20 = (f32[64,128]{1,0:T(8,128)S(1)}, f32[64,128]{1,0:T(8,128)S(1)}, u32[]{:S(2)}, u32[]{:S(2)}) collective-permute-start(f32[64,128]{1,0:T(8,128)S(1)} %bitcast_subtract_fusion.rest0), channel_id=1, source_target_pairs={{0,192},{64,0},{128,64},{192,128},{1,193},{65,1},{129,65},{193,129... | collective-permute-start | bytes 98312 | tf_op jit(solution)/shard_map/ppermute | solution.py:26
